TPU v7x, 512 devices: a whole 4x8x8 slice. The times are simulated.
512 devices in a mesh: dp: 4 (over x), tensor: 128 (over z, y, core).
Axes of the slice: x: 4, y: 8, z: 8, core: 2. Of those that a mesh axis runs over, the one named last changes fastest.
Arguments:
- hidden: bfloat16 [8192, 2048], P(('dp', 'tensor')), may hold values from -6 to 6
- norm_gain: float32 [2048], replicated, may hold values from 0.5 to 1.5
- head_weight: bfloat16 [2048, 102400], P('dp', 'tensor'), as said below
- token_ids: int32 [8192], P(('dp', 'tensor')), may hold values from 0 to 102399
- lengths: int32 [4, 4], P('dp'), may hold values from 1 to 512, 1024 in all within a row
Outputs:
- logprob: float32 [8192], P(('dp', 'tensor'))
- entropy: float32 [8192], P(('dp', 'tensor'))
Inputs may be any that keep to these rules, and one draw needn't show every extreme that they name: Each index of dp has 4 lengths that sum to exactly 1024, and one of them equals 512. `head_weight`: head weights.
All inputs are finite; a program needn't handle non-finite values.
Results may differ from a plain program's by a relative error of at most 0.0045.
Values may be sent and summed in bfloat16 or wider, within the bound.
No kernel may reach another device: no remote copies, remote signals or barrier semaphores. Data moves between devices by JAX's collectives and lax.ppermute only.
A program may use at most 64 MiB of HBM per device.

v0:
```python
import jax
import jax.numpy as jnp
from jax import lax
from jax.sharding import PartitionSpec as P

SEQ_DP = 4
SLOT = 512


def per_device(hidden, norm_gain, head_weight, token_ids, lengths):
    row_dev = hidden.shape[0]
    tensor_idx = lax.axis_index("tensor")
    wide = hidden.astype(jnp.float32)
    meansq = jnp.mean(wide * wide, axis=-1, keepdims=True)
    normed = (wide * lax.rsqrt(meansq + 1e-06) * norm_gain).astype(jnp.bfloat16)
    weight = lax.all_gather(head_weight, "dp", axis=0, tiled=True)
    vocab_dev = weight.shape[1]
    vstart = tensor_idx * vocab_dev
    seq_len = lengths[0]
    seq_iota = jnp.arange(SEQ_DP, dtype=jnp.int32)
    vocab_iota = jnp.arange(vocab_dev, dtype=jnp.int32)
    own_rows = tensor_idx * row_dev + jnp.arange(row_dev, dtype=jnp.int32)
    logits = jnp.dot(
        lax.all_gather(normed, "tensor", axis=0, tiled=True),
        weight,
        preferred_element_type=jnp.float32,
    )
    top = jnp.max(logits, axis=1)
    expo = jnp.exp(logits - top[:, None])
    total = jnp.sum(expo, axis=1)
    moment = jnp.sum(expo * logits, axis=1)
    hit = (lax.all_gather(token_ids, "tensor", axis=0, tiled=True) - vstart)[:, None] == vocab_iota[
        None, :
    ]
    chosen = jnp.sum(jnp.where(hit, logits, 0.0), axis=1)
    fresh = (top, total, moment, chosen)
    top, total, moment, chosen = tuple((new for new in fresh))
    onehot = (own_rows // SLOT)[:, None] == seq_iota[None, :]
    length_of = jnp.sum(jnp.where(onehot, seq_len[None, :], 0), axis=1)
    within = own_rows % SLOT
    scored = within < length_of
    top_all = lax.pmax(top, "tensor")
    rescale = jnp.exp(top - top_all)
    top_own = top_all[own_rows]
    total_all, moment_all, chosen_all = lax.psum(
        (total * rescale, moment * rescale, chosen), "tensor"
    )
    total_own, moment_own, chosen_own = (
        total_all[own_rows],
        moment_all[own_rows],
        chosen_all[own_rows],
    )
    safe_total = jnp.where(scored, total_own, 1.0)
    lse = top_own + jnp.log(safe_total)
    logprob = jnp.where(scored, chosen_own - lse, 0.0)
    entropy = jnp.where(scored, lse - moment_own / safe_total, 0.0)
    return (logprob, entropy)


def solution(mesh):
    return jax.shard_map(
        per_device,
        mesh=mesh,
        in_specs=(
            P(("dp", "tensor"), None),
            P(),
            P("dp", "tensor"),
            P(("dp", "tensor")),
            P("dp", None),
        ),
        out_specs=(P(("dp", "tensor")), P(("dp", "tensor"))),
        check_vma=False,
    )
```

profile of v0, /device:TPU:6, one launch (start us, length us, event | category | flops | bytes accessed | tf_op | source)
XLA Modules:
  0.0 922.9 jit_solution(2070822759771183285)
XLA Ops:
  7.2 0.0 all-gather.5.cloned.1.call-start
  7.2 0.7 all-gather.5.cloned.1.call-update
  7.9 0.0 all-gather.3.cloned.1.call-start
  7.9 1.0 fusion.1
  8.9 1.6 fusion.3
  10.5 0.0 all-gather.3.cloned.1.call-update
  10.5 1.3 dynamic-slice
  12.5 0.9 dynamic-update-slice
  13.3 32.3 %all-reduce = s32[2048]{0:T(1024)S(1)} all-reduce(s32[2048]{0:T(1024)S(1)} %dynamic-update-slice), channel_id=1, replica_groups=mesh['dp'=4,'tensor'=128] {'tensor'}, use_global_device_ids=true, to_apply=%add | all-reduce | flops 2048 | bytes 16384
  45.6 0.7 select_reduce_fusion.1
  46.4 12.5 %all-gather.5.cloned.1.call-done = bf16[2048,800]{0,1:T(8,128)(2,1)} async-done(((bf16[512,800]{0,1:T(8,128)(2,1)}), bf16[2048,800]{0,1:T(8,128)(2,1)}) %all-gather.5.cloned.1.call-update) | async-done | bytes 3276816 | tf_op jit(solution)/shard_map/all_gather | solution.py:16
  58.8 93.4 %all-gather.3.cloned.1.call-done = bf16[2048,2048]{1,0:T(8,128)(2,1)} async-done(((bf16[16,2048]{1,0:T(8,128)(2,1)}), bf16[2048,2048]{1,0:T(8,128)(2,1)}) %all-gather.3.cloned.1.call-update) | async-done | bytes 8388624 | tf_op jit(solution)/shard_map/all_gather | solution.py:24
  152.2 12.1 %fusion.8 = (f32[2048]{0:T(1024)S(1)}, f32[2048,800]{0,1:T(8,128)}) fusion(bf16[2048,2048]{1,0:T(8,128)(2,1)} %all-gather.3.cloned.1.call-done, bf16[2048,800]{0,1:T(8,128)(2,1)} %all-gather.5.cloned.1.call-done), kind=kOutput, calls=%fused_computation.35 | convolution fusion | flops 6712522752 | bytes 18227200 | tf_op jit(solution)/shard_map/dot_general | solution.py:23
  164.3 253.6 %pmax.7 = f32[2048]{0:T(1024)S(1)} all-reduce(f32[2048]{0:T(1024)S(1)} %get-tuple-element.12), channel_id=1, replica_groups=mesh['dp'=4,'tensor'=128] {'tensor'}, use_global_device_ids=true, to_apply=%region_5.6 | all-reduce | flops 2048 | bytes 16384 | tf_op jit(solution)/shard_map/pmax | solution.py:42
  417.9 4.1 multiply_reduce_fusion
  422.0 0.7 gather_fusion.1
  422.7 490.9 %all-reduce.1 = (f32[2048]{0:T(1024)S(1)}, f32[2048]{0:T(1024)S(1)}, f32[2048]{0:T(1024)S(1)}) all-reduce(f32[2048]{0:T(1024)S(1)} %get-tuple-element.4, f32[2048]{0:T(1024)S(1)} %get-tuple-element.9, f32[2048]{0:T(1024)S(1)} %get-tuple-element.8), channel_id=1, replica_groups=mesh['dp'=4,'tensor'=128] {'tensor'}, use_global_device_ids=true, to_apply=%region_3.0 | all-reduce | flops 6144 | bytes 49152 | tf_op jit(solution)/shard_map/psum | solution.py:45
  913.6 0.7 gather_fusion
  914.2 0.7 gather_fusion.2
  914.9 0.7 gather_fusion.3
  915.5 0.5 subtract_select_fusion
  (7 shorter events, 0.0 us)
Async XLA Ops:
  7.2 51.7 %all-gather.5.cloned.1.call-start = ((), (), s32[]{:S(2)}) async-start(), calls=%async_computation.1 | async-start | bytes 4096000 | tf_op jit(solution)/shard_map/all_gather | solution.py:16
  7.9 144.3 %all-gather.3.cloned.1.call-start = ((), (), s32[]{:S(2)}) async-start(), calls=%async_computation | async-start | bytes 8454144 | tf_op jit(solution)/shard_map/all_gather | solution.py:24
Sparse Core Ops, SparseCore 0:
  10.1 48.6 all-gather.4
  62.0 90.2 all-gather.2
where the time goes:
time: 923 us
  blocking collectives  777 us (84%)
  waiting for transfers between devices  107 us (12%)
  between operations  14.7 us (2%)
  matrix products  12.1 us (1%)
    psum x1, blocking collectives, per_device(): lax.psum((total * rescale, moment * rescale, chosen), 'tensor')  491 us
    pmax x1, blocking collectives, per_device(): top_all = lax.pmax(top, 'tensor')  254 us
    all_gather x1, waiting for transfers between devices, per_device(): lax.all_gather(normed, 'tensor', axis=0, tiled=True)  93.4 us
    unnamed x1, blocking collectives  32.3 us
  transfers between devices with their start and end apart: 2, of which 2 were waited for; matrix products, arithmetic and copies ran while one was open for 1% of the time, Pallas kernels for 0%

commit v1 on v0

v1 whole, which is shorter than its diff:
```python
import functools

import jax
import jax.numpy as jnp
from jax import lax
from jax.experimental import pallas as pl
from jax.experimental.pallas import tpu as pltpu
from jax.sharding import PartitionSpec as P

SEQ_DP = 4
SLOT = 512
BLOCK = 256
N_DP = 4


def head_kernel(len_ref, x_ref, ids_ref, w0, w1, w2, w3, out_ref, w_all, sem):
    step = pl.program_id(0)
    me = lax.axis_index("dp")
    vocab_dev, depth = w0.shape
    pieces = (w0, w1, w2, w3)

    @pl.when(step == 0)
    def _():
        copies = []
        for k in range(N_DP):
            src = lax.rem(me - k + N_DP, N_DP)
            copies.append(
                pltpu.make_async_copy(
                    pieces[k],
                    w_all.at[:, pl.ds(pl.multiple_of(src * depth, depth), depth)],
                    sem.at[k],
                )
            )
        for c in copies:
            c.start()
        for c in copies:
            c.wait()

    per_slot = SLOT // BLOCK
    live = len_ref[0, step // per_slot] > lax.rem(step, per_slot) * BLOCK

    @pl.when(live)
    def _():
        logits = lax.dot_general(
            w_all[...],
            x_ref[...],
            (((1,), (1,)), ((), ())),
            preferred_element_type=jnp.float32,
        )
        top = jnp.max(logits, axis=0, keepdims=True)
        expo = jnp.exp(logits - top)
        vocab = lax.axis_index("tensor") * vocab_dev + lax.broadcasted_iota(
            jnp.int32, logits.shape, 0
        )
        out_ref[0:1, :] = top
        out_ref[1:2, :] = jnp.sum(expo, axis=0, keepdims=True)
        out_ref[2:3, :] = jnp.sum(expo * logits, axis=0, keepdims=True)
        out_ref[3:4, :] = jnp.sum(
            jnp.where(vocab == ids_ref[...], logits, 0.0), axis=0, keepdims=True
        )

    @pl.when(jnp.logical_not(live))
    def _():
        out_ref[...] = jnp.zeros_like(out_ref)


def per_device(hidden, norm_gain, head_weight, token_ids, lengths):
    row_dev, width = hidden.shape
    vocab_dev = head_weight.shape[1]
    n_t = lax.axis_size("tensor")
    rows = row_dev * n_t
    tensor_idx = lax.axis_index("tensor")

    wide = hidden.astype(jnp.float32)
    meansq = jnp.mean(wide * wide, axis=-1, keepdims=True)
    normed = (wide * lax.rsqrt(meansq + 1e-06) * norm_gain).astype(jnp.bfloat16)
    pieces = [head_weight] + [
        lax.ppermute(head_weight, "dp", [(i, (i + k) % N_DP) for i in range(N_DP)])
        for k in range(1, N_DP)
    ]
    pieces = [p.T for p in pieces]
    everyone = lax.all_gather(normed, "tensor", axis=0, tiled=True)
    ids = lax.all_gather(token_ids, "tensor", axis=0, tiled=True)

    stats = pl.pallas_call(
        head_kernel,
        grid=(rows // BLOCK,),
        in_specs=[
            pl.BlockSpec(memory_space=pltpu.SMEM),
            pl.BlockSpec((BLOCK, width), lambda i: (i, 0)),
            pl.BlockSpec((1, BLOCK), lambda i: (0, i)),
        ]
        + [pl.BlockSpec(memory_space=pl.ANY)] * N_DP,
        out_specs=pl.BlockSpec((4, BLOCK), lambda i: (0, i)),
        out_shape=jax.ShapeDtypeStruct((4, rows), jnp.float32),
        scratch_shapes=[
            pltpu.VMEM((vocab_dev, width), jnp.bfloat16),
            pltpu.SemaphoreType.DMA((N_DP,)),
        ],
        compiler_params=pltpu.CompilerParams(vmem_limit_bytes=32 << 20),
        cost_estimate=pl.CostEstimate(
            flops=2 * rows * width * vocab_dev,
            bytes_accessed=2 * width * (rows + vocab_dev),
            transcendentals=rows * vocab_dev,
        ),
    )(lengths, everyone, ids[None, :], *pieces)

    sent = stats.reshape(4, n_t, row_dev).transpose(1, 0, 2).reshape(n_t, 4 * row_dev)
    back = lax.all_to_all(sent, "tensor", 0, 0).reshape(n_t, 4, row_dev)
    top, total, moment, chosen = (back[:, k] for k in range(4))
    top_own = jnp.max(top, axis=0)
    rescale = jnp.exp(top - top_own)
    total_own = jnp.sum(total * rescale, axis=0)
    moment_own = jnp.sum(moment * rescale, axis=0)
    chosen_own = jnp.sum(chosen, axis=0)

    own_rows = tensor_idx * row_dev + jnp.arange(row_dev, dtype=jnp.int32)
    onehot = (own_rows // SLOT)[:, None] == jnp.arange(SEQ_DP, dtype=jnp.int32)[None, :]
    length_of = jnp.sum(jnp.where(onehot, lengths[0][None, :], 0), axis=1)
    scored = own_rows % SLOT < length_of
    safe_total = jnp.where(scored, total_own, 1.0)
    lse = top_own + jnp.log(safe_total)
    logprob = jnp.where(scored, chosen_own - lse, 0.0)
    entropy = jnp.where(scored, lse - moment_own / safe_total, 0.0)
    return (logprob, entropy)


def solution(mesh):
    return jax.shard_map(
        per_device,
        mesh=mesh,
        in_specs=(
            P(("dp", "tensor"), None),
            P(),
            P("dp", "tensor"),
            P(("dp", "tensor")),
            P("dp", None),
        ),
        out_specs=(P(("dp", "tensor")), P(("dp", "tensor"))),
        check_vma=False,
    )
```

time: 923 us -> 150 us (0.16)
  blocking collectives: 777 us -> 28.6 us
  waiting for transfers between devices: 107 us -> 61.4 us
  starting transfers between devices: 0.08 us -> 22.4 us
  matrix products: 12.1 us -> 0 us
    psum x1 -> x0, blocking collectives: 491 us -> none  [per_device(): lax.psum((total * rescale, moment * rescale, chosen), 'tensor')]
    pmax x1 -> x0, blocking collectives: 254 us -> none  [per_device(): top_all = lax.pmax(top, 'tensor')]
    all_gather x2 -> x1, waiting for transfers between devices: 106 us -> 50.3 us  [per_device(): everyone = lax.all_gather(normed, 'tensor', axis=0, tiled=True)]
    ppermute x0 -> x3, starting transfers between devices: none -> 12.5 us  [per_device(): lax.ppermute(head_weight, 'dp', [(i, (i + k) % N_DP) for i in range(N_DP)])]
    dot_general x1 -> x0, matrix products: 12.1 us -> none  [per_device(): jnp.dot(lax.all_gather(normed, 'tensor', axis=0, tiled=True), weight, pre...]
    all_to_all x0 -> x1, waiting for transfers between devices: none -> 11 us  [per_device(): back = lax.all_to_all(sent, 'tensor', 0, 0).reshape(n_t, 4, row_dev)]
    all_to_all x0 -> x1, starting transfers between devices: none -> 9.92 us  [per_device(): back = lax.all_to_all(sent, 'tensor', 0, 0).reshape(n_t, 4, row_dev)]
  transfers between devices with their start and end apart: 2 -> 5, of which waited for: 2 -> 2; matrix products, arithmetic and copies ran while one was open for 1% -> 2% of each run, Pallas kernels for 0% -> 0%
where the time goes in v1:
time: 150 us; the launch traced here: 148 us
  waiting for transfers between devices  61.4 us (41%)
  blocking collectives  28.6 us (19%)
  starting transfers between devices  22.4 us (15%)
  between operations  14.8 us (10%)
  Pallas kernels  9.16 us (6%)
  local copies, waits for them, and re-layouts  8.34 us (6%)
  other arithmetic  3.5 us (2%)
    all_gather x1, waiting for transfers between devices, per_device(): everyone = lax.all_gather(normed, 'tensor', axis=0, tiled=True)  50.3 us
    unnamed x1, blocking collectives  28.6 us
    ppermute x3, starting transfers between devices, per_device(): lax.ppermute(head_weight, 'dp', [(i, (i + k) % N_DP) for i in range(N_DP)])  12.5 us
    all_to_all x1, waiting for transfers between devices, per_device(): back = lax.all_to_all(sent, 'tensor', 0, 0).reshape(n_t, 4, row_dev)  11 us
    all_to_all x1, starting transfers between devices, per_device(): back = lax.all_to_all(sent, 'tensor', 0, 0).reshape(n_t, 4, row_dev)  9.92 us
    pallas_call x1, Pallas kernels, per_device(): pl.pallas_call(head_kernel, grid=(rows // BLOCK,), in_specs=[pl.BlockSpec...  9.16 us
    unnamed x11, local copies, waits for them, and re-layouts  7.32 us
  transfers between devices with their start and end apart: 5, of which 2 were waited for; matrix products, arithmetic and copies ran while one was open for 2% of the time, Pallas kernels for 0%

profile of v1, /device:TPU:6, one launch (start us, length us, event | category | flops | bytes accessed | tf_op | source)
XLA Modules:
  0.0 148.2 jit_solution(11600970046889336262)
XLA Ops:
  7.2 0.0 all-gather.2.cloned.1.call-start
  7.2 1.0 fusion
  8.2 1.6 %fusion.2 = bf16[16,2048]{1,0:T(8,128)(2,1)} fusion(bf16[16,2048]{1,0:T(8,128)(2,1)} %param.5, f32[2048]{0:T(1024)} %param.6, f32[16]{0:T(128)S(1)} %add_rsqrt_fusion), kind=kLoop, calls=%fused_computation.4 | loop fusion | flops 131072 | bytes 139328 | tf_op jit(solution)/shard_map/convert_element_type | solution.py:76
  9.7 0.0 all-gather.2.cloned.1.call-update
  9.8 7.8 %collective-permute-start = (bf16[512,800]{0,1:T(8,128)(2,1)}, bf16[512,800]{0,1:T(8,128)(2,1)S(1)}, u32[]{:S(2)}, u32[]{:S(2)}) collective-permute-start(bf16[512,800]{0,1:T(8,128)(2,1)} %param.7), channel_id=1, source_target_pairs={{0,128},{128,256},{256,384},{384,0},{1,129},{129,257},{257,385},{3... | collective-permute-start | bytes 2457608 | tf_op jit(solution)/shard_map/ppermute | solution.py:78
  17.5 1.9 %collective-permute-start.1 = (bf16[512,800]{0,1:T(8,128)(2,1)}, bf16[512,800]{0,1:T(8,128)(2,1)S(1)}, u32[]{:S(2)}, u32[]{:S(2)}) collective-permute-start(bf16[512,800]{0,1:T(8,128)(2,1)} %param.7), channel_id=1, source_target_pairs={{0,256},{128,384},{256,0},{384,128},{1,257},{129,385},{257,1},{385... | collective-permute-start | bytes 2457608 | tf_op jit(solution)/shard_map/ppermute | solution.py:78
  19.5 2.8 %collective-permute-start.2 = (bf16[512,800]{0,1:T(8,128)(2,1)}, bf16[512,800]{0,1:T(8,128)(2,1)S(1)}, u32[]{:S(2)}, u32[]{:S(2)}) collective-permute-start(bf16[512,800]{0,1:T(8,128)(2,1)} %param.7), channel_id=1, source_target_pairs={{0,384},{128,0},{256,128},{384,256},{1,385},{129,1},{257,129},{385... | collective-permute-start | bytes 2457608 | tf_op jit(solution)/shard_map/ppermute | solution.py:78
  22.3 1.3 dynamic-slice
  24.2 0.9 dynamic-update-slice
  25.1 28.6 %all-reduce = s32[2048]{0:T(1024)S(1)} all-reduce(s32[2048]{0:T(1024)S(1)} %dynamic-update-slice), channel_id=1, replica_groups=mesh['dp'=4,'tensor'=128] {'tensor'}, use_global_device_ids=true, to_apply=%add | all-reduce | flops 2048 | bytes 16384
  53.6 0.0 collective-permute-done
  53.7 0.0 collective-permute-done.1
  53.7 0.0 collective-permute-done.2
  53.7 50.3 %all-gather.2.cloned.1.call-done.x_ref = bf16[2048,2048]{1,0:T(8,128)(2,1)} async-done(((bf16[16,2048]{1,0:T(8,128)(2,1)}), bf16[2048,2048]{1,0:T(8,128)(2,1)}) %all-gather.2.cloned.1.call-update) | async-done | bytes 8388624 | tf_op jit(solution)/shard_map/all_gather | solution.py:82
  104.0 0.0 copy-start
  104.0 3.4 %copy-done = bf16[2048,2048]{1,0:T(8,128)(2,1)S(1)} copy-done((bf16[2048,2048]{1,0:T(8,128)(2,1)S(1)}, bf16[2048,2048]{1,0:T(8,128)(2,1)}, u32[]{:S(2)}) %copy-start) | copy-done | bytes 8388632
  107.4 0.0 copy-start.1
  107.4 1.1 copy-done.1
  108.5 0.0 copy-start.2
  108.5 0.7 copy-done.2
  109.2 0.0 copy-start.3
  109.2 9.2 %shard_map.68 = f32[4,2048]{1,0:T(4,128)S(1)} custom-call(s32[1,4]{1,0:T(1,128)S(1)} %copy-done.2, bf16[2048,2048]{1,0:T(8,128)(2,1)S(1)} %copy-done, s32[1,2048]{1,0:T(1,128)S(1)} %bitcast.30, bf16[800,512]{1,0:T(8,128)(2,1)S(1)} %bitcast.31, bf16[800,512]{1,0:T(8,128)(2,1)S(1)} %bitcast.32, bf16[800,512]{1,0:T(8,128)(2,1)S(1)} %bitcast.33, ...), custom_call_target="tpu_custom_call" | custom-call | flops 6710886400 | bytes 11665408 | tf_op jit(solution)/shard_map/pallas_call | solution.py:85
  118.4 0.1 reshape.44
  118.5 0.1 copy.13
  118.6 0.7 copy.14
  119.3 9.9 %all-to-all-start = ((f32[128,1,64]{2,1,0:T(1,128)}), f32[128,1,64]{2,1,0:T(1,128)S(1)}, u32[]{:S(2)}, u32[]{:S(2)}) async-start(f32[128,1,64]{2,1,0:T(1,128)} %copy.14), calls=%async_computation | async-start | bytes 131072 | tf_op jit(solution)/shard_map/all_to_all | solution.py:109
  129.3 0.0 copy-done.3
  129.3 0.1 select_reduce_fusion
  129.3 11.0 %all-to-all-done = f32[128,1,64]{2,1,0:T(1,128)S(1)} async-done(((f32[128,1,64]{2,1,0:T(1,128)}), f32[128,1,64]{2,1,0:T(1,128)S(1)}, u32[]{:S(2)}, u32[]{:S(2)}) %all-to-all-start) | async-done | bytes 32800 | tf_op jit(solution)/shard_map/all_to_all | solution.py:109
  140.4 0.1 copy.15
  140.4 0.1 slice_reduce_fusion.1
  140.6 0.2 fusion.4
  140.8 0.5 subtract_select_fusion
  (3 shorter events, 0.0 us)
Async XLA Ops:
  7.2 96.8 %all-gather.2.cloned.1.call-start = ((), (), s32[]{:S(2)}) async-start(), calls=%async_computation.1 | async-start | bytes 8454144 | tf_op jit(solution)/shard_map/all_gather | solution.py:82
  9.8 43.9 %collective-permute-start = (bf16[512,800]{0,1:T(8,128)(2,1)}, bf16[512,800]{0,1:T(8,128)(2,1)S(1)}, u32[]{:S(2)}, u32[]{:S(2)}) collective-permute-start(bf16[512,800]{0,1:T(8,128)(2,1)} %param.7), channel_id=1, source_target_pairs={{0,128},{128,256},{256,384},{384,0},{1,129},{129,257},{257,385},{3... | collective-permute-start | bytes 2457608 | tf_op jit(solution)/shard_map/ppermute | solution.py:78
  17.5 36.1 %collective-permute-start.1 = (bf16[512,800]{0,1:T(8,128)(2,1)}, bf16[512,800]{0,1:T(8,128)(2,1)S(1)}, u32[]{:S(2)}, u32[]{:S(2)}) collective-permute-start(bf16[512,800]{0,1:T(8,128)(2,1)} %param.7), channel_id=1, source_target_pairs={{0,256},{128,384},{256,0},{384,128},{1,257},{129,385},{257,1},{385... | collective-permute-start | bytes 2457608 | tf_op jit(solution)/shard_map/ppermute | solution.py:78
  19.5 34.2 %collective-permute-start.2 = (bf16[512,800]{0,1:T(8,128)(2,1)}, bf16[512,800]{0,1:T(8,128)(2,1)S(1)}, u32[]{:S(2)}, u32[]{:S(2)}) collective-permute-start(bf16[512,800]{0,1:T(8,128)(2,1)} %param.7), channel_id=1, source_target_pairs={{0,384},{128,0},{256,128},{384,256},{1,385},{129,1},{257,129},{385... | collective-permute-start | bytes 2457608 | tf_op jit(solution)/shard_map/ppermute | solution.py:78
  104.0 3.4 %copy-start = (bf16[2048,2048]{1,0:T(8,128)(2,1)S(1)}, bf16[2048,2048]{1,0:T(8,128)(2,1)}, u32[]{:S(2)}) copy-start(bf16[2048,2048]{1,0:T(8,128)(2,1)} %all-gather.2.cloned.1.call-done.x_ref) | copy-start | bytes 25165828
  107.4 1.1 copy-start.1
  108.5 0.7 copy-start.2
  109.2 20.1 %copy-start.3 = (s32[1,4]{1,0:T(1,128)S(1)}, s32[1,4]{1,0:T(1,128)}, u32[]{:S(2)}) copy-start(s32[1,4]{1,0:T(1,128)} %len_ref.1) | copy-start | bytes 52
  119.3 21.1 %all-to-all-start = ((f32[128,1,64]{2,1,0:T(1,128)}), f32[128,1,64]{2,1,0:T(1,128)S(1)}, u32[]{:S(2)}, u32[]{:S(2)}) async-start(f32[128,1,64]{2,1,0:T(1,128)} %copy.14), calls=%async_computation | async-start | bytes 131072 | tf_op jit(solution)/shard_map/all_to_all | solution.py:109
Sparse Core Ops, SparseCore 0:
  11.1 92.8 all-gather.1

commit v2 on v0

v2 whole, which is shorter than its diff:
```python
import functools

import jax
import jax.numpy as jnp
from jax import lax
from jax.experimental import pallas as pl
from jax.experimental.pallas import tpu as pltpu
from jax.sharding import PartitionSpec as P

SEQ_DP = 4
SLOT = 512
N_DP = 4
N_Z, N_Y, N_CORE = 8, 8, 2
PER_CLASS = 2
CAP = 72
LANES = 128
DIGIT = 64
PITCH = SLOT // (N_Y * 2)
STATS = 4


def class_layout(len_ref, y_class, core):
    first = core * (N_Y * PER_CLASS) + y_class * PER_CLASS
    starts, counts, at = [], [], 0
    for s in range(SEQ_DP):
        n = jnp.clip(lax.div(len_ref[0, s] - first + (PITCH - 1), PITCH), 0, SLOT // PITCH)
        starts.append(at)
        counts.append(n * PER_CLASS)
        at = at + n * PER_CLASS
    return starts, counts


def my_place():
    t = lax.axis_index("tensor")
    return lax.rem(lax.div(t, N_CORE), N_Y), lax.rem(t, N_CORE)


def pack_kernel(len_ref, recv_ref, gain_ref, out_ref):
    width = gain_ref.shape[1]
    y, core = my_place()
    starts, counts = class_layout(len_ref, y, core)
    shape = (LANES, LANES)
    k = lax.broadcasted_iota(jnp.int32, shape, 0)
    i = lax.broadcasted_iota(jnp.int32, shape, 1)
    pick = jnp.zeros(shape, jnp.float32)
    for s in range(SEQ_DP):
        rel = k - starts[s]
        hit = (rel >= 0) & (rel < counts[s]) & (i == rel + s * (PER_CLASS * SLOT // PITCH))
        pick = jnp.where(hit, 1.0, pick)
    pick = pick.astype(jnp.bfloat16)
    rows = jnp.dot(pick[:CAP], recv_ref[:, :width], preferred_element_type=jnp.float32)
    meansq = jnp.mean(rows * rows, axis=-1, keepdims=True)
    normed = rows * lax.rsqrt(meansq + 1e-06) * gain_ref[...]
    digits = lax.dot_general(
        recv_ref[:, width:],
        pick,
        (((0,), (1,)), ((), ())),
        preferred_element_type=jnp.float32,
    ).astype(jnp.bfloat16)
    shape = (CAP, LANES)
    place = lax.broadcasted_iota(jnp.int32, shape, 0) - (CAP - 3)
    place = jnp.where(place == lax.broadcasted_iota(jnp.int32, shape, 1), 1.0, 0.0)
    tail = jnp.dot(place.astype(jnp.bfloat16), digits, preferred_element_type=jnp.float32)
    out_ref[...] = normed.astype(jnp.bfloat16)
    out_ref[:, :LANES] = (normed[:, :LANES] + tail).astype(jnp.bfloat16)


def head_kernel(offsets, last, len_ref, *refs):
    n = len(offsets)
    x_refs, w_refs = refs[:n], refs[n : n + 2 * N_DP]
    refs = refs[n + 2 * N_DP :]
    prev_ref = None
    if len(refs) == 4:
        prev_ref, refs = refs[0], refs[1:]
    out_ref, logit_ref, stat_ref = refs
    vocab_dev, depth = w_refs[0].shape
    y, core = my_place()
    me = lax.axis_index("dp")
    t = lax.axis_index("tensor")
    sibling = t + 1 - 2 * core
    wide = 2 * LANES

    x_all = jnp.concatenate([r[...] for r in x_refs], axis=0) if n > 1 else x_refs[0][...]
    ids = jnp.zeros((1, wide), jnp.float32)
    for j in range(n):
        d = x_refs[j][CAP - 8 :, :LANES].astype(jnp.float32)
        d = (d[5:6] * DIGIT + d[6:7]) * DIGIT + d[7:8]
        d = jnp.concatenate([d, jnp.zeros_like(d)], axis=1)
        ids = ids + (pltpu.roll(d, j * CAP, 1) if j else d)
    ids = ids[:, : n * CAP].astype(jnp.int32)

    for half, base in ((0, t), (1, sibling)):
        acc = None
        for k in range(N_DP):
            src = lax.rem(me - k + N_DP, N_DP)
            cols = pl.ds(pl.multiple_of(src * depth, depth), depth)
            x_k = jnp.concatenate([r[:, cols] for r in x_refs], axis=0)
            part = lax.dot_general(
                w_refs[half * N_DP + k][...],
                x_k,
                (((1,), (1,)), ((), ())),
                preferred_element_type=jnp.float32,
            )
            acc = part if acc is None else acc + part
        logit_ref[half * vocab_dev : (half + 1) * vocab_dev, :] = acc

    logits = logit_ref[...]
    row = lax.broadcasted_iota(jnp.int32, logits.shape, 0)
    vocab = row + jnp.where(row < vocab_dev, t * vocab_dev, (sibling - 1) * vocab_dev)
    top = jnp.max(logits, axis=0, keepdims=True)
    expo = jnp.exp(logits - top)
    stat_ref[...] = jnp.zeros_like(stat_ref)
    stat_ref[0:1, : n * CAP] = top
    stat_ref[1:2, : n * CAP] = jnp.sum(expo, axis=0, keepdims=True)
    stat_ref[2:3, : n * CAP] = jnp.sum(expo * logits, axis=0, keepdims=True)
    stat_ref[3:4, : n * CAP] = jnp.sum(
        jnp.where(vocab == ids, logits, 0.0), axis=0, keepdims=True
    )

    if prev_ref is not None:
        out_ref[...] = prev_ref[...]
    lane = lax.broadcasted_iota(jnp.int32, (8, LANES), 1)
    per_slot = PER_CLASS * SLOT // PITCH
    stats = stat_ref[...]
    for j, offset in enumerate(offsets):
        y_class = lax.rem(y + offset + N_Y, N_Y)
        starts, _ = class_layout(len_ref, y_class, core)
        spread = jnp.zeros((8, LANES), jnp.float32)
        for s in range(SEQ_DP):
            shift = lax.rem(s * per_slot - j * CAP - starts[s] + 2 * wide, wide)
            moved = pltpu.roll(stats, shift, 1)[:, :LANES]
            spread = jnp.where(lane // per_slot == s, moved, spread)
        out_ref[pl.ds(y_class, 1)] = spread[None]


def run_head(offsets, lengths, shards, weights, prev):
    n = len(offsets)
    vocab_dev, depth = weights[0].shape
    vmem = pl.BlockSpec(memory_space=pltpu.VMEM)
    args = [lengths, *shards, *weights] + ([] if prev is None else [prev])
    return pl.pallas_call(
        functools.partial(head_kernel, offsets, False),
        in_specs=[pl.BlockSpec(memory_space=pltpu.SMEM)] + [vmem] * (len(args) - 1),
        out_specs=vmem,
        out_shape=jax.ShapeDtypeStruct((N_Y, 8, LANES), jnp.float32),
        scratch_shapes=[
            pltpu.VMEM((2 * vocab_dev, n * CAP), jnp.float32),
            pltpu.VMEM((8, 2 * LANES), jnp.float32),
        ],
        compiler_params=pltpu.CompilerParams(vmem_limit_bytes=40 << 20),
        cost_estimate=pl.CostEstimate(
            flops=2 * n * CAP * depth * N_DP * 2 * vocab_dev,
            bytes_accessed=2 * depth * N_DP * (n * CAP + 2 * vocab_dev),
            transcendentals=n * CAP * 2 * vocab_dev,
        ),
    )(*args)


def per_device(hidden, norm_gain, head_weight, token_ids, lengths):
    row_dev, width = hidden.shape
    n_t = N_Z * N_Y * N_CORE
    n_chip = N_Z * N_Y
    tensor_idx = lax.axis_index("tensor")
    same_core = [[N_CORE * k + c for k in range(n_chip)] for c in range(N_CORE)]
    other_core = [(i, i ^ 1) for i in range(n_t)]

    def along_y(by):
        step = []
        for i in range(n_t):
            y = (i // N_CORE) % N_Y
            step.append((i, i + ((y + by) % N_Y - y) * N_CORE))
        return step

    pieces = [head_weight] + [
        lax.ppermute(head_weight, "dp", [(i, (i + k) % N_DP) for i in range(N_DP)])
        for k in (1, 2, 3)
    ]

    digits = jnp.stack(
        [token_ids // (DIGIT * DIGIT), token_ids // DIGIT % DIGIT, token_ids % DIGIT], axis=1
    ).astype(jnp.bfloat16)
    digits = jnp.pad(digits, ((0, 0), (0, LANES - 3)))
    sent = jnp.concatenate([hidden, digits], axis=1).reshape(N_Y, PER_CLASS, width + LANES)
    sent = jnp.broadcast_to(sent[None], (N_Z,) + sent.shape).reshape(
        n_chip, PER_CLASS, width + LANES
    )
    recv = lax.all_to_all(sent, "tensor", 0, 0, axis_index_groups=same_core)
    recv = recv.reshape(n_chip * PER_CLASS, width + LANES)

    vmem = pl.BlockSpec(memory_space=pltpu.VMEM)
    own = pl.pallas_call(
        pack_kernel,
        in_specs=[pl.BlockSpec(memory_space=pltpu.SMEM), vmem, vmem],
        out_specs=vmem,
        out_shape=jax.ShapeDtypeStruct((CAP, width), jnp.bfloat16),
        cost_estimate=pl.CostEstimate(
            flops=2 * CAP * LANES * width, bytes_accessed=2 * (CAP + LANES) * width, transcendentals=0
        ),
    )(lengths, recv, norm_gain[None, :])

    up = [own]
    down = [own]
    for _ in range(N_Y // 2 - 1):
        pair = (
            lax.ppermute(up[-1], "tensor", along_y(1)),
            lax.ppermute(down[-1], "tensor", along_y(-1)),
        )
        pair = lax.optimization_barrier(pair)
        up.append(pair[0])
        down.append(pair[1])
    up.append(lax.ppermute(up[-1], "tensor", along_y(1)))

    late = lax.optimization_barrier((*pieces[1:], up[2], down[2]))
    weights = [p.T for p in pieces]
    weights += [
        lax.ppermute(p, "tensor", other_core).T for p in (head_weight, *late[: N_DP - 1])
    ]
    stats = run_head((0, -1, 1), lengths, [own, up[1], down[1]], weights, None)
    stats = run_head((-2, 2), lengths, [up[2], down[2]], weights, stats)
    stats = run_head((-3, 3, -4), lengths, [up[3], down[3], up[4]], weights, stats)

    sent = stats[:, :STATS].reshape(N_Y, STATS, n_chip, PER_CLASS)
    sent = sent.transpose(2, 1, 0, 3).reshape(n_chip, STATS * row_dev)
    back = lax.all_to_all(sent, "tensor", 0, 0, axis_index_groups=same_core)
    back = back.reshape(n_chip, STATS, row_dev)
    top, total, moment, chosen = (back[:, k] for k in range(STATS))
    top_own = jnp.max(top, axis=0)
    rescale = jnp.exp(top - top_own)
    total_own = jnp.sum(total * rescale, axis=0)
    moment_own = jnp.sum(moment * rescale, axis=0)
    chosen_own = jnp.sum(chosen, axis=0)

    own_rows = tensor_idx * row_dev + jnp.arange(row_dev, dtype=jnp.int32)
    onehot = (own_rows // SLOT)[:, None] == jnp.arange(SEQ_DP, dtype=jnp.int32)[None, :]
    length_of = jnp.sum(jnp.where(onehot, lengths[0][None, :], 0), axis=1)
    scored = own_rows % SLOT < length_of
    safe_total = jnp.where(scored, total_own, 1.0)
    lse = top_own + jnp.log(safe_total)
    logprob = jnp.where(scored, chosen_own - lse, 0.0)
    entropy = jnp.where(scored, lse - moment_own / safe_total, 0.0)
    return (logprob, entropy)


def solution(mesh):
    return jax.shard_map(
        per_device,
        mesh=mesh,
        in_specs=(
            P(("dp", "tensor"), None),
            P(),
            P("dp", "tensor"),
            P(("dp", "tensor")),
            P("dp", None),
        ),
        out_specs=(P(("dp", "tensor")), P(("dp", "tensor"))),
        check_vma=False,
    )
```

time: 923 us -> 143 us (0.15)
  blocking collectives: 777 us -> 0 us
  starting transfers between devices: 0.08 us -> 64.4 us
  waiting for transfers between devices: 107 us -> 47.1 us
  Pallas kernels: 0 us -> 16.2 us
  between operations: 14.7 us -> 0.95 us
  matrix products: 12.1 us -> 0 us
    psum x1 -> x0, blocking collectives: 491 us -> none  [per_device(): lax.psum((total * rescale, moment * rescale, chosen), 'tensor')]
    pmax x1 -> x0, blocking collectives: 254 us -> none  [per_device(): top_all = lax.pmax(top, 'tensor')]
    all_gather x2 -> x0, waiting for transfers between devices: 106 us -> none  [the longest x1 93.4 us: per_device(): lax.all_gather(normed, 'tensor', axis=0, tiled=True)]
    ppermute x0 -> x14, starting transfers between devices: none -> 39.3 us  [the longest x3 11.7 us: per_device(): lax.ppermute(down[-1], 'tensor', along_y(-1))]
    unnamed x1 -> x0, blocking collectives: 32.3 us -> none
    all_to_all x0 -> x2, starting transfers between devices: none -> 25.1 us  [the longest x1 16.8 us: per_device(): recv = lax.all_to_all(sent, 'tensor', 0, 0, axis_index_groups=same_core)]
    ppermute x0 -> x14, waiting for transfers between devices: none -> 23.6 us  [the longest x3 13.6 us: per_device(): lax.ppermute(up[-1], 'tensor', along_y(1))]
    all_to_all x0 -> x2, waiting for transfers between devices: none -> 23.5 us  [the longest x1 11.9 us: per_device(): back = lax.all_to_all(sent, 'tensor', 0, 0, axis_index_groups=same_core)]
  transfers between devices with their start and end apart: 2 -> 16, of which waited for: 2 -> 8; matrix products, arithmetic and copies ran while one was open for 1% -> 2% of each run, Pallas kernels for 0% -> 8%
where the time goes in v2:
time: 143 us; the launch traced here: 142 us
  starting transfers between devices  64.4 us (45%)
  waiting for transfers between devices  47.1 us (33%)
  Pallas kernels  16.2 us (11%)
  local copies, waits for them, and re-layouts  10.8 us (8%)
  other arithmetic  2.49 us (2%)
    all_to_all x1, starting transfers between devices, per_device(): recv = lax.all_to_all(sent, 'tensor', 0, 0, axis_index_groups=same_core)  16.8 us
    pallas_call x3, Pallas kernels, run_head(): pl.pallas_call(functools.partial(head_kernel, offsets, False), in_specs=[...  13.9 us
    ppermute x3, waiting for transfers between devices, per_device(): lax.ppermute(up[-1], 'tensor', along_y(1))  13.6 us
    all_to_all x1, waiting for transfers between devices, per_device(): back = lax.all_to_all(sent, 'tensor', 0, 0, axis_index_groups=same_core)  11.9 us
    ppermute x3, starting transfers between devices, per_device(): lax.ppermute(down[-1], 'tensor', along_y(-1))  11.7 us
    all_to_all x1, waiting for transfers between devices, per_device(): recv = lax.all_to_all(sent, 'tensor', 0, 0, axis_index_groups=same_core)  11.6 us
    ppermute x3, waiting for transfers between devices, per_device(): lax.ppermute(down[-1], 'tensor', along_y(-1))  9.94 us
    ppermute x3, starting transfers between devices, per_device(): lax.ppermute(up[-1], 'tensor', along_y(1))  8.96 us
  transfers between devices with their start and end apart: 16, of which 8 were waited for; matrix products, arithmetic and copies ran while one was open for 2% of the time, Pallas kernels for 8%

profile of v2, /device:TPU:6, one launch (start us, length us, event | category | flops | bytes accessed | tf_op | source)
XLA Modules:
  0.0 141.9 jit_solution(10190741875801184044)
XLA Ops:
  0.6 0.7 convert_bitcast_fusion
  1.3 0.1 copy.23
  1.4 0.8 fusion.1
  2.3 1.1 broadcast_in_dim.39
  3.4 16.8 %all-to-all-start = ((bf16[64,2,2176]{2,1,0:T(2,128)(2,1)}), bf16[64,2,2176]{2,1,0:T(2,128)(2,1)}, u32[]{:S(2)}, u32[]{:S(2)}) async-start(bf16[64,2,2176]{2,1,0:T(2,128)(2,1)} %bitcast.4), calls=%async_computation | async-start | bytes 1114112 | tf_op jit(solution)/shard_map/all_to_all | solution.py:187
  20.2 2.4 %collective-permute-start.7 = (bf16[512,800]{0,1:T(8,128)(2,1)S(1)}, bf16[512,800]{0,1:T(8,128)(2,1)S(1)}, u32[]{:S(2)}, u32[]{:S(2)}) collective-permute-start(bf16[512,800]{0,1:T(8,128)(2,1)S(1)} %copy-done), channel_id=1, source_target_pairs={{0,128},{128,256},{256,384},{384,0},{1,129},{129,257},{257,385},{3... | collective-permute-start | bytes 2457608 | tf_op jit(solution)/shard_map/ppermute | solution.py:175
  22.6 4.3 %collective-permute-start.8 = (bf16[512,800]{0,1:T(8,128)(2,1)S(1)}, bf16[512,800]{0,1:T(8,128)(2,1)S(1)}, u32[]{:S(2)}, u32[]{:S(2)}) collective-permute-start(bf16[512,800]{0,1:T(8,128)(2,1)S(1)} %copy-done), channel_id=1, source_target_pairs={{0,256},{128,384},{256,0},{384,128},{1,257},{129,385},{257,1},{385... | collective-permute-start | bytes 2457608 | tf_op jit(solution)/shard_map/ppermute | solution.py:175
  27.0 1.9 %collective-permute-start.9 = (bf16[512,800]{0,1:T(8,128)(2,1)S(1)}, bf16[512,800]{0,1:T(8,128)(2,1)S(1)}, u32[]{:S(2)}, u32[]{:S(2)}) collective-permute-start(bf16[512,800]{0,1:T(8,128)(2,1)S(1)} %copy-done), channel_id=1, source_target_pairs={{0,384},{128,0},{256,128},{384,256},{1,385},{129,1},{257,129},{385... | collective-permute-start | bytes 2457608 | tf_op jit(solution)/shard_map/ppermute | solution.py:175
  28.9 11.6 %all-to-all-done = bf16[64,2,2176]{2,1,0:T(2,128)(2,1)} async-done(((bf16[64,2,2176]{2,1,0:T(2,128)(2,1)}), bf16[64,2,2176]{2,1,0:T(2,128)(2,1)}, u32[]{:S(2)}, u32[]{:S(2)}) %all-to-all-start) | async-done | bytes 557088 | tf_op jit(solution)/shard_map/all_to_all | solution.py:187
  40.5 2.1 %reshape.43.recv_ref = bf16[128,2176]{1,0:T(8,128)(2,1)} reshape(bf16[64,2,2176]{2,1,0:T(2,128)(2,1)} %all-to-all-done) | data formatting | bytes 1114112 | tf_op jit(solution)/shard_map/reshape | solution.py:188
  42.6 2.2 %shard_map.68.refs_0_ = bf16[72,2048]{1,0:T(8,128)(2,1)} custom-call(s32[1,4]{1,0:T(1,128)} %len_ref.7, bf16[128,2176]{1,0:T(8,128)(2,1)} %reshape.43.recv_ref, f32[1,2048]{1,0:T(1,128)} %bitcast.59), custom_call_target="tpu_custom_call" | custom-call | flops 37748736 | bytes 819200 | tf_op jit(solution)/shard_map/pallas_call | solution.py:191
  44.9 3.1 %collective-permute-start = (bf16[72,2048]{1,0:T(8,128)(2,1)}, bf16[72,2048]{1,0:T(8,128)(2,1)S(1)}, u32[]{:S(2)}, u32[]{:S(2)}) collective-permute-start(bf16[72,2048]{1,0:T(8,128)(2,1)} %shard_map.68.refs_0_), channel_id=1, source_target_pairs={{0,2},{1,3},{2,4},{3,5},{4,6},{5,7},{6,8},{7,9},{8,10},{9,11},{10,... | collective-permute-start | bytes 884744 | tf_op jit(solution)/shard_map/ppermute | solution.py:205
  48.0 3.9 %collective-permute-start.1 = (bf16[72,2048]{1,0:T(8,128)(2,1)}, bf16[72,2048]{1,0:T(8,128)(2,1)S(1)}, u32[]{:S(2)}, u32[]{:S(2)}) collective-permute-start(bf16[72,2048]{1,0:T(8,128)(2,1)} %shard_map.68.refs_0_), channel_id=1, source_target_pairs={{0,14},{1,15},{2,0},{3,1},{4,2},{5,3},{6,4},{7,5},{8,6},{9,7},{10,... | collective-permute-start | bytes 884744 | tf_op jit(solution)/shard_map/ppermute | solution.py:206
  51.9 3.0 %collective-permute-done.refs_1_ = bf16[72,2048]{1,0:T(8,128)(2,1)S(1)} collective-permute-done((bf16[72,2048]{1,0:T(8,128)(2,1)}, bf16[72,2048]{1,0:T(8,128)(2,1)S(1)}, u32[]{:S(2)}, u32[]{:S(2)}) %collective-permute-start) | collective-permute-done | bytes 294944 | tf_op jit(solution)/shard_map/ppermute | solution.py:205
  54.9 1.9 %collective-permute-done.1.refs_2_ = bf16[72,2048]{1,0:T(8,128)(2,1)S(1)} collective-permute-done((bf16[72,2048]{1,0:T(8,128)(2,1)}, bf16[72,2048]{1,0:T(8,128)(2,1)S(1)}, u32[]{:S(2)}, u32[]{:S(2)}) %collective-permute-start.1) | collective-permute-done | bytes 294944 | tf_op jit(solution)/shard_map/ppermute | solution.py:206
  56.8 2.9 %collective-permute-start.2 = (bf16[72,2048]{1,0:T(8,128)(2,1)S(1)}, bf16[72,2048]{1,0:T(8,128)(2,1)S(1)}, u32[]{:S(2)}, u32[]{:S(2)}) collective-permute-start(bf16[72,2048]{1,0:T(8,128)(2,1)S(1)} %collective-permute-done.refs_1_), channel_id=1, source_target_pairs={{0,2},{1,3},{2,4},{3,5},{4,6},{5,7},{6,8},{7,9},{8,10},{9,11},{10,... | collective-permute-start | bytes 884744 | tf_op jit(solution)/shard_map/ppermute | solution.py:205
  59.8 0.7 copy-done.4
  60.5 4.1 %collective-permute-start.3 = (bf16[72,2048]{1,0:T(8,128)(2,1)S(1)}, bf16[72,2048]{1,0:T(8,128)(2,1)}, u32[]{:S(2)}, u32[]{:S(2)}) collective-permute-start(bf16[72,2048]{1,0:T(8,128)(2,1)S(1)} %collective-permute-done.1.refs_2_), channel_id=1, source_target_pairs={{0,14},{1,15},{2,0},{3,1},{4,2},{5,3},{6,4},{7,5},{8,6},{9,7},{10,... | collective-permute-start | bytes 884744 | tf_op jit(solution)/shard_map/ppermute | solution.py:206
  64.6 0.7 copy-done.6
  65.3 1.3 collective-permute-done.2.refs_0_
  66.6 1.9 %collective-permute-start.10 = (bf16[512,800]{0,1:T(8,128)(2,1)S(1)}, bf16[512,800]{0,1:T(8,128)(2,1)}, u32[]{:S(2)}, u32[]{:S(2)}) collective-permute-start(bf16[512,800]{0,1:T(8,128)(2,1)S(1)} %copy-done), channel_id=1, source_target_pairs={{0,1},{1,0},{2,3},{3,2},{4,5},{5,4},{6,7},{7,6},{8,9},{9,8},{10,11... | collective-permute-start | bytes 2457608 | tf_op jit(solution)/shard_map/ppermute | solution.py:216
  68.6 0.6 collective-permute-done.3.refs_1_
  69.2 1.9 %collective-permute-start.11 = (bf16[512,800]{0,1:T(8,128)(2,1)S(1)}, bf16[512,800]{0,1:T(8,128)(2,1)}, u32[]{:S(2)}, u32[]{:S(2)}) collective-permute-start(bf16[512,800]{0,1:T(8,128)(2,1)S(1)} %collective-permute-done.7), channel_id=1, source_target_pairs={{0,1},{1,0},{2,3},{3,2},{4,5},{5,4},{6,7},{7,6},{8,9},{9,8},{10,11... | collective-permute-start | bytes 2457608 | tf_op jit(solution)/shard_map/ppermute | solution.py:216
  71.1 2.4 %collective-permute-start.12 = (bf16[512,800]{0,1:T(8,128)(2,1)S(1)}, bf16[512,800]{0,1:T(8,128)(2,1)}, u32[]{:S(2)}, u32[]{:S(2)}) collective-permute-start(bf16[512,800]{0,1:T(8,128)(2,1)S(1)} %collective-permute-done.8), channel_id=1, source_target_pairs={{0,1},{1,0},{2,3},{3,2},{4,5},{5,4},{6,7},{7,6},{8,9},{9,8},{10,11... | collective-permute-start | bytes 2457608 | tf_op jit(solution)/shard_map/ppermute | solution.py:216
  73.5 1.9 %collective-permute-start.13 = (bf16[512,800]{0,1:T(8,128)(2,1)S(1)}, bf16[512,800]{0,1:T(8,128)(2,1)}, u32[]{:S(2)}, u32[]{:S(2)}) collective-permute-start(bf16[512,800]{0,1:T(8,128)(2,1)S(1)} %collective-permute-done.9), channel_id=1, source_target_pairs={{0,1},{1,0},{2,3},{3,2},{4,5},{5,4},{6,7},{7,6},{8,9},{9,8},{10,11... | collective-permute-start | bytes 2457608 | tf_op jit(solution)/shard_map/ppermute | solution.py:216
  75.5 2.9 %collective-permute-start.4 = (bf16[72,2048]{1,0:T(8,128)(2,1)S(1)}, bf16[72,2048]{1,0:T(8,128)(2,1)S(1)}, u32[]{:S(2)}, u32[]{:S(2)}) collective-permute-start(bf16[72,2048]{1,0:T(8,128)(2,1)S(1)} %collective-permute-done.2.refs_0_), channel_id=1, source_target_pairs={{0,2},{1,3},{2,4},{3,5},{4,6},{5,7},{6,8},{7,9},{8,10},{9,11},{10,... | collective-permute-start | bytes 884744 | tf_op jit(solution)/shard_map/ppermute | solution.py:205
  78.4 0.7 copy-done.2
  79.1 9.3 %collective-permute-done.4.refs_0_ = bf16[72,2048]{1,0:T(8,128)(2,1)S(1)} collective-permute-done((bf16[72,2048]{1,0:T(8,128)(2,1)S(1)}, bf16[72,2048]{1,0:T(8,128)(2,1)S(1)}, u32[]{:S(2)}, u32[]{:S(2)}) %collective-permute-start.4) | collective-permute-done | bytes 294944 | tf_op jit(solution)/shard_map/ppermute | solution.py:205
  88.5 0.7 copy-done.8
  89.2 3.6 %collective-permute-start.5 = (bf16[72,2048]{1,0:T(8,128)(2,1)}, bf16[72,2048]{1,0:T(8,128)(2,1)}, u32[]{:S(2)}, u32[]{:S(2)}) collective-permute-start(bf16[72,2048]{1,0:T(8,128)(2,1)} %collective-permute-done.3.refs_1_), channel_id=1, source_target_pairs={{0,14},{1,15},{2,0},{3,1},{4,2},{5,3},{6,4},{7,5},{8,6},{9,7},{10,... | collective-permute-start | bytes 884744 | tf_op jit(solution)/shard_map/ppermute | solution.py:206
  92.8 7.4 %collective-permute-done.5.refs_1_ = bf16[72,2048]{1,0:T(8,128)(2,1)} collective-permute-done((bf16[72,2048]{1,0:T(8,128)(2,1)}, bf16[72,2048]{1,0:T(8,128)(2,1)}, u32[]{:S(2)}, u32[]{:S(2)}) %collective-permute-start.5) | collective-permute-done | bytes 294944 | tf_op jit(solution)/shard_map/ppermute | solution.py:206
  100.2 1.9 %collective-permute-start.6 = (bf16[72,2048]{1,0:T(8,128)(2,1)}, bf16[72,2048]{1,0:T(8,128)(2,1)S(1)}, u32[]{:S(2)}, u32[]{:S(2)}) collective-permute-start(bf16[72,2048]{1,0:T(8,128)(2,1)} %copy-done.8), channel_id=1, source_target_pairs={{0,2},{1,3},{2,4},{3,5},{4,6},{5,7},{6,8},{7,9},{8,10},{9,11},{10,... | collective-permute-start | bytes 884744 | tf_op jit(solution)/shard_map/ppermute | solution.py:211
  102.2 0.6 copy-done.10
  102.9 1.0 copy-done.1
  103.8 1.0 copy-done.5
  104.8 1.0 copy-done.7
  105.7 4.6 %shard_map.69.refs_10_ = f32[8,8,128]{2,1,0:T(8,128)S(1)} custom-call(s32[1,4]{1,0:T(1,128)S(1)} %copy-done.10, bf16[72,2048]{1,0:T(8,128)(2,1)S(1)} %copy-done.1, bf16[72,2048]{1,0:T(8,128)(2,1)S(1)} %copy-done.5, bf16[72,2048]{1,0:T(8,128)(2,1)S(1)} %copy-done.7, bf16[800,512]{1,0:T(8,128)(2,1)S(1)} %bitcast.42, bf16[800,512]{1,0:T(8,128)(2,1)S(1)} %bitcast.45, ...), custom_call_target="tpu_custom_call" | custom-call | flops 1415577600 | bytes 7438336 | tf_op jit(solution)/shard_map/pallas_call | solution.py:141
  110.4 4.7 %shard_map.70.refs_11_ = f32[8,8,128]{2,1,0:T(8,128)S(1)} custom-call(s32[1,4]{1,0:T(1,128)S(1)} %copy-done.10, bf16[72,2048]{1,0:T(8,128)(2,1)S(1)} %copy-done.3, bf16[72,2048]{1,0:T(8,128)(2,1)} %collective-permute-done.3.refs_1_, bf16[800,512]{1,0:T(8,128)(2,1)S(1)} %bitcast.43, bf16[800,512]{1,0:T(8,128)(2,1)S(1)} %bitcast.46, ...), custom_call_target="tpu_custom_call" | custom-call | flops 943718400 | bytes 7143424 | tf_op jit(solution)/shard_map/pallas_call | solution.py:141
  115.1 4.7 %shard_map.71 = f32[8,8,128]{2,1,0:T(8,128)S(1)} custom-call(s32[1,4]{1,0:T(1,128)S(1)} %copy-done.10, bf16[72,2048]{1,0:T(8,128)(2,1)S(1)} %copy-done.9, bf16[72,2048]{1,0:T(8,128)(2,1)} %collective-permute-done.5.refs_1_, bf16[72,2048]{1,0:T(8,128)(2,1)S(1)} %collective-permute-done.6.refs_2_, bf16[800,512]{1,0:T(8,128)(2,1)S(1)} %bitcast.44, ...), custom_call_target="tpu_custom_call" | custom-call | flops 1415577600 | bytes 7438336 | tf_op jit(solution)/shard_map/pallas_call | solution.py:141
  119.7 0.1 copy.19
  119.9 0.1 copy.20
  120.0 0.7 copy.21
  120.7 8.3 %all-to-all-start.1 = ((f32[64,1,64]{2,1,0:T(1,128)}), f32[64,1,64]{2,1,0:T(1,128)S(1)}, u32[]{:S(2)}, u32[]{:S(2)}) async-start(f32[64,1,64]{2,1,0:T(1,128)} %copy.21), calls=%async_computation.1 | async-start | bytes 65536 | tf_op jit(solution)/shard_map/all_to_all | solution.py:224
  129.0 0.1 select_reduce_fusion
  129.1 11.9 %all-to-all-done.1 = f32[64,1,64]{2,1,0:T(1,128)S(1)} async-done(((f32[64,1,64]{2,1,0:T(1,128)}), f32[64,1,64]{2,1,0:T(1,128)S(1)}, u32[]{:S(2)}, u32[]{:S(2)}) %all-to-all-start.1) | async-done | bytes 16416 | tf_op jit(solution)/shard_map/all_to_all | solution.py:224
  141.0 0.1 slice_reduce_fusion.1
  141.1 0.2 fusion.3
  141.3 0.5 subtract_select_fusion
  (27 shorter events, 0.2 us)
Async XLA Ops:
  2.3 17.9 %copy-start = (bf16[512,800]{0,1:T(8,128)(2,1)S(1)}, bf16[512,800]{0,1:T(8,128)(2,1)}, u32[]{:S(2)}) copy-start(bf16[512,800]{0,1:T(8,128)(2,1)} %param.7) | copy-start | bytes 2457604
  3.4 37.1 %all-to-all-start = ((bf16[64,2,2176]{2,1,0:T(2,128)(2,1)}), bf16[64,2,2176]{2,1,0:T(2,128)(2,1)}, u32[]{:S(2)}, u32[]{:S(2)}) async-start(bf16[64,2,2176]{2,1,0:T(2,128)(2,1)} %bitcast.4), calls=%async_computation | async-start | bytes 1114112 | tf_op jit(solution)/shard_map/all_to_all | solution.py:187
  20.2 48.9 %collective-permute-start.7 = (bf16[512,800]{0,1:T(8,128)(2,1)S(1)}, bf16[512,800]{0,1:T(8,128)(2,1)S(1)}, u32[]{:S(2)}, u32[]{:S(2)}) collective-permute-start(bf16[512,800]{0,1:T(8,128)(2,1)S(1)} %copy-done), channel_id=1, source_target_pairs={{0,128},{128,256},{256,384},{384,0},{1,129},{129,257},{257,385},{3... | collective-permute-start | bytes 2457608 | tf_op jit(solution)/shard_map/ppermute | solution.py:175
  22.6 46.5 %collective-permute-start.8 = (bf16[512,800]{0,1:T(8,128)(2,1)S(1)}, bf16[512,800]{0,1:T(8,128)(2,1)S(1)}, u32[]{:S(2)}, u32[]{:S(2)}) collective-permute-start(bf16[512,800]{0,1:T(8,128)(2,1)S(1)} %copy-done), channel_id=1, source_target_pairs={{0,256},{128,384},{256,0},{384,128},{1,257},{129,385},{257,1},{385... | collective-permute-start | bytes 2457608 | tf_op jit(solution)/shard_map/ppermute | solution.py:175
  27.0 42.2 %collective-permute-start.9 = (bf16[512,800]{0,1:T(8,128)(2,1)S(1)}, bf16[512,800]{0,1:T(8,128)(2,1)S(1)}, u32[]{:S(2)}, u32[]{:S(2)}) collective-permute-start(bf16[512,800]{0,1:T(8,128)(2,1)S(1)} %copy-done), channel_id=1, source_target_pairs={{0,384},{128,0},{256,128},{384,256},{1,385},{129,1},{257,129},{385... | collective-permute-start | bytes 2457608 | tf_op jit(solution)/shard_map/ppermute | solution.py:175
  44.9 10.0 %collective-permute-start = (bf16[72,2048]{1,0:T(8,128)(2,1)}, bf16[72,2048]{1,0:T(8,128)(2,1)S(1)}, u32[]{:S(2)}, u32[]{:S(2)}) collective-permute-start(bf16[72,2048]{1,0:T(8,128)(2,1)} %shard_map.68.refs_0_), channel_id=1, source_target_pairs={{0,2},{1,3},{2,4},{3,5},{4,6},{5,7},{6,8},{7,9},{8,10},{9,11},{10,... | collective-permute-start | bytes 884744 | tf_op jit(solution)/shard_map/ppermute | solution.py:205
  48.0 8.8 %collective-permute-start.1 = (bf16[72,2048]{1,0:T(8,128)(2,1)}, bf16[72,2048]{1,0:T(8,128)(2,1)S(1)}, u32[]{:S(2)}, u32[]{:S(2)}) collective-permute-start(bf16[72,2048]{1,0:T(8,128)(2,1)} %shard_map.68.refs_0_), channel_id=1, source_target_pairs={{0,14},{1,15},{2,0},{3,1},{4,2},{5,3},{6,4},{7,5},{8,6},{9,7},{10,... | collective-permute-start | bytes 884744 | tf_op jit(solution)/shard_map/ppermute | solution.py:206
  56.8 9.8 %collective-permute-start.2 = (bf16[72,2048]{1,0:T(8,128)(2,1)S(1)}, bf16[72,2048]{1,0:T(8,128)(2,1)S(1)}, u32[]{:S(2)}, u32[]{:S(2)}) collective-permute-start(bf16[72,2048]{1,0:T(8,128)(2,1)S(1)} %collective-permute-done.refs_1_), channel_id=1, source_target_pairs={{0,2},{1,3},{2,4},{3,5},{4,6},{5,7},{6,8},{7,9},{8,10},{9,11},{10,... | collective-permute-start | bytes 884744 | tf_op jit(solution)/shard_map/ppermute | solution.py:205
  59.7 0.7 copy-start.4
  60.5 8.7 %collective-permute-start.3 = (bf16[72,2048]{1,0:T(8,128)(2,1)S(1)}, bf16[72,2048]{1,0:T(8,128)(2,1)}, u32[]{:S(2)}, u32[]{:S(2)}) collective-permute-start(bf16[72,2048]{1,0:T(8,128)(2,1)S(1)} %collective-permute-done.1.refs_2_), channel_id=1, source_target_pairs={{0,14},{1,15},{2,0},{3,1},{4,2},{5,3},{6,4},{7,5},{8,6},{9,7},{10,... | collective-permute-start | bytes 884744 | tf_op jit(solution)/shard_map/ppermute | solution.py:206
  64.6 0.7 copy-start.6
  66.6 35.5 %collective-permute-start.10 = (bf16[512,800]{0,1:T(8,128)(2,1)S(1)}, bf16[512,800]{0,1:T(8,128)(2,1)}, u32[]{:S(2)}, u32[]{:S(2)}) collective-permute-start(bf16[512,800]{0,1:T(8,128)(2,1)S(1)} %copy-done), channel_id=1, source_target_pairs={{0,1},{1,0},{2,3},{3,2},{4,5},{5,4},{6,7},{7,6},{8,9},{9,8},{10,11... | collective-permute-start | bytes 2457608 | tf_op jit(solution)/shard_map/ppermute | solution.py:216
  69.2 33.0 %collective-permute-start.11 = (bf16[512,800]{0,1:T(8,128)(2,1)S(1)}, bf16[512,800]{0,1:T(8,128)(2,1)}, u32[]{:S(2)}, u32[]{:S(2)}) collective-permute-start(bf16[512,800]{0,1:T(8,128)(2,1)S(1)} %collective-permute-done.7), channel_id=1, source_target_pairs={{0,1},{1,0},{2,3},{3,2},{4,5},{5,4},{6,7},{7,6},{8,9},{9,8},{10,11... | collective-permute-start | bytes 2457608 | tf_op jit(solution)/shard_map/ppermute | solution.py:216
  71.1 31.1 %collective-permute-start.12 = (bf16[512,800]{0,1:T(8,128)(2,1)S(1)}, bf16[512,800]{0,1:T(8,128)(2,1)}, u32[]{:S(2)}, u32[]{:S(2)}) collective-permute-start(bf16[512,800]{0,1:T(8,128)(2,1)S(1)} %collective-permute-done.8), channel_id=1, source_target_pairs={{0,1},{1,0},{2,3},{3,2},{4,5},{5,4},{6,7},{7,6},{8,9},{9,8},{10,11... | collective-permute-start | bytes 2457608 | tf_op jit(solution)/shard_map/ppermute | solution.py:216
  73.5 28.7 %collective-permute-start.13 = (bf16[512,800]{0,1:T(8,128)(2,1)S(1)}, bf16[512,800]{0,1:T(8,128)(2,1)}, u32[]{:S(2)}, u32[]{:S(2)}) collective-permute-start(bf16[512,800]{0,1:T(8,128)(2,1)S(1)} %collective-permute-done.9), channel_id=1, source_target_pairs={{0,1},{1,0},{2,3},{3,2},{4,5},{5,4},{6,7},{7,6},{8,9},{9,8},{10,11... | collective-permute-start | bytes 2457608 | tf_op jit(solution)/shard_map/ppermute | solution.py:216
  75.5 13.0 %collective-permute-start.4 = (bf16[72,2048]{1,0:T(8,128)(2,1)S(1)}, bf16[72,2048]{1,0:T(8,128)(2,1)S(1)}, u32[]{:S(2)}, u32[]{:S(2)}) collective-permute-start(bf16[72,2048]{1,0:T(8,128)(2,1)S(1)} %collective-permute-done.2.refs_0_), channel_id=1, source_target_pairs={{0,2},{1,3},{2,4},{3,5},{4,6},{5,7},{6,8},{7,9},{8,10},{9,11},{10,... | collective-permute-start | bytes 884744 | tf_op jit(solution)/shard_map/ppermute | solution.py:205
  78.4 0.7 copy-start.2
  88.5 0.7 copy-start.8
  89.2 11.0 %collective-permute-start.5 = (bf16[72,2048]{1,0:T(8,128)(2,1)}, bf16[72,2048]{1,0:T(8,128)(2,1)}, u32[]{:S(2)}, u32[]{:S(2)}) collective-permute-start(bf16[72,2048]{1,0:T(8,128)(2,1)} %collective-permute-done.3.refs_1_), channel_id=1, source_target_pairs={{0,14},{1,15},{2,0},{3,1},{4,2},{5,3},{6,4},{7,5},{8,6},{9,7},{10,... | collective-permute-start | bytes 884744 | tf_op jit(solution)/shard_map/ppermute | solution.py:206
  100.2 14.8 %collective-permute-start.6 = (bf16[72,2048]{1,0:T(8,128)(2,1)}, bf16[72,2048]{1,0:T(8,128)(2,1)S(1)}, u32[]{:S(2)}, u32[]{:S(2)}) collective-permute-start(bf16[72,2048]{1,0:T(8,128)(2,1)} %copy-done.8), channel_id=1, source_target_pairs={{0,2},{1,3},{2,4},{3,5},{4,6},{5,7},{6,8},{7,9},{8,10},{9,11},{10,... | collective-permute-start | bytes 884744 | tf_op jit(solution)/shard_map/ppermute | solution.py:211
  102.2 0.7 copy-start.10
  102.8 1.0 copy-start.1
  103.8 1.0 copy-start.5
  104.8 1.0 copy-start.7
  105.7 4.6 %copy-start.3 = (bf16[72,2048]{1,0:T(8,128)(2,1)S(1)}, bf16[72,2048]{1,0:T(8,128)(2,1)}, u32[]{:S(2)}) copy-start(bf16[72,2048]{1,0:T(8,128)(2,1)} %copy-done.2) | copy-start | bytes 884740
  110.4 4.7 %copy-start.9 = (bf16[72,2048]{1,0:T(8,128)(2,1)S(1)}, bf16[72,2048]{1,0:T(8,128)(2,1)}, u32[]{:S(2)}) copy-start(bf16[72,2048]{1,0:T(8,128)(2,1)} %copy-done.8) | copy-start | bytes 884740
  120.7 20.2 %all-to-all-start.1 = ((f32[64,1,64]{2,1,0:T(1,128)}), f32[64,1,64]{2,1,0:T(1,128)S(1)}, u32[]{:S(2)}, u32[]{:S(2)}) async-start(f32[64,1,64]{2,1,0:T(1,128)} %copy.21), calls=%async_computation.1 | async-start | bytes 65536 | tf_op jit(solution)/shard_map/all_to_all | solution.py:224

commit v3 on v2

--- a/solution.py
+++ b/solution.py
@@ -15,6 +15,7 @@
 CAP = 72
 LANES = 128
 DIGIT = 64
+TILE = 400
 PITCH = SLOT // (N_Y * 2)
 STATS = 4
 
@@ -65,22 +66,34 @@
     out_ref[:, :LANES] = (normed[:, :LANES] + tail).astype(jnp.bfloat16)
 
 
-def head_kernel(offsets, last, len_ref, *refs):
+def stack_kernel(w0, w1, w2, w3, out_ref, sem):
+    me = lax.axis_index("dp")
+    depth = w0.shape[1]
+    copies = []
+    for k, piece in enumerate((w0, w1, w2, w3)):
+        src = lax.rem(me - k + N_DP, N_DP)
+        cols = pl.ds(pl.multiple_of(src * depth, depth), depth)
+        copies.append(pltpu.make_async_copy(piece, out_ref.at[:, cols], sem.at[k]))
+    for c in copies:
+        c.start()
+    for c in copies:
+        c.wait()
+
+
+def head_kernel(offsets, len_ref, *refs):
     n = len(offsets)
-    x_refs, w_refs = refs[:n], refs[n : n + 2 * N_DP]
-    refs = refs[n + 2 * N_DP :]
+    x_refs, w_refs, refs = refs[:n], refs[n : n + 2], refs[n + 2 :]
     prev_ref = None
-    if len(refs) == 4:
+    if len(refs) == 3:
         prev_ref, refs = refs[0], refs[1:]
-    out_ref, logit_ref, stat_ref = refs
-    vocab_dev, depth = w_refs[0].shape
+    out_ref, stat_ref = refs
+    vocab_dev = w_refs[0].shape[0]
     y, core = my_place()
-    me = lax.axis_index("dp")
     t = lax.axis_index("tensor")
     sibling = t + 1 - 2 * core
     wide = 2 * LANES
 
-    x_all = jnp.concatenate([r[...] for r in x_refs], axis=0) if n > 1 else x_refs[0][...]
+    x_all = jnp.concatenate([r[...] for r in x_refs], axis=0)
     ids = jnp.zeros((1, wide), jnp.float32)
     for j in range(n):
         d = x_refs[j][CAP - 8 :, :LANES].astype(jnp.float32)
@@ -89,33 +102,30 @@
         ids = ids + (pltpu.roll(d, j * CAP, 1) if j else d)
     ids = ids[:, : n * CAP].astype(jnp.int32)
 
-    for half, base in ((0, t), (1, sibling)):
-        acc = None
-        for k in range(N_DP):
-            src = lax.rem(me - k + N_DP, N_DP)
-            cols = pl.ds(pl.multiple_of(src * depth, depth), depth)
-            x_k = jnp.concatenate([r[:, cols] for r in x_refs], axis=0)
-            part = lax.dot_general(
-                w_refs[half * N_DP + k][...],
-                x_k,
+    parts = []
+    for w_ref, owner in zip(w_refs, (t, sibling)):
+        for at in range(0, vocab_dev, TILE):
+            logits = lax.dot_general(
+                w_ref[at : at + TILE, :],
+                x_all,
                 (((1,), (1,)), ((), ())),
                 preferred_element_type=jnp.float32,
             )
-            acc = part if acc is None else acc + part
-        logit_ref[half * vocab_dev : (half + 1) * vocab_dev, :] = acc
-
-    logits = logit_ref[...]
-    row = lax.broadcasted_iota(jnp.int32, logits.shape, 0)
-    vocab = row + jnp.where(row < vocab_dev, t * vocab_dev, (sibling - 1) * vocab_dev)
-    top = jnp.max(logits, axis=0, keepdims=True)
-    expo = jnp.exp(logits - top)
+            row = lax.broadcasted_iota(jnp.int32, logits.shape, 0)
+            top = jnp.max(logits, axis=0, keepdims=True)
+            expo = jnp.exp(logits - top)
+            total = jnp.sum(expo, axis=0, keepdims=True)
+            moment = jnp.sum(expo * logits, axis=0, keepdims=True)
+            hit = row == ids - (owner * vocab_dev + at)
+            chosen = jnp.sum(jnp.where(hit, logits, 0.0), axis=0, keepdims=True)
+            parts.append((top, total, moment, chosen))
+    top = functools.reduce(jnp.maximum, [p[0] for p in parts])
+    scale = [jnp.exp(p[0] - top) for p in parts]
     stat_ref[...] = jnp.zeros_like(stat_ref)
     stat_ref[0:1, : n * CAP] = top
-    stat_ref[1:2, : n * CAP] = jnp.sum(expo, axis=0, keepdims=True)
-    stat_ref[2:3, : n * CAP] = jnp.sum(expo * logits, axis=0, keepdims=True)
-    stat_ref[3:4, : n * CAP] = jnp.sum(
-        jnp.where(vocab == ids, logits, 0.0), axis=0, keepdims=True
-    )
+    stat_ref[1:2, : n * CAP] = sum(p[1] * f for p, f in zip(parts, scale))
+    stat_ref[2:3, : n * CAP] = sum(p[2] * f for p, f in zip(parts, scale))
+    stat_ref[3:4, : n * CAP] = sum(p[3] for p in parts)
 
     if prev_ref is not None:
         out_ref[...] = prev_ref[...]
@@ -135,22 +145,19 @@
 
 def run_head(offsets, lengths, shards, weights, prev):
     n = len(offsets)
-    vocab_dev, depth = weights[0].shape
+    vocab_dev, width = weights[0].shape
     vmem = pl.BlockSpec(memory_space=pltpu.VMEM)
     args = [lengths, *shards, *weights] + ([] if prev is None else [prev])
     return pl.pallas_call(
-        functools.partial(head_kernel, offsets, False),
+        functools.partial(head_kernel, offsets),
         in_specs=[pl.BlockSpec(memory_space=pltpu.SMEM)] + [vmem] * (len(args) - 1),
         out_specs=vmem,
         out_shape=jax.ShapeDtypeStruct((N_Y, 8, LANES), jnp.float32),
-        scratch_shapes=[
-            pltpu.VMEM((2 * vocab_dev, n * CAP), jnp.float32),
-            pltpu.VMEM((8, 2 * LANES), jnp.float32),
-        ],
+        scratch_shapes=[pltpu.VMEM((8, 2 * LANES), jnp.float32)],
         compiler_params=pltpu.CompilerParams(vmem_limit_bytes=40 << 20),
         cost_estimate=pl.CostEstimate(
-            flops=2 * n * CAP * depth * N_DP * 2 * vocab_dev,
-            bytes_accessed=2 * depth * N_DP * (n * CAP + 2 * vocab_dev),
+            flops=2 * n * CAP * width * 2 * vocab_dev,
+            bytes_accessed=2 * width * (n * CAP + 2 * vocab_dev),
             transcendentals=n * CAP * 2 * vocab_dev,
         ),
     )(*args)
@@ -210,11 +217,20 @@
         down.append(pair[1])
     up.append(lax.ppermute(up[-1], "tensor", along_y(1)))
 
-    late = lax.optimization_barrier((*pieces[1:], up[2], down[2]))
-    weights = [p.T for p in pieces]
-    weights += [
-        lax.ppermute(p, "tensor", other_core).T for p in (head_weight, *late[: N_DP - 1])
-    ]
+    late = lax.optimization_barrier((*pieces, up[2], down[2]))
+    anywhere = pl.BlockSpec(memory_space=pl.ANY)
+    vocab_dev = head_weight.shape[1]
+    weight = pl.pallas_call(
+        stack_kernel,
+        in_specs=[anywhere] * N_DP,
+        out_specs=anywhere,
+        out_shape=jax.ShapeDtypeStruct((vocab_dev, width), jnp.bfloat16),
+        scratch_shapes=[pltpu.SemaphoreType.DMA((N_DP,))],
+        cost_estimate=pl.CostEstimate(
+            flops=0, bytes_accessed=4 * vocab_dev * width, transcendentals=0
+        ),
+    )(*[p.T for p in late[:N_DP]])
+    weights = [weight, lax.ppermute(weight, "tensor", other_core)]
     stats = run_head((0, -1, 1), lengths, [own, up[1], down[1]], weights, None)
     stats = run_head((-2, 2), lengths, [up[2], down[2]], weights, stats)
     stats = run_head((-3, 3, -4), lengths, [up[3], down[3], up[4]], weights, stats)

time: 143 us -> 227 us (1.59)
  Pallas kernels: 16.2 us -> 113 us
  waiting for transfers between devices: 47.1 us -> 39.6 us
  starting transfers between devices: 64.4 us -> 59.6 us
    pallas_call x3 -> x4, Pallas kernels: 13.9 us -> 111 us  [the longest x1 100 us: per_device(): pl.pallas_call(stack_kernel, in_specs=[anywhere] * N_DP, out_specs=anywhe...]
    ppermute x4 -> x1, starting transfers between devices: 8.16 us -> 1.92 us  [per_device(): weights = [weight, lax.ppermute(weight, 'tensor', other_core)]]
    ppermute x3, waiting for transfers between devices: 9.94 us -> 5.57 us  [per_device(): lax.ppermute(down[-1], 'tensor', along_y(-1))]
    ppermute x3, waiting for transfers between devices: 13.6 us -> 10.4 us  [per_device(): lax.ppermute(up[-1], 'tensor', along_y(1))]
    unnamed x23 -> x21, local copies, waits for them, and re-layouts: 6.53 us -> 7.75 us
  transfers between devices with their start and end apart: 16 -> 13, of which waited for: 8 -> 8; matrix products, arithmetic and copies ran while one was open for 2% -> 0% of each run, Pallas kernels for 8% -> 4%
where the time goes in v3:
time: 227 us; the launch traced here: 226 us
  Pallas kernels  113 us (50%)
  starting transfers between devices  59.6 us (26%)
  waiting for transfers between devices  39.6 us (17%)
  local copies, waits for them, and re-layouts  10.9 us (5%)
  other arithmetic  2.49 us (1%)
    pallas_call x1, Pallas kernels, per_device(): pl.pallas_call(stack_kernel, in_specs=[anywhere] * N_DP, out_specs=anywhe...  100 us
    all_to_all x1, starting transfers between devices, per_device(): recv = lax.all_to_all(sent, 'tensor', 0, 0, axis_index_groups=same_core)  16.6 us
    ppermute x3, starting transfers between devices, per_device(): lax.ppermute(down[-1], 'tensor', along_y(-1))  12.4 us
    all_to_all x1, waiting for transfers between devices, per_device(): back = lax.all_to_all(sent, 'tensor', 0, 0, axis_index_groups=same_core)  11.9 us
    all_to_all x1, waiting for transfers between devices, per_device(): recv = lax.all_to_all(sent, 'tensor', 0, 0, axis_index_groups=same_core)  11.8 us
    ppermute x3, waiting for transfers between devices, per_device(): lax.ppermute(up[-1], 'tensor', along_y(1))  10.4 us
    pallas_call x3, Pallas kernels, run_head(): pl.pallas_call(functools.partial(head_kernel, offsets), in_specs=[pl.Bloc...  10.2 us
    ppermute x3, starting transfers between devices, per_device(): lax.ppermute(up[-1], 'tensor', along_y(1))  8.97 us
  transfers between devices with their start and end apart: 13, of which 8 were waited for; matrix products, arithmetic and copies ran while one was open for 0% of the time, Pallas kernels for 4%

profile of v3, /device:TPU:6, one launch (start us, length us, event | category | flops | bytes accessed | tf_op | source)
XLA Modules:
  0.0 226.4 jit_solution(4482767441039548879)
XLA Ops:
  0.6 0.7 convert_bitcast_fusion
  1.3 0.1 copy.23
  1.4 0.8 fusion.1
  2.3 1.1 broadcast_in_dim.39
  3.4 16.6 %all-to-all-start = ((bf16[64,2,2176]{2,1,0:T(2,128)(2,1)}), bf16[64,2,2176]{2,1,0:T(2,128)(2,1)S(1)}, u32[]{:S(2)}, u32[]{:S(2)}) async-start(bf16[64,2,2176]{2,1,0:T(2,128)(2,1)} %bitcast.4), calls=%async_computation | async-start | bytes 1114112 | tf_op jit(solution)/shard_map/all_to_all | solution.py:194
  20.0 2.4 %collective-permute-start.7 = (bf16[512,800]{0,1:T(8,128)(2,1)}, bf16[512,800]{0,1:T(8,128)(2,1)S(1)}, u32[]{:S(2)}, u32[]{:S(2)}) collective-permute-start(bf16[512,800]{0,1:T(8,128)(2,1)} %param.7), channel_id=1, source_target_pairs={{0,128},{128,256},{256,384},{384,0},{1,129},{129,257},{257,385},{3... | collective-permute-start | bytes 2457608 | tf_op jit(solution)/shard_map/ppermute | solution.py:182
  22.4 4.3 %collective-permute-start.8 = (bf16[512,800]{0,1:T(8,128)(2,1)}, bf16[512,800]{0,1:T(8,128)(2,1)S(1)}, u32[]{:S(2)}, u32[]{:S(2)}) collective-permute-start(bf16[512,800]{0,1:T(8,128)(2,1)} %param.7), channel_id=1, source_target_pairs={{0,256},{128,384},{256,0},{384,128},{1,257},{129,385},{257,1},{385... | collective-permute-start | bytes 2457608 | tf_op jit(solution)/shard_map/ppermute | solution.py:182
  26.7 1.9 collective-permute-start.9
  28.7 11.8 %all-to-all-done = bf16[64,2,2176]{2,1,0:T(2,128)(2,1)S(1)} async-done(((bf16[64,2,2176]{2,1,0:T(2,128)(2,1)}), bf16[64,2,2176]{2,1,0:T(2,128)(2,1)S(1)}, u32[]{:S(2)}, u32[]{:S(2)}) %all-to-all-start) | async-done | bytes 557088 | tf_op jit(solution)/shard_map/all_to_all | solution.py:194
  40.4 1.0 reshape.43.recv_ref
  41.4 2.2 shard_map.68.refs_0_
  43.7 3.1 %collective-permute-start = (bf16[72,2048]{1,0:T(8,128)(2,1)}, bf16[72,2048]{1,0:T(8,128)(2,1)S(1)}, u32[]{:S(2)}, u32[]{:S(2)}) collective-permute-start(bf16[72,2048]{1,0:T(8,128)(2,1)} %shard_map.68.refs_0_), channel_id=1, source_target_pairs={{0,2},{1,3},{2,4},{3,5},{4,6},{5,7},{6,8},{7,9},{8,10},{9,11},{10,... | collective-permute-start | bytes 884744 | tf_op jit(solution)/shard_map/ppermute | solution.py:212
  46.8 3.9 %collective-permute-start.1 = (bf16[72,2048]{1,0:T(8,128)(2,1)}, bf16[72,2048]{1,0:T(8,128)(2,1)S(1)}, u32[]{:S(2)}, u32[]{:S(2)}) collective-permute-start(bf16[72,2048]{1,0:T(8,128)(2,1)} %shard_map.68.refs_0_), channel_id=1, source_target_pairs={{0,14},{1,15},{2,0},{3,1},{4,2},{5,3},{6,4},{7,5},{8,6},{9,7},{10,... | collective-permute-start | bytes 884744 | tf_op jit(solution)/shard_map/ppermute | solution.py:213
  50.7 3.0 %collective-permute-done.refs_1_ = bf16[72,2048]{1,0:T(8,128)(2,1)S(1)} collective-permute-done((bf16[72,2048]{1,0:T(8,128)(2,1)}, bf16[72,2048]{1,0:T(8,128)(2,1)S(1)}, u32[]{:S(2)}, u32[]{:S(2)}) %collective-permute-start) | collective-permute-done | bytes 294944 | tf_op jit(solution)/shard_map/ppermute | solution.py:212
  53.7 1.9 collective-permute-done.1.refs_2_
  55.6 2.9 %collective-permute-start.2 = (bf16[72,2048]{1,0:T(8,128)(2,1)S(1)}, bf16[72,2048]{1,0:T(8,128)(2,1)}, u32[]{:S(2)}, u32[]{:S(2)}) collective-permute-start(bf16[72,2048]{1,0:T(8,128)(2,1)S(1)} %collective-permute-done.refs_1_), channel_id=1, source_target_pairs={{0,2},{1,3},{2,4},{3,5},{4,6},{5,7},{6,8},{7,9},{8,10},{9,11},{10,... | collective-permute-start | bytes 884744 | tf_op jit(solution)/shard_map/ppermute | solution.py:212
  58.6 0.7 copy-done.2
  59.3 4.1 %collective-permute-start.3 = (bf16[72,2048]{1,0:T(8,128)(2,1)S(1)}, bf16[72,2048]{1,0:T(8,128)(2,1)}, u32[]{:S(2)}, u32[]{:S(2)}) collective-permute-start(bf16[72,2048]{1,0:T(8,128)(2,1)S(1)} %collective-permute-done.1.refs_2_), channel_id=1, source_target_pairs={{0,14},{1,15},{2,0},{3,1},{4,2},{5,3},{6,4},{7,5},{8,6},{9,7},{10,... | collective-permute-start | bytes 884744 | tf_op jit(solution)/shard_map/ppermute | solution.py:213
  63.4 0.7 copy-done.4
  64.1 1.4 collective-permute-done.2.refs_0_
  65.5 2.4 %collective-permute-done.3.refs_1_ = bf16[72,2048]{1,0:T(8,128)(2,1)} collective-permute-done((bf16[72,2048]{1,0:T(8,128)(2,1)S(1)}, bf16[72,2048]{1,0:T(8,128)(2,1)}, u32[]{:S(2)}, u32[]{:S(2)}) %collective-permute-start.3) | collective-permute-done | bytes 294944 | tf_op jit(solution)/shard_map/ppermute | solution.py:213
  68.0 0.9 copy-done.7
  68.9 0.3 copy-done.8
  69.2 0.2 copy-done.9
  69.4 100.4 %shard_map.69.refs_3_.refs_2_ = bf16[800,2048]{1,0:T(8,128)(2,1)} custom-call(bf16[800,512]{1,0:T(8,128)(2,1)} %bitcast.40, bf16[800,512]{1,0:T(8,128)(2,1)} %bitcast.41, bf16[800,512]{1,0:T(8,128)(2,1)} %bitcast.42, bf16[800,512]{1,0:T(8,128)(2,1)} %bitcast.43), custom_call_target="tpu_custom_call" | custom-call | bytes 6553600 | tf_op jit(solution)/shard_map/pallas_call | solution.py:223
  169.8 1.9 collective-permute-start.10
  171.8 2.9 %collective-permute-start.4 = (bf16[72,2048]{1,0:T(8,128)(2,1)}, bf16[72,2048]{1,0:T(8,128)(2,1)}, u32[]{:S(2)}, u32[]{:S(2)}) collective-permute-start(bf16[72,2048]{1,0:T(8,128)(2,1)} %collective-permute-done.2.refs_0_), channel_id=1, source_target_pairs={{0,2},{1,3},{2,4},{3,5},{4,6},{5,7},{6,8},{7,9},{8,10},{9,11},{10,... | collective-permute-start | bytes 884744 | tf_op jit(solution)/shard_map/ppermute | solution.py:212
  174.7 4.3 %collective-permute-start.5 = (bf16[72,2048]{1,0:T(8,128)(2,1)}, bf16[72,2048]{1,0:T(8,128)(2,1)}, u32[]{:S(2)}, u32[]{:S(2)}) collective-permute-start(bf16[72,2048]{1,0:T(8,128)(2,1)} %collective-permute-done.3.refs_1_), channel_id=1, source_target_pairs={{0,14},{1,15},{2,0},{3,1},{4,2},{5,3},{6,4},{7,5},{8,6},{9,7},{10,... | collective-permute-start | bytes 884744 | tf_op jit(solution)/shard_map/ppermute | solution.py:213
  179.1 6.0 %collective-permute-done.4.refs_0_ = bf16[72,2048]{1,0:T(8,128)(2,1)} collective-permute-done((bf16[72,2048]{1,0:T(8,128)(2,1)}, bf16[72,2048]{1,0:T(8,128)(2,1)}, u32[]{:S(2)}, u32[]{:S(2)}) %collective-permute-start.4) | collective-permute-done | bytes 294944 | tf_op jit(solution)/shard_map/ppermute | solution.py:212
  185.1 1.2 collective-permute-done.5.refs_1_
  186.3 3.6 %collective-permute-start.6 = (bf16[72,2048]{1,0:T(8,128)(2,1)}, bf16[72,2048]{1,0:T(8,128)(2,1)S(1)}, u32[]{:S(2)}, u32[]{:S(2)}) collective-permute-start(bf16[72,2048]{1,0:T(8,128)(2,1)} %collective-permute-done.4.refs_0_), channel_id=1, source_target_pairs={{0,2},{1,3},{2,4},{3,5},{4,6},{5,7},{6,8},{7,9},{8,10},{9,11},{10,... | collective-permute-start | bytes 884744 | tf_op jit(solution)/shard_map/ppermute | solution.py:218
  190.0 1.9 copy-done
  191.9 1.0 copy-done.1
  192.9 1.0 copy-done.3
  193.8 1.0 copy-done.5
  194.8 3.1 %shard_map.70.refs_4_ = f32[8,8,128]{2,1,0:T(8,128)S(1)} custom-call(s32[1,4]{1,0:T(1,128)S(1)} %copy-done.6, bf16[72,2048]{1,0:T(8,128)(2,1)S(1)} %copy-done.1, bf16[72,2048]{1,0:T(8,128)(2,1)S(1)} %copy-done.3, bf16[72,2048]{1,0:T(8,128)(2,1)S(1)} %copy-done.5, bf16[800,2048]{1,0:T(8,128)(2,1)S(1)} %copy-done, ...), custom_call_target="tpu_custom_call" | custom-call | flops 1415577600 | bytes 7438336 | tf_op jit(solution)/shard_map/pallas_call | solution.py:151
  197.8 3.5 %shard_map.71.refs_5_ = f32[8,8,128]{2,1,0:T(8,128)S(1)} custom-call(s32[1,4]{1,0:T(1,128)S(1)} %copy-done.6, bf16[72,2048]{1,0:T(8,128)(2,1)} %collective-permute-done.2.refs_0_, bf16[72,2048]{1,0:T(8,128)(2,1)} %collective-permute-done.3.refs_1_, bf16[800,2048]{1,0:T(8,128)(2,1)S(1)} %copy-done, ...), custom_call_target="tpu_custom_call" | custom-call | flops 943718400 | bytes 7143424 | tf_op jit(solution)/shard_map/pallas_call | solution.py:151
  201.4 3.6 %shard_map.72 = f32[8,8,128]{2,1,0:T(8,128)S(1)} custom-call(s32[1,4]{1,0:T(1,128)S(1)} %copy-done.6, bf16[72,2048]{1,0:T(8,128)(2,1)} %collective-permute-done.4.refs_0_, bf16[72,2048]{1,0:T(8,128)(2,1)} %collective-permute-done.5.refs_1_, bf16[72,2048]{1,0:T(8,128)(2,1)S(1)} %collective-permute-done.6.refs_2_, bf16[800,2048]{1,0:T(8,128)(2,1)S(1)} %copy-done, ...), custom_call_target="tpu_custom_call" | custom-call | flops 1415577600 | bytes 7438336 | tf_op jit(solution)/shard_map/pallas_call | solution.py:151
  205.0 0.1 copy.19
  205.1 0.1 copy.20
  205.3 0.7 copy.21
  206.0 7.5 %all-to-all-start.1 = ((f32[64,1,64]{2,1,0:T(1,128)}), f32[64,1,64]{2,1,0:T(1,128)S(1)}, u32[]{:S(2)}, u32[]{:S(2)}) async-start(f32[64,1,64]{2,1,0:T(1,128)} %copy.21), calls=%async_computation.1 | async-start | bytes 65536 | tf_op jit(solution)/shard_map/all_to_all | solution.py:240
  213.5 0.1 select_reduce_fusion
  213.6 11.9 %all-to-all-done.1 = f32[64,1,64]{2,1,0:T(1,128)S(1)} async-done(((f32[64,1,64]{2,1,0:T(1,128)}), f32[64,1,64]{2,1,0:T(1,128)S(1)}, u32[]{:S(2)}, u32[]{:S(2)}) %all-to-all-start.1) | async-done | bytes 16416 | tf_op jit(solution)/shard_map/all_to_all | solution.py:240
  225.5 0.1 copy.22
  225.5 0.1 slice_reduce_fusion.1
  225.7 0.2 fusion.3
  225.9 0.5 subtract_select_fusion
  (20 shorter events, 0.1 us)
Async XLA Ops:
  3.4 37.0 %all-to-all-start = ((bf16[64,2,2176]{2,1,0:T(2,128)(2,1)}), bf16[64,2,2176]{2,1,0:T(2,128)(2,1)S(1)}, u32[]{:S(2)}, u32[]{:S(2)}) async-start(bf16[64,2,2176]{2,1,0:T(2,128)(2,1)} %bitcast.4), calls=%async_computation | async-start | bytes 1114112 | tf_op jit(solution)/shard_map/all_to_all | solution.py:194
  20.0 48.0 %collective-permute-start.7 = (bf16[512,800]{0,1:T(8,128)(2,1)}, bf16[512,800]{0,1:T(8,128)(2,1)S(1)}, u32[]{:S(2)}, u32[]{:S(2)}) collective-permute-start(bf16[512,800]{0,1:T(8,128)(2,1)} %param.7), channel_id=1, source_target_pairs={{0,128},{128,256},{256,384},{384,0},{1,129},{129,257},{257,385},{3... | collective-permute-start | bytes 2457608 | tf_op jit(solution)/shard_map/ppermute | solution.py:182
  22.4 45.6 %collective-permute-start.8 = (bf16[512,800]{0,1:T(8,128)(2,1)}, bf16[512,800]{0,1:T(8,128)(2,1)S(1)}, u32[]{:S(2)}, u32[]{:S(2)}) collective-permute-start(bf16[512,800]{0,1:T(8,128)(2,1)} %param.7), channel_id=1, source_target_pairs={{0,256},{128,384},{256,0},{384,128},{1,257},{129,385},{257,1},{385... | collective-permute-start | bytes 2457608 | tf_op jit(solution)/shard_map/ppermute | solution.py:182
  26.7 41.3 %collective-permute-start.9 = (bf16[512,800]{0,1:T(8,128)(2,1)}, bf16[512,800]{0,1:T(8,128)(2,1)S(1)}, u32[]{:S(2)}, u32[]{:S(2)}) collective-permute-start(bf16[512,800]{0,1:T(8,128)(2,1)} %param.7), channel_id=1, source_target_pairs={{0,384},{128,0},{256,128},{384,256},{1,385},{129,1},{257,129},{385... | collective-permute-start | bytes 2457608 | tf_op jit(solution)/shard_map/ppermute | solution.py:182
  43.7 10.0 %collective-permute-start = (bf16[72,2048]{1,0:T(8,128)(2,1)}, bf16[72,2048]{1,0:T(8,128)(2,1)S(1)}, u32[]{:S(2)}, u32[]{:S(2)}) collective-permute-start(bf16[72,2048]{1,0:T(8,128)(2,1)} %shard_map.68.refs_0_), channel_id=1, source_target_pairs={{0,2},{1,3},{2,4},{3,5},{4,6},{5,7},{6,8},{7,9},{8,10},{9,11},{10,... | collective-permute-start | bytes 884744 | tf_op jit(solution)/shard_map/ppermute | solution.py:212
  46.8 8.8 %collective-permute-start.1 = (bf16[72,2048]{1,0:T(8,128)(2,1)}, bf16[72,2048]{1,0:T(8,128)(2,1)S(1)}, u32[]{:S(2)}, u32[]{:S(2)}) collective-permute-start(bf16[72,2048]{1,0:T(8,128)(2,1)} %shard_map.68.refs_0_), channel_id=1, source_target_pairs={{0,14},{1,15},{2,0},{3,1},{4,2},{5,3},{6,4},{7,5},{8,6},{9,7},{10,... | collective-permute-start | bytes 884744 | tf_op jit(solution)/shard_map/ppermute | solution.py:213
  55.6 9.9 %collective-permute-start.2 = (bf16[72,2048]{1,0:T(8,128)(2,1)S(1)}, bf16[72,2048]{1,0:T(8,128)(2,1)}, u32[]{:S(2)}, u32[]{:S(2)}) collective-permute-start(bf16[72,2048]{1,0:T(8,128)(2,1)S(1)} %collective-permute-done.refs_1_), channel_id=1, source_target_pairs={{0,2},{1,3},{2,4},{3,5},{4,6},{5,7},{6,8},{7,9},{8,10},{9,11},{10,... | collective-permute-start | bytes 884744 | tf_op jit(solution)/shard_map/ppermute | solution.py:212
  58.6 0.7 copy-start.2
  59.3 8.7 %collective-permute-start.3 = (bf16[72,2048]{1,0:T(8,128)(2,1)S(1)}, bf16[72,2048]{1,0:T(8,128)(2,1)}, u32[]{:S(2)}, u32[]{:S(2)}) collective-permute-start(bf16[72,2048]{1,0:T(8,128)(2,1)S(1)} %collective-permute-done.1.refs_2_), channel_id=1, source_target_pairs={{0,14},{1,15},{2,0},{3,1},{4,2},{5,3},{6,4},{7,5},{8,6},{9,7},{10,... | collective-permute-start | bytes 884744 | tf_op jit(solution)/shard_map/ppermute | solution.py:213
  63.4 0.7 copy-start.4
  68.0 0.9 copy-start.7
  68.0 1.2 copy-start.8
  68.0 1.4 copy-start.9
  69.4 120.5 %copy-start.6 = (s32[1,4]{1,0:T(1,128)S(1)}, s32[1,4]{1,0:T(1,128)}, u32[]{:S(2)}) copy-start(s32[1,4]{1,0:T(1,128)} %len_ref.7) | copy-start | bytes 52
  169.8 20.1 %collective-permute-start.10 = (bf16[800,2048]{1,0:T(8,128)(2,1)}, bf16[800,2048]{1,0:T(8,128)(2,1)S(1)}, u32[]{:S(2)}, u32[]{:S(2)}) collective-permute-start(bf16[800,2048]{1,0:T(8,128)(2,1)} %shard_map.69.refs_3_.refs_2_), channel_id=1, source_target_pairs={{0,1},{1,0},{2,3},{3,2},{4,5},{5,4},{6,7},{7,6},{8,9},{9,8},{10,11... | collective-permute-start | bytes 9830408 | tf_op jit(solution)/shard_map/ppermute | solution.py:233
  171.8 13.3 %collective-permute-start.4 = (bf16[72,2048]{1,0:T(8,128)(2,1)}, bf16[72,2048]{1,0:T(8,128)(2,1)}, u32[]{:S(2)}, u32[]{:S(2)}) collective-permute-start(bf16[72,2048]{1,0:T(8,128)(2,1)} %collective-permute-done.2.refs_0_), channel_id=1, source_target_pairs={{0,2},{1,3},{2,4},{3,5},{4,6},{5,7},{6,8},{7,9},{8,10},{9,11},{10,... | collective-permute-start | bytes 884744 | tf_op jit(solution)/shard_map/ppermute | solution.py:212
  174.7 11.6 %collective-permute-start.5 = (bf16[72,2048]{1,0:T(8,128)(2,1)}, bf16[72,2048]{1,0:T(8,128)(2,1)}, u32[]{:S(2)}, u32[]{:S(2)}) collective-permute-start(bf16[72,2048]{1,0:T(8,128)(2,1)} %collective-permute-done.3.refs_1_), channel_id=1, source_target_pairs={{0,14},{1,15},{2,0},{3,1},{4,2},{5,3},{6,4},{7,5},{8,6},{9,7},{10,... | collective-permute-start | bytes 884744 | tf_op jit(solution)/shard_map/ppermute | solution.py:213
  186.3 15.1 %collective-permute-start.6 = (bf16[72,2048]{1,0:T(8,128)(2,1)}, bf16[72,2048]{1,0:T(8,128)(2,1)S(1)}, u32[]{:S(2)}, u32[]{:S(2)}) collective-permute-start(bf16[72,2048]{1,0:T(8,128)(2,1)} %collective-permute-done.4.refs_0_), channel_id=1, source_target_pairs={{0,2},{1,3},{2,4},{3,5},{4,6},{5,7},{6,8},{7,9},{8,10},{9,11},{10,... | collective-permute-start | bytes 884744 | tf_op jit(solution)/shard_map/ppermute | solution.py:218
  190.0 1.9 copy-start
  191.9 1.0 copy-start.1
  192.8 1.0 copy-start.3
  193.8 1.0 copy-start.5
  206.0 19.5 %all-to-all-start.1 = ((f32[64,1,64]{2,1,0:T(1,128)}), f32[64,1,64]{2,1,0:T(1,128)S(1)}, u32[]{:S(2)}, u32[]{:S(2)}) async-start(f32[64,1,64]{2,1,0:T(1,128)} %copy.21), calls=%async_computation.1 | async-start | bytes 65536 | tf_op jit(solution)/shard_map/all_to_all | solution.py:240

commit v4 on v3

--- a/solution.py
+++ b/solution.py
@@ -20,8 +20,8 @@
 STATS = 4
 
 
-def class_layout(len_ref, y_class, core):
-    first = core * (N_Y * PER_CLASS) + y_class * PER_CLASS
+def class_layout(len_ref, place, core):
+    first = core * (N_Y * PER_CLASS) + place * PER_CLASS
     starts, counts, at = [], [], 0
     for s in range(SEQ_DP):
         n = jnp.clip(lax.div(len_ref[0, s] - first + (PITCH - 1), PITCH), 0, SLOT // PITCH)
@@ -33,13 +33,16 @@
 
 def my_place():
     t = lax.axis_index("tensor")
-    return lax.rem(lax.div(t, N_CORE), N_Y), lax.rem(t, N_CORE)
+    core = lax.rem(t, N_CORE)
+    y = lax.rem(lax.div(t, N_CORE), N_Y)
+    z = lax.div(t, N_CORE * N_Y)
+    return jnp.where(core == 0, y, z), core
 
 
 def pack_kernel(len_ref, recv_ref, gain_ref, out_ref):
     width = gain_ref.shape[1]
-    y, core = my_place()
-    starts, counts = class_layout(len_ref, y, core)
+    mine, core = my_place()
+    starts, counts = class_layout(len_ref, mine, core)
     shape = (LANES, LANES)
     k = lax.broadcasted_iota(jnp.int32, shape, 0)
     i = lax.broadcasted_iota(jnp.int32, shape, 1)
@@ -66,7 +69,8 @@
     out_ref[:, :LANES] = (normed[:, :LANES] + tail).astype(jnp.bfloat16)
 
 
-def stack_kernel(w0, w1, w2, w3, out_ref, sem):
+def stack_kernel(w0, w1, w2, w3, up_ref, down_ref, out_ref, sem):
+    del up_ref, down_ref
     me = lax.axis_index("dp")
     depth = w0.shape[1]
     copies = []
@@ -84,41 +88,53 @@
     n = len(offsets)
     x_refs, w_refs, refs = refs[:n], refs[n : n + 2], refs[n + 2 :]
     prev_ref = None
-    if len(refs) == 3:
+    if len(refs) == 6:
         prev_ref, refs = refs[0], refs[1:]
-    out_ref, stat_ref = refs
+    out_ref, stat_ref, x_ref, w_ref, sem = refs
     vocab_dev = w_refs[0].shape[0]
-    y, core = my_place()
+    mine, core = my_place()
     t = lax.axis_index("tensor")
     sibling = t + 1 - 2 * core
     wide = 2 * LANES
 
-    x_all = jnp.concatenate([r[...] for r in x_refs], axis=0)
+    copies = [pltpu.make_async_copy(r, x_ref.at[j], sem.at[j]) for j, r in enumerate(x_refs)]
+    tiles = []
+    for half, ref in enumerate(w_refs):
+        for at in range(0, vocab_dev, TILE):
+            i = len(tiles)
+            copy = pltpu.make_async_copy(ref.at[at : at + TILE, :], w_ref.at[i], sem.at[n + i])
+            tiles.append((copy, half, at))
+    for c in copies + [tile[0] for tile in tiles]:
+        c.start()
+    for c in copies:
+        c.wait()
+    x_all = jnp.concatenate([x_ref[j] for j in range(n)], axis=0)
     ids = jnp.zeros((1, wide), jnp.float32)
     for j in range(n):
-        d = x_refs[j][CAP - 8 :, :LANES].astype(jnp.float32)
+        d = x_ref[j, CAP - 8 :, :LANES].astype(jnp.float32)
         d = (d[5:6] * DIGIT + d[6:7]) * DIGIT + d[7:8]
         d = jnp.concatenate([d, jnp.zeros_like(d)], axis=1)
         ids = ids + (pltpu.roll(d, j * CAP, 1) if j else d)
     ids = ids[:, : n * CAP].astype(jnp.int32)
 
     parts = []
-    for w_ref, owner in zip(w_refs, (t, sibling)):
-        for at in range(0, vocab_dev, TILE):
-            logits = lax.dot_general(
-                w_ref[at : at + TILE, :],
-                x_all,
-                (((1,), (1,)), ((), ())),
-                preferred_element_type=jnp.float32,
-            )
-            row = lax.broadcasted_iota(jnp.int32, logits.shape, 0)
-            top = jnp.max(logits, axis=0, keepdims=True)
-            expo = jnp.exp(logits - top)
-            total = jnp.sum(expo, axis=0, keepdims=True)
-            moment = jnp.sum(expo * logits, axis=0, keepdims=True)
-            hit = row == ids - (owner * vocab_dev + at)
-            chosen = jnp.sum(jnp.where(hit, logits, 0.0), axis=0, keepdims=True)
-            parts.append((top, total, moment, chosen))
+    for i, (copy, half, at) in enumerate(tiles):
+        owner = sibling if half else t
+        copy.wait()
+        logits = lax.dot_general(
+            w_ref[i],
+            x_all,
+            (((1,), (1,)), ((), ())),
+            preferred_element_type=jnp.float32,
+        )
+        row = lax.broadcasted_iota(jnp.int32, logits.shape, 0)
+        top = jnp.max(logits, axis=0, keepdims=True)
+        expo = jnp.exp(logits - top)
+        total = jnp.sum(expo, axis=0, keepdims=True)
+        moment = jnp.sum(expo * logits, axis=0, keepdims=True)
+        hit = row == ids - (owner * vocab_dev + at)
+        chosen = jnp.sum(jnp.where(hit, logits, 0.0), axis=0, keepdims=True)
+        parts.append((top, total, moment, chosen))
     top = functools.reduce(jnp.maximum, [p[0] for p in parts])
     scale = [jnp.exp(p[0] - top) for p in parts]
     stat_ref[...] = jnp.zeros_like(stat_ref)
@@ -133,28 +149,35 @@
     per_slot = PER_CLASS * SLOT // PITCH
     stats = stat_ref[...]
     for j, offset in enumerate(offsets):
-        y_class = lax.rem(y + offset + N_Y, N_Y)
-        starts, _ = class_layout(len_ref, y_class, core)
+        place = lax.rem(mine + offset + N_Y, N_Y)
+        starts, _ = class_layout(len_ref, place, core)
         spread = jnp.zeros((8, LANES), jnp.float32)
         for s in range(SEQ_DP):
             shift = lax.rem(s * per_slot - j * CAP - starts[s] + 2 * wide, wide)
             moved = pltpu.roll(stats, shift, 1)[:, :LANES]
             spread = jnp.where(lane // per_slot == s, moved, spread)
-        out_ref[pl.ds(y_class, 1)] = spread[None]
+        out_ref[pl.ds(place, 1)] = spread[None]
 
 
 def run_head(offsets, lengths, shards, weights, prev):
     n = len(offsets)
     vocab_dev, width = weights[0].shape
     vmem = pl.BlockSpec(memory_space=pltpu.VMEM)
+    anywhere = pl.BlockSpec(memory_space=pl.ANY)
     args = [lengths, *shards, *weights] + ([] if prev is None else [prev])
     return pl.pallas_call(
         functools.partial(head_kernel, offsets),
-        in_specs=[pl.BlockSpec(memory_space=pltpu.SMEM)] + [vmem] * (len(args) - 1),
+        in_specs=[pl.BlockSpec(memory_space=pltpu.SMEM)]
+        + [anywhere] * (n + 2)
+        + [vmem] * (len(args) - 3 - n),
         out_specs=vmem,
         out_shape=jax.ShapeDtypeStruct((N_Y, 8, LANES), jnp.float32),
-        scratch_shapes=[pltpu.VMEM((8, 2 * LANES), jnp.float32)],
-        compiler_params=pltpu.CompilerParams(vmem_limit_bytes=40 << 20),
+        scratch_shapes=[
+            pltpu.VMEM((8, 2 * LANES), jnp.float32),
+            pltpu.VMEM((n, CAP, width), jnp.bfloat16),
+            pltpu.VMEM((2 * vocab_dev // TILE, TILE, width), jnp.bfloat16),
+            pltpu.SemaphoreType.DMA((n + 2 * vocab_dev // TILE,)),
+        ],
         cost_estimate=pl.CostEstimate(
             flops=2 * n * CAP * width * 2 * vocab_dev,
             bytes_accessed=2 * width * (n * CAP + 2 * vocab_dev),
@@ -171,11 +194,15 @@
     same_core = [[N_CORE * k + c for k in range(n_chip)] for c in range(N_CORE)]
     other_core = [(i, i ^ 1) for i in range(n_t)]
 
-    def along_y(by):
+    def along(by):
         step = []
         for i in range(n_t):
-            y = (i // N_CORE) % N_Y
-            step.append((i, i + ((y + by) % N_Y - y) * N_CORE))
+            z, y, core = i // (N_Y * N_CORE), i // N_CORE % N_Y, i % N_CORE
+            if core == 0:
+                y = (y + by) % N_Y
+            else:
+                z = (z + by) % N_Z
+            step.append((i, (z * N_Y + y) * N_CORE + core))
         return step
 
     pieces = [head_weight] + [
@@ -188,9 +215,12 @@
     ).astype(jnp.bfloat16)
     digits = jnp.pad(digits, ((0, 0), (0, LANES - 3)))
     sent = jnp.concatenate([hidden, digits], axis=1).reshape(N_Y, PER_CLASS, width + LANES)
-    sent = jnp.broadcast_to(sent[None], (N_Z,) + sent.shape).reshape(
-        n_chip, PER_CLASS, width + LANES
-    )
+    square = (N_Z, N_Y) + sent.shape[1:]
+    sent = jnp.where(
+        tensor_idx % N_CORE == 0,
+        jnp.broadcast_to(sent[None], square),
+        jnp.broadcast_to(sent[:, None], square),
+    ).reshape(n_chip, PER_CLASS, width + LANES)
     recv = lax.all_to_all(sent, "tensor", 0, 0, axis_index_groups=same_core)
     recv = recv.reshape(n_chip * PER_CLASS, width + LANES)
 
@@ -209,27 +239,24 @@
     down = [own]
     for _ in range(N_Y // 2 - 1):
         pair = (
-            lax.ppermute(up[-1], "tensor", along_y(1)),
-            lax.ppermute(down[-1], "tensor", along_y(-1)),
+            lax.ppermute(up[-1], "tensor", along(1)),
+            lax.ppermute(down[-1], "tensor", along(-1)),
         )
-        pair = lax.optimization_barrier(pair)
         up.append(pair[0])
         down.append(pair[1])
-    up.append(lax.ppermute(up[-1], "tensor", along_y(1)))
-
-    late = lax.optimization_barrier((*pieces, up[2], down[2]))
-    anywhere = pl.BlockSpec(memory_space=pl.ANY)
+    up.append(lax.ppermute(up[-1], "tensor", along(1)))
+
     vocab_dev = head_weight.shape[1]
     weight = pl.pallas_call(
         stack_kernel,
-        in_specs=[anywhere] * N_DP,
-        out_specs=anywhere,
+        in_specs=[pl.BlockSpec(memory_space=pl.ANY)] * (N_DP + 2),
+        out_specs=vmem,
         out_shape=jax.ShapeDtypeStruct((vocab_dev, width), jnp.bfloat16),
         scratch_shapes=[pltpu.SemaphoreType.DMA((N_DP,))],
         cost_estimate=pl.CostEstimate(
             flops=0, bytes_accessed=4 * vocab_dev * width, transcendentals=0
         ),
-    )(*[p.T for p in late[:N_DP]])
+    )(*[p.T for p in pieces], up[2], down[2])
     weights = [weight, lax.ppermute(weight, "tensor", other_core)]
     stats = run_head((0, -1, 1), lengths, [own, up[1], down[1]], weights, None)
     stats = run_head((-2, 2), lengths, [up[2], down[2]], weights, stats)

time: 227 us -> 137 us (0.60)
  Pallas kernels: 113 us -> 29.3 us
  waiting for transfers between devices: 39.6 us -> 33.9 us
  local copies, waits for them, and re-layouts: 10.9 us -> 5.33 us
    pallas_call x1, Pallas kernels: 100 us -> 3.61 us  [per_device(): pl.pallas_call(stack_kernel, in_specs=[pl.BlockSpec(memory_space=pl.ANY)]...]
    pallas_call x3, Pallas kernels: 10.2 us -> 23.4 us  [run_head(): pl.pallas_call(functools.partial(head_kernel, offsets), in_specs=[pl.Bloc...]
    ppermute x7, waiting for transfers between devices: 16 us -> 8.05 us  [the longest x3 6.56 us: per_device(): lax.ppermute(up[-1], 'tensor', along(1))]
    unnamed x21 -> x19, local copies, waits for them, and re-layouts: 7.75 us -> 2.5 us
    all_to_all x1, starting transfers between devices: 7.52 us -> 10.9 us  [per_device(): back = lax.all_to_all(sent, 'tensor', 0, 0, axis_index_groups=same_core)]
  transfers between devices with their start and end apart: 13 -> 13, of which waited for: 8 -> 7; matrix products, arithmetic and copies ran while one was open for 0% -> 1% of each run, Pallas kernels for 4% -> 13%
where the time goes in v4:
time: 137 us; the launch traced here: 135 us
  starting transfers between devices  61.6 us (45%)
  waiting for transfers between devices  33.9 us (25%)
  Pallas kernels  29.3 us (21%)
  local copies, waits for them, and re-layouts  5.33 us (4%)
  other arithmetic  3.71 us (3%)
    pallas_call x3, Pallas kernels, run_head(): pl.pallas_call(functools.partial(head_kernel, offsets), in_specs=[pl.Bloc...  23.4 us
    all_to_all x1, starting transfers between devices, per_device(): recv = lax.all_to_all(sent, 'tensor', 0, 0, axis_index_groups=same_core)  16.6 us
    ppermute x3, starting transfers between devices, per_device(): lax.ppermute(down[-1], 'tensor', along(-1))  14.4 us
    all_to_all x1, waiting for transfers between devices, per_device(): back = lax.all_to_all(sent, 'tensor', 0, 0, axis_index_groups=same_core)  11.9 us
    all_to_all x1, waiting for transfers between devices, per_device(): recv = lax.all_to_all(sent, 'tensor', 0, 0, axis_index_groups=same_core)  11.8 us
    all_to_all x1, starting transfers between devices, per_device(): back = lax.all_to_all(sent, 'tensor', 0, 0, axis_index_groups=same_core)  10.9 us
    ppermute x3, starting transfers between devices, per_device(): lax.ppermute(head_weight, 'dp', [(i, (i + k) % N_DP) for i in range(N_DP)])  8.64 us
    ppermute x3, starting transfers between devices, per_device(): lax.ppermute(up[-1], 'tensor', along(1))  7.24 us
  transfers between devices with their start and end apart: 13, of which 7 were waited for; matrix products, arithmetic and copies ran while one was open for 1% of the time, Pallas kernels for 13%

profile of v4, /device:TPU:6, one launch (start us, length us, event | category | flops | bytes accessed | tf_op | source)
XLA Modules:
  0.0 134.7 jit_solution(14980158341835882622)
XLA Ops:
  0.6 0.7 convert_bitcast_fusion
  1.3 0.1 copy.23
  1.4 0.8 fusion.1
  2.3 1.2 broadcast_select_fusion
  3.5 16.6 %all-to-all-start = ((bf16[64,2,2176]{2,1,0:T(2,128)(2,1)}), bf16[64,2,2176]{2,1,0:T(2,128)(2,1)S(1)}, u32[]{:S(2)}, u32[]{:S(2)}) async-start(bf16[64,2,2176]{2,1,0:T(2,128)(2,1)} %bitcast.4), calls=%async_computation | async-start | bytes 1114112 | tf_op jit(solution)/shard_map/all_to_all | solution.py:224
  20.1 2.4 %collective-permute-start.7 = (bf16[512,800]{0,1:T(8,128)(2,1)}, bf16[512,800]{0,1:T(8,128)(2,1)S(1)}, u32[]{:S(2)}, u32[]{:S(2)}) collective-permute-start(bf16[512,800]{0,1:T(8,128)(2,1)} %param.7), channel_id=1, source_target_pairs={{0,128},{128,256},{256,384},{384,0},{1,129},{129,257},{257,385},{3... | collective-permute-start | bytes 2457608 | tf_op jit(solution)/shard_map/ppermute | solution.py:209
  22.5 4.3 %collective-permute-start.8 = (bf16[512,800]{0,1:T(8,128)(2,1)}, bf16[512,800]{0,1:T(8,128)(2,1)S(1)}, u32[]{:S(2)}, u32[]{:S(2)}) collective-permute-start(bf16[512,800]{0,1:T(8,128)(2,1)} %param.7), channel_id=1, source_target_pairs={{0,256},{128,384},{256,0},{384,128},{1,257},{129,385},{257,1},{385... | collective-permute-start | bytes 2457608 | tf_op jit(solution)/shard_map/ppermute | solution.py:209
  26.9 1.9 %collective-permute-start.9 = (bf16[512,800]{0,1:T(8,128)(2,1)}, bf16[512,800]{0,1:T(8,128)(2,1)S(1)}, u32[]{:S(2)}, u32[]{:S(2)}) collective-permute-start(bf16[512,800]{0,1:T(8,128)(2,1)} %param.7), channel_id=1, source_target_pairs={{0,384},{128,0},{256,128},{384,256},{1,385},{129,1},{257,129},{385... | collective-permute-start | bytes 2457608 | tf_op jit(solution)/shard_map/ppermute | solution.py:209
  28.8 11.8 %all-to-all-done = bf16[64,2,2176]{2,1,0:T(2,128)(2,1)S(1)} async-done(((bf16[64,2,2176]{2,1,0:T(2,128)(2,1)}), bf16[64,2,2176]{2,1,0:T(2,128)(2,1)S(1)}, u32[]{:S(2)}, u32[]{:S(2)}) %all-to-all-start) | async-done | bytes 557088 | tf_op jit(solution)/shard_map/all_to_all | solution.py:224
  40.6 1.0 reshape.45.recv_ref
  41.6 2.2 %shard_map.68.refs_0_ = bf16[72,2048]{1,0:T(8,128)(2,1)} custom-call(s32[1,4]{1,0:T(1,128)} %len_ref.7, bf16[128,2176]{1,0:T(8,128)(2,1)} %reshape.45.recv_ref, f32[1,2048]{1,0:T(1,128)} %bitcast.46), custom_call_target="tpu_custom_call" | custom-call | flops 37748736 | bytes 819200 | tf_op jit(solution)/shard_map/pallas_call | solution.py:228
  43.8 3.1 %collective-permute-start = (bf16[72,2048]{1,0:T(8,128)(2,1)}, bf16[72,2048]{1,0:T(8,128)(2,1)S(1)}, u32[]{:S(2)}, u32[]{:S(2)}) collective-permute-start(bf16[72,2048]{1,0:T(8,128)(2,1)} %shard_map.68.refs_0_), channel_id=1, source_target_pairs={{0,2},{1,17},{2,4},{3,19},{4,6},{5,21},{6,8},{7,23},{8,10},{9,25},... | collective-permute-start | bytes 884744 | tf_op jit(solution)/shard_map/ppermute | solution.py:242
  46.9 3.9 %collective-permute-start.3 = (bf16[72,2048]{1,0:T(8,128)(2,1)}, bf16[72,2048]{1,0:T(8,128)(2,1)S(1)}, u32[]{:S(2)}, u32[]{:S(2)}) collective-permute-start(bf16[72,2048]{1,0:T(8,128)(2,1)} %shard_map.68.refs_0_), channel_id=1, source_target_pairs={{0,14},{1,113},{2,0},{3,115},{4,2},{5,117},{6,4},{7,119},{8,6},{9,... | collective-permute-start | bytes 884744 | tf_op jit(solution)/shard_map/ppermute | solution.py:243
  50.8 3.0 %collective-permute-done.refs_1_ = bf16[72,2048]{1,0:T(8,128)(2,1)S(1)} collective-permute-done((bf16[72,2048]{1,0:T(8,128)(2,1)}, bf16[72,2048]{1,0:T(8,128)(2,1)S(1)}, u32[]{:S(2)}, u32[]{:S(2)}) %collective-permute-start) | collective-permute-done | bytes 294944 | tf_op jit(solution)/shard_map/ppermute | solution.py:242
  53.8 1.9 %collective-permute-start.1 = (bf16[72,2048]{1,0:T(8,128)(2,1)S(1)}, bf16[72,2048]{1,0:T(8,128)(2,1)S(1)}, u32[]{:S(2)}, u32[]{:S(2)}) collective-permute-start(bf16[72,2048]{1,0:T(8,128)(2,1)S(1)} %collective-permute-done.refs_1_), channel_id=1, source_target_pairs={{0,2},{1,17},{2,4},{3,19},{4,6},{5,21},{6,8},{7,23},{8,10},{9,25},... | collective-permute-start | bytes 884744 | tf_op jit(solution)/shard_map/ppermute | solution.py:242
  55.7 0.0 collective-permute-done.3.refs_2_
  55.8 5.1 %collective-permute-start.4 = (bf16[72,2048]{1,0:T(8,128)(2,1)S(1)}, bf16[72,2048]{1,0:T(8,128)(2,1)S(1)}, u32[]{:S(2)}, u32[]{:S(2)}) collective-permute-start(bf16[72,2048]{1,0:T(8,128)(2,1)S(1)} %collective-permute-done.3.refs_2_), channel_id=1, source_target_pairs={{0,14},{1,113},{2,0},{3,115},{4,2},{5,117},{6,4},{7,119},{8,6},{9,... | collective-permute-start | bytes 884744 | tf_op jit(solution)/shard_map/ppermute | solution.py:243
  60.9 0.0 collective-permute-done.7
  60.9 0.0 collective-permute-done.8
  60.9 2.2 %collective-permute-done.9 = bf16[512,800]{0,1:T(8,128)(2,1)S(1)} collective-permute-done((bf16[512,800]{0,1:T(8,128)(2,1)}, bf16[512,800]{0,1:T(8,128)(2,1)S(1)}, u32[]{:S(2)}, u32[]{:S(2)}) %collective-permute-start.9) | collective-permute-done | bytes 819232 | tf_op jit(solution)/shard_map/ppermute | solution.py:209
  63.1 0.5 collective-permute-done.1.up_ref.refs_0_
  63.6 1.5 %collective-permute-done.4.down_ref.refs_1_ = bf16[72,2048]{1,0:T(8,128)(2,1)S(1)} collective-permute-done((bf16[72,2048]{1,0:T(8,128)(2,1)S(1)}, bf16[72,2048]{1,0:T(8,128)(2,1)S(1)}, u32[]{:S(2)}, u32[]{:S(2)}) %collective-permute-start.4) | collective-permute-done | bytes 294944 | tf_op jit(solution)/shard_map/ppermute | solution.py:243
  65.2 0.7 copy-done.2
  65.8 3.6 %shard_map.69.refs_3_.refs_2_ = bf16[800,2048]{1,0:T(8,128)(2,1)} custom-call(bf16[800,512]{1,0:T(8,128)(2,1)} %bitcast.39, bf16[800,512]{1,0:T(8,128)(2,1)} %bitcast.40, bf16[800,512]{1,0:T(8,128)(2,1)} %bitcast.41, bf16[800,512]{1,0:T(8,128)(2,1)} %bitcast.42, bf16[72,2048]{1,0:T(8,128)(2,1)} %copy-done.1, bf16[72,2048]{1,0:T(8,128)(2,1)} %copy-done.2), custom_call_target="tpu_custom_call" | custom-call | bytes 6553600 | tf_op jit(solution)/shard_map/pallas_call | solution.py:250
  69.4 1.9 %collective-permute-start.10 = (bf16[800,2048]{1,0:T(8,128)(2,1)}, bf16[800,2048]{1,0:T(8,128)(2,1)S(1)}, u32[]{:S(2)}, u32[]{:S(2)}) collective-permute-start(bf16[800,2048]{1,0:T(8,128)(2,1)} %shard_map.69.refs_3_.refs_2_), channel_id=1, source_target_pairs={{0,1},{1,0},{2,3},{3,2},{4,5},{5,4},{6,7},{7,6},{8,9},{9,8},{10,11... | collective-permute-start | bytes 9830408 | tf_op jit(solution)/shard_map/ppermute | solution.py:260
  71.4 2.2 %collective-permute-start.2 = (bf16[72,2048]{1,0:T(8,128)(2,1)}, bf16[72,2048]{1,0:T(8,128)(2,1)}, u32[]{:S(2)}, u32[]{:S(2)}) collective-permute-start(bf16[72,2048]{1,0:T(8,128)(2,1)} %copy-done.1), channel_id=1, source_target_pairs={{0,2},{1,17},{2,4},{3,19},{4,6},{5,21},{6,8},{7,23},{8,10},{9,25},... | collective-permute-start | bytes 884744 | tf_op jit(solution)/shard_map/ppermute | solution.py:242
  73.6 5.3 %collective-permute-start.5 = (bf16[72,2048]{1,0:T(8,128)(2,1)}, bf16[72,2048]{1,0:T(8,128)(2,1)}, u32[]{:S(2)}, u32[]{:S(2)}) collective-permute-start(bf16[72,2048]{1,0:T(8,128)(2,1)} %copy-done.2), channel_id=1, source_target_pairs={{0,14},{1,113},{2,0},{3,115},{4,2},{5,117},{6,4},{7,119},{8,6},{9,... | collective-permute-start | bytes 884744 | tf_op jit(solution)/shard_map/ppermute | solution.py:243
  78.9 3.1 %collective-permute-done.2.refs_0_ = bf16[72,2048]{1,0:T(8,128)(2,1)} collective-permute-done((bf16[72,2048]{1,0:T(8,128)(2,1)}, bf16[72,2048]{1,0:T(8,128)(2,1)}, u32[]{:S(2)}, u32[]{:S(2)}) %collective-permute-start.2) | collective-permute-done | bytes 294944 | tf_op jit(solution)/shard_map/ppermute | solution.py:242
  82.0 1.9 %collective-permute-start.6 = (bf16[72,2048]{1,0:T(8,128)(2,1)}, bf16[72,2048]{1,0:T(8,128)(2,1)}, u32[]{:S(2)}, u32[]{:S(2)}) collective-permute-start(bf16[72,2048]{1,0:T(8,128)(2,1)} %collective-permute-done.2.refs_0_), channel_id=1, source_target_pairs={{0,2},{1,17},{2,4},{3,19},{4,6},{5,21},{6,8},{7,23},{8,10},{9,25},... | collective-permute-start | bytes 884744 | tf_op jit(solution)/shard_map/ppermute | solution.py:247
  83.9 0.0 collective-permute-done.10.refs_4_.refs_3_
  83.9 1.7 %copy-done = bf16[800,2048]{1,0:T(8,128)(2,1)} copy-done((bf16[800,2048]{1,0:T(8,128)(2,1)}, bf16[800,2048]{1,0:T(8,128)(2,1)S(1)}, u32[]{:S(2)}) %copy-start) | copy-done | bytes 3276824
  85.6 7.8 %shard_map.70.refs_4_ = f32[8,8,128]{2,1,0:T(8,128)} custom-call(s32[1,4]{1,0:T(1,128)} %len_ref.7, bf16[72,2048]{1,0:T(8,128)(2,1)} %shard_map.68.refs_0_, bf16[72,2048]{1,0:T(8,128)(2,1)} %copy-done.6, bf16[72,2048]{1,0:T(8,128)(2,1)} %copy-done.7, bf16[800,2048]{1,0:T(8,128)(2,1)} %shard_map.69.refs_3_.refs_2_, bf16[800,2048]{1,0:T(8,128)(2,1)} %copy-done), custom_call_target="tpu_custom_call" | custom-call | flops 1415577600 | bytes 7438336 | tf_op jit(solution)/shard_map/pallas_call | solution.py:168
  93.5 7.7 %shard_map.71.refs_5_ = f32[8,8,128]{2,1,0:T(8,128)} custom-call(s32[1,4]{1,0:T(1,128)} %len_ref.7, bf16[72,2048]{1,0:T(8,128)(2,1)} %copy-done.1, bf16[72,2048]{1,0:T(8,128)(2,1)} %copy-done.2, bf16[800,2048]{1,0:T(8,128)(2,1)} %shard_map.69.refs_3_.refs_2_, bf16[800,2048]{1,0:T(8,128)(2,1)} %copy-done, f32[8,8,128]{2,1,0:T(8,128)} %shard_map.70.refs_4_), custom_call_target="tpu_custom_call" | custom-call | flops 943718400 | bytes 7143424 | tf_op jit(solution)/shard_map/pallas_call | solution.py:168
  101.2 0.0 copy-start.8
  101.2 0.0 collective-permute-done.5.refs_1_
  101.2 0.0 collective-permute-done.6.refs_2_
  101.2 7.9 %shard_map.72 = f32[8,8,128]{2,1,0:T(8,128)} custom-call(s32[1,4]{1,0:T(1,128)} %len_ref.7, bf16[72,2048]{1,0:T(8,128)(2,1)} %collective-permute-done.2.refs_0_, bf16[72,2048]{1,0:T(8,128)(2,1)} %collective-permute-done.5.refs_1_, bf16[72,2048]{1,0:T(8,128)(2,1)} %collective-permute-done.6.refs_2_, bf16[800,2048]{1,0:T(8,128)(2,1)} %shard_map.69.refs_3_.refs_2_, ...), custom_call_target="tpu_custom_call" | custom-call | flops 1415577600 | bytes 7438336 | tf_op jit(solution)/shard_map/pallas_call | solution.py:168
  109.1 0.8 slice.20
  109.9 0.1 copy.19
  110.0 0.1 copy.20
  110.1 0.7 copy.21
  110.9 10.9 %all-to-all-start.1 = ((f32[64,1,64]{2,1,0:T(1,128)}), f32[64,1,64]{2,1,0:T(1,128)S(1)}, u32[]{:S(2)}, u32[]{:S(2)}) async-start(f32[64,1,64]{2,1,0:T(1,128)} %copy.21), calls=%async_computation.1 | async-start | bytes 65536 | tf_op jit(solution)/shard_map/all_to_all | solution.py:267
  121.8 0.1 select_reduce_fusion
  121.9 11.9 %all-to-all-done.1 = f32[64,1,64]{2,1,0:T(1,128)S(1)} async-done(((f32[64,1,64]{2,1,0:T(1,128)}), f32[64,1,64]{2,1,0:T(1,128)S(1)}, u32[]{:S(2)}, u32[]{:S(2)}) %all-to-all-start.1) | async-done | bytes 16416 | tf_op jit(solution)/shard_map/all_to_all | solution.py:267
  133.8 0.1 copy.22
  133.8 0.1 slice_reduce_fusion.1
  134.0 0.2 fusion.3
  134.1 0.5 subtract_select_fusion
  (18 shorter events, 0.1 us)
Async XLA Ops:
  3.5 37.0 %all-to-all-start = ((bf16[64,2,2176]{2,1,0:T(2,128)(2,1)}), bf16[64,2,2176]{2,1,0:T(2,128)(2,1)S(1)}, u32[]{:S(2)}, u32[]{:S(2)}) async-start(bf16[64,2,2176]{2,1,0:T(2,128)(2,1)} %bitcast.4), calls=%async_computation | async-start | bytes 1114112 | tf_op jit(solution)/shard_map/all_to_all | solution.py:224
  20.1 40.8 %collective-permute-start.7 = (bf16[512,800]{0,1:T(8,128)(2,1)}, bf16[512,800]{0,1:T(8,128)(2,1)S(1)}, u32[]{:S(2)}, u32[]{:S(2)}) collective-permute-start(bf16[512,800]{0,1:T(8,128)(2,1)} %param.7), channel_id=1, source_target_pairs={{0,128},{128,256},{256,384},{384,0},{1,129},{129,257},{257,385},{3... | collective-permute-start | bytes 2457608 | tf_op jit(solution)/shard_map/ppermute | solution.py:209
  22.5 38.4 %collective-permute-start.8 = (bf16[512,800]{0,1:T(8,128)(2,1)}, bf16[512,800]{0,1:T(8,128)(2,1)S(1)}, u32[]{:S(2)}, u32[]{:S(2)}) collective-permute-start(bf16[512,800]{0,1:T(8,128)(2,1)} %param.7), channel_id=1, source_target_pairs={{0,256},{128,384},{256,0},{384,128},{1,257},{129,385},{257,1},{385... | collective-permute-start | bytes 2457608 | tf_op jit(solution)/shard_map/ppermute | solution.py:209
  26.9 36.3 %collective-permute-start.9 = (bf16[512,800]{0,1:T(8,128)(2,1)}, bf16[512,800]{0,1:T(8,128)(2,1)S(1)}, u32[]{:S(2)}, u32[]{:S(2)}) collective-permute-start(bf16[512,800]{0,1:T(8,128)(2,1)} %param.7), channel_id=1, source_target_pairs={{0,384},{128,0},{256,128},{384,256},{1,385},{129,1},{257,129},{385... | collective-permute-start | bytes 2457608 | tf_op jit(solution)/shard_map/ppermute | solution.py:209
  43.8 10.0 %collective-permute-start = (bf16[72,2048]{1,0:T(8,128)(2,1)}, bf16[72,2048]{1,0:T(8,128)(2,1)S(1)}, u32[]{:S(2)}, u32[]{:S(2)}) collective-permute-start(bf16[72,2048]{1,0:T(8,128)(2,1)} %shard_map.68.refs_0_), channel_id=1, source_target_pairs={{0,2},{1,17},{2,4},{3,19},{4,6},{5,21},{6,8},{7,23},{8,10},{9,25},... | collective-permute-start | bytes 884744 | tf_op jit(solution)/shard_map/ppermute | solution.py:242
  46.9 8.8 %collective-permute-start.3 = (bf16[72,2048]{1,0:T(8,128)(2,1)}, bf16[72,2048]{1,0:T(8,128)(2,1)S(1)}, u32[]{:S(2)}, u32[]{:S(2)}) collective-permute-start(bf16[72,2048]{1,0:T(8,128)(2,1)} %shard_map.68.refs_0_), channel_id=1, source_target_pairs={{0,14},{1,113},{2,0},{3,115},{4,2},{5,117},{6,4},{7,119},{8,6},{9,... | collective-permute-start | bytes 884744 | tf_op jit(solution)/shard_map/ppermute | solution.py:243
  53.8 11.3 %copy-start.6 = (bf16[72,2048]{1,0:T(8,128)(2,1)}, bf16[72,2048]{1,0:T(8,128)(2,1)S(1)}, u32[]{:S(2)}) copy-start(bf16[72,2048]{1,0:T(8,128)(2,1)S(1)} %collective-permute-done.refs_1_) | copy-start | bytes 884740
  53.8 9.8 %collective-permute-start.1 = (bf16[72,2048]{1,0:T(8,128)(2,1)S(1)}, bf16[72,2048]{1,0:T(8,128)(2,1)S(1)}, u32[]{:S(2)}, u32[]{:S(2)}) collective-permute-start(bf16[72,2048]{1,0:T(8,128)(2,1)S(1)} %collective-permute-done.refs_1_), channel_id=1, source_target_pairs={{0,2},{1,17},{2,4},{3,19},{4,6},{5,21},{6,8},{7,23},{8,10},{9,25},... | collective-permute-start | bytes 884744 | tf_op jit(solution)/shard_map/ppermute | solution.py:242
  55.8 9.4 %copy-start.7 = (bf16[72,2048]{1,0:T(8,128)(2,1)}, bf16[72,2048]{1,0:T(8,128)(2,1)S(1)}, u32[]{:S(2)}) copy-start(bf16[72,2048]{1,0:T(8,128)(2,1)S(1)} %collective-permute-done.3.refs_2_) | copy-start | bytes 884740
  55.8 9.4 %collective-permute-start.4 = (bf16[72,2048]{1,0:T(8,128)(2,1)S(1)}, bf16[72,2048]{1,0:T(8,128)(2,1)S(1)}, u32[]{:S(2)}, u32[]{:S(2)}) collective-permute-start(bf16[72,2048]{1,0:T(8,128)(2,1)S(1)} %collective-permute-done.3.refs_2_), channel_id=1, source_target_pairs={{0,14},{1,113},{2,0},{3,115},{4,2},{5,117},{6,4},{7,119},{8,6},{9,... | collective-permute-start | bytes 884744 | tf_op jit(solution)/shard_map/ppermute | solution.py:243
  60.9 4.2 %copy-start.3 = (bf16[512,800]{0,1:T(8,128)(2,1)}, bf16[512,800]{0,1:T(8,128)(2,1)S(1)}, u32[]{:S(2)}) copy-start(bf16[512,800]{0,1:T(8,128)(2,1)S(1)} %collective-permute-done.7) | copy-start | bytes 2457604
  60.9 4.2 %copy-start.4 = (bf16[512,800]{0,1:T(8,128)(2,1)}, bf16[512,800]{0,1:T(8,128)(2,1)S(1)}, u32[]{:S(2)}) copy-start(bf16[512,800]{0,1:T(8,128)(2,1)S(1)} %collective-permute-done.8) | copy-start | bytes 2457604
  63.1 2.0 %copy-start.5 = (bf16[512,800]{0,1:T(8,128)(2,1)}, bf16[512,800]{0,1:T(8,128)(2,1)S(1)}, u32[]{:S(2)}) copy-start(bf16[512,800]{0,1:T(8,128)(2,1)S(1)} %collective-permute-done.9) | copy-start | bytes 2457604
  63.6 1.5 %copy-start.1 = (bf16[72,2048]{1,0:T(8,128)(2,1)}, bf16[72,2048]{1,0:T(8,128)(2,1)S(1)}, u32[]{:S(2)}) copy-start(bf16[72,2048]{1,0:T(8,128)(2,1)S(1)} %collective-permute-done.1.up_ref.refs_0_) | copy-start | bytes 884740
  65.1 0.7 copy-start.2
  69.4 14.5 %collective-permute-start.10 = (bf16[800,2048]{1,0:T(8,128)(2,1)}, bf16[800,2048]{1,0:T(8,128)(2,1)S(1)}, u32[]{:S(2)}, u32[]{:S(2)}) collective-permute-start(bf16[800,2048]{1,0:T(8,128)(2,1)} %shard_map.69.refs_3_.refs_2_), channel_id=1, source_target_pairs={{0,1},{1,0},{2,3},{3,2},{4,5},{5,4},{6,7},{7,6},{8,9},{9,8},{10,11... | collective-permute-start | bytes 9830408 | tf_op jit(solution)/shard_map/ppermute | solution.py:260
  71.4 10.6 %collective-permute-start.2 = (bf16[72,2048]{1,0:T(8,128)(2,1)}, bf16[72,2048]{1,0:T(8,128)(2,1)}, u32[]{:S(2)}, u32[]{:S(2)}) collective-permute-start(bf16[72,2048]{1,0:T(8,128)(2,1)} %copy-done.1), channel_id=1, source_target_pairs={{0,2},{1,17},{2,4},{3,19},{4,6},{5,21},{6,8},{7,23},{8,10},{9,25},... | collective-permute-start | bytes 884744 | tf_op jit(solution)/shard_map/ppermute | solution.py:242
  73.6 27.6 %collective-permute-start.5 = (bf16[72,2048]{1,0:T(8,128)(2,1)}, bf16[72,2048]{1,0:T(8,128)(2,1)}, u32[]{:S(2)}, u32[]{:S(2)}) collective-permute-start(bf16[72,2048]{1,0:T(8,128)(2,1)} %copy-done.2), channel_id=1, source_target_pairs={{0,14},{1,113},{2,0},{3,115},{4,2},{5,117},{6,4},{7,119},{8,6},{9,... | collective-permute-start | bytes 884744 | tf_op jit(solution)/shard_map/ppermute | solution.py:243
  82.0 19.2 %collective-permute-start.6 = (bf16[72,2048]{1,0:T(8,128)(2,1)}, bf16[72,2048]{1,0:T(8,128)(2,1)}, u32[]{:S(2)}, u32[]{:S(2)}) collective-permute-start(bf16[72,2048]{1,0:T(8,128)(2,1)} %collective-permute-done.2.refs_0_), channel_id=1, source_target_pairs={{0,2},{1,17},{2,4},{3,19},{4,6},{5,21},{6,8},{7,23},{8,10},{9,25},... | collective-permute-start | bytes 884744 | tf_op jit(solution)/shard_map/ppermute | solution.py:247
  83.9 1.7 %copy-start = (bf16[800,2048]{1,0:T(8,128)(2,1)}, bf16[800,2048]{1,0:T(8,128)(2,1)S(1)}, u32[]{:S(2)}) copy-start(bf16[800,2048]{1,0:T(8,128)(2,1)S(1)} %collective-permute-done.10.refs_4_.refs_3_) | copy-start | bytes 9830404
  101.2 20.6 %copy-start.8 = (s32[1,4]{1,0:T(1,128)S(1)}, s32[1,4]{1,0:T(1,128)}, u32[]{:S(2)}) copy-start(s32[1,4]{1,0:T(1,128)} %len_ref.7) | copy-start | bytes 52
  110.9 22.9 %all-to-all-start.1 = ((f32[64,1,64]{2,1,0:T(1,128)}), f32[64,1,64]{2,1,0:T(1,128)S(1)}, u32[]{:S(2)}, u32[]{:S(2)}) async-start(f32[64,1,64]{2,1,0:T(1,128)} %copy.21), calls=%async_computation.1 | async-start | bytes 65536 | tf_op jit(solution)/shard_map/all_to_all | solution.py:267

commit v5 on v4

v5 whole, which is shorter than its diff:
```python
import functools

import jax
import jax.numpy as jnp
from jax import lax
from jax.experimental import pallas as pl
from jax.experimental.pallas import tpu as pltpu
from jax.sharding import PartitionSpec as P

SEQ_DP = 4
SLOT = 512
N_DP = 4
N_Z, N_Y, N_CORE = 8, 8, 2
PER_CLASS = 2
CAP = 72
LANES = 128
DIGIT = 64
TILE = 200
PITCH = SLOT // (N_Y * 2)
STATS = 4


def class_layout(len_ref, place, core):
    first = core * (N_Y * PER_CLASS) + place * PER_CLASS
    starts, counts, at = [], [], 0
    for s in range(SEQ_DP):
        n = jnp.clip(lax.div(len_ref[0, s] - first + (PITCH - 1), PITCH), 0, SLOT // PITCH)
        starts.append(at)
        counts.append(n * PER_CLASS)
        at = at + n * PER_CLASS
    return starts, counts


def my_place():
    t = lax.axis_index("tensor")
    core = lax.rem(t, N_CORE)
    y = lax.rem(lax.div(t, N_CORE), N_Y)
    z = lax.div(t, N_CORE * N_Y)
    return jnp.where(core == 0, y, z), core


def pack_kernel(len_ref, recv_ref, gain_ref, out_ref):
    width = gain_ref.shape[1]
    mine, core = my_place()
    starts, counts = class_layout(len_ref, mine, core)
    shape = (LANES, LANES)
    k = lax.broadcasted_iota(jnp.int32, shape, 0)
    i = lax.broadcasted_iota(jnp.int32, shape, 1)
    pick = jnp.zeros(shape, jnp.float32)
    for s in range(SEQ_DP):
        rel = k - starts[s]
        hit = (rel >= 0) & (rel < counts[s]) & (i == rel + s * (PER_CLASS * SLOT // PITCH))
        pick = jnp.where(hit, 1.0, pick)
    pick = pick.astype(jnp.bfloat16)
    rows = jnp.dot(pick[:CAP], recv_ref[:, :width], preferred_element_type=jnp.float32)
    meansq = jnp.mean(rows * rows, axis=-1, keepdims=True)
    normed = rows * lax.rsqrt(meansq + 1e-06) * gain_ref[...]
    digits = lax.dot_general(
        recv_ref[:, width:],
        pick,
        (((0,), (1,)), ((), ())),
        preferred_element_type=jnp.float32,
    ).astype(jnp.bfloat16)
    shape = (CAP, LANES)
    place = lax.broadcasted_iota(jnp.int32, shape, 0) - (CAP - 3)
    place = jnp.where(place == lax.broadcasted_iota(jnp.int32, shape, 1), 1.0, 0.0)
    tail = jnp.dot(place.astype(jnp.bfloat16), digits, preferred_element_type=jnp.float32)
    out_ref[...] = normed.astype(jnp.bfloat16)
    out_ref[:, :LANES] = (normed[:, :LANES] + tail).astype(jnp.bfloat16)


def stack_kernel(own, before, after, far_top, far_low, up_ref, down_ref, out_ref, sem):
    del up_ref, down_ref
    me = lax.axis_index("dp")
    depth = own.shape[1]
    half = far_top.shape[0]
    copies = []
    for k, (piece, at, by) in enumerate(
        ((own, 0, 0), (before, 0, 3), (after, 0, 1), (far_top, 0, 2), (far_low, half, 2))
    ):
        src = lax.rem(me + by, N_DP)
        cols = pl.ds(pl.multiple_of(src * depth, depth), depth)
        rows = slice(at, at + piece.shape[0])
        copies.append(pltpu.make_async_copy(piece, out_ref.at[rows, cols], sem.at[k]))
    for c in copies:
        c.start()
    for c in copies:
        c.wait()


def head_kernel(offsets, jobs, carried, final, len_ref, *refs):
    n = len(offsets)
    n_w = 1 + max(w for w, _ in jobs)
    x_refs, w_refs, refs = refs[:n], refs[n : n + n_w], refs[n + n_w :]
    if carried:
        prev_ref, refs = refs[0], refs[1:]
    out_ref, acc_ref, stat_ref, x_ref, w_ref, sem = refs
    vocab_dev = w_refs[0].shape[0]
    mine, core = my_place()
    t = lax.axis_index("tensor")
    owners = (t, t + 1 - 2 * core)
    wide = 2 * LANES
    lane = lax.broadcasted_iota(jnp.int32, (1, LANES), 1)
    per_slot = PER_CLASS * SLOT // PITCH

    loads = [pltpu.make_async_copy(r, x_ref.at[j], sem.at[j]) for j, r in enumerate(x_refs)]
    tiles = {}
    for w, _ in jobs:
        for at in range(0, vocab_dev, TILE):
            if (w, at) not in tiles:
                i = len(tiles)
                rows = w_refs[w].at[at : at + TILE, :]
                tiles[w, at] = (i, pltpu.make_async_copy(rows, w_ref.at[i], sem.at[n + i]))
    order = [copy for _, copy in tiles.values()]
    for c in [order[0]] + loads:
        c.start()
    if carried:
        acc_ref[...] = prev_ref[...]
    else:
        row = lax.broadcasted_iota(jnp.int32, acc_ref.shape, 1)
        acc_ref[...] = jnp.where(row == 0, -1e30, 0.0)
    for c in [order[0]] + loads:
        c.wait()
    for c in order[1:]:
        c.start()
    ready = {0}

    for w, picks in jobs:
        x_all = jnp.concatenate([x_ref[j] for j in picks], axis=0) if len(picks) > 1 else x_ref[picks[0]]
        width_n = len(picks) * CAP
        ids = jnp.zeros((1, wide), jnp.float32)
        for p, j in enumerate(picks):
            d = x_ref[j, CAP - 8 :, :LANES].astype(jnp.float32)
            d = (d[5:6] * DIGIT + d[6:7]) * DIGIT + d[7:8]
            d = jnp.concatenate([d, jnp.zeros_like(d)], axis=1)
            ids = ids + (pltpu.roll(d, p * CAP, 1) if p else d)
        ids = ids[:, :width_n].astype(jnp.int32)
        parts = []
        for at in range(0, vocab_dev, TILE):
            i, copy = tiles[w, at]
            if i not in ready:
                copy.wait()
                ready.add(i)
            logits = lax.dot_general(
                w_ref[i],
                x_all,
                (((1,), (1,)), ((), ())),
                preferred_element_type=jnp.float32,
            )
            row = lax.broadcasted_iota(jnp.int32, logits.shape, 0)
            top = jnp.max(logits, axis=0, keepdims=True)
            expo = jnp.exp(logits - top)
            total = jnp.sum(expo, axis=0, keepdims=True)
            moment = jnp.sum(expo * logits, axis=0, keepdims=True)
            hit = row == ids - (owners[w] * vocab_dev + at)
            chosen = jnp.sum(jnp.where(hit, logits, 0.0), axis=0, keepdims=True)
            parts.append((top, total, moment, chosen))
        top = functools.reduce(jnp.maximum, [p[0] for p in parts])
        scale = [jnp.exp(p[0] - top) for p in parts]
        stat_ref[...] = jnp.zeros_like(stat_ref)
        stat_ref[0:1, :width_n] = top
        stat_ref[1:2, :width_n] = sum(p[1] * f for p, f in zip(parts, scale))
        stat_ref[2:3, :width_n] = sum(p[2] * f for p, f in zip(parts, scale))
        stat_ref[3:4, :width_n] = sum(p[3] for p in parts)
        stats = stat_ref[...]
        for p, j in enumerate(picks):
            place = lax.rem(mine + offsets[j] + N_Y, N_Y)
            starts, _ = class_layout(len_ref, place, core)
            spread = jnp.zeros((8, LANES), jnp.float32)
            for s in range(SEQ_DP):
                shift = lax.rem(s * per_slot - p * CAP - starts[s] + 2 * wide, wide)
                moved = pltpu.roll(stats, shift, 1)[:, :LANES]
                spread = jnp.where(lane // per_slot == s, moved, spread)
            old = acc_ref[pl.ds(place, 1)][0]
            top = jnp.maximum(old[0:1], spread[0:1])
            f_old, f_new = jnp.exp(old[0:1] - top), jnp.exp(spread[0:1] - top)
            new = jnp.concatenate(
                [
                    top,
                    old[1:3] * f_old + spread[1:3] * f_new,
                    old[3:4] + spread[3:4],
                    jnp.zeros((4, LANES), jnp.float32),
                ],
                axis=0,
            )
            acc_ref[pl.ds(place, 1)] = new[None]

    if final:
        rows = jnp.concatenate([acc_ref[:, k, :] for k in range(STATS)], axis=0)
        out_ref[...] = jnp.transpose(rows)
    else:
        out_ref[...] = acc_ref[...]


def run_head(offsets, jobs, lengths, shards, weights, prev, final):
    n, n_w = len(offsets), len(weights)
    vocab_dev, width = weights[0].shape
    n_tiles = len({w for w, _ in jobs}) * (vocab_dev // TILE)
    vmem = pl.BlockSpec(memory_space=pltpu.VMEM)
    anywhere = pl.BlockSpec(memory_space=pl.ANY)
    args = [lengths, *shards, *weights] + ([] if prev is None else [prev])
    columns = sum(len(picks) for _, picks in jobs) * CAP
    shape = (LANES, STATS * N_Y) if final else (N_Y, 8, LANES)
    return pl.pallas_call(
        functools.partial(head_kernel, offsets, jobs, prev is not None, final),
        in_specs=[pl.BlockSpec(memory_space=pltpu.SMEM)]
        + [anywhere] * (n + n_w)
        + [vmem] * (len(args) - 1 - n - n_w),
        out_specs=vmem,
        out_shape=jax.ShapeDtypeStruct(shape, jnp.float32),
        scratch_shapes=[
            pltpu.VMEM((N_Y, 8, LANES), jnp.float32),
            pltpu.VMEM((8, 2 * LANES), jnp.float32),
            pltpu.VMEM((n, CAP, width), jnp.bfloat16),
            pltpu.VMEM((n_tiles, TILE, width), jnp.bfloat16),
            pltpu.SemaphoreType.DMA((n + n_tiles,)),
        ],
        cost_estimate=pl.CostEstimate(
            flops=2 * columns * width * vocab_dev,
            bytes_accessed=2 * width * (n * CAP + n_w * vocab_dev),
            transcendentals=columns * vocab_dev,
        ),
    )(*args)


def per_device(hidden, norm_gain, head_weight, token_ids, lengths):
    row_dev, width = hidden.shape
    n_t = N_Z * N_Y * N_CORE
    n_chip = N_Z * N_Y
    tensor_idx = lax.axis_index("tensor")
    same_core = [[N_CORE * k + c for k in range(n_chip)] for c in range(N_CORE)]
    other_core = [(i, i ^ 1) for i in range(n_t)]

    def along(by):
        step = []
        for i in range(n_t):
            z, y, core = i // (N_Y * N_CORE), i // N_CORE % N_Y, i % N_CORE
            if core == 0:
                y = (y + by) % N_Y
            else:
                z = (z + by) % N_Z
            step.append((i, (z * N_Y + y) * N_CORE + core))
        return step

    vocab_dev = head_weight.shape[1]
    half = vocab_dev // 2
    ahead = [(i, (i + 1) % N_DP) for i in range(N_DP)]
    behind = [(i, (i - 1) % N_DP) for i in range(N_DP)]
    from_before = lax.ppermute(head_weight, "dp", ahead)
    from_after = lax.ppermute(head_weight, "dp", behind)
    pieces = [
        head_weight,
        from_before,
        from_after,
        lax.ppermute(from_before[:, :half], "dp", ahead),
        lax.ppermute(from_after[:, half:], "dp", behind),
    ]

    digits = jnp.stack(
        [token_ids // (DIGIT * DIGIT), token_ids // DIGIT % DIGIT, token_ids % DIGIT], axis=1
    ).astype(jnp.bfloat16)
    digits = jnp.pad(digits, ((0, 0), (0, LANES - 3)))
    sent = jnp.concatenate([hidden, digits], axis=1).reshape(N_Y, PER_CLASS, width + LANES)
    square = (N_Z, N_Y) + sent.shape[1:]
    sent = jnp.where(
        tensor_idx % N_CORE == 0,
        jnp.broadcast_to(sent[None], square),
        jnp.broadcast_to(sent[:, None], square),
    ).reshape(n_chip, PER_CLASS, width + LANES)
    recv = lax.all_to_all(sent, "tensor", 0, 0, axis_index_groups=same_core)
    recv = recv.reshape(n_chip * PER_CLASS, width + LANES)

    vmem = pl.BlockSpec(memory_space=pltpu.VMEM)
    own = pl.pallas_call(
        pack_kernel,
        in_specs=[pl.BlockSpec(memory_space=pltpu.SMEM), vmem, vmem],
        out_specs=vmem,
        out_shape=jax.ShapeDtypeStruct((CAP, width), jnp.bfloat16),
        cost_estimate=pl.CostEstimate(
            flops=2 * CAP * LANES * width, bytes_accessed=2 * (CAP + LANES) * width, transcendentals=0
        ),
    )(lengths, recv, norm_gain[None, :])

    up = [own]
    down = [own]
    for _ in range(N_Y // 2 - 1):
        pair = (
            lax.ppermute(up[-1], "tensor", along(1)),
            lax.ppermute(down[-1], "tensor", along(-1)),
        )
        up.append(pair[0])
        down.append(pair[1])
    up.append(lax.ppermute(up[-1], "tensor", along(1)))

    weight = pl.pallas_call(
        stack_kernel,
        in_specs=[pl.BlockSpec(memory_space=pl.ANY)] * (len(pieces) + 2),
        out_specs=vmem,
        out_shape=jax.ShapeDtypeStruct((vocab_dev, width), jnp.bfloat16),
        scratch_shapes=[pltpu.SemaphoreType.DMA((len(pieces),))],
        cost_estimate=pl.CostEstimate(
            flops=0, bytes_accessed=4 * vocab_dev * width, transcendentals=0
        ),
    )(*[p.T for p in pieces], up[3], down[3])
    weights = [weight, lax.ppermute(weight, "tensor", other_core)]
    shards = [own, up[1], down[1], up[2], down[2], up[3], down[3], up[4]]
    offsets = (0, -1, 1, -2, 2, -3, 3, -4)
    early = ((0, (0, 1, 2)), (0, (3, 4)), (0, (5, 6)))
    late = ((1, (0, 1, 2)), (1, (3, 4, 5)), (1, (6, 7)), (0, (7,)))
    stats = run_head(offsets[:7], early, lengths, shards[:7], weights[:1], None, False)
    stats = run_head(offsets, late, lengths, shards, weights, stats, True)

    sent = stats.reshape(n_chip, PER_CLASS, STATS * N_Y)
    back = lax.all_to_all(sent, "tensor", 0, 0, axis_index_groups=same_core)
    back = back.reshape(n_chip, PER_CLASS, STATS, N_Y)
    top, total, moment, chosen = (back[:, :, k] for k in range(STATS))
    top_own = jnp.max(top, axis=0)
    rescale = jnp.exp(top - top_own)
    total_own = jnp.sum(total * rescale, axis=0)
    moment_own = jnp.sum(moment * rescale, axis=0)
    chosen_own = jnp.sum(chosen, axis=0)
    top_own, total_own, moment_own, chosen_own = (
        v.T.reshape(row_dev) for v in (top_own, total_own, moment_own, chosen_own)
    )

    own_rows = tensor_idx * row_dev + jnp.arange(row_dev, dtype=jnp.int32)
    onehot = (own_rows // SLOT)[:, None] == jnp.arange(SEQ_DP, dtype=jnp.int32)[None, :]
    length_of = jnp.sum(jnp.where(onehot, lengths[0][None, :], 0), axis=1)
    scored = own_rows % SLOT < length_of
    safe_total = jnp.where(scored, total_own, 1.0)
    lse = top_own + jnp.log(safe_total)
    logprob = jnp.where(scored, chosen_own - lse, 0.0)
    entropy = jnp.where(scored, lse - moment_own / safe_total, 0.0)
    return (logprob, entropy)


def solution(mesh):
    return jax.shard_map(
        per_device,
        mesh=mesh,
        in_specs=(
            P(("dp", "tensor"), None),
            P(),
            P("dp", "tensor"),
            P(("dp", "tensor")),
            P("dp", None),
        ),
        out_specs=(P(("dp", "tensor")), P(("dp", "tensor"))),
        check_vma=False,
    )
```

time: 137 us -> 134 us (0.978); the launches traced: 135 us -> 133 us
  starting transfers between devices: 61.6 us -> 64.9 us
  Pallas kernels: 29.3 us -> 26.5 us
    ppermute x3 -> x4, starting transfers between devices: 8.64 us -> 14.1 us  [the longest x1 4.32 us: per_device(): from_before = lax.ppermute(head_weight, 'dp', ahead)]
    pallas_call x3 -> x2, Pallas kernels: 23.4 us -> 20.7 us  [run_head(): pl.pallas_call(functools.partial(head_kernel, offsets, jobs, prev is not...]
    ppermute x3 -> x4, waiting for transfers between devices: 2.18 us -> 0.01 us  [the longest x1 0.01 us: per_device(): from_after = lax.ppermute(head_weight, 'dp', behind)]
    all_to_all x1, starting transfers between devices: 10.9 us -> 9.07 us  [per_device(): back = lax.all_to_all(sent, 'tensor', 0, 0, axis_index_groups=same_core)]
    all_to_all x1, waiting for transfers between devices: 11.8 us -> 13.3 us  [per_device(): recv = lax.all_to_all(sent, 'tensor', 0, 0, axis_index_groups=same_core)]
  transfers between devices with their start and end apart: 13 -> 14, of which waited for: 7 -> 5; matrix products, arithmetic and copies ran while one was open for 1% -> 1% of each run, Pallas kernels for 13% -> 8%
where the time goes in v5:
time: 134 us; the launch traced here: 133 us
  starting transfers between devices  64.9 us (48%)
  waiting for transfers between devices  32.6 us (24%)
  Pallas kernels  26.5 us (20%)
  local copies, waits for them, and re-layouts  4.38 us (3%)
  other arithmetic  3.77 us (3%)
    pallas_call x2, Pallas kernels, run_head(): pl.pallas_call(functools.partial(head_kernel, offsets, jobs, prev is not...  20.7 us
    all_to_all x1, starting transfers between devices, per_device(): recv = lax.all_to_all(sent, 'tensor', 0, 0, axis_index_groups=same_core)  16.6 us
    ppermute x3, starting transfers between devices, per_device(): lax.ppermute(down[-1], 'tensor', along(-1))  14.2 us
    all_to_all x1, waiting for transfers between devices, per_device(): recv = lax.all_to_all(sent, 'tensor', 0, 0, axis_index_groups=same_core)  13.3 us
    all_to_all x1, waiting for transfers between devices, per_device(): back = lax.all_to_all(sent, 'tensor', 0, 0, axis_index_groups=same_core)  12.1 us
    all_to_all x1, starting transfers between devices, per_device(): back = lax.all_to_all(sent, 'tensor', 0, 0, axis_index_groups=same_core)  9.07 us
    ppermute x3, starting transfers between devices, per_device(): lax.ppermute(up[-1], 'tensor', along(1))  6.96 us
    ppermute x3, waiting for transfers between devices, per_device(): lax.ppermute(up[-1], 'tensor', along(1))  5.66 us
  transfers between devices with their start and end apart: 14, of which 5 were waited for; matrix products, arithmetic and copies ran while one was open for 1% of the time, Pallas kernels for 8%

profile of v5, /device:TPU:6, one launch (start us, length us, event | category | flops | bytes accessed | tf_op | source)
XLA Modules:
  0.0 133.2 jit_solution(16927354064106877959)
XLA Ops:
  0.6 0.7 convert_bitcast_fusion
  1.3 0.1 copy.34
  1.4 0.8 fusion.1
  2.3 1.2 broadcast_select_fusion
  3.6 16.6 %all-to-all-start = ((bf16[64,2,2176]{2,1,0:T(2,128)(2,1)}), bf16[64,2,2176]{2,1,0:T(2,128)(2,1)S(1)}, u32[]{:S(2)}, u32[]{:S(2)}) async-start(bf16[64,2,2176]{2,1,0:T(2,128)(2,1)} %bitcast.4), calls=%async_computation | async-start | bytes 1114112 | tf_op jit(solution)/shard_map/all_to_all | solution.py:270
  20.1 2.7 %collective-permute-start.8 = (bf16[512,800]{0,1:T(8,128)(2,1)}, bf16[512,800]{0,1:T(8,128)(2,1)S(1)}, u32[]{:S(2)}, u32[]{:S(2)}) collective-permute-start(bf16[512,800]{0,1:T(8,128)(2,1)} %param.7), channel_id=1, source_target_pairs={{0,384},{128,0},{256,128},{384,256},{1,385},{129,1},{257,129},{385... | collective-permute-start | bytes 2457608 | tf_op jit(solution)/shard_map/ppermute | solution.py:250
  22.9 4.3 %collective-permute-start.7 = (bf16[512,800]{0,1:T(8,128)(2,1)}, bf16[512,800]{0,1:T(8,128)(2,1)S(1)}, u32[]{:S(2)}, u32[]{:S(2)}) collective-permute-start(bf16[512,800]{0,1:T(8,128)(2,1)} %param.7), channel_id=1, source_target_pairs={{0,128},{128,256},{256,384},{384,0},{1,129},{129,257},{257,385},{3... | collective-permute-start | bytes 2457608 | tf_op jit(solution)/shard_map/ppermute | solution.py:249
  27.2 13.3 %all-to-all-done = bf16[64,2,2176]{2,1,0:T(2,128)(2,1)S(1)} async-done(((bf16[64,2,2176]{2,1,0:T(2,128)(2,1)}), bf16[64,2,2176]{2,1,0:T(2,128)(2,1)S(1)}, u32[]{:S(2)}, u32[]{:S(2)}) %all-to-all-start) | async-done | bytes 557088 | tf_op jit(solution)/shard_map/all_to_all | solution.py:270
  40.6 1.0 reshape.52.recv_ref
  41.6 2.2 %shard_map.68.refs_0_ = bf16[72,2048]{1,0:T(8,128)(2,1)} custom-call(s32[1,4]{1,0:T(1,128)} %len_ref.5, bf16[128,2176]{1,0:T(8,128)(2,1)} %reshape.52.recv_ref, f32[1,2048]{1,0:T(1,128)} %bitcast.55), custom_call_target="tpu_custom_call" | custom-call | flops 37748736 | bytes 819200 | tf_op jit(solution)/shard_map/pallas_call | solution.py:274
  43.8 3.1 %collective-permute-start = (bf16[72,2048]{1,0:T(8,128)(2,1)}, bf16[72,2048]{1,0:T(8,128)(2,1)S(1)}, u32[]{:S(2)}, u32[]{:S(2)}) collective-permute-start(bf16[72,2048]{1,0:T(8,128)(2,1)} %shard_map.68.refs_0_), channel_id=1, source_target_pairs={{0,2},{1,17},{2,4},{3,19},{4,6},{5,21},{6,8},{7,23},{8,10},{9,25},... | collective-permute-start | bytes 884744 | tf_op jit(solution)/shard_map/ppermute | solution.py:288
  47.0 3.9 %collective-permute-start.1 = (bf16[72,2048]{1,0:T(8,128)(2,1)}, bf16[72,2048]{1,0:T(8,128)(2,1)S(1)}, u32[]{:S(2)}, u32[]{:S(2)}) collective-permute-start(bf16[72,2048]{1,0:T(8,128)(2,1)} %shard_map.68.refs_0_), channel_id=1, source_target_pairs={{0,14},{1,113},{2,0},{3,115},{4,2},{5,117},{6,4},{7,119},{8,6},{9,... | collective-permute-start | bytes 884744 | tf_op jit(solution)/shard_map/ppermute | solution.py:289
  50.9 3.0 %collective-permute-done.refs_1_ = bf16[72,2048]{1,0:T(8,128)(2,1)S(1)} collective-permute-done((bf16[72,2048]{1,0:T(8,128)(2,1)}, bf16[72,2048]{1,0:T(8,128)(2,1)S(1)}, u32[]{:S(2)}, u32[]{:S(2)}) %collective-permute-start) | collective-permute-done | bytes 294944 | tf_op jit(solution)/shard_map/ppermute | solution.py:288
  53.9 1.9 %collective-permute-start.2 = (bf16[72,2048]{1,0:T(8,128)(2,1)S(1)}, bf16[72,2048]{1,0:T(8,128)(2,1)S(1)}, u32[]{:S(2)}, u32[]{:S(2)}) collective-permute-start(bf16[72,2048]{1,0:T(8,128)(2,1)S(1)} %collective-permute-done.refs_1_), channel_id=1, source_target_pairs={{0,2},{1,17},{2,4},{3,19},{4,6},{5,21},{6,8},{7,23},{8,10},{9,25},... | collective-permute-start | bytes 884744 | tf_op jit(solution)/shard_map/ppermute | solution.py:288
  55.8 0.0 collective-permute-done.1.refs_2_
  55.8 5.1 %collective-permute-start.3 = (bf16[72,2048]{1,0:T(8,128)(2,1)S(1)}, bf16[72,2048]{1,0:T(8,128)(2,1)S(1)}, u32[]{:S(2)}, u32[]{:S(2)}) collective-permute-start(bf16[72,2048]{1,0:T(8,128)(2,1)S(1)} %collective-permute-done.1.refs_2_), channel_id=1, source_target_pairs={{0,14},{1,113},{2,0},{3,115},{4,2},{5,117},{6,4},{7,119},{8,6},{9,... | collective-permute-start | bytes 884744 | tf_op jit(solution)/shard_map/ppermute | solution.py:289
  60.9 0.0 collective-permute-done.8
  61.0 2.7 %collective-permute-start.10 = (bf16[512,400]{0,1:T(8,128)(2,1)S(1)}, bf16[512,400]{0,1:T(8,128)(2,1)S(1)}, u32[]{:S(2)}, u32[]{:S(2)}) collective-permute-start(bf16[512,400]{0,1:T(8,128)(2,1)S(1)} %slice.25), channel_id=1, source_target_pairs={{0,384},{128,0},{256,128},{384,256},{1,385},{129,1},{257,129},{385... | collective-permute-start | bytes 1228808 | tf_op jit(solution)/shard_map/ppermute | solution.py:256
  63.7 0.0 collective-permute-done.7
  63.8 4.3 %collective-permute-start.9 = (bf16[512,400]{0,1:T(8,128)(2,1)S(1)}, bf16[512,400]{0,1:T(8,128)(2,1)S(1)}, u32[]{:S(2)}, u32[]{:S(2)}) collective-permute-start(bf16[512,400]{0,1:T(8,128)(2,1)S(1)} %slice.24), channel_id=1, source_target_pairs={{0,128},{128,256},{256,384},{384,0},{1,129},{129,257},{257,385},{3... | collective-permute-start | bytes 1228808 | tf_op jit(solution)/shard_map/ppermute | solution.py:255
  68.2 1.9 %collective-permute-start.4 = (bf16[72,2048]{1,0:T(8,128)(2,1)S(1)}, bf16[72,2048]{1,0:T(8,128)(2,1)S(1)}, u32[]{:S(2)}, u32[]{:S(2)}) collective-permute-start(bf16[72,2048]{1,0:T(8,128)(2,1)S(1)} %collective-permute-done.2.refs_3_), channel_id=1, source_target_pairs={{0,2},{1,17},{2,4},{3,19},{4,6},{5,21},{6,8},{7,23},{8,10},{9,25},... | collective-permute-start | bytes 884744 | tf_op jit(solution)/shard_map/ppermute | solution.py:288
  70.1 5.1 %collective-permute-start.5 = (bf16[72,2048]{1,0:T(8,128)(2,1)S(1)}, bf16[72,2048]{1,0:T(8,128)(2,1)S(1)}, u32[]{:S(2)}, u32[]{:S(2)}) collective-permute-start(bf16[72,2048]{1,0:T(8,128)(2,1)S(1)} %collective-permute-done.3.refs_4_), channel_id=1, source_target_pairs={{0,14},{1,113},{2,0},{3,115},{4,2},{5,117},{6,4},{7,119},{8,6},{9,... | collective-permute-start | bytes 884744 | tf_op jit(solution)/shard_map/ppermute | solution.py:289
  75.3 2.7 %collective-permute-done.4.up_ref.refs_5_ = bf16[72,2048]{1,0:T(8,128)(2,1)S(1)} collective-permute-done((bf16[72,2048]{1,0:T(8,128)(2,1)S(1)}, bf16[72,2048]{1,0:T(8,128)(2,1)S(1)}, u32[]{:S(2)}, u32[]{:S(2)}) %collective-permute-start.4) | collective-permute-done | bytes 294944 | tf_op jit(solution)/shard_map/ppermute | solution.py:288
  78.0 1.5 %collective-permute-done.5.down_ref.refs_6_ = bf16[72,2048]{1,0:T(8,128)(2,1)S(1)} collective-permute-done((bf16[72,2048]{1,0:T(8,128)(2,1)S(1)}, bf16[72,2048]{1,0:T(8,128)(2,1)S(1)}, u32[]{:S(2)}, u32[]{:S(2)}) %collective-permute-start.5) | collective-permute-done | bytes 294944 | tf_op jit(solution)/shard_map/ppermute | solution.py:289
  79.5 0.7 copy-done.4
  80.2 3.6 %shard_map.69.refs_7_.refs_8_ = bf16[800,2048]{1,0:T(8,128)(2,1)} custom-call(bf16[800,512]{1,0:T(8,128)(2,1)} %bitcast.47, bf16[800,512]{1,0:T(8,128)(2,1)} %bitcast.46, bf16[800,512]{1,0:T(8,128)(2,1)} %bitcast.45, bf16[400,512]{1,0:T(8,128)(2,1)} %bitcast.49, bf16[400,512]{1,0:T(8,128)(2,1)} %bitcast.48, bf16[72,2048]{1,0:T(8,128)(2,1)} %copy-done.3, ...), custom_call_target="tpu_custom_call" | custom-call | bytes 6553600 | tf_op jit(solution)/shard_map/pallas_call | solution.py:295
  83.8 1.9 %collective-permute-start.11 = (bf16[800,2048]{1,0:T(8,128)(2,1)}, bf16[800,2048]{1,0:T(8,128)(2,1)S(1)}, u32[]{:S(2)}, u32[]{:S(2)}) collective-permute-start(bf16[800,2048]{1,0:T(8,128)(2,1)} %shard_map.69.refs_7_.refs_8_), channel_id=1, source_target_pairs={{0,1},{1,0},{2,3},{3,2},{4,5},{5,4},{6,7},{7,6},{8,9},{9,8},{10,11... | collective-permute-start | bytes 9830408 | tf_op jit(solution)/shard_map/ppermute | solution.py:305
  85.7 2.1 %collective-permute-start.6 = (bf16[72,2048]{1,0:T(8,128)(2,1)}, bf16[72,2048]{1,0:T(8,128)(2,1)}, u32[]{:S(2)}, u32[]{:S(2)}) collective-permute-start(bf16[72,2048]{1,0:T(8,128)(2,1)} %copy-done.3), channel_id=1, source_target_pairs={{0,2},{1,17},{2,4},{3,19},{4,6},{5,21},{6,8},{7,23},{8,10},{9,25},... | collective-permute-start | bytes 884744 | tf_op jit(solution)/shard_map/ppermute | solution.py:293
  87.8 8.8 %shard_map.70.refs_10_ = f32[8,8,128]{2,1,0:T(8,128)} custom-call(s32[1,4]{1,0:T(1,128)} %len_ref.5, bf16[72,2048]{1,0:T(8,128)(2,1)} %shard_map.68.refs_0_, bf16[72,2048]{1,0:T(8,128)(2,1)} %copy-done.7, bf16[72,2048]{1,0:T(8,128)(2,1)} %copy-done.8, bf16[72,2048]{1,0:T(8,128)(2,1)} %copy-done.9, bf16[72,2048]{1,0:T(8,128)(2,1)} %copy-done.10, ...), custom_call_target="tpu_custom_call" | custom-call | flops 1651507200 | bytes 5341184 | tf_op jit(solution)/shard_map/pallas_call | solution.py:204
  96.7 0.0 copy-start.11
  96.7 1.7 %copy-done = bf16[800,2048]{1,0:T(8,128)(2,1)} copy-done((bf16[800,2048]{1,0:T(8,128)(2,1)}, bf16[800,2048]{1,0:T(8,128)(2,1)S(1)}, u32[]{:S(2)}) %copy-start) | copy-done | bytes 3276824
  98.4 11.9 %shard_map.71 = f32[128,32]{1,0:T(8,128)} custom-call(s32[1,4]{1,0:T(1,128)} %len_ref.5, bf16[72,2048]{1,0:T(8,128)(2,1)} %shard_map.68.refs_0_, bf16[72,2048]{1,0:T(8,128)(2,1)} %copy-done.7, bf16[72,2048]{1,0:T(8,128)(2,1)} %copy-done.8, bf16[72,2048]{1,0:T(8,128)(2,1)} %copy-done.9, bf16[72,2048]{1,0:T(8,128)(2,1)} %copy-done.10, ...), custom_call_target="tpu_custom_call" | custom-call | flops 2123366400 | bytes 8912896 | tf_op jit(solution)/shard_map/pallas_call | solution.py:204
  110.3 9.1 %all-to-all-start.1 = ((f32[64,2,32]{2,1,0:T(2,128)}), f32[64,2,32]{2,1,0:T(2,128)S(1)}, u32[]{:S(2)}, u32[]{:S(2)}) async-start(f32[64,2,32]{2,1,0:T(2,128)} %bitcast.50), calls=%async_computation.1 | async-start | bytes 131072 | tf_op jit(solution)/shard_map/all_to_all | solution.py:314
  119.4 0.1 select_reduce_fusion
  119.5 12.1 %all-to-all-done.1 = f32[64,2,32]{2,1,0:T(2,128)S(1)} async-done(((f32[64,2,32]{2,1,0:T(2,128)}), f32[64,2,32]{2,1,0:T(2,128)S(1)}, u32[]{:S(2)}, u32[]{:S(2)}) %all-to-all-start.1) | async-done | bytes 16416 | tf_op jit(solution)/shard_map/all_to_all | solution.py:314
  131.6 0.1 copy.25
  131.7 0.1 bitcast_reduce_fusion
  131.8 0.1 slice_reduce_fusion
  131.9 0.2 fusion.3
  132.0 0.1 copy.30
  132.1 0.1 reshape.57
  132.2 0.1 copy.31
  132.3 0.1 reshape.58
  132.4 0.1 copy.26
  132.4 0.1 reshape.55
  132.5 0.1 copy.28
  132.6 0.1 reshape.56
  132.7 0.6 subtract_select_fusion
  (32 shorter events, 0.2 us)
Async XLA Ops:
  3.6 37.0 %all-to-all-start = ((bf16[64,2,2176]{2,1,0:T(2,128)(2,1)}), bf16[64,2,2176]{2,1,0:T(2,128)(2,1)S(1)}, u32[]{:S(2)}, u32[]{:S(2)}) async-start(bf16[64,2,2176]{2,1,0:T(2,128)(2,1)} %bitcast.4), calls=%async_computation | async-start | bytes 1114112 | tf_op jit(solution)/shard_map/all_to_all | solution.py:270
  20.1 40.8 %collective-permute-start.8 = (bf16[512,800]{0,1:T(8,128)(2,1)}, bf16[512,800]{0,1:T(8,128)(2,1)S(1)}, u32[]{:S(2)}, u32[]{:S(2)}) collective-permute-start(bf16[512,800]{0,1:T(8,128)(2,1)} %param.7), channel_id=1, source_target_pairs={{0,384},{128,0},{256,128},{384,256},{1,385},{129,1},{257,129},{385... | collective-permute-start | bytes 2457608 | tf_op jit(solution)/shard_map/ppermute | solution.py:250
  22.9 40.8 %collective-permute-start.7 = (bf16[512,800]{0,1:T(8,128)(2,1)}, bf16[512,800]{0,1:T(8,128)(2,1)S(1)}, u32[]{:S(2)}, u32[]{:S(2)}) collective-permute-start(bf16[512,800]{0,1:T(8,128)(2,1)} %param.7), channel_id=1, source_target_pairs={{0,128},{128,256},{256,384},{384,0},{1,129},{129,257},{257,385},{3... | collective-permute-start | bytes 2457608 | tf_op jit(solution)/shard_map/ppermute | solution.py:249
  43.8 10.0 %collective-permute-start = (bf16[72,2048]{1,0:T(8,128)(2,1)}, bf16[72,2048]{1,0:T(8,128)(2,1)S(1)}, u32[]{:S(2)}, u32[]{:S(2)}) collective-permute-start(bf16[72,2048]{1,0:T(8,128)(2,1)} %shard_map.68.refs_0_), channel_id=1, source_target_pairs={{0,2},{1,17},{2,4},{3,19},{4,6},{5,21},{6,8},{7,23},{8,10},{9,25},... | collective-permute-start | bytes 884744 | tf_op jit(solution)/shard_map/ppermute | solution.py:288
  47.0 8.8 %collective-permute-start.1 = (bf16[72,2048]{1,0:T(8,128)(2,1)}, bf16[72,2048]{1,0:T(8,128)(2,1)S(1)}, u32[]{:S(2)}, u32[]{:S(2)}) collective-permute-start(bf16[72,2048]{1,0:T(8,128)(2,1)} %shard_map.68.refs_0_), channel_id=1, source_target_pairs={{0,14},{1,113},{2,0},{3,115},{4,2},{5,117},{6,4},{7,119},{8,6},{9,... | collective-permute-start | bytes 884744 | tf_op jit(solution)/shard_map/ppermute | solution.py:289
  53.9 14.3 %copy-start.7 = (bf16[72,2048]{1,0:T(8,128)(2,1)}, bf16[72,2048]{1,0:T(8,128)(2,1)S(1)}, u32[]{:S(2)}) copy-start(bf16[72,2048]{1,0:T(8,128)(2,1)S(1)} %collective-permute-done.refs_1_) | copy-start | bytes 884740
  53.9 14.3 %collective-permute-start.2 = (bf16[72,2048]{1,0:T(8,128)(2,1)S(1)}, bf16[72,2048]{1,0:T(8,128)(2,1)S(1)}, u32[]{:S(2)}, u32[]{:S(2)}) collective-permute-start(bf16[72,2048]{1,0:T(8,128)(2,1)S(1)} %collective-permute-done.refs_1_), channel_id=1, source_target_pairs={{0,2},{1,17},{2,4},{3,19},{4,6},{5,21},{6,8},{7,23},{8,10},{9,25},... | collective-permute-start | bytes 884744 | tf_op jit(solution)/shard_map/ppermute | solution.py:288
  55.8 14.3 %copy-start.8 = (bf16[72,2048]{1,0:T(8,128)(2,1)}, bf16[72,2048]{1,0:T(8,128)(2,1)S(1)}, u32[]{:S(2)}) copy-start(bf16[72,2048]{1,0:T(8,128)(2,1)S(1)} %collective-permute-done.1.refs_2_) | copy-start | bytes 884740
  55.8 14.3 %collective-permute-start.3 = (bf16[72,2048]{1,0:T(8,128)(2,1)S(1)}, bf16[72,2048]{1,0:T(8,128)(2,1)S(1)}, u32[]{:S(2)}, u32[]{:S(2)}) collective-permute-start(bf16[72,2048]{1,0:T(8,128)(2,1)S(1)} %collective-permute-done.1.refs_2_), channel_id=1, source_target_pairs={{0,14},{1,113},{2,0},{3,115},{4,2},{5,117},{6,4},{7,119},{8,6},{9,... | collective-permute-start | bytes 884744 | tf_op jit(solution)/shard_map/ppermute | solution.py:289
  60.9 18.5 %copy-start.1 = (bf16[512,800]{0,1:T(8,128)(2,1)}, bf16[512,800]{0,1:T(8,128)(2,1)S(1)}, u32[]{:S(2)}) copy-start(bf16[512,800]{0,1:T(8,128)(2,1)S(1)} %collective-permute-done.8) | copy-start | bytes 2457604
  61.0 14.3 %collective-permute-start.10 = (bf16[512,400]{0,1:T(8,128)(2,1)S(1)}, bf16[512,400]{0,1:T(8,128)(2,1)S(1)}, u32[]{:S(2)}, u32[]{:S(2)}) collective-permute-start(bf16[512,400]{0,1:T(8,128)(2,1)S(1)} %slice.25), channel_id=1, source_target_pairs={{0,384},{128,0},{256,128},{384,256},{1,385},{129,1},{257,129},{385... | collective-permute-start | bytes 1228808 | tf_op jit(solution)/shard_map/ppermute | solution.py:256
  63.7 15.7 %copy-start.2 = (bf16[512,800]{0,1:T(8,128)(2,1)}, bf16[512,800]{0,1:T(8,128)(2,1)S(1)}, u32[]{:S(2)}) copy-start(bf16[512,800]{0,1:T(8,128)(2,1)S(1)} %collective-permute-done.7) | copy-start | bytes 2457604
  63.8 11.5 %collective-permute-start.9 = (bf16[512,400]{0,1:T(8,128)(2,1)S(1)}, bf16[512,400]{0,1:T(8,128)(2,1)S(1)}, u32[]{:S(2)}, u32[]{:S(2)}) collective-permute-start(bf16[512,400]{0,1:T(8,128)(2,1)S(1)} %slice.24), channel_id=1, source_target_pairs={{0,128},{128,256},{256,384},{384,0},{1,129},{129,257},{257,385},{3... | collective-permute-start | bytes 1228808 | tf_op jit(solution)/shard_map/ppermute | solution.py:255
  68.1 11.3 %copy-start.9 = (bf16[72,2048]{1,0:T(8,128)(2,1)}, bf16[72,2048]{1,0:T(8,128)(2,1)S(1)}, u32[]{:S(2)}) copy-start(bf16[72,2048]{1,0:T(8,128)(2,1)S(1)} %collective-permute-done.2.refs_3_) | copy-start | bytes 884740
  68.2 9.8 %collective-permute-start.4 = (bf16[72,2048]{1,0:T(8,128)(2,1)S(1)}, bf16[72,2048]{1,0:T(8,128)(2,1)S(1)}, u32[]{:S(2)}, u32[]{:S(2)}) collective-permute-start(bf16[72,2048]{1,0:T(8,128)(2,1)S(1)} %collective-permute-done.2.refs_3_), channel_id=1, source_target_pairs={{0,2},{1,17},{2,4},{3,19},{4,6},{5,21},{6,8},{7,23},{8,10},{9,25},... | collective-permute-start | bytes 884744 | tf_op jit(solution)/shard_map/ppermute | solution.py:288
  70.1 9.4 %copy-start.10 = (bf16[72,2048]{1,0:T(8,128)(2,1)}, bf16[72,2048]{1,0:T(8,128)(2,1)S(1)}, u32[]{:S(2)}) copy-start(bf16[72,2048]{1,0:T(8,128)(2,1)S(1)} %collective-permute-done.3.refs_4_) | copy-start | bytes 884740
  70.1 9.4 %collective-permute-start.5 = (bf16[72,2048]{1,0:T(8,128)(2,1)S(1)}, bf16[72,2048]{1,0:T(8,128)(2,1)S(1)}, u32[]{:S(2)}, u32[]{:S(2)}) collective-permute-start(bf16[72,2048]{1,0:T(8,128)(2,1)S(1)} %collective-permute-done.3.refs_4_), channel_id=1, source_target_pairs={{0,14},{1,113},{2,0},{3,115},{4,2},{5,117},{6,4},{7,119},{8,6},{9,... | collective-permute-start | bytes 884744 | tf_op jit(solution)/shard_map/ppermute | solution.py:289
  75.3 4.2 %copy-start.5 = (bf16[512,400]{0,1:T(8,128)(2,1)}, bf16[512,400]{0,1:T(8,128)(2,1)S(1)}, u32[]{:S(2)}) copy-start(bf16[512,400]{0,1:T(8,128)(2,1)S(1)} %collective-permute-done.10) | copy-start | bytes 1228804
  75.3 4.2 %copy-start.6 = (bf16[512,400]{0,1:T(8,128)(2,1)}, bf16[512,400]{0,1:T(8,128)(2,1)S(1)}, u32[]{:S(2)}) copy-start(bf16[512,400]{0,1:T(8,128)(2,1)S(1)} %collective-permute-done.9) | copy-start | bytes 1228804
  78.0 1.5 %copy-start.3 = (bf16[72,2048]{1,0:T(8,128)(2,1)}, bf16[72,2048]{1,0:T(8,128)(2,1)S(1)}, u32[]{:S(2)}) copy-start(bf16[72,2048]{1,0:T(8,128)(2,1)S(1)} %collective-permute-done.4.up_ref.refs_5_) | copy-start | bytes 884740
  79.5 0.7 copy-start.4
  83.8 12.9 %collective-permute-start.11 = (bf16[800,2048]{1,0:T(8,128)(2,1)}, bf16[800,2048]{1,0:T(8,128)(2,1)S(1)}, u32[]{:S(2)}, u32[]{:S(2)}) collective-permute-start(bf16[800,2048]{1,0:T(8,128)(2,1)} %shard_map.69.refs_7_.refs_8_), channel_id=1, source_target_pairs={{0,1},{1,0},{2,3},{3,2},{4,5},{5,4},{6,7},{7,6},{8,9},{9,8},{10,11... | collective-permute-start | bytes 9830408 | tf_op jit(solution)/shard_map/ppermute | solution.py:305
  85.7 11.0 %collective-permute-start.6 = (bf16[72,2048]{1,0:T(8,128)(2,1)}, bf16[72,2048]{1,0:T(8,128)(2,1)}, u32[]{:S(2)}, u32[]{:S(2)}) collective-permute-start(bf16[72,2048]{1,0:T(8,128)(2,1)} %copy-done.3), channel_id=1, source_target_pairs={{0,2},{1,17},{2,4},{3,19},{4,6},{5,21},{6,8},{7,23},{8,10},{9,25},... | collective-permute-start | bytes 884744 | tf_op jit(solution)/shard_map/ppermute | solution.py:293
  96.7 22.7 %copy-start.11 = (s32[1,4]{1,0:T(1,128)S(1)}, s32[1,4]{1,0:T(1,128)}, u32[]{:S(2)}) copy-start(s32[1,4]{1,0:T(1,128)} %len_ref.5) | copy-start | bytes 52
  96.7 1.7 %copy-start = (bf16[800,2048]{1,0:T(8,128)(2,1)}, bf16[800,2048]{1,0:T(8,128)(2,1)S(1)}, u32[]{:S(2)}) copy-start(bf16[800,2048]{1,0:T(8,128)(2,1)S(1)} %collective-permute-done.11.refs_9_) | copy-start | bytes 9830404
  110.3 21.3 %all-to-all-start.1 = ((f32[64,2,32]{2,1,0:T(2,128)}), f32[64,2,32]{2,1,0:T(2,128)S(1)}, u32[]{:S(2)}, u32[]{:S(2)}) async-start(f32[64,2,32]{2,1,0:T(2,128)} %bitcast.50), calls=%async_computation.1 | async-start | bytes 131072 | tf_op jit(solution)/shard_map/all_to_all | solution.py:314

commit v6 on v0

v6 whole, which is shorter than its diff:
```python
import functools

import jax
import jax.numpy as jnp
from jax import lax
from jax.experimental import pallas as pl
from jax.experimental.pallas import tpu as pltpu
from jax.sharding import PartitionSpec as P

SEQ_DP = 4
SLOT = 512
N_LINE = 8
N_CORE = 2
LANES = 128
DIGIT = 64
BLOCK = 16
LIVE = 34
STATS = 4
TILE = 400
PITCH = BLOCK * N_CORE
PER_SLOT = SLOT // PITCH


def block_starts(len_ref, core):
    starts, at = [], 0
    for s in range(SEQ_DP):
        starts.append(at)
        n = lax.div(len_ref[0, s] - core * BLOCK + (PITCH - 1), PITCH)
        at = at + jnp.clip(n, 0, PER_SLOT)
    return starts, at


def owner_of(k, starts):
    owner = k
    for s in range(1, SEQ_DP):
        owner = jnp.where(k >= starts[s], k - starts[s] + s * PER_SLOT, owner)
    return owner


def norm_kernel(hidden_ref, gain_ref, digit_ref, out_ref):
    wide = hidden_ref[...].astype(jnp.float32)
    meansq = jnp.mean(wide * wide, axis=-1, keepdims=True)
    normed = (wide * lax.rsqrt(meansq + 1e-06) * gain_ref[...]).astype(jnp.bfloat16)
    both = jnp.concatenate([normed, digit_ref[...]], axis=1)
    for j in range(N_LINE):
        out_ref[j] = both


def head_kernel(len_ref, h_ref, own_ref, other_ref, out_ref, x_ref, w_ref, sem):
    vocab_dev, width = own_ref.shape
    t = lax.axis_index("tensor")
    core = lax.rem(t, N_CORE)
    owners = (t, t + 1 - 2 * core)
    starts, total_blocks = block_starts(len_ref, core)

    loads = []
    for k in range(LIVE):
        owner = jnp.minimum(owner_of(k, starts), N_LINE * N_LINE - 1)
        z, y = lax.div(owner, N_LINE), lax.rem(owner, N_LINE)
        line = jnp.where(core == 0, y, z)
        row = jnp.where(core == 0, z, y) * BLOCK
        block = h_ref.at[line, pl.ds(pl.multiple_of(row, BLOCK), BLOCK), :]
        loads.append(pltpu.make_async_copy(block, x_ref.at[k], sem.at[k]))
    tiles = []
    for half, ref in enumerate((own_ref, other_ref)):
        for at in range(0, vocab_dev, TILE):
            i = len(tiles)
            copy = pltpu.make_async_copy(
                ref.at[at : at + TILE, :], w_ref.at[i], sem.at[LIVE + i]
            )
            tiles.append((copy, owners[half] * vocab_dev + at))
    tiles[0][0].start()
    for c in loads:
        c.start()
    for c in loads:
        c.wait()
    for copy, _ in tiles[1:]:
        copy.start()

    n = LIVE * BLOCK
    x_all = x_ref[:, :, :width].reshape(n, width)
    extra = x_ref[:, :, width:].reshape(n, LANES)
    eye = lax.broadcasted_iota(jnp.int32, (8, LANES), 0) == lax.broadcasted_iota(
        jnp.int32, (8, LANES), 1
    )
    d = lax.dot_general(
        jnp.where(eye, 1.0, 0.0).astype(jnp.bfloat16),
        extra,
        (((1,), (1,)), ((), ())),
        preferred_element_type=jnp.float32,
    )
    ids = ((d[0:1] * DIGIT + d[1:2]) * DIGIT + d[2:3]).astype(jnp.int32)

    parts = []
    for i, (copy, first) in enumerate(tiles):
        copy.wait()
        logits = lax.dot_general(
            w_ref[i],
            x_all,
            (((1,), (1,)), ((), ())),
            preferred_element_type=jnp.float32,
        )
        row = lax.broadcasted_iota(jnp.int32, logits.shape, 0)
        top = jnp.max(logits, axis=0, keepdims=True)
        expo = jnp.exp(logits - top)
        total = jnp.sum(expo, axis=0, keepdims=True)
        moment = jnp.sum(expo * logits, axis=0, keepdims=True)
        hit = row == ids - first
        chosen = jnp.sum(jnp.where(hit, logits, 0.0), axis=0, keepdims=True)
        parts.append((top, total, moment, chosen))
    top = functools.reduce(jnp.maximum, [p[0] for p in parts])
    scale = [jnp.exp(p[0] - top) for p in parts]
    stats = (
        top,
        sum(p[1] * f for p, f in zip(parts, scale)),
        sum(p[2] * f for p, f in zip(parts, scale)),
        sum(p[3] for p in parts),
    )

    lane = lax.broadcasted_iota(jnp.int32, (1, n), 1)
    block = lane // BLOCK
    owner = jnp.where(block < total_blocks, owner_of(block, starts), -1)
    chips = N_LINE * N_LINE
    mine = owner == lax.broadcasted_iota(jnp.int32, (chips, n), 0)
    place = lax.broadcasted_iota(jnp.int32, (n, STATS * BLOCK), 0) % BLOCK
    column = lax.broadcasted_iota(jnp.int32, (n, STATS * BLOCK), 1)
    out = jnp.zeros((chips, STATS * BLOCK), jnp.float32)
    for k, stat in enumerate(stats):
        spot = jnp.where(column == place + k * BLOCK, 1.0, 0.0)
        out = out + jnp.dot(
            jnp.where(mine, stat, 0.0),
            spot,
            precision=lax.Precision.HIGHEST,
            preferred_element_type=jnp.float32,
        )
    out_ref[...] = out


def run_head(lengths, lines, own, other):
    vocab_dev, width = own.shape
    n_tiles = 2 * vocab_dev // TILE
    anywhere = pl.BlockSpec(memory_space=pl.ANY)
    n = LIVE * BLOCK
    return pl.pallas_call(
        head_kernel,
        in_specs=[pl.BlockSpec(memory_space=pltpu.SMEM)] + [anywhere] * 3,
        out_specs=pl.BlockSpec(memory_space=pltpu.VMEM),
        out_shape=jax.ShapeDtypeStruct((N_LINE * N_LINE, STATS * BLOCK), jnp.float32),
        scratch_shapes=[
            pltpu.VMEM((LIVE, BLOCK, width + LANES), jnp.bfloat16),
            pltpu.VMEM((n_tiles, TILE, width), jnp.bfloat16),
            pltpu.SemaphoreType.DMA((LIVE + n_tiles,)),
        ],
        cost_estimate=pl.CostEstimate(
            flops=4 * n * width * vocab_dev,
            bytes_accessed=2 * width * (n + 2 * vocab_dev),
            transcendentals=2 * n * vocab_dev,
        ),
    )(lengths, lines, own, other)


def per_device(hidden, norm_gain, head_weight, token_ids, lengths):
    row_dev, width = hidden.shape
    vocab_dev = head_weight.shape[1]
    n_chip = N_LINE * N_LINE
    n_t = n_chip * N_CORE
    tensor_idx = lax.axis_index("tensor")
    same_core = [[N_CORE * k + c for k in range(n_chip)] for c in range(N_CORE)]
    other_core = [(i, i ^ 1) for i in range(n_t)]
    along_z = [[[(z * N_LINE + y) * N_CORE + c for z in range(N_LINE)] for y in range(N_LINE)] for c in range(N_CORE)]
    along_y = [[[(z * N_LINE + y) * N_CORE + c for y in range(N_LINE)] for z in range(N_LINE)] for c in range(N_CORE)]
    first_lines = along_z[0] + along_y[1]
    second_lines = along_y[0] + along_z[1]

    weight = lax.all_gather(head_weight, "dp", axis=0, tiled=True).T

    vmem = pl.BlockSpec(memory_space=pltpu.VMEM)
    digits = jnp.stack(
        [token_ids // (DIGIT * DIGIT), token_ids // DIGIT % DIGIT, token_ids % DIGIT], axis=1
    ).astype(jnp.bfloat16)
    digits = jnp.pad(digits, ((0, 0), (0, LANES - 3)))
    block = pl.pallas_call(
        norm_kernel,
        in_specs=[vmem] * 3,
        out_specs=vmem,
        out_shape=jax.ShapeDtypeStruct((N_LINE, row_dev, width + LANES), jnp.bfloat16),
    )(hidden, norm_gain[None, :], digits)
    line = lax.all_to_all(block, "tensor", 0, 0, axis_index_groups=first_lines)
    fan = jnp.broadcast_to(line[None], (N_LINE,) + line.shape)
    fan = fan.reshape(N_LINE, N_LINE * row_dev, width + LANES)
    lines = lax.all_to_all(fan, "tensor", 0, 0, axis_index_groups=second_lines)

    stats = run_head(lengths, lines, weight, lax.ppermute(weight, "tensor", other_core))

    back = lax.all_to_all(stats, "tensor", 0, 0, axis_index_groups=same_core, tiled=True)
    back = back.reshape(n_chip, STATS, row_dev)
    top, total, moment, chosen = (back[:, k] for k in range(STATS))
    top_own = jnp.max(top, axis=0)
    rescale = jnp.exp(top - top_own)
    total_own = jnp.sum(total * rescale, axis=0)
    moment_own = jnp.sum(moment * rescale, axis=0)
    chosen_own = jnp.sum(chosen, axis=0)

    own_rows = tensor_idx * row_dev + jnp.arange(row_dev, dtype=jnp.int32)
    onehot = (own_rows // SLOT)[:, None] == jnp.arange(SEQ_DP, dtype=jnp.int32)[None, :]
    length_of = jnp.sum(jnp.where(onehot, lengths[0][None, :], 0), axis=1)
    scored = own_rows % SLOT < length_of
    safe_total = jnp.where(scored, total_own, 1.0)
    lse = top_own + jnp.log(safe_total)
    logprob = jnp.where(scored, chosen_own - lse, 0.0)
    entropy = jnp.where(scored, lse - moment_own / safe_total, 0.0)
    return (logprob, entropy)


def solution(mesh):
    return jax.shard_map(
        per_device,
        mesh=mesh,
        in_specs=(
            P(("dp", "tensor"), None),
            P(),
            P("dp", "tensor"),
            P(("dp", "tensor")),
            P("dp", None),
        ),
        out_specs=(P(("dp", "tensor")), P(("dp", "tensor"))),
        check_vma=False,
    )
```

time: 923 us -> 138 us (0.15)
  blocking collectives: 777 us -> 0 us
  waiting for transfers between devices: 107 us -> 79.2 us
  starting transfers between devices: 0.08 us -> 23.9 us
  Pallas kernels: 0 us -> 14.8 us
  matrix products: 12.1 us -> 0 us
    psum x1 -> x0, blocking collectives: 491 us -> none  [per_device(): lax.psum((total * rescale, moment * rescale, chosen), 'tensor')]
    pmax x1 -> x0, blocking collectives: 254 us -> none  [per_device(): top_all = lax.pmax(top, 'tensor')]
    all_gather x2 -> x1, waiting for transfers between devices: 106 us -> 25.2 us  [per_device(): weight = lax.all_gather(head_weight, 'dp', axis=0, tiled=True).T]
    all_to_all x0 -> x3, waiting for transfers between devices: none -> 47.4 us  [the longest x1 22.6 us: per_device(): lines = lax.all_to_all(fan, 'tensor', 0, 0, axis_index_groups=second_lines)]
    unnamed x1 -> x0, blocking collectives: 32.3 us -> none
    all_to_all x0 -> x3, starting transfers between devices: none -> 22 us  [the longest x1 10.3 us: per_device(): line = lax.all_to_all(block, 'tensor', 0, 0, axis_index_groups=first_lines)]
    pallas_call x0 -> x2, Pallas kernels: none -> 14.8 us  [the longest x1 13 us: run_head(): pl.pallas_call(head_kernel, in_specs=[pl.BlockSpec(memory_space=pltpu.SME...]
    dot_general x1 -> x0, matrix products: 12.1 us -> none  [per_device(): jnp.dot(lax.all_gather(normed, 'tensor', axis=0, tiled=True), weight, pre...]
  transfers between devices with their start and end apart: 2 -> 5, of which waited for: 2 -> 5; matrix products, arithmetic and copies ran while one was open for 1% -> 2% of each run, Pallas kernels for 0% -> 0%
where the time goes in v6:
time: 138 us; the launch traced here: 137 us
  waiting for transfers between devices  79.2 us (57%)
  starting transfers between devices  23.9 us (17%)
  Pallas kernels  14.8 us (11%)
  between operations  14.1 us (10%)
  local copies, waits for them, and re-layouts  3.44 us (2%)
  other arithmetic  1.64 us (1%)
    all_gather x1, waiting for transfers between devices, per_device(): weight = lax.all_gather(head_weight, 'dp', axis=0, tiled=True).T  25.2 us
    all_to_all x1, waiting for transfers between devices, per_device(): lines = lax.all_to_all(fan, 'tensor', 0, 0, axis_index_groups=second_lines)  22.6 us
    pallas_call x1, Pallas kernels, run_head(): pl.pallas_call(head_kernel, in_specs=[pl.BlockSpec(memory_space=pltpu.SME...  13 us
    all_to_all x1, waiting for transfers between devices, per_device(): line = lax.all_to_all(block, 'tensor', 0, 0, axis_index_groups=first_lines)  12.9 us
    all_to_all x1, waiting for transfers between devices, per_device(): lax.all_to_all(stats, 'tensor', 0, 0, axis_index_groups=same_core, tiled=...  11.9 us
    all_to_all x1, starting transfers between devices, per_device(): line = lax.all_to_all(block, 'tensor', 0, 0, axis_index_groups=first_lines)  10.3 us
    all_to_all x1, starting transfers between devices, per_device(): lines = lax.all_to_all(fan, 'tensor', 0, 0, axis_index_groups=second_lines)  7.1 us
    ppermute x1, waiting for transfers between devices, per_device(): lax.ppermute(weight, 'tensor', other_core)  5.99 us
  transfers between devices with their start and end apart: 5, of which 5 were waited for; matrix products, arithmetic and copies ran while one was open for 2% of the time, Pallas kernels for 0%

profile of v6, /device:TPU:6, one launch (start us, length us, event | category | flops | bytes accessed | tf_op | source)
XLA Modules:
  0.0 137.2 jit_solution(7668188942056461275)
XLA Ops:
  7.2 0.7 convert_bitcast_fusion
  7.9 0.1 copy.19
  8.0 0.6 pad.4.digit_ref
  8.6 1.8 %shard_map.68 = bf16[8,16,2176]{2,1,0:T(8,128)(2,1)} custom-call(bf16[16,2048]{1,0:T(8,128)(2,1)} %hidden_ref.1, f32[1,2048]{1,0:T(1,128)} %bitcast.38, bf16[16,128]{1,0:T(8,128)(2,1)} %pad.4.digit_ref), custom_call_target="tpu_custom_call" | custom-call | tf_op jit(solution)/shard_map/pallas_call | solution.py:182
  10.4 10.3 %all-to-all-start = ((bf16[8,16,2176]{2,1,0:T(8,128)(2,1)}), bf16[8,16,2176]{2,1,0:T(8,128)(2,1)S(1)}, u32[]{:S(2)}, u32[]{:S(2)}) async-start(bf16[8,16,2176]{2,1,0:T(8,128)(2,1)} %shard_map.68), calls=%async_computation | async-start | bytes 1114112 | tf_op jit(solution)/shard_map/all_to_all | solution.py:188
  20.7 0.0 all-gather.2.cloned.1.call-start
  20.7 0.7 all-gather.2.cloned.1.call-update
  21.4 12.9 %all-to-all-done = bf16[8,16,2176]{2,1,0:T(8,128)(2,1)S(1)} async-done(((bf16[8,16,2176]{2,1,0:T(8,128)(2,1)}), bf16[8,16,2176]{2,1,0:T(8,128)(2,1)S(1)}, u32[]{:S(2)}, u32[]{:S(2)}) %all-to-all-start) | async-done | bytes 557088 | tf_op jit(solution)/shard_map/all_to_all | solution.py:188
  34.3 2.7 %broadcast_in_dim.41 = bf16[8,128,2176]{2,1,0:T(8,128)(2,1)} broadcast(bf16[128,2176]{1,0:T(8,128)(2,1)S(1)} %bitcast.34), dimensions={1,2} | broadcast | bytes 5013504 | tf_op jit(solution)/shard_map/broadcast_in_dim | solution.py:189
  37.0 7.1 %all-to-all-start.1 = ((bf16[8,128,2176]{2,1,0:T(8,128)(2,1)}), bf16[8,128,2176]{2,1,0:T(8,128)(2,1)}, u32[]{:S(2)}, u32[]{:S(2)}) async-start(bf16[8,128,2176]{2,1,0:T(8,128)(2,1)} %broadcast_in_dim.41), calls=%async_computation.1 | async-start | bytes 8912896 | tf_op jit(solution)/shard_map/all_to_all | solution.py:191
  44.1 25.2 %all-gather.2.cloned.1.call-done = bf16[2048,800]{0,1:T(8,128)(2,1)} async-done(((bf16[512,800]{0,1:T(8,128)(2,1)}), bf16[2048,800]{0,1:T(8,128)(2,1)}) %all-gather.2.cloned.1.call-update) | async-done | bytes 3276816 | tf_op jit(solution)/shard_map/all_gather | solution.py:175
  69.2 1.9 %collective-permute-start = (bf16[800,2048]{1,0:T(8,128)(2,1)}, bf16[800,2048]{1,0:T(8,128)(2,1)S(1)}, u32[]{:S(2)}, u32[]{:S(2)}) collective-permute-start(bf16[800,2048]{1,0:T(8,128)(2,1)} %bitcast.39), channel_id=1, source_target_pairs={{0,1},{1,0},{2,3},{3,2},{4,5},{5,4},{6,7},{7,6},{8,9},{9,8},{10,11... | collective-permute-start | bytes 9830408 | tf_op jit(solution)/shard_map/ppermute | solution.py:193
  71.2 0.0 copy-start.1
  71.2 6.0 %collective-permute-done.other_ref = bf16[800,2048]{1,0:T(8,128)(2,1)S(1)} collective-permute-done((bf16[800,2048]{1,0:T(8,128)(2,1)}, bf16[800,2048]{1,0:T(8,128)(2,1)S(1)}, u32[]{:S(2)}, u32[]{:S(2)}) %collective-permute-start) | collective-permute-done | bytes 3276832 | tf_op jit(solution)/shard_map/ppermute | solution.py:193
  77.2 0.0 copy-start
  77.2 22.6 %all-to-all-done.1.h_ref = bf16[8,128,2176]{2,1,0:T(8,128)(2,1)} async-done(((bf16[8,128,2176]{2,1,0:T(8,128)(2,1)}), bf16[8,128,2176]{2,1,0:T(8,128)(2,1)}, u32[]{:S(2)}, u32[]{:S(2)}) %all-to-all-start.1) | async-done | bytes 4456480 | tf_op jit(solution)/shard_map/all_to_all | solution.py:191
  99.8 0.0 copy-done
  99.8 13.0 %shard_map.69 = f32[64,64]{1,0:T(8,128)} custom-call(s32[1,4]{1,0:T(1,128)} %len_ref.1, bf16[8,128,2176]{2,1,0:T(8,128)(2,1)} %all-to-all-done.1.h_ref, bf16[800,2048]{1,0:T(8,128)(2,1)} %bitcast.40, bf16[800,2048]{1,0:T(8,128)(2,1)} %copy-done), custom_call_target="tpu_custom_call" | custom-call | flops 3565158400 | bytes 8781824 | tf_op jit(solution)/shard_map/pallas_call | solution.py:144
  112.8 4.6 %all-to-all-start.2 = ((f32[64,1,64]{2,1,0:T(1,128)}), f32[64,1,64]{2,1,0:T(1,128)S(1)}, u32[]{:S(2)}, u32[]{:S(2)}) async-start(f32[64,1,64]{2,1,0:T(1,128)} %bitcast.37), calls=%async_computation.2 | async-start | bytes 65536 | tf_op jit(solution)/shard_map/all_to_all | solution.py:195
  117.4 0.0 copy-done.1
  117.4 0.1 select_reduce_fusion
  117.5 11.9 %all-to-all-done.2 = f32[64,1,64]{2,1,0:T(1,128)S(1)} async-done(((f32[64,1,64]{2,1,0:T(1,128)}), f32[64,1,64]{2,1,0:T(1,128)S(1)}, u32[]{:S(2)}, u32[]{:S(2)}) %all-to-all-start.2) | async-done | bytes 16416 | tf_op jit(solution)/shard_map/all_to_all | solution.py:195
  129.4 0.1 copy.21
  129.5 0.1 slice_reduce_fusion.1
  129.6 0.2 fusion.1
  129.8 0.5 subtract_select_fusion
  (2 shorter events, 0.0 us)
Async XLA Ops:
  10.4 24.0 %all-to-all-start = ((bf16[8,16,2176]{2,1,0:T(8,128)(2,1)}), bf16[8,16,2176]{2,1,0:T(8,128)(2,1)S(1)}, u32[]{:S(2)}, u32[]{:S(2)}) async-start(bf16[8,16,2176]{2,1,0:T(8,128)(2,1)} %shard_map.68), calls=%async_computation | async-start | bytes 1114112 | tf_op jit(solution)/shard_map/all_to_all | solution.py:188
  20.7 48.6 %all-gather.2.cloned.1.call-start = ((), (), s32[]{:S(2)}) async-start(), calls=%async_computation.3 | async-start | bytes 4096000 | tf_op jit(solution)/shard_map/all_gather | solution.py:175
  37.0 62.8 %all-to-all-start.1 = ((bf16[8,128,2176]{2,1,0:T(8,128)(2,1)}), bf16[8,128,2176]{2,1,0:T(8,128)(2,1)}, u32[]{:S(2)}, u32[]{:S(2)}) async-start(bf16[8,128,2176]{2,1,0:T(8,128)(2,1)} %broadcast_in_dim.41), calls=%async_computation.1 | async-start | bytes 8912896 | tf_op jit(solution)/shard_map/all_to_all | solution.py:191
  69.2 7.9 %collective-permute-start = (bf16[800,2048]{1,0:T(8,128)(2,1)}, bf16[800,2048]{1,0:T(8,128)(2,1)S(1)}, u32[]{:S(2)}, u32[]{:S(2)}) collective-permute-start(bf16[800,2048]{1,0:T(8,128)(2,1)} %bitcast.39), channel_id=1, source_target_pairs={{0,1},{1,0},{2,3},{3,2},{4,5},{5,4},{6,7},{7,6},{8,9},{9,8},{10,11... | collective-permute-start | bytes 9830408 | tf_op jit(solution)/shard_map/ppermute | solution.py:193
  71.2 46.2 %copy-start.1 = (s32[1,4]{1,0:T(1,128)S(1)}, s32[1,4]{1,0:T(1,128)}, u32[]{:S(2)}) copy-start(s32[1,4]{1,0:T(1,128)} %len_ref.1) | copy-start | bytes 52
  77.2 22.6 %copy-start = (bf16[800,2048]{1,0:T(8,128)(2,1)}, bf16[800,2048]{1,0:T(8,128)(2,1)S(1)}, u32[]{:S(2)}) copy-start(bf16[800,2048]{1,0:T(8,128)(2,1)S(1)} %collective-permute-done.other_ref) | copy-start | bytes 9830404
  112.8 16.6 %all-to-all-start.2 = ((f32[64,1,64]{2,1,0:T(1,128)}), f32[64,1,64]{2,1,0:T(1,128)S(1)}, u32[]{:S(2)}, u32[]{:S(2)}) async-start(f32[64,1,64]{2,1,0:T(1,128)} %bitcast.37), calls=%async_computation.2 | async-start | bytes 65536 | tf_op jit(solution)/shard_map/all_to_all | solution.py:195
Sparse Core Ops, SparseCore 0:
  23.6 45.5 all-gather.1

commit v7 on v6

--- a/solution.py
+++ b/solution.py
@@ -19,6 +19,7 @@
 TILE = 400
 PITCH = BLOCK * N_CORE
 PER_SLOT = SLOT // PITCH
+OFFSETS = (0, -1, 1, -2, 2, -3, 3, -4)
 
 
 def block_starts(len_ref, core):
@@ -46,34 +47,46 @@
         out_ref[j] = both
 
 
-def head_kernel(len_ref, h_ref, own_ref, other_ref, out_ref, x_ref, w_ref, sem):
+def head_kernel(len_ref, *refs):
+    line_refs, (own_ref, other_ref, out_ref, x_ref, w_ref, sem) = refs[:N_LINE], refs[N_LINE:]
     vocab_dev, width = own_ref.shape
     t = lax.axis_index("tensor")
     core = lax.rem(t, N_CORE)
     owners = (t, t + 1 - 2 * core)
     starts, total_blocks = block_starts(len_ref, core)
 
+    mine = jnp.where(core == 0, lax.rem(lax.div(t, N_CORE), N_LINE), lax.div(t, N_CORE * N_LINE))
     loads = []
-    for k in range(LIVE):
-        owner = jnp.minimum(owner_of(k, starts), N_LINE * N_LINE - 1)
-        z, y = lax.div(owner, N_LINE), lax.rem(owner, N_LINE)
-        line = jnp.where(core == 0, y, z)
-        row = jnp.where(core == 0, z, y) * BLOCK
-        block = h_ref.at[line, pl.ds(pl.multiple_of(row, BLOCK), BLOCK), :]
-        loads.append(pltpu.make_async_copy(block, x_ref.at[k], sem.at[k]))
+    for offset, ref in zip(OFFSETS, line_refs):
+        line = lax.rem(mine + offset + N_LINE, N_LINE)
+        for m in range(N_LINE):
+            owner = jnp.where(core == 0, m * N_LINE + line, line * N_LINE + m)
+            slot, at = lax.div(owner, PER_SLOT), lax.rem(owner, PER_SLOT)
+            live = at * PITCH + core * BLOCK < len_ref[0, slot]
+            first = starts[0]
+            for s in range(1, SEQ_DP):
+                first = jnp.where(slot == s, starts[s], first)
+            rows = ref.at[m * BLOCK : (m + 1) * BLOCK, :]
+            loads.append((live, rows, first + at, len(loads)))
+
+    def each_load(act):
+        for live, rows, k, i in loads:
+
+            @pl.when(live)
+            def _(rows=rows, k=k, i=i):
+                act(pltpu.make_async_copy(rows, x_ref.at[k], sem.at[i]))
+
     tiles = []
     for half, ref in enumerate((own_ref, other_ref)):
         for at in range(0, vocab_dev, TILE):
             i = len(tiles)
             copy = pltpu.make_async_copy(
-                ref.at[at : at + TILE, :], w_ref.at[i], sem.at[LIVE + i]
+                ref.at[at : at + TILE, :], w_ref.at[i], sem.at[N_LINE * N_LINE + i]
             )
             tiles.append((copy, owners[half] * vocab_dev + at))
+    each_load(lambda copy: copy.start())
     tiles[0][0].start()
-    for c in loads:
-        c.start()
-    for c in loads:
-        c.wait()
+    each_load(lambda copy: copy.wait())
     for copy, _ in tiles[1:]:
         copy.start()
 
@@ -121,19 +134,22 @@
     block = lane // BLOCK
     owner = jnp.where(block < total_blocks, owner_of(block, starts), -1)
     chips = N_LINE * N_LINE
-    mine = owner == lax.broadcasted_iota(jnp.int32, (chips, n), 0)
-    place = lax.broadcasted_iota(jnp.int32, (n, STATS * BLOCK), 0) % BLOCK
-    column = lax.broadcasted_iota(jnp.int32, (n, STATS * BLOCK), 1)
-    out = jnp.zeros((chips, STATS * BLOCK), jnp.float32)
-    for k, stat in enumerate(stats):
-        spot = jnp.where(column == place + k * BLOCK, 1.0, 0.0)
-        out = out + jnp.dot(
-            jnp.where(mine, stat, 0.0),
-            spot,
-            precision=lax.Precision.HIGHEST,
-            preferred_element_type=jnp.float32,
-        )
-    out_ref[...] = out
+    here = owner == lax.broadcasted_iota(jnp.int32, (chips, n), 0)
+    rows = []
+    for stat in stats:
+        for _ in range(3):
+            part = stat.astype(jnp.bfloat16).astype(jnp.float32)
+            rows.append(jnp.where(here, part, 0.0).astype(jnp.bfloat16))
+            stat = stat - part
+    place = lax.broadcasted_iota(jnp.int32, (n, BLOCK), 0) % BLOCK
+    spot = jnp.where(place == lax.broadcasted_iota(jnp.int32, (n, BLOCK), 1), 1.0, 0.0)
+    moved = jnp.dot(
+        jnp.concatenate(rows, axis=0),
+        spot.astype(jnp.bfloat16),
+        preferred_element_type=jnp.float32,
+    ).reshape(STATS, 3, chips, BLOCK)
+    moved = moved[:, 0] + moved[:, 1] + moved[:, 2]
+    out_ref[...] = jnp.concatenate([moved[k] for k in range(STATS)], axis=1)
 
 
 def run_head(lengths, lines, own, other):
@@ -143,20 +159,20 @@
     n = LIVE * BLOCK
     return pl.pallas_call(
         head_kernel,
-        in_specs=[pl.BlockSpec(memory_space=pltpu.SMEM)] + [anywhere] * 3,
+        in_specs=[pl.BlockSpec(memory_space=pltpu.SMEM)] + [anywhere] * (N_LINE + 2),
         out_specs=pl.BlockSpec(memory_space=pltpu.VMEM),
         out_shape=jax.ShapeDtypeStruct((N_LINE * N_LINE, STATS * BLOCK), jnp.float32),
         scratch_shapes=[
             pltpu.VMEM((LIVE, BLOCK, width + LANES), jnp.bfloat16),
             pltpu.VMEM((n_tiles, TILE, width), jnp.bfloat16),
-            pltpu.SemaphoreType.DMA((LIVE + n_tiles,)),
+            pltpu.SemaphoreType.DMA((N_LINE * N_LINE + n_tiles,)),
         ],
         cost_estimate=pl.CostEstimate(
             flops=4 * n * width * vocab_dev,
             bytes_accessed=2 * width * (n + 2 * vocab_dev),
             transcendentals=2 * n * vocab_dev,
         ),
-    )(lengths, lines, own, other)
+    )(lengths, *lines, own, other)
 
 
 def per_device(hidden, norm_gain, head_weight, token_ids, lengths):
@@ -167,10 +183,19 @@
     tensor_idx = lax.axis_index("tensor")
     same_core = [[N_CORE * k + c for k in range(n_chip)] for c in range(N_CORE)]
     other_core = [(i, i ^ 1) for i in range(n_t)]
-    along_z = [[[(z * N_LINE + y) * N_CORE + c for z in range(N_LINE)] for y in range(N_LINE)] for c in range(N_CORE)]
-    along_y = [[[(z * N_LINE + y) * N_CORE + c for y in range(N_LINE)] for z in range(N_LINE)] for c in range(N_CORE)]
-    first_lines = along_z[0] + along_y[1]
-    second_lines = along_y[0] + along_z[1]
+    along_z = [[(z * N_LINE + y) * N_CORE for z in range(N_LINE)] for y in range(N_LINE)]
+    along_y = [[(z * N_LINE + y) * N_CORE + 1 for y in range(N_LINE)] for z in range(N_LINE)]
+
+    def along(by):
+        step = []
+        for i in range(n_t):
+            z, y, core = i // (N_LINE * N_CORE), i // N_CORE % N_LINE, i % N_CORE
+            if core == 0:
+                y = (y + by) % N_LINE
+            else:
+                z = (z + by) % N_LINE
+            step.append((i, (z * N_LINE + y) * N_CORE + core))
+        return step
 
     weight = lax.all_gather(head_weight, "dp", axis=0, tiled=True).T
 
@@ -185,11 +210,16 @@
         out_specs=vmem,
         out_shape=jax.ShapeDtypeStruct((N_LINE, row_dev, width + LANES), jnp.bfloat16),
     )(hidden, norm_gain[None, :], digits)
-    line = lax.all_to_all(block, "tensor", 0, 0, axis_index_groups=first_lines)
-    fan = jnp.broadcast_to(line[None], (N_LINE,) + line.shape)
-    fan = fan.reshape(N_LINE, N_LINE * row_dev, width + LANES)
-    lines = lax.all_to_all(fan, "tensor", 0, 0, axis_index_groups=second_lines)
-
+    line = lax.all_to_all(block, "tensor", 0, 0, axis_index_groups=along_z + along_y)
+    own = line.reshape(N_LINE * row_dev, width + LANES)
+    up, down = [own], [own]
+    for _ in range(N_LINE // 2 - 1):
+        up.append(lax.ppermute(up[-1], "tensor", along(1)))
+        down.append(lax.ppermute(down[-1], "tensor", along(-1)))
+    up.append(lax.ppermute(up[-1], "tensor", along(1)))
+    lines = [own, up[1], down[1], up[2], down[2], up[3], down[3], up[4]]
+
+    weight, _, _ = lax.optimization_barrier((weight, up[3], down[3]))
     stats = run_head(lengths, lines, weight, lax.ppermute(weight, "tensor", other_core))
 
     back = lax.all_to_all(stats, "tensor", 0, 0, axis_index_groups=same_core, tiled=True)

time: 138 us -> 131 us (0.949)
  waiting for transfers between devices: 79.2 us -> 40.7 us
  blocking collectives: 0 us -> 24 us
  starting transfers between devices: 23.9 us -> 34.5 us
  local copies, waits for them, and re-layouts: 3.44 us -> 0.79 us
    all_to_all x2 -> x0, waiting for transfers between devices: 35.5 us -> none  [the longest x1 22.6 us: per_device(): lines = lax.all_to_all(fan, 'tensor', 0, 0, axis_index_groups=second_lines)]
    ppermute x0 -> x7, waiting for transfers between devices: none -> 28.1 us  [the longest x4 26.6 us: per_device(): up.append(lax.ppermute(up[-1], 'tensor', along(1)))]
    all_gather x1, waiting for transfers between devices: 25.2 us -> 0.01 us  [per_device(): weight = lax.all_gather(head_weight, 'dp', axis=0, tiled=True).T]
    ppermute x0 -> x7, starting transfers between devices: none -> 24.7 us  [the longest x3 14 us: per_device(): down.append(lax.ppermute(down[-1], 'tensor', along(-1)))]
    all_to_all x0 -> x1, blocking collectives: none -> 24 us  [per_device(): lax.all_to_all(block, 'tensor', 0, 0, axis_index_groups=along_z + along_y)]
    all_to_all x2 -> x0, starting transfers between devices: 17.4 us -> none  [the longest x1 10.3 us: per_device(): line = lax.all_to_all(block, 'tensor', 0, 0, axis_index_groups=first_lines)]
    ppermute x1, waiting for transfers between devices: 5.99 us -> 0.01 us  [per_device(): lax.ppermute(weight, 'tensor', other_core)]
    all_to_all x1, starting transfers between devices: 4.58 us -> 7.87 us  [per_device(): lax.all_to_all(stats, 'tensor', 0, 0, axis_index_groups=same_core, tiled=...]
  transfers between devices with their start and end apart: 5 -> 10, of which waited for: 5 -> 6; matrix products, arithmetic and copies ran while one was open for 2% -> 1% of each run, Pallas kernels for 0% -> 1%
where the time goes in v7:
time: 131 us; the launch traced here: 130 us
  waiting for transfers between devices  40.7 us (31%)
  starting transfers between devices  34.5 us (26%)
  blocking collectives  24 us (18%)
  Pallas kernels  14.6 us (11%)
  between operations  14.2 us (11%)
  other arithmetic  1.64 us (1%)
    ppermute x4, waiting for transfers between devices, per_device(): up.append(lax.ppermute(up[-1], 'tensor', along(1)))  26.6 us
    all_to_all x1, blocking collectives, per_device(): lax.all_to_all(block, 'tensor', 0, 0, axis_index_groups=along_z + along_y)  24 us
    ppermute x3, starting transfers between devices, per_device(): down.append(lax.ppermute(down[-1], 'tensor', along(-1)))  14 us
    pallas_call x1, Pallas kernels, run_head(): pl.pallas_call(head_kernel, in_specs=[pl.BlockSpec(memory_space=pltpu.SME...  12.8 us
    all_to_all x1, waiting for transfers between devices, per_device(): lax.all_to_all(stats, 'tensor', 0, 0, axis_index_groups=same_core, tiled=...  11.9 us
    ppermute x4, starting transfers between devices, per_device(): up.append(lax.ppermute(up[-1], 'tensor', along(1)))  10.7 us
    all_to_all x1, starting transfers between devices, per_device(): lax.all_to_all(stats, 'tensor', 0, 0, axis_index_groups=same_core, tiled=...  7.87 us
  transfers between devices with their start and end apart: 10, of which 6 were waited for; matrix products, arithmetic and copies ran while one was open for 1% of the time, Pallas kernels for 1%

profile of v7, /device:TPU:6, one launch (start us, length us, event | category | flops | bytes accessed | tf_op | source)
XLA Modules:
  0.0 130.4 jit_solution(4430777348726140076)
XLA Ops:
  7.2 0.0 all-gather.2.cloned.1.call-start
  7.2 0.7 all-gather.2.cloned.1.call-update
  7.9 0.7 convert_bitcast_fusion
  8.6 0.1 copy.19
  8.7 0.6 pad.4.digit_ref
  9.3 1.8 %shard_map.68 = bf16[8,16,2176]{2,1,0:T(8,128)(2,1)} custom-call(bf16[16,2048]{1,0:T(8,128)(2,1)} %hidden_ref.1, f32[1,2048]{1,0:T(1,128)} %bitcast.40, bf16[16,128]{1,0:T(8,128)(2,1)} %pad.4.digit_ref), custom_call_target="tpu_custom_call" | custom-call | tf_op jit(solution)/shard_map/pallas_call | solution.py:207
  11.1 24.0 %all_to_all.14 = bf16[8,16,2176]{2,1,0:T(8,128)(2,1)S(1)} all-to-all(bf16[8,16,2176]{2,1,0:T(8,128)(2,1)} %shard_map.68), channel_id=1, replica_groups={{0,16,32,48,64,80,96,112},{2,18,34,50,66,82,98,114},{4,20,36,52,68,84,1..., dimensions={0} | all-to-all | bytes 1114112 | tf_op jit(solution)/shard_map/all_to_all | solution.py:213
  35.0 0.0 copy-start
  35.0 3.5 %collective-permute-start = (bf16[128,2176]{1,0:T(8,128)(2,1)S(1)}, bf16[128,2176]{1,0:T(8,128)(2,1)S(1)}, u32[]{:S(2)}, u32[]{:S(2)}) collective-permute-start(bf16[128,2176]{1,0:T(8,128)(2,1)S(1)} %bitcast.34), channel_id=1, source_target_pairs={{0,2},{1,17},{2,4},{3,19},{4,6},{5,21},{6,8},{7,23},{8,10},{9,25},... | collective-permute-start | bytes 1671176 | tf_op jit(solution)/shard_map/ppermute | solution.py:217
  38.5 3.8 %collective-permute-start.1 = (bf16[128,2176]{1,0:T(8,128)(2,1)S(1)}, bf16[128,2176]{1,0:T(8,128)(2,1)S(1)}, u32[]{:S(2)}, u32[]{:S(2)}) collective-permute-start(bf16[128,2176]{1,0:T(8,128)(2,1)S(1)} %bitcast.35), channel_id=1, source_target_pairs={{0,14},{1,113},{2,0},{3,115},{4,2},{5,117},{6,4},{7,119},{8,6},{9,... | collective-permute-start | bytes 1671176 | tf_op jit(solution)/shard_map/ppermute | solution.py:218
  42.3 5.6 %collective-permute-done.refs_1_ = bf16[128,2176]{1,0:T(8,128)(2,1)S(1)} collective-permute-done((bf16[128,2176]{1,0:T(8,128)(2,1)S(1)}, bf16[128,2176]{1,0:T(8,128)(2,1)S(1)}, u32[]{:S(2)}, u32[]{:S(2)}) %collective-permute-start) | collective-permute-done | bytes 557088 | tf_op jit(solution)/shard_map/ppermute | solution.py:217
  47.9 0.0 copy-start.1
  47.9 2.0 %collective-permute-start.2 = (bf16[128,2176]{1,0:T(8,128)(2,1)S(1)}, bf16[128,2176]{1,0:T(8,128)(2,1)S(1)}, u32[]{:S(2)}, u32[]{:S(2)}) collective-permute-start(bf16[128,2176]{1,0:T(8,128)(2,1)S(1)} %collective-permute-done.refs_1_), channel_id=1, source_target_pairs={{0,2},{1,17},{2,4},{3,19},{4,6},{5,21},{6,8},{7,23},{8,10},{9,25},... | collective-permute-start | bytes 1671176 | tf_op jit(solution)/shard_map/ppermute | solution.py:217
  49.9 0.0 collective-permute-done.1.refs_2_
  49.9 0.0 copy-start.2
  50.0 5.0 %collective-permute-start.3 = (bf16[128,2176]{1,0:T(8,128)(2,1)S(1)}, bf16[128,2176]{1,0:T(8,128)(2,1)S(1)}, u32[]{:S(2)}, u32[]{:S(2)}) collective-permute-start(bf16[128,2176]{1,0:T(8,128)(2,1)S(1)} %collective-permute-done.1.refs_2_), channel_id=1, source_target_pairs={{0,14},{1,113},{2,0},{3,115},{4,2},{5,117},{6,4},{7,119},{8,6},{9,... | collective-permute-start | bytes 1671176 | tf_op jit(solution)/shard_map/ppermute | solution.py:218
  55.0 5.5 %collective-permute-done.2.refs_3_ = bf16[128,2176]{1,0:T(8,128)(2,1)S(1)} collective-permute-done((bf16[128,2176]{1,0:T(8,128)(2,1)S(1)}, bf16[128,2176]{1,0:T(8,128)(2,1)S(1)}, u32[]{:S(2)}, u32[]{:S(2)}) %collective-permute-start.2) | collective-permute-done | bytes 557088 | tf_op jit(solution)/shard_map/ppermute | solution.py:217
  60.5 0.0 copy-start.3
  60.5 1.9 %collective-permute-start.4 = (bf16[128,2176]{1,0:T(8,128)(2,1)S(1)}, bf16[128,2176]{1,0:T(8,128)(2,1)S(1)}, u32[]{:S(2)}, u32[]{:S(2)}) collective-permute-start(bf16[128,2176]{1,0:T(8,128)(2,1)S(1)} %collective-permute-done.2.refs_3_), channel_id=1, source_target_pairs={{0,2},{1,17},{2,4},{3,19},{4,6},{5,21},{6,8},{7,23},{8,10},{9,25},... | collective-permute-start | bytes 1671176 | tf_op jit(solution)/shard_map/ppermute | solution.py:217
  62.5 0.0 collective-permute-done.3.refs_4_
  62.5 0.0 copy-start.4
  62.5 5.1 %collective-permute-start.5 = (bf16[128,2176]{1,0:T(8,128)(2,1)S(1)}, bf16[128,2176]{1,0:T(8,128)(2,1)}, u32[]{:S(2)}, u32[]{:S(2)}) collective-permute-start(bf16[128,2176]{1,0:T(8,128)(2,1)S(1)} %collective-permute-done.3.refs_4_), channel_id=1, source_target_pairs={{0,14},{1,113},{2,0},{3,115},{4,2},{5,117},{6,4},{7,119},{8,6},{9,... | collective-permute-start | bytes 1671176 | tf_op jit(solution)/shard_map/ppermute | solution.py:218
  67.6 5.5 %collective-permute-done.4.refs_5_ = bf16[128,2176]{1,0:T(8,128)(2,1)S(1)} collective-permute-done((bf16[128,2176]{1,0:T(8,128)(2,1)S(1)}, bf16[128,2176]{1,0:T(8,128)(2,1)S(1)}, u32[]{:S(2)}, u32[]{:S(2)}) %collective-permute-start.4) | collective-permute-done | bytes 557088 | tf_op jit(solution)/shard_map/ppermute | solution.py:217
  73.2 0.0 copy-start.5
  73.2 1.5 %collective-permute-done.5.refs_6_ = bf16[128,2176]{1,0:T(8,128)(2,1)} collective-permute-done((bf16[128,2176]{1,0:T(8,128)(2,1)S(1)}, bf16[128,2176]{1,0:T(8,128)(2,1)}, u32[]{:S(2)}, u32[]{:S(2)}) %collective-permute-start.5) | collective-permute-done | bytes 557088 | tf_op jit(solution)/shard_map/ppermute | solution.py:218
  74.6 0.0 all-gather.2.cloned.1.call-done
  74.7 1.9 %collective-permute-start.7 = (bf16[800,2048]{1,0:T(8,128)(2,1)}, bf16[800,2048]{1,0:T(8,128)(2,1)}, u32[]{:S(2)}, u32[]{:S(2)}) collective-permute-start(bf16[800,2048]{1,0:T(8,128)(2,1)} %bitcast.41), channel_id=1, source_target_pairs={{0,1},{1,0},{2,3},{3,2},{4,5},{5,4},{6,7},{7,6},{8,9},{9,8},{10,11... | collective-permute-start | bytes 9830408 | tf_op jit(solution)/shard_map/ppermute | solution.py:223
  76.6 3.3 %collective-permute-start.6 = (bf16[128,2176]{1,0:T(8,128)(2,1)S(1)}, bf16[128,2176]{1,0:T(8,128)(2,1)}, u32[]{:S(2)}, u32[]{:S(2)}) collective-permute-start(bf16[128,2176]{1,0:T(8,128)(2,1)S(1)} %collective-permute-done.4.refs_5_), channel_id=1, source_target_pairs={{0,2},{1,17},{2,4},{3,19},{4,6},{5,21},{6,8},{7,23},{8,10},{9,25},... | collective-permute-start | bytes 1671176 | tf_op jit(solution)/shard_map/ppermute | solution.py:219
  79.9 0.0 copy-start.6
  79.9 10.0 %collective-permute-done.6.refs_7_ = bf16[128,2176]{1,0:T(8,128)(2,1)} collective-permute-done((bf16[128,2176]{1,0:T(8,128)(2,1)S(1)}, bf16[128,2176]{1,0:T(8,128)(2,1)}, u32[]{:S(2)}, u32[]{:S(2)}) %collective-permute-start.6) | collective-permute-done | bytes 557088 | tf_op jit(solution)/shard_map/ppermute | solution.py:219
  89.9 0.0 collective-permute-done.7.refs_9_
  89.9 0.0 copy-done
  89.9 0.0 copy-done.1
  89.9 0.0 copy-done.2
  89.9 0.0 copy-done.3
  89.9 0.0 copy-done.4
  89.9 0.0 copy-done.5
  89.9 12.8 %shard_map.69 = f32[64,64]{1,0:T(8,128)} custom-call(s32[1,4]{1,0:T(1,128)} %len_ref.1, bf16[128,2176]{1,0:T(8,128)(2,1)} %bitcast.36, bf16[128,2176]{1,0:T(8,128)(2,1)} %copy-done.1, bf16[128,2176]{1,0:T(8,128)(2,1)} %copy-done.2, bf16[128,2176]{1,0:T(8,128)(2,1)} %copy-done.3, bf16[128,2176]{1,0:T(8,128)(2,1)} %copy-done.4, bf16[128,2176]{1,0:T(8,128)(2,1)} %copy-done.5, ...), custom_call_target="tpu_custom_call" | custom-call | flops 3565158400 | bytes 8781824 | tf_op jit(solution)/shard_map/pallas_call | solution.py:160
  102.7 7.9 %all-to-all-start.1 = ((f32[64,1,64]{2,1,0:T(1,128)}), f32[64,1,64]{2,1,0:T(1,128)S(1)}, u32[]{:S(2)}, u32[]{:S(2)}) async-start(f32[64,1,64]{2,1,0:T(1,128)} %bitcast.39), calls=%async_computation.1 | async-start | bytes 65536 | tf_op jit(solution)/shard_map/all_to_all | solution.py:225
  110.6 0.0 copy-done.6
  110.6 0.1 select_reduce_fusion
  110.7 11.9 %all-to-all-done.1 = f32[64,1,64]{2,1,0:T(1,128)S(1)} async-done(((f32[64,1,64]{2,1,0:T(1,128)}), f32[64,1,64]{2,1,0:T(1,128)S(1)}, u32[]{:S(2)}, u32[]{:S(2)}) %all-to-all-start.1) | async-done | bytes 16416 | tf_op jit(solution)/shard_map/all_to_all | solution.py:225
  122.6 0.1 copy.21
  122.7 0.1 slice_reduce_fusion.1
  122.8 0.2 fusion.1
  123.0 0.5 subtract_select_fusion
  (2 shorter events, 0.0 us)
Async XLA Ops:
  7.2 67.5 %all-gather.2.cloned.1.call-start = ((), (), s32[]{:S(2)}) async-start(), calls=%async_computation.2 | async-start | bytes 4096000 | tf_op jit(solution)/shard_map/all_gather | solution.py:200
  35.0 54.9 %copy-start = (bf16[8,16,2176]{2,1,0:T(8,128)(2,1)}, bf16[8,16,2176]{2,1,0:T(8,128)(2,1)S(1)}, u32[]{:S(2)}) copy-start(bf16[8,16,2176]{2,1,0:T(8,128)(2,1)S(1)} %all_to_all.14) | copy-start | bytes 1671172
  35.0 12.9 %collective-permute-start = (bf16[128,2176]{1,0:T(8,128)(2,1)S(1)}, bf16[128,2176]{1,0:T(8,128)(2,1)S(1)}, u32[]{:S(2)}, u32[]{:S(2)}) collective-permute-start(bf16[128,2176]{1,0:T(8,128)(2,1)S(1)} %bitcast.34), channel_id=1, source_target_pairs={{0,2},{1,17},{2,4},{3,19},{4,6},{5,21},{6,8},{7,23},{8,10},{9,25},... | collective-permute-start | bytes 1671176 | tf_op jit(solution)/shard_map/ppermute | solution.py:217
  38.5 11.4 %collective-permute-start.1 = (bf16[128,2176]{1,0:T(8,128)(2,1)S(1)}, bf16[128,2176]{1,0:T(8,128)(2,1)S(1)}, u32[]{:S(2)}, u32[]{:S(2)}) collective-permute-start(bf16[128,2176]{1,0:T(8,128)(2,1)S(1)} %bitcast.35), channel_id=1, source_target_pairs={{0,14},{1,113},{2,0},{3,115},{4,2},{5,117},{6,4},{7,119},{8,6},{9,... | collective-permute-start | bytes 1671176 | tf_op jit(solution)/shard_map/ppermute | solution.py:218
  47.9 42.0 %copy-start.1 = (bf16[128,2176]{1,0:T(8,128)(2,1)}, bf16[128,2176]{1,0:T(8,128)(2,1)S(1)}, u32[]{:S(2)}) copy-start(bf16[128,2176]{1,0:T(8,128)(2,1)S(1)} %collective-permute-done.refs_1_) | copy-start | bytes 1671172
  47.9 12.6 %collective-permute-start.2 = (bf16[128,2176]{1,0:T(8,128)(2,1)S(1)}, bf16[128,2176]{1,0:T(8,128)(2,1)S(1)}, u32[]{:S(2)}, u32[]{:S(2)}) collective-permute-start(bf16[128,2176]{1,0:T(8,128)(2,1)S(1)} %collective-permute-done.refs_1_), channel_id=1, source_target_pairs={{0,2},{1,17},{2,4},{3,19},{4,6},{5,21},{6,8},{7,23},{8,10},{9,25},... | collective-permute-start | bytes 1671176 | tf_op jit(solution)/shard_map/ppermute | solution.py:217
  49.9 39.9 %copy-start.2 = (bf16[128,2176]{1,0:T(8,128)(2,1)}, bf16[128,2176]{1,0:T(8,128)(2,1)S(1)}, u32[]{:S(2)}) copy-start(bf16[128,2176]{1,0:T(8,128)(2,1)S(1)} %collective-permute-done.1.refs_2_) | copy-start | bytes 1671172
  50.0 12.5 %collective-permute-start.3 = (bf16[128,2176]{1,0:T(8,128)(2,1)S(1)}, bf16[128,2176]{1,0:T(8,128)(2,1)S(1)}, u32[]{:S(2)}, u32[]{:S(2)}) collective-permute-start(bf16[128,2176]{1,0:T(8,128)(2,1)S(1)} %collective-permute-done.1.refs_2_), channel_id=1, source_target_pairs={{0,14},{1,113},{2,0},{3,115},{4,2},{5,117},{6,4},{7,119},{8,6},{9,... | collective-permute-start | bytes 1671176 | tf_op jit(solution)/shard_map/ppermute | solution.py:218
  60.5 29.4 %copy-start.3 = (bf16[128,2176]{1,0:T(8,128)(2,1)}, bf16[128,2176]{1,0:T(8,128)(2,1)S(1)}, u32[]{:S(2)}) copy-start(bf16[128,2176]{1,0:T(8,128)(2,1)S(1)} %collective-permute-done.2.refs_3_) | copy-start | bytes 1671172
  60.5 12.6 %collective-permute-start.4 = (bf16[128,2176]{1,0:T(8,128)(2,1)S(1)}, bf16[128,2176]{1,0:T(8,128)(2,1)S(1)}, u32[]{:S(2)}, u32[]{:S(2)}) collective-permute-start(bf16[128,2176]{1,0:T(8,128)(2,1)S(1)} %collective-permute-done.2.refs_3_), channel_id=1, source_target_pairs={{0,2},{1,17},{2,4},{3,19},{4,6},{5,21},{6,8},{7,23},{8,10},{9,25},... | collective-permute-start | bytes 1671176 | tf_op jit(solution)/shard_map/ppermute | solution.py:217
  62.5 27.4 %copy-start.4 = (bf16[128,2176]{1,0:T(8,128)(2,1)}, bf16[128,2176]{1,0:T(8,128)(2,1)S(1)}, u32[]{:S(2)}) copy-start(bf16[128,2176]{1,0:T(8,128)(2,1)S(1)} %collective-permute-done.3.refs_4_) | copy-start | bytes 1671172
  62.5 12.2 %collective-permute-start.5 = (bf16[128,2176]{1,0:T(8,128)(2,1)S(1)}, bf16[128,2176]{1,0:T(8,128)(2,1)}, u32[]{:S(2)}, u32[]{:S(2)}) collective-permute-start(bf16[128,2176]{1,0:T(8,128)(2,1)S(1)} %collective-permute-done.3.refs_4_), channel_id=1, source_target_pairs={{0,14},{1,113},{2,0},{3,115},{4,2},{5,117},{6,4},{7,119},{8,6},{9,... | collective-permute-start | bytes 1671176 | tf_op jit(solution)/shard_map/ppermute | solution.py:218
  73.2 16.8 %copy-start.5 = (bf16[128,2176]{1,0:T(8,128)(2,1)}, bf16[128,2176]{1,0:T(8,128)(2,1)S(1)}, u32[]{:S(2)}) copy-start(bf16[128,2176]{1,0:T(8,128)(2,1)S(1)} %collective-permute-done.4.refs_5_) | copy-start | bytes 1671172
  74.7 15.2 %collective-permute-start.7 = (bf16[800,2048]{1,0:T(8,128)(2,1)}, bf16[800,2048]{1,0:T(8,128)(2,1)}, u32[]{:S(2)}, u32[]{:S(2)}) collective-permute-start(bf16[800,2048]{1,0:T(8,128)(2,1)} %bitcast.41), channel_id=1, source_target_pairs={{0,1},{1,0},{2,3},{3,2},{4,5},{5,4},{6,7},{7,6},{8,9},{9,8},{10,11... | collective-permute-start | bytes 9830408 | tf_op jit(solution)/shard_map/ppermute | solution.py:223
  76.6 13.3 %collective-permute-start.6 = (bf16[128,2176]{1,0:T(8,128)(2,1)S(1)}, bf16[128,2176]{1,0:T(8,128)(2,1)}, u32[]{:S(2)}, u32[]{:S(2)}) collective-permute-start(bf16[128,2176]{1,0:T(8,128)(2,1)S(1)} %collective-permute-done.4.refs_5_), channel_id=1, source_target_pairs={{0,2},{1,17},{2,4},{3,19},{4,6},{5,21},{6,8},{7,23},{8,10},{9,25},... | collective-permute-start | bytes 1671176 | tf_op jit(solution)/shard_map/ppermute | solution.py:219
  79.9 30.7 %copy-start.6 = (s32[1,4]{1,0:T(1,128)S(1)}, s32[1,4]{1,0:T(1,128)}, u32[]{:S(2)}) copy-start(s32[1,4]{1,0:T(1,128)} %len_ref.1) | copy-start | bytes 52
  102.7 19.9 %all-to-all-start.1 = ((f32[64,1,64]{2,1,0:T(1,128)}), f32[64,1,64]{2,1,0:T(1,128)S(1)}, u32[]{:S(2)}, u32[]{:S(2)}) async-start(f32[64,1,64]{2,1,0:T(1,128)} %bitcast.39), calls=%async_computation.1 | async-start | bytes 65536 | tf_op jit(solution)/shard_map/all_to_all | solution.py:225
Sparse Core Ops, SparseCore 0:
  10.1 48.6 all-gather.1

commit v8 on v7

v8 whole, which is shorter than its diff:
```python
import functools

import jax
import jax.numpy as jnp
from jax import lax
from jax.experimental import pallas as pl
from jax.experimental.pallas import tpu as pltpu
from jax.sharding import PartitionSpec as P

SEQ_DP = 4
SLOT = 512
N_DP = 4
N_LINE = 8
N_CORE = 2
LANES = 128
DIGIT = 64
BLOCK = 16
LIVE = 34
STATS = 4
TILE = 400
PITCH = BLOCK * N_CORE
PER_SLOT = SLOT // PITCH
OFFSETS = (0, -1, 1, -2, 2, -3, 3, -4)


def block_starts(len_ref, core):
    starts, at = [], 0
    for s in range(SEQ_DP):
        starts.append(at)
        n = lax.div(len_ref[0, s] - core * BLOCK + (PITCH - 1), PITCH)
        at = at + jnp.clip(n, 0, PER_SLOT)
    return starts, at


def owner_of(k, starts):
    owner = k
    for s in range(1, SEQ_DP):
        owner = jnp.where(k >= starts[s], k - starts[s] + s * PER_SLOT, owner)
    return owner


def norm_kernel(hidden_ref, gain_ref, id_ref, out_ref):
    wide = hidden_ref[...].astype(jnp.float32)
    meansq = jnp.mean(wide * wide, axis=-1, keepdims=True)
    normed = (wide * lax.rsqrt(meansq + 1e-06) * gain_ref[...]).astype(jnp.bfloat16)
    rows = wide.shape[0]
    square = (rows, rows)
    eye = lax.broadcasted_iota(jnp.int32, square, 0) == lax.broadcasted_iota(jnp.int32, square, 1)
    ids = jnp.sum(jnp.where(eye, id_ref[...], 0), axis=1, keepdims=True)
    lane = lax.broadcasted_iota(jnp.int32, (rows, LANES), 1)
    shift = jnp.where(lane == 0, 12, jnp.where(lane == 1, 6, 0))
    digit = jnp.where(lane < 3, lax.shift_right_logical(ids, shift) & (DIGIT - 1), 0)
    both = jnp.concatenate([normed, digit.astype(jnp.float32).astype(jnp.bfloat16)], axis=1)
    for j in range(N_LINE):
        out_ref[j] = both


def stack_kernel(own, before, far, after, up_ref, down_ref, out_ref, sem):
    del up_ref, down_ref
    me = lax.axis_index("dp")
    depth = own.shape[1]
    copies = []
    for k, piece in enumerate((own, before, far, after)):
        src = lax.rem(me - k + N_DP, N_DP)
        cols = pl.ds(pl.multiple_of(src * depth, depth), depth)
        copies.append(pltpu.make_async_copy(piece, out_ref.at[:, cols], sem.at[k]))
    for c in copies:
        c.start()
    for c in copies:
        c.wait()


def my_core():
    t = lax.axis_index("tensor")
    core = lax.rem(t, N_CORE)
    y, z = lax.rem(lax.div(t, N_CORE), N_LINE), lax.div(t, N_CORE * N_LINE)
    return t, core, jnp.where(core == 0, y, z)


def block_copies(len_ref, line_refs, x_ref, sem):
    _, core, mine = my_core()
    starts, _ = block_starts(len_ref, core)
    loads = []
    for offset, ref in zip(OFFSETS, line_refs):
        line = lax.rem(mine + offset + N_LINE, N_LINE)
        for m in range(N_LINE):
            owner = jnp.where(core == 0, m * N_LINE + line, line * N_LINE + m)
            slot, at = lax.div(owner, PER_SLOT), lax.rem(owner, PER_SLOT)
            live = at * PITCH + core * BLOCK < len_ref[0, slot]
            first = starts[0]
            for s in range(1, SEQ_DP):
                first = jnp.where(slot == s, starts[s], first)
            rows = ref.at[m * BLOCK : (m + 1) * BLOCK, :]
            loads.append((live, rows, first + at, len(loads)))

    def each(act):
        for live, rows, k, i in loads:

            @pl.when(live)
            def _(rows=rows, k=k, i=i):
                act(pltpu.make_async_copy(rows, x_ref.at[k], sem.at[i]))

    return each


def weight_copies(ref, w_ref, base, sem, sem_base):
    out = []
    for i, at in enumerate(range(0, ref.shape[0], TILE)):
        rows = ref.at[at : at + TILE, :]
        out.append(pltpu.make_async_copy(rows, w_ref.at[base + i], sem.at[sem_base + base + i]))
    return out


def token_row(extra):
    shape = (8, LANES)
    eye = lax.broadcasted_iota(jnp.int32, shape, 0) == lax.broadcasted_iota(jnp.int32, shape, 1)
    d = lax.dot_general(
        jnp.where(eye, 1.0, 0.0).astype(jnp.bfloat16),
        extra,
        (((1,), (1,)), ((), ())),
        preferred_element_type=jnp.float32,
    )
    return ((d[0:1] * DIGIT + d[1:2]) * DIGIT + d[2:3]).astype(jnp.int32)


def tile_stats(weight, x, ids):
    logits = lax.dot_general(
        weight, x, (((1,), (1,)), ((), ())), preferred_element_type=jnp.float32
    )
    row = lax.broadcasted_iota(jnp.int32, logits.shape, 0)
    top = jnp.max(logits, axis=0, keepdims=True)
    expo = jnp.exp(logits - top)
    total = jnp.sum(expo, axis=0, keepdims=True)
    moment = jnp.sum(expo * logits, axis=0, keepdims=True)
    chosen = jnp.sum(jnp.where(row == ids, logits, 0.0), axis=0, keepdims=True)
    return (top, total, moment, chosen)


def merge(parts):
    top = functools.reduce(jnp.maximum, [p[0] for p in parts])
    scale = [jnp.exp(p[0] - top) for p in parts]
    return (
        top,
        sum(p[1] * f for p, f in zip(parts, scale)),
        sum(p[2] * f for p, f in zip(parts, scale)),
        sum(p[3] for p in parts),
    )


def to_owners(stats, owner):
    n = owner.shape[1]
    chips = N_LINE * N_LINE
    here = owner == lax.broadcasted_iota(jnp.int32, (chips, n), 0)
    rows = []
    for stat in stats:
        for _ in range(3):
            part = stat.astype(jnp.bfloat16).astype(jnp.float32)
            rows.append(jnp.where(here, part, 0.0).astype(jnp.bfloat16))
            stat = stat - part
    place = lax.broadcasted_iota(jnp.int32, (n, BLOCK), 0) % BLOCK
    spot = jnp.where(place == lax.broadcasted_iota(jnp.int32, (n, BLOCK), 1), 1.0, 0.0)
    moved = jnp.dot(
        jnp.concatenate(rows, axis=0),
        spot.astype(jnp.bfloat16),
        preferred_element_type=jnp.float32,
    ).reshape(STATS, 3, chips, BLOCK)
    moved = moved[:, 0] + moved[:, 1] + moved[:, 2]
    return [moved[k] for k in range(STATS)]


def early_kernel(len_ref, *refs):
    n_in = N_LINE - 1
    line_refs, (own_ref, out_ref, x_ref, w_ref, sem) = refs[:n_in], refs[n_in:]
    vocab_dev, width = own_ref.shape
    t, _, _ = my_core()
    each = block_copies(len_ref, line_refs, x_ref, sem)
    tiles = weight_copies(own_ref, w_ref, 0, sem, N_LINE * N_LINE)
    each(lambda copy: copy.start())
    tiles[0].start()
    each(lambda copy: copy.wait())
    for copy in tiles[1:]:
        copy.start()
    n = LIVE * BLOCK
    x = x_ref[:, :, :width].reshape(n, width)
    ids = token_row(x_ref[:, :, width:].reshape(n, LANES)) - t * vocab_dev
    parts = []
    for i, copy in enumerate(tiles):
        copy.wait()
        parts.append(tile_stats(w_ref[i], x, ids - i * TILE))
    out_ref[...] = jnp.zeros_like(out_ref)
    for k, stat in enumerate(merge(parts)):
        out_ref[k : k + 1, :] = stat


def late_kernel(len_ref, *refs):
    line_refs = refs[:N_LINE]
    own_ref, other_ref, early_ref, out_ref, x_ref, last_ref, w_ref, sem = refs[N_LINE:]
    vocab_dev, width = own_ref.shape
    t, core, mine = my_core()
    starts, total_blocks = block_starts(len_ref, core)
    line = lax.rem(mine + OFFSETS[-1] + N_LINE, N_LINE)
    sems = N_LINE * N_LINE
    each = block_copies(len_ref, line_refs, x_ref, sem)
    other = weight_copies(other_ref, w_ref, 0, sem, sems)
    own = weight_copies(own_ref, w_ref, len(other), sem, sems)
    last = pltpu.make_async_copy(line_refs[-1], last_ref, sem.at[sems + 2 * len(other)])
    each(lambda copy: copy.start())
    other[0].start()
    each(lambda copy: copy.wait())
    for copy in other[1:] + [last] + own:
        copy.start()

    n = LIVE * BLOCK
    x = x_ref[:, :, :width].reshape(n, width)
    ids = token_row(x_ref[:, :, width:].reshape(n, LANES)) - (t + 1 - 2 * core) * vocab_dev
    lane = lax.broadcasted_iota(jnp.int32, (1, n), 1) // BLOCK
    owner = jnp.where(lane < total_blocks, owner_of(lane, starts), -1)

    def line_of(o):
        return jnp.where(core == 0, o % N_LINE, o // N_LINE)

    missing = line_of(owner) == line
    parts = [
        tuple(
            jnp.where(missing, rest, early_ref[k : k + 1, :])
            for k, rest in enumerate((-1e30, 0.0, 0.0, 0.0))
        )
    ]
    for i, copy in enumerate(other):
        copy.wait()
        parts.append(tile_stats(w_ref[i], x, ids - i * TILE))
    most = to_owners(merge(parts), owner)

    last.wait()
    x = last_ref[:, :width]
    ids = token_row(last_ref[:, width:]) - t * vocab_dev
    parts = []
    for i, copy in enumerate(own):
        copy.wait()
        parts.append(tile_stats(w_ref[len(other) + i], x, ids - i * TILE))
    m = lax.broadcasted_iota(jnp.int32, (1, N_LINE * BLOCK), 1) // BLOCK
    rest = to_owners(merge(parts), jnp.where(core == 0, m * N_LINE + line, line * N_LINE + m))
    chips = N_LINE * N_LINE
    added = line_of(lax.broadcasted_iota(jnp.int32, (chips, BLOCK), 0)) == line
    rest[0] = jnp.where(added, rest[0], -1e30)
    out_ref[...] = jnp.concatenate(merge([most, rest]), axis=1)


def run_head(kernel, lengths, lines, weights, before, out_shape, scratch):
    vocab_dev, width = weights[0].shape
    n_tiles = len(weights) * (vocab_dev // TILE)
    anywhere = pl.BlockSpec(memory_space=pl.ANY)
    vmem = pl.BlockSpec(memory_space=pltpu.VMEM)
    n = LIVE * BLOCK
    return pl.pallas_call(
        kernel,
        in_specs=[pl.BlockSpec(memory_space=pltpu.SMEM)]
        + [anywhere] * (len(lines) + len(weights))
        + [vmem] * len(before),
        out_specs=vmem,
        out_shape=jax.ShapeDtypeStruct(out_shape, jnp.float32),
        scratch_shapes=[pltpu.VMEM((LIVE, BLOCK, width + LANES), jnp.bfloat16)]
        + scratch
        + [
            pltpu.VMEM((n_tiles, TILE, width), jnp.bfloat16),
            pltpu.SemaphoreType.DMA((N_LINE * N_LINE + n_tiles + 1,)),
        ],
        cost_estimate=pl.CostEstimate(
            flops=2 * n * width * vocab_dev,
            bytes_accessed=2 * width * (n + len(weights) * vocab_dev),
            transcendentals=n * vocab_dev,
        ),
    )(lengths, *lines, *weights, *before)


def per_device(hidden, norm_gain, head_weight, token_ids, lengths):
    row_dev, width = hidden.shape
    vocab_dev = head_weight.shape[1]
    n_chip = N_LINE * N_LINE
    n_t = n_chip * N_CORE
    tensor_idx = lax.axis_index("tensor")
    same_core = [[N_CORE * k + c for k in range(n_chip)] for c in range(N_CORE)]
    other_core = [(i, i ^ 1) for i in range(n_t)]
    along_z = [[(z * N_LINE + y) * N_CORE for z in range(N_LINE)] for y in range(N_LINE)]
    along_y = [[(z * N_LINE + y) * N_CORE + 1 for y in range(N_LINE)] for z in range(N_LINE)]

    def along(by):
        step = []
        for i in range(n_t):
            z, y, core = i // (N_LINE * N_CORE), i // N_CORE % N_LINE, i % N_CORE
            if core == 0:
                y = (y + by) % N_LINE
            else:
                z = (z + by) % N_LINE
            step.append((i, (z * N_LINE + y) * N_CORE + core))
        return step

    from_before, far, from_after = (
        lax.ppermute(head_weight, "dp", [(i, (i + k) % N_DP) for i in range(N_DP)])
        for k in (1, 2, 3)
    )

    vmem = pl.BlockSpec(memory_space=pltpu.VMEM)
    block = pl.pallas_call(
        norm_kernel,
        in_specs=[vmem] * 3,
        out_specs=vmem,
        out_shape=jax.ShapeDtypeStruct((N_LINE, row_dev, width + LANES), jnp.bfloat16),
    )(hidden, norm_gain[None, :], token_ids[None, :])
    line = lax.all_to_all(block, "tensor", 0, 0, axis_index_groups=along_z + along_y)
    own = line.reshape(N_LINE * row_dev, width + LANES)
    up, down = [own], [own]
    for k in range(N_LINE // 2 - 1):
        pair = (
            lax.ppermute(up[-1], "tensor", along(1)),
            lax.ppermute(down[-1], "tensor", along(-1)),
        )
        if k == 0:
            *pair, from_before, from_after = lax.optimization_barrier(
                (*pair, from_before, from_after)
            )
        if k == 1:
            *pair, far = lax.optimization_barrier((*pair, far))
        up.append(pair[0])
        down.append(pair[1])
    pieces = [head_weight, from_before, far, from_after]
    up.append(lax.ppermute(up[-1], "tensor", along(1)))
    lines = [own, up[1], down[1], up[2], down[2], up[3], down[3], up[4]]

    weight = pl.pallas_call(
        stack_kernel,
        in_specs=[pl.BlockSpec(memory_space=pl.ANY)] * (len(pieces) + 2),
        out_specs=vmem,
        out_shape=jax.ShapeDtypeStruct((vocab_dev, width), jnp.bfloat16),
        scratch_shapes=[pltpu.SemaphoreType.DMA((len(pieces),))],
        cost_estimate=pl.CostEstimate(
            flops=0, bytes_accessed=4 * vocab_dev * width, transcendentals=0
        ),
    )(*[p.T for p in pieces], up[3], down[3])
    other = lax.ppermute(weight, "tensor", other_core)
    early = run_head(
        early_kernel, lengths, lines[:-1], [weight], [], (8, LIVE * BLOCK), []
    )
    stats = run_head(
        late_kernel,
        lengths,
        lines,
        [weight, other],
        [early],
        (n_chip, STATS * BLOCK),
        [pltpu.VMEM((N_LINE * BLOCK, width + LANES), jnp.bfloat16)],
    )

    back = lax.all_to_all(stats, "tensor", 0, 0, axis_index_groups=same_core, tiled=True)
    back = back.reshape(n_chip, STATS, row_dev)
    top, total, moment, chosen = (back[:, k] for k in range(STATS))
    top_own = jnp.max(top, axis=0)
    rescale = jnp.exp(top - top_own)
    total_own = jnp.sum(total * rescale, axis=0)
    moment_own = jnp.sum(moment * rescale, axis=0)
    chosen_own = jnp.sum(chosen, axis=0)

    own_rows = tensor_idx * row_dev + jnp.arange(row_dev, dtype=jnp.int32)
    onehot = (own_rows // SLOT)[:, None] == jnp.arange(SEQ_DP, dtype=jnp.int32)[None, :]
    length_of = jnp.sum(jnp.where(onehot, lengths[0][None, :], 0), axis=1)
    scored = own_rows % SLOT < length_of
    safe_total = jnp.where(scored, total_own, 1.0)
    lse = top_own + jnp.log(safe_total)
    logprob = jnp.where(scored, chosen_own - lse, 0.0)
    entropy = jnp.where(scored, lse - moment_own / safe_total, 0.0)
    return (logprob, entropy)


def solution(mesh):
    return jax.shard_map(
        per_device,
        mesh=mesh,
        in_specs=(
            P(("dp", "tensor"), None),
            P(),
            P("dp", "tensor"),
            P(("dp", "tensor")),
            P("dp", None),
        ),
        out_specs=(P(("dp", "tensor")), P(("dp", "tensor"))),
        check_vma=False,
    )
```

time: 131 us -> 143 us (1.092)
  starting transfers between devices: 34.5 us -> 70.5 us
  blocking collectives: 24 us -> 0 us
  between operations: 14.2 us -> 0.88 us
  Pallas kernels: 14.6 us -> 24.9 us
  waiting for transfers between devices: 40.7 us -> 43.1 us
    ppermute x4 -> x10, starting transfers between devices: 15.9 us -> 43.1 us  [the longest x1 12.5 us: per_device(): other = lax.ppermute(weight, 'tensor', other_core)]
    ppermute x4 -> x1, waiting for transfers between devices: 26.6 us -> 1.53 us  [per_device(): up.append(lax.ppermute(up[-1], 'tensor', along(1)))]
    all_to_all x1 -> x0, blocking collectives: 24 us -> none  [per_device(): lax.all_to_all(block, 'tensor', 0, 0, axis_index_groups=along_z + along_y)]
    ppermute x4 -> x10, waiting for transfers between devices: 1.49 us -> 21.9 us  [the longest x3 9.58 us: per_device(): lax.ppermute(head_weight, 'dp', [(i, (i + k) % N_DP) for i in range(N_DP)])]
    all_to_all x0 -> x1, starting transfers between devices: none -> 10.3 us  [per_device(): lax.all_to_all(block, 'tensor', 0, 0, axis_index_groups=along_z + along_y)]
    pallas_call x1 -> x3, Pallas kernels: 12.8 us -> 23 us  [the longest x2 19.4 us: run_head(): pl.pallas_call(kernel, in_specs=[pl.BlockSpec(memory_space=pltpu.SMEM)] +...]
    all_to_all x0 -> x1, waiting for transfers between devices: none -> 7.79 us  [per_device(): lax.all_to_all(block, 'tensor', 0, 0, axis_index_groups=along_z + along_y)]
    ppermute x4 -> x1, starting transfers between devices: 10.7 us -> 3.48 us  [per_device(): up.append(lax.ppermute(up[-1], 'tensor', along(1)))]
  transfers between devices with their start and end apart: 10 -> 13, of which waited for: 6 -> 8; matrix products, arithmetic and copies ran while one was open for 1% -> 0% of each run, Pallas kernels for 1% -> 6%
where the time goes in v8:
time: 143 us; the launch traced here: 142 us
  starting transfers between devices  70.5 us (49%)
  waiting for transfers between devices  43.1 us (30%)
  Pallas kernels  24.9 us (17%)
  local copies, waits for them, and re-layouts  1.72 us (1%)
    pallas_call x2, Pallas kernels, run_head(): pl.pallas_call(kernel, in_specs=[pl.BlockSpec(memory_space=pltpu.SMEM)] +...  19.4 us
    all_to_all x1, starting transfers between devices, per_device(): lax.all_to_all(stats, 'tensor', 0, 0, axis_index_groups=same_core, tiled=...  13.6 us
    ppermute x1, starting transfers between devices, per_device(): other = lax.ppermute(weight, 'tensor', other_core)  12.5 us
    all_to_all x1, waiting for transfers between devices, per_device(): lax.all_to_all(stats, 'tensor', 0, 0, axis_index_groups=same_core, tiled=...  11.9 us
    ppermute x3, starting transfers between devices, per_device(): lax.ppermute(down[-1], 'tensor', along(-1))  10.7 us
    ppermute x3, starting transfers between devices, per_device(): lax.ppermute(up[-1], 'tensor', along(1))  10.6 us
    all_to_all x1, starting transfers between devices, per_device(): lax.all_to_all(block, 'tensor', 0, 0, axis_index_groups=along_z + along_y)  10.3 us
    ppermute x3, waiting for transfers between devices, per_device(): lax.ppermute(head_weight, 'dp', [(i, (i + k) % N_DP) for i in range(N_DP)])  9.58 us
  transfers between devices with their start and end apart: 13, of which 8 were waited for; matrix products, arithmetic and copies ran while one was open for 0% of the time, Pallas kernels for 6%

profile of v8, /device:TPU:6, one launch (start us, length us, event | category | flops | bytes accessed | tf_op | source)
XLA Modules:
  0.0 142.0 jit_solution(7416529756249245504)
XLA Ops:
  0.6 1.8 %shard_map.68 = bf16[8,16,2176]{2,1,0:T(8,128)(2,1)} custom-call(bf16[16,2048]{1,0:T(8,128)(2,1)} %hidden_ref.1, f32[1,2048]{1,0:T(1,128)} %bitcast.42, s32[1,16]{1,0:T(1,128)} %bitcast.44), custom_call_target="tpu_custom_call" | custom-call | tf_op jit(solution)/shard_map/pallas_call | solution.py:304
  2.4 10.3 %all-to-all-start = ((bf16[8,16,2176]{2,1,0:T(8,128)(2,1)}), bf16[8,16,2176]{2,1,0:T(8,128)(2,1)S(1)}, u32[]{:S(2)}, u32[]{:S(2)}) async-start(bf16[8,16,2176]{2,1,0:T(8,128)(2,1)} %shard_map.68), calls=%async_computation | async-start | bytes 1114112 | tf_op jit(solution)/shard_map/all_to_all | solution.py:310
  12.8 2.4 %collective-permute-start.2 = (bf16[512,800]{0,1:T(8,128)(2,1)}, bf16[512,800]{0,1:T(8,128)(2,1)S(1)}, u32[]{:S(2)}, u32[]{:S(2)}) collective-permute-start(bf16[512,800]{0,1:T(8,128)(2,1)} %param.7), channel_id=1, source_target_pairs={{0,128},{128,256},{256,384},{384,0},{1,129},{129,257},{257,385},{3... | collective-permute-start | bytes 2457608 | tf_op jit(solution)/shard_map/ppermute | solution.py:299
  15.1 3.5 %collective-permute-start.3 = (bf16[512,800]{0,1:T(8,128)(2,1)}, bf16[512,800]{0,1:T(8,128)(2,1)}, u32[]{:S(2)}, u32[]{:S(2)}) collective-permute-start(bf16[512,800]{0,1:T(8,128)(2,1)} %param.7), channel_id=1, source_target_pairs={{0,384},{128,0},{256,128},{384,256},{1,385},{129,1},{257,129},{385... | collective-permute-start | bytes 2457608 | tf_op jit(solution)/shard_map/ppermute | solution.py:299
  18.6 7.8 %all-to-all-done = bf16[8,16,2176]{2,1,0:T(8,128)(2,1)S(1)} async-done(((bf16[8,16,2176]{2,1,0:T(8,128)(2,1)}), bf16[8,16,2176]{2,1,0:T(8,128)(2,1)S(1)}, u32[]{:S(2)}, u32[]{:S(2)}) %all-to-all-start) | async-done | bytes 557088 | tf_op jit(solution)/shard_map/all_to_all | solution.py:310
  26.4 3.5 %collective-permute-start = (bf16[128,2176]{1,0:T(8,128)(2,1)S(1)}, bf16[128,2176]{1,0:T(8,128)(2,1)S(1)}, u32[]{:S(2)}, u32[]{:S(2)}) collective-permute-start(bf16[128,2176]{1,0:T(8,128)(2,1)S(1)} %bitcast.32), channel_id=1, source_target_pairs={{0,2},{1,17},{2,4},{3,19},{4,6},{5,21},{6,8},{7,23},{8,10},{9,25},... | collective-permute-start | bytes 1671176 | tf_op jit(solution)/shard_map/ppermute | solution.py:315
  29.9 3.8 %collective-permute-start.1 = (bf16[128,2176]{1,0:T(8,128)(2,1)S(1)}, bf16[128,2176]{1,0:T(8,128)(2,1)S(1)}, u32[]{:S(2)}, u32[]{:S(2)}) collective-permute-start(bf16[128,2176]{1,0:T(8,128)(2,1)S(1)} %bitcast.33), channel_id=1, source_target_pairs={{0,14},{1,113},{2,0},{3,115},{4,2},{5,117},{6,4},{7,119},{8,6},{9,... | collective-permute-start | bytes 1671176 | tf_op jit(solution)/shard_map/ppermute | solution.py:316
  33.7 3.3 %collective-permute-start.6 = (bf16[512,800]{0,1:T(8,128)(2,1)}, bf16[512,800]{0,1:T(8,128)(2,1)S(1)}, u32[]{:S(2)}, u32[]{:S(2)}) collective-permute-start(bf16[512,800]{0,1:T(8,128)(2,1)} %param.7), channel_id=1, source_target_pairs={{0,256},{128,384},{256,0},{384,128},{1,257},{129,385},{257,1},{385... | collective-permute-start | bytes 2457608 | tf_op jit(solution)/shard_map/ppermute | solution.py:299
  37.0 0.0 collective-permute-done.2
  37.0 0.0 copy-start.7
  37.0 0.0 collective-permute-done.3
  37.1 2.2 %collective-permute-done.refs_1_ = bf16[128,2176]{1,0:T(8,128)(2,1)S(1)} collective-permute-done((bf16[128,2176]{1,0:T(8,128)(2,1)S(1)}, bf16[128,2176]{1,0:T(8,128)(2,1)S(1)}, u32[]{:S(2)}, u32[]{:S(2)}) %collective-permute-start) | collective-permute-done | bytes 557088 | tf_op jit(solution)/shard_map/ppermute | solution.py:315
  39.3 2.0 %collective-permute-done.1.refs_2_ = bf16[128,2176]{1,0:T(8,128)(2,1)S(1)} collective-permute-done((bf16[128,2176]{1,0:T(8,128)(2,1)S(1)}, bf16[128,2176]{1,0:T(8,128)(2,1)S(1)}, u32[]{:S(2)}, u32[]{:S(2)}) %collective-permute-start.1) | collective-permute-done | bytes 557088 | tf_op jit(solution)/shard_map/ppermute | solution.py:316
  41.3 3.5 %collective-permute-start.4 = (bf16[128,2176]{1,0:T(8,128)(2,1)S(1)}, bf16[128,2176]{1,0:T(8,128)(2,1)S(1)}, u32[]{:S(2)}, u32[]{:S(2)}) collective-permute-start(bf16[128,2176]{1,0:T(8,128)(2,1)S(1)} %collective-permute-done.refs_1_), channel_id=1, source_target_pairs={{0,2},{1,17},{2,4},{3,19},{4,6},{5,21},{6,8},{7,23},{8,10},{9,25},... | collective-permute-start | bytes 1671176 | tf_op jit(solution)/shard_map/ppermute | solution.py:315
  44.8 3.6 %collective-permute-start.5 = (bf16[128,2176]{1,0:T(8,128)(2,1)S(1)}, bf16[128,2176]{1,0:T(8,128)(2,1)S(1)}, u32[]{:S(2)}, u32[]{:S(2)}) collective-permute-start(bf16[128,2176]{1,0:T(8,128)(2,1)S(1)} %collective-permute-done.1.refs_2_), channel_id=1, source_target_pairs={{0,14},{1,113},{2,0},{3,115},{4,2},{5,117},{6,4},{7,119},{8,6},{9,... | collective-permute-start | bytes 1671176 | tf_op jit(solution)/shard_map/ppermute | solution.py:316
  48.4 9.6 %collective-permute-done.6 = bf16[512,800]{0,1:T(8,128)(2,1)S(1)} collective-permute-done((bf16[512,800]{0,1:T(8,128)(2,1)}, bf16[512,800]{0,1:T(8,128)(2,1)S(1)}, u32[]{:S(2)}, u32[]{:S(2)}) %collective-permute-start.6) | collective-permute-done | bytes 819232 | tf_op jit(solution)/shard_map/ppermute | solution.py:299
  57.9 0.0 collective-permute-done.4.refs_3_
  57.9 0.0 copy-done.7
  58.0 0.0 copy-start.5
  58.0 0.0 collective-permute-done.5.refs_4_
  58.0 0.0 copy-start.6
  58.0 3.7 %collective-permute-start.7 = (bf16[128,2176]{1,0:T(8,128)(2,1)S(1)}, bf16[128,2176]{1,0:T(8,128)(2,1)S(1)}, u32[]{:S(2)}, u32[]{:S(2)}) collective-permute-start(bf16[128,2176]{1,0:T(8,128)(2,1)S(1)} %collective-permute-done.4.refs_3_), channel_id=1, source_target_pairs={{0,2},{1,17},{2,4},{3,19},{4,6},{5,21},{6,8},{7,23},{8,10},{9,25},... | collective-permute-start | bytes 1671176 | tf_op jit(solution)/shard_map/ppermute | solution.py:315
  61.7 3.4 %collective-permute-start.8 = (bf16[128,2176]{1,0:T(8,128)(2,1)S(1)}, bf16[128,2176]{1,0:T(8,128)(2,1)S(1)}, u32[]{:S(2)}, u32[]{:S(2)}) collective-permute-start(bf16[128,2176]{1,0:T(8,128)(2,1)S(1)} %collective-permute-done.5.refs_4_), channel_id=1, source_target_pairs={{0,14},{1,113},{2,0},{3,115},{4,2},{5,117},{6,4},{7,119},{8,6},{9,... | collective-permute-start | bytes 1671176 | tf_op jit(solution)/shard_map/ppermute | solution.py:316
  65.1 5.6 %collective-permute-done.7.up_ref.refs_5_ = bf16[128,2176]{1,0:T(8,128)(2,1)S(1)} collective-permute-done((bf16[128,2176]{1,0:T(8,128)(2,1)S(1)}, bf16[128,2176]{1,0:T(8,128)(2,1)S(1)}, u32[]{:S(2)}, u32[]{:S(2)}) %collective-permute-start.7) | collective-permute-done | bytes 557088 | tf_op jit(solution)/shard_map/ppermute | solution.py:315
  70.6 2.5 %collective-permute-done.8.down_ref.refs_6_ = bf16[128,2176]{1,0:T(8,128)(2,1)S(1)} collective-permute-done((bf16[128,2176]{1,0:T(8,128)(2,1)S(1)}, bf16[128,2176]{1,0:T(8,128)(2,1)S(1)}, u32[]{:S(2)}, u32[]{:S(2)}) %collective-permute-start.8) | collective-permute-done | bytes 557088 | tf_op jit(solution)/shard_map/ppermute | solution.py:316
  73.1 0.0 copy-done.6
  73.1 0.0 copy-done.8
  73.1 0.0 copy-done.1
  73.1 0.8 copy-done.2
  73.9 3.6 %shard_map.69.refs_7_.refs_8_ = bf16[800,2048]{1,0:T(8,128)(2,1)} custom-call(bf16[800,512]{1,0:T(8,128)(2,1)} %bitcast.36, bf16[800,512]{1,0:T(8,128)(2,1)} %bitcast.37, bf16[800,512]{1,0:T(8,128)(2,1)} %bitcast.38, bf16[800,512]{1,0:T(8,128)(2,1)} %bitcast.7.after, bf16[128,2176]{1,0:T(8,128)(2,1)} %copy-done.1, bf16[128,2176]{1,0:T(8,128)(2,1)} %copy-done.2), custom_call_target="tpu_custom_call" | custom-call | bytes 6553600 | tf_op jit(solution)/shard_map/pallas_call | solution.py:330
  77.5 0.0 copy-done
  77.5 12.5 %collective-permute-start.10 = (bf16[800,2048]{1,0:T(8,128)(2,1)}, bf16[800,2048]{1,0:T(8,128)(2,1)}, u32[]{:S(2)}, u32[]{:S(2)}) collective-permute-start(bf16[800,2048]{1,0:T(8,128)(2,1)} %shard_map.69.refs_7_.refs_8_), channel_id=1, source_target_pairs={{0,1},{1,0},{2,3},{3,2},{4,5},{5,4},{6,7},{7,6},{8,9},{9,8},{10,11... | collective-permute-start | bytes 9830408 | tf_op jit(solution)/shard_map/ppermute | solution.py:340
  90.1 3.5 %collective-permute-start.9 = (bf16[128,2176]{1,0:T(8,128)(2,1)}, bf16[128,2176]{1,0:T(8,128)(2,1)S(1)}, u32[]{:S(2)}, u32[]{:S(2)}) collective-permute-start(bf16[128,2176]{1,0:T(8,128)(2,1)} %copy-done.1), channel_id=1, source_target_pairs={{0,2},{1,17},{2,4},{3,19},{4,6},{5,21},{6,8},{7,23},{8,10},{9,25},... | collective-permute-start | bytes 1671176 | tf_op jit(solution)/shard_map/ppermute | solution.py:327
  93.6 0.0 copy-done.3
  93.6 8.3 %shard_map.70.refs_10_ = f32[8,544]{1,0:T(8,128)} custom-call(s32[1,4]{1,0:T(1,128)} %len_ref.3, bf16[128,2176]{1,0:T(8,128)(2,1)} %bitcast.34, bf16[128,2176]{1,0:T(8,128)(2,1)} %copy-done.3, bf16[128,2176]{1,0:T(8,128)(2,1)} %copy-done.4, bf16[128,2176]{1,0:T(8,128)(2,1)} %copy-done.5, bf16[128,2176]{1,0:T(8,128)(2,1)} %copy-done.6, ...), custom_call_target="tpu_custom_call" | custom-call | flops 1782579200 | bytes 5505024 | tf_op jit(solution)/shard_map/pallas_call | solution.py:255
  101.9 0.0 copy-start.10
  101.9 1.5 %collective-permute-done.9.refs_7_ = bf16[128,2176]{1,0:T(8,128)(2,1)S(1)} collective-permute-done((bf16[128,2176]{1,0:T(8,128)(2,1)}, bf16[128,2176]{1,0:T(8,128)(2,1)S(1)}, u32[]{:S(2)}, u32[]{:S(2)}) %collective-permute-start.9) | collective-permute-done | bytes 557088 | tf_op jit(solution)/shard_map/ppermute | solution.py:327
  103.5 0.0 collective-permute-done.10.refs_9_
  103.5 0.8 copy-done.9
  104.3 11.2 %shard_map.71 = f32[64,64]{1,0:T(8,128)} custom-call(s32[1,4]{1,0:T(1,128)} %len_ref.3, bf16[128,2176]{1,0:T(8,128)(2,1)} %bitcast.35, bf16[128,2176]{1,0:T(8,128)(2,1)} %copy-done.3, bf16[128,2176]{1,0:T(8,128)(2,1)} %copy-done.4, bf16[128,2176]{1,0:T(8,128)(2,1)} %copy-done.5, bf16[128,2176]{1,0:T(8,128)(2,1)} %copy-done.6, bf16[128,2176]{1,0:T(8,128)(2,1)} %copy-done.1, ...), custom_call_target="tpu_custom_call" | custom-call | flops 1782579200 | bytes 8781824 | tf_op jit(solution)/shard_map/pallas_call | solution.py:255
  115.4 13.6 %all-to-all-start.1 = ((f32[64,1,64]{2,1,0:T(1,128)}), f32[64,1,64]{2,1,0:T(1,128)S(1)}, u32[]{:S(2)}, u32[]{:S(2)}) async-start(f32[64,1,64]{2,1,0:T(1,128)} %bitcast.41), calls=%async_computation.1 | async-start | bytes 65536 | tf_op jit(solution)/shard_map/all_to_all | solution.py:354
  129.1 0.0 copy-done.10
  129.1 0.1 select_reduce_fusion
  129.2 11.9 %all-to-all-done.1 = f32[64,1,64]{2,1,0:T(1,128)S(1)} async-done(((f32[64,1,64]{2,1,0:T(1,128)}), f32[64,1,64]{2,1,0:T(1,128)S(1)}, u32[]{:S(2)}, u32[]{:S(2)}) %all-to-all-start.1) | async-done | bytes 16416 | tf_op jit(solution)/shard_map/all_to_all | solution.py:354
  141.1 0.1 copy.13
  141.1 0.1 slice_reduce_fusion.1
  141.3 0.2 fusion.1
  141.5 0.5 subtract_select_fusion
  (10 shorter events, 0.0 us)
Async XLA Ops:
  2.4 24.0 %all-to-all-start = ((bf16[8,16,2176]{2,1,0:T(8,128)(2,1)}), bf16[8,16,2176]{2,1,0:T(8,128)(2,1)S(1)}, u32[]{:S(2)}, u32[]{:S(2)}) async-start(bf16[8,16,2176]{2,1,0:T(8,128)(2,1)} %shard_map.68), calls=%async_computation | async-start | bytes 1114112 | tf_op jit(solution)/shard_map/all_to_all | solution.py:310
  12.8 24.3 %collective-permute-start.2 = (bf16[512,800]{0,1:T(8,128)(2,1)}, bf16[512,800]{0,1:T(8,128)(2,1)S(1)}, u32[]{:S(2)}, u32[]{:S(2)}) collective-permute-start(bf16[512,800]{0,1:T(8,128)(2,1)} %param.7), channel_id=1, source_target_pairs={{0,128},{128,256},{256,384},{384,0},{1,129},{129,257},{257,385},{3... | collective-permute-start | bytes 2457608 | tf_op jit(solution)/shard_map/ppermute | solution.py:299
  15.1 21.9 %collective-permute-start.3 = (bf16[512,800]{0,1:T(8,128)(2,1)}, bf16[512,800]{0,1:T(8,128)(2,1)}, u32[]{:S(2)}, u32[]{:S(2)}) collective-permute-start(bf16[512,800]{0,1:T(8,128)(2,1)} %param.7), channel_id=1, source_target_pairs={{0,384},{128,0},{256,128},{384,256},{1,385},{129,1},{257,129},{385... | collective-permute-start | bytes 2457608 | tf_op jit(solution)/shard_map/ppermute | solution.py:299
  26.4 51.1 %copy-start = (bf16[8,16,2176]{2,1,0:T(8,128)(2,1)}, bf16[8,16,2176]{2,1,0:T(8,128)(2,1)S(1)}, u32[]{:S(2)}) copy-start(bf16[8,16,2176]{2,1,0:T(8,128)(2,1)S(1)} %all-to-all-done) | copy-start | bytes 1671172
  26.4 12.9 %collective-permute-start = (bf16[128,2176]{1,0:T(8,128)(2,1)S(1)}, bf16[128,2176]{1,0:T(8,128)(2,1)S(1)}, u32[]{:S(2)}, u32[]{:S(2)}) collective-permute-start(bf16[128,2176]{1,0:T(8,128)(2,1)S(1)} %bitcast.32), channel_id=1, source_target_pairs={{0,2},{1,17},{2,4},{3,19},{4,6},{5,21},{6,8},{7,23},{8,10},{9,25},... | collective-permute-start | bytes 1671176 | tf_op jit(solution)/shard_map/ppermute | solution.py:315
  29.9 11.4 %collective-permute-start.1 = (bf16[128,2176]{1,0:T(8,128)(2,1)S(1)}, bf16[128,2176]{1,0:T(8,128)(2,1)S(1)}, u32[]{:S(2)}, u32[]{:S(2)}) collective-permute-start(bf16[128,2176]{1,0:T(8,128)(2,1)S(1)} %bitcast.33), channel_id=1, source_target_pairs={{0,14},{1,113},{2,0},{3,115},{4,2},{5,117},{6,4},{7,119},{8,6},{9,... | collective-permute-start | bytes 1671176 | tf_op jit(solution)/shard_map/ppermute | solution.py:316
  33.7 24.2 %collective-permute-start.6 = (bf16[512,800]{0,1:T(8,128)(2,1)}, bf16[512,800]{0,1:T(8,128)(2,1)S(1)}, u32[]{:S(2)}, u32[]{:S(2)}) collective-permute-start(bf16[512,800]{0,1:T(8,128)(2,1)} %param.7), channel_id=1, source_target_pairs={{0,256},{128,384},{256,0},{384,128},{1,257},{129,385},{257,1},{385... | collective-permute-start | bytes 2457608 | tf_op jit(solution)/shard_map/ppermute | solution.py:299
  37.0 20.9 %copy-start.7 = (bf16[512,800]{0,1:T(8,128)(2,1)}, bf16[512,800]{0,1:T(8,128)(2,1)S(1)}, u32[]{:S(2)}) copy-start(bf16[512,800]{0,1:T(8,128)(2,1)S(1)} %collective-permute-done.2) | copy-start | bytes 2457604
  39.3 54.3 %copy-start.3 = (bf16[128,2176]{1,0:T(8,128)(2,1)}, bf16[128,2176]{1,0:T(8,128)(2,1)S(1)}, u32[]{:S(2)}) copy-start(bf16[128,2176]{1,0:T(8,128)(2,1)S(1)} %collective-permute-done.refs_1_) | copy-start | bytes 1671172
  41.3 52.3 %copy-start.4 = (bf16[128,2176]{1,0:T(8,128)(2,1)}, bf16[128,2176]{1,0:T(8,128)(2,1)S(1)}, u32[]{:S(2)}) copy-start(bf16[128,2176]{1,0:T(8,128)(2,1)S(1)} %collective-permute-done.1.refs_2_) | copy-start | bytes 1671172
  41.3 16.6 %collective-permute-start.4 = (bf16[128,2176]{1,0:T(8,128)(2,1)S(1)}, bf16[128,2176]{1,0:T(8,128)(2,1)S(1)}, u32[]{:S(2)}, u32[]{:S(2)}) collective-permute-start(bf16[128,2176]{1,0:T(8,128)(2,1)S(1)} %collective-permute-done.refs_1_), channel_id=1, source_target_pairs={{0,2},{1,17},{2,4},{3,19},{4,6},{5,21},{6,8},{7,23},{8,10},{9,25},... | collective-permute-start | bytes 1671176 | tf_op jit(solution)/shard_map/ppermute | solution.py:315
  44.8 13.2 %collective-permute-start.5 = (bf16[128,2176]{1,0:T(8,128)(2,1)S(1)}, bf16[128,2176]{1,0:T(8,128)(2,1)S(1)}, u32[]{:S(2)}, u32[]{:S(2)}) collective-permute-start(bf16[128,2176]{1,0:T(8,128)(2,1)S(1)} %collective-permute-done.1.refs_2_), channel_id=1, source_target_pairs={{0,14},{1,113},{2,0},{3,115},{4,2},{5,117},{6,4},{7,119},{8,6},{9,... | collective-permute-start | bytes 1671176 | tf_op jit(solution)/shard_map/ppermute | solution.py:316
  57.9 15.2 %copy-start.8 = (bf16[512,800]{0,1:T(8,128)(2,1)}, bf16[512,800]{0,1:T(8,128)(2,1)S(1)}, u32[]{:S(2)}) copy-start(bf16[512,800]{0,1:T(8,128)(2,1)S(1)} %collective-permute-done.6) | copy-start | bytes 2457604
  58.0 35.7 %copy-start.5 = (bf16[128,2176]{1,0:T(8,128)(2,1)}, bf16[128,2176]{1,0:T(8,128)(2,1)S(1)}, u32[]{:S(2)}) copy-start(bf16[128,2176]{1,0:T(8,128)(2,1)S(1)} %collective-permute-done.4.refs_3_) | copy-start | bytes 1671172
  58.0 15.1 %copy-start.6 = (bf16[128,2176]{1,0:T(8,128)(2,1)}, bf16[128,2176]{1,0:T(8,128)(2,1)S(1)}, u32[]{:S(2)}) copy-start(bf16[128,2176]{1,0:T(8,128)(2,1)S(1)} %collective-permute-done.5.refs_4_) | copy-start | bytes 1671172
  58.0 12.6 %collective-permute-start.7 = (bf16[128,2176]{1,0:T(8,128)(2,1)S(1)}, bf16[128,2176]{1,0:T(8,128)(2,1)S(1)}, u32[]{:S(2)}, u32[]{:S(2)}) collective-permute-start(bf16[128,2176]{1,0:T(8,128)(2,1)S(1)} %collective-permute-done.4.refs_3_), channel_id=1, source_target_pairs={{0,2},{1,17},{2,4},{3,19},{4,6},{5,21},{6,8},{7,23},{8,10},{9,25},... | collective-permute-start | bytes 1671176 | tf_op jit(solution)/shard_map/ppermute | solution.py:315
  61.7 11.4 %collective-permute-start.8 = (bf16[128,2176]{1,0:T(8,128)(2,1)S(1)}, bf16[128,2176]{1,0:T(8,128)(2,1)S(1)}, u32[]{:S(2)}, u32[]{:S(2)}) collective-permute-start(bf16[128,2176]{1,0:T(8,128)(2,1)S(1)} %collective-permute-done.5.refs_4_), channel_id=1, source_target_pairs={{0,14},{1,113},{2,0},{3,115},{4,2},{5,117},{6,4},{7,119},{8,6},{9,... | collective-permute-start | bytes 1671176 | tf_op jit(solution)/shard_map/ppermute | solution.py:316
  70.6 2.5 %copy-start.1 = (bf16[128,2176]{1,0:T(8,128)(2,1)}, bf16[128,2176]{1,0:T(8,128)(2,1)S(1)}, u32[]{:S(2)}) copy-start(bf16[128,2176]{1,0:T(8,128)(2,1)S(1)} %collective-permute-done.7.up_ref.refs_5_) | copy-start | bytes 1671172
  73.1 0.8 copy-start.2
  77.5 25.9 %collective-permute-start.10 = (bf16[800,2048]{1,0:T(8,128)(2,1)}, bf16[800,2048]{1,0:T(8,128)(2,1)}, u32[]{:S(2)}, u32[]{:S(2)}) collective-permute-start(bf16[800,2048]{1,0:T(8,128)(2,1)} %shard_map.69.refs_7_.refs_8_), channel_id=1, source_target_pairs={{0,1},{1,0},{2,3},{3,2},{4,5},{5,4},{6,7},{7,6},{8,9},{9,8},{10,11... | collective-permute-start | bytes 9830408 | tf_op jit(solution)/shard_map/ppermute | solution.py:340
  90.1 13.4 %collective-permute-start.9 = (bf16[128,2176]{1,0:T(8,128)(2,1)}, bf16[128,2176]{1,0:T(8,128)(2,1)S(1)}, u32[]{:S(2)}, u32[]{:S(2)}) collective-permute-start(bf16[128,2176]{1,0:T(8,128)(2,1)} %copy-done.1), channel_id=1, source_target_pairs={{0,2},{1,17},{2,4},{3,19},{4,6},{5,21},{6,8},{7,23},{8,10},{9,25},... | collective-permute-start | bytes 1671176 | tf_op jit(solution)/shard_map/ppermute | solution.py:327
  101.9 27.1 %copy-start.10 = (s32[1,4]{1,0:T(1,128)S(1)}, s32[1,4]{1,0:T(1,128)}, u32[]{:S(2)}) copy-start(s32[1,4]{1,0:T(1,128)} %len_ref.3) | copy-start | bytes 52
  103.5 0.8 copy-start.9
  115.4 25.6 %all-to-all-start.1 = ((f32[64,1,64]{2,1,0:T(1,128)}), f32[64,1,64]{2,1,0:T(1,128)S(1)}, u32[]{:S(2)}, u32[]{:S(2)}) async-start(f32[64,1,64]{2,1,0:T(1,128)} %bitcast.41), calls=%async_computation.1 | async-start | bytes 65536 | tf_op jit(solution)/shard_map/all_to_all | solution.py:354

commit v9 on v8

--- a/solution.py
+++ b/solution.py
@@ -9,7 +9,6 @@
 
 SEQ_DP = 4
 SLOT = 512
-N_DP = 4
 N_LINE = 8
 N_CORE = 2
 LANES = 128
@@ -55,21 +54,6 @@
         out_ref[j] = both
 
 
-def stack_kernel(own, before, far, after, up_ref, down_ref, out_ref, sem):
-    del up_ref, down_ref
-    me = lax.axis_index("dp")
-    depth = own.shape[1]
-    copies = []
-    for k, piece in enumerate((own, before, far, after)):
-        src = lax.rem(me - k + N_DP, N_DP)
-        cols = pl.ds(pl.multiple_of(src * depth, depth), depth)
-        copies.append(pltpu.make_async_copy(piece, out_ref.at[:, cols], sem.at[k]))
-    for c in copies:
-        c.start()
-    for c in copies:
-        c.wait()
-
-
 def my_core():
     t = lax.axis_index("tensor")
     core = lax.rem(t, N_CORE)
@@ -77,11 +61,11 @@
     return t, core, jnp.where(core == 0, y, z)
 
 
-def block_copies(len_ref, line_refs, x_ref, sem):
+def block_copies(len_ref, offsets, line_refs, x_ref, sem):
     _, core, mine = my_core()
     starts, _ = block_starts(len_ref, core)
     loads = []
-    for offset, ref in zip(OFFSETS, line_refs):
+    for offset, ref in zip(offsets, line_refs):
         line = lax.rem(mine + offset + N_LINE, N_LINE)
         for m in range(N_LINE):
             owner = jnp.where(core == 0, m * N_LINE + line, line * N_LINE + m)
@@ -173,7 +157,7 @@
     line_refs, (own_ref, out_ref, x_ref, w_ref, sem) = refs[:n_in], refs[n_in:]
     vocab_dev, width = own_ref.shape
     t, _, _ = my_core()
-    each = block_copies(len_ref, line_refs, x_ref, sem)
+    each = block_copies(len_ref, OFFSETS[:-1], line_refs, x_ref, sem)
     tiles = weight_copies(own_ref, w_ref, 0, sem, N_LINE * N_LINE)
     each(lambda copy: copy.start())
     tiles[0].start()
@@ -192,22 +176,35 @@
         out_ref[k : k + 1, :] = stat
 
 
-def late_kernel(len_ref, *refs):
-    line_refs = refs[:N_LINE]
-    own_ref, other_ref, early_ref, out_ref, x_ref, last_ref, w_ref, sem = refs[N_LINE:]
+def late_kernel(
+    len_ref, packed_ref, line_ref, own_ref, other_ref, early_ref, out_ref,
+    x_ref, last_ref, w_ref, sem,
+):
     vocab_dev, width = own_ref.shape
     t, core, mine = my_core()
     starts, total_blocks = block_starts(len_ref, core)
     line = lax.rem(mine + OFFSETS[-1] + N_LINE, N_LINE)
-    sems = N_LINE * N_LINE
-    each = block_copies(len_ref, line_refs, x_ref, sem)
-    other = weight_copies(other_ref, w_ref, 0, sem, sems)
-    own = weight_copies(own_ref, w_ref, len(other), sem, sems)
-    last = pltpu.make_async_copy(line_refs[-1], last_ref, sem.at[sems + 2 * len(other)])
+    other = weight_copies(other_ref, w_ref, 0, sem, N_LINE)
+    own = weight_copies(own_ref, w_ref, len(other), sem, N_LINE)
+    spare = N_LINE + 2 * len(other)
+    last = pltpu.make_async_copy(line_ref, last_ref, sem.at[spare])
+    half = LIVE // 2
+    packed = [
+        pltpu.make_async_copy(
+            packed_ref.at[k * half : (k + 1) * half],
+            x_ref.at[k * half : (k + 1) * half],
+            sem.at[spare + 1 + k],
+        )
+        for k in range(2)
+    ]
+    for copy in packed + [other[0], last]:
+        copy.start()
+    for copy in packed:
+        copy.wait()
+    each = block_copies(len_ref, OFFSETS[-1:], [line_ref], x_ref, sem)
     each(lambda copy: copy.start())
-    other[0].start()
     each(lambda copy: copy.wait())
-    for copy in other[1:] + [last] + own:
+    for copy in other[1:] + own:
         copy.start()
 
     n = LIVE * BLOCK
@@ -246,31 +243,46 @@
     out_ref[...] = jnp.concatenate(merge([most, rest]), axis=1)
 
 
-def run_head(kernel, lengths, lines, weights, before, out_shape, scratch):
-    vocab_dev, width = weights[0].shape
-    n_tiles = len(weights) * (vocab_dev // TILE)
+def run_heads(lengths, lines, weight, other):
+    vocab_dev, width = weight.shape
+    tiles = vocab_dev // TILE
     anywhere = pl.BlockSpec(memory_space=pl.ANY)
     vmem = pl.BlockSpec(memory_space=pltpu.VMEM)
+    smem = pl.BlockSpec(memory_space=pltpu.SMEM)
     n = LIVE * BLOCK
+    deep = width + LANES
+    cost = pl.CostEstimate(
+        flops=2 * n * width * vocab_dev,
+        bytes_accessed=2 * width * (n + vocab_dev),
+        transcendentals=n * vocab_dev,
+    )
+    early, packed = pl.pallas_call(
+        early_kernel,
+        in_specs=[smem] + [anywhere] * N_LINE,
+        out_specs=(vmem, vmem),
+        out_shape=(
+            jax.ShapeDtypeStruct((8, n), jnp.float32),
+            jax.ShapeDtypeStruct((LIVE, BLOCK, deep), jnp.bfloat16),
+        ),
+        scratch_shapes=[
+            pltpu.VMEM((tiles, TILE, width), jnp.bfloat16),
+            pltpu.SemaphoreType.DMA((N_LINE * N_LINE + tiles,)),
+        ],
+        cost_estimate=cost,
+    )(lengths, *lines[:-1], weight)
     return pl.pallas_call(
-        kernel,
-        in_specs=[pl.BlockSpec(memory_space=pltpu.SMEM)]
-        + [anywhere] * (len(lines) + len(weights))
-        + [vmem] * len(before),
+        late_kernel,
+        in_specs=[smem] + [anywhere] * 4 + [vmem],
         out_specs=vmem,
-        out_shape=jax.ShapeDtypeStruct(out_shape, jnp.float32),
-        scratch_shapes=[pltpu.VMEM((LIVE, BLOCK, width + LANES), jnp.bfloat16)]
-        + scratch
-        + [
-            pltpu.VMEM((n_tiles, TILE, width), jnp.bfloat16),
-            pltpu.SemaphoreType.DMA((N_LINE * N_LINE + n_tiles + 1,)),
+        out_shape=jax.ShapeDtypeStruct((N_LINE * N_LINE, STATS * BLOCK), jnp.float32),
+        scratch_shapes=[
+            pltpu.VMEM((LIVE, BLOCK, deep), jnp.bfloat16),
+            pltpu.VMEM((N_LINE * BLOCK, deep), jnp.bfloat16),
+            pltpu.VMEM((2 * tiles, TILE, width), jnp.bfloat16),
+            pltpu.SemaphoreType.DMA((N_LINE + 2 * tiles + 3,)),
         ],
-        cost_estimate=pl.CostEstimate(
-            flops=2 * n * width * vocab_dev,
-            bytes_accessed=2 * width * (n + len(weights) * vocab_dev),
-            transcendentals=n * vocab_dev,
-        ),
-    )(lengths, *lines, *weights, *before)
+        cost_estimate=cost,
+    )(lengths, packed, lines[-1], weight, other, early)
 
 
 def per_device(hidden, norm_gain, head_weight, token_ids, lengths):
@@ -295,10 +307,7 @@
             step.append((i, (z * N_LINE + y) * N_CORE + core))
         return step
 
-    from_before, far, from_after = (
-        lax.ppermute(head_weight, "dp", [(i, (i + k) % N_DP) for i in range(N_DP)])
-        for k in (1, 2, 3)
-    )
+    weight = lax.all_gather(head_weight, "dp", axis=0, tiled=True).T
 
     vmem = pl.BlockSpec(memory_space=pltpu.VMEM)
     block = pl.pallas_call(
@@ -310,46 +319,15 @@
     line = lax.all_to_all(block, "tensor", 0, 0, axis_index_groups=along_z + along_y)
     own = line.reshape(N_LINE * row_dev, width + LANES)
     up, down = [own], [own]
-    for k in range(N_LINE // 2 - 1):
-        pair = (
-            lax.ppermute(up[-1], "tensor", along(1)),
-            lax.ppermute(down[-1], "tensor", along(-1)),
-        )
-        if k == 0:
-            *pair, from_before, from_after = lax.optimization_barrier(
-                (*pair, from_before, from_after)
-            )
-        if k == 1:
-            *pair, far = lax.optimization_barrier((*pair, far))
-        up.append(pair[0])
-        down.append(pair[1])
-    pieces = [head_weight, from_before, far, from_after]
+    for _ in range(N_LINE // 2 - 1):
+        up.append(lax.ppermute(up[-1], "tensor", along(1)))
+        down.append(lax.ppermute(down[-1], "tensor", along(-1)))
     up.append(lax.ppermute(up[-1], "tensor", along(1)))
     lines = [own, up[1], down[1], up[2], down[2], up[3], down[3], up[4]]
 
-    weight = pl.pallas_call(
-        stack_kernel,
-        in_specs=[pl.BlockSpec(memory_space=pl.ANY)] * (len(pieces) + 2),
-        out_specs=vmem,
-        out_shape=jax.ShapeDtypeStruct((vocab_dev, width), jnp.bfloat16),
-        scratch_shapes=[pltpu.SemaphoreType.DMA((len(pieces),))],
-        cost_estimate=pl.CostEstimate(
-            flops=0, bytes_accessed=4 * vocab_dev * width, transcendentals=0
-        ),
-    )(*[p.T for p in pieces], up[3], down[3])
+    weight, _, _ = lax.optimization_barrier((weight, up[3], down[3]))
     other = lax.ppermute(weight, "tensor", other_core)
-    early = run_head(
-        early_kernel, lengths, lines[:-1], [weight], [], (8, LIVE * BLOCK), []
-    )
-    stats = run_head(
-        late_kernel,
-        lengths,
-        lines,
-        [weight, other],
-        [early],
-        (n_chip, STATS * BLOCK),
-        [pltpu.VMEM((N_LINE * BLOCK, width + LANES), jnp.bfloat16)],
-    )
+    stats = run_heads(lengths, lines, weight, other)
 
     back = lax.all_to_all(stats, "tensor", 0, 0, axis_index_groups=same_core, tiled=True)
     back = back.reshape(n_chip, STATS, row_dev)

time: 143 us -> 130 us (0.909)
  starting transfers between devices: 70.5 us -> 34.6 us
  blocking collectives: 0 us -> 24 us
  between operations: 0.88 us -> 14.2 us
  waiting for transfers between devices: 43.1 us -> 31.8 us
  Pallas kernels: 24.9 us -> 21.5 us
    all_to_all x0 -> x1, blocking collectives: none -> 24 us  [per_device(): lax.all_to_all(block, 'tensor', 0, 0, axis_index_groups=along_z + along_y)]
    ppermute x9 -> x3, waiting for transfers between devices: 21.9 us -> 0.69 us  [per_device(): down.append(lax.ppermute(down[-1], 'tensor', along(-1)))]
    ppermute x1 -> x4, waiting for transfers between devices: 1.53 us -> 18.5 us  [per_device(): up.append(lax.ppermute(up[-1], 'tensor', along(1)))]
    ppermute x9 -> x3, starting transfers between devices: 30.5 us -> 14 us  [per_device(): down.append(lax.ppermute(down[-1], 'tensor', along(-1)))]
    ppermute x1, starting transfers between devices: 12.5 us -> 1.91 us  [per_device(): other = lax.ppermute(weight, 'tensor', other_core)]
    all_to_all x1 -> x0, starting transfers between devices: 10.3 us -> none  [per_device(): lax.all_to_all(block, 'tensor', 0, 0, axis_index_groups=along_z + along_y)]
    all_to_all x1 -> x0, waiting for transfers between devices: 7.79 us -> none  [per_device(): lax.all_to_all(block, 'tensor', 0, 0, axis_index_groups=along_z + along_y)]
    ppermute x1 -> x4, starting transfers between devices: 3.48 us -> 10.7 us  [per_device(): up.append(lax.ppermute(up[-1], 'tensor', along(1)))]
  transfers between devices with their start and end apart: 13 -> 10, of which waited for: 8 -> 6; matrix products, arithmetic and copies ran while one was open for 0% -> 0% of each run, Pallas kernels for 6% -> 8%
where the time goes in v9:
time: 130 us
  starting transfers between devices  34.6 us (27%)
  waiting for transfers between devices  31.8 us (24%)
  blocking collectives  24 us (18%)
  Pallas kernels  21.5 us (17%)
  between operations  14.2 us (11%)
  local copies, waits for them, and re-layouts  2.67 us (2%)
    all_to_all x1, blocking collectives, per_device(): lax.all_to_all(block, 'tensor', 0, 0, axis_index_groups=along_z + along_y)  24 us
    ppermute x4, waiting for transfers between devices, per_device(): up.append(lax.ppermute(up[-1], 'tensor', along(1)))  18.5 us
    ppermute x3, starting transfers between devices, per_device(): down.append(lax.ppermute(down[-1], 'tensor', along(-1)))  14 us
    all_to_all x1, waiting for transfers between devices, per_device(): lax.all_to_all(stats, 'tensor', 0, 0, axis_index_groups=same_core, tiled=...  11.9 us
    pallas_call x1, Pallas kernels, run_heads(): pl.pallas_call(late_kernel, in_specs=[smem] + [anywhere] * 4 + [vmem], ou...  11.4 us
    ppermute x4, starting transfers between devices, per_device(): up.append(lax.ppermute(up[-1], 'tensor', along(1)))  10.7 us
    pallas_call x1, Pallas kernels, run_heads(): pl.pallas_call(early_kernel, in_specs=[smem] + [anywhere] * N_LINE, out_s...  8.29 us
    all_to_all x1, starting transfers between devices, per_device(): lax.all_to_all(stats, 'tensor', 0, 0, axis_index_groups=same_core, tiled=...  7.95 us
  transfers between devices with their start and end apart: 10, of which 6 were waited for; matrix products, arithmetic and copies ran while one was open for 0% of the time, Pallas kernels for 8%

profile of v9, /device:TPU:6, one launch (start us, length us, event | category | flops | bytes accessed | tf_op | source)
XLA Modules:
  0.0 129.6 jit_solution(1031232216767312847)
XLA Ops:
  7.2 0.0 all-gather.2.cloned.1.call-start
  7.2 0.7 all-gather.2.cloned.1.call-update
  7.9 1.8 %shard_map.68 = bf16[8,16,2176]{2,1,0:T(8,128)(2,1)} custom-call(bf16[16,2048]{1,0:T(8,128)(2,1)} %hidden_ref.1, f32[1,2048]{1,0:T(1,128)} %bitcast.38, s32[1,16]{1,0:T(1,128)} %bitcast.40), custom_call_target="tpu_custom_call" | custom-call | tf_op jit(solution)/shard_map/pallas_call | solution.py:313
  9.7 24.0 %all_to_all.14 = bf16[8,16,2176]{2,1,0:T(8,128)(2,1)S(1)} all-to-all(bf16[8,16,2176]{2,1,0:T(8,128)(2,1)} %shard_map.68), channel_id=1, replica_groups={{0,16,32,48,64,80,96,112},{2,18,34,50,66,82,98,114},{4,20,36,52,68,84,1..., dimensions={0} | all-to-all | bytes 1114112 | tf_op jit(solution)/shard_map/all_to_all | solution.py:319
  33.7 0.0 copy-start.1
  33.7 3.5 %collective-permute-start = (bf16[128,2176]{1,0:T(8,128)(2,1)S(1)}, bf16[128,2176]{1,0:T(8,128)(2,1)S(1)}, u32[]{:S(2)}, u32[]{:S(2)}) collective-permute-start(bf16[128,2176]{1,0:T(8,128)(2,1)S(1)} %bitcast.32), channel_id=1, source_target_pairs={{0,2},{1,17},{2,4},{3,19},{4,6},{5,21},{6,8},{7,23},{8,10},{9,25},... | collective-permute-start | bytes 1671176 | tf_op jit(solution)/shard_map/ppermute | solution.py:323
  37.1 0.0 copy-done.1
  37.1 3.8 %collective-permute-start.1 = (bf16[128,2176]{1,0:T(8,128)(2,1)S(1)}, bf16[128,2176]{1,0:T(8,128)(2,1)S(1)}, u32[]{:S(2)}, u32[]{:S(2)}) collective-permute-start(bf16[128,2176]{1,0:T(8,128)(2,1)S(1)} %bitcast.33), channel_id=1, source_target_pairs={{0,14},{1,113},{2,0},{3,115},{4,2},{5,117},{6,4},{7,119},{8,6},{9,... | collective-permute-start | bytes 1671176 | tf_op jit(solution)/shard_map/ppermute | solution.py:324
  41.0 5.6 %collective-permute-done.refs_1_ = bf16[128,2176]{1,0:T(8,128)(2,1)S(1)} collective-permute-done((bf16[128,2176]{1,0:T(8,128)(2,1)S(1)}, bf16[128,2176]{1,0:T(8,128)(2,1)S(1)}, u32[]{:S(2)}, u32[]{:S(2)}) %collective-permute-start) | collective-permute-done | bytes 557088 | tf_op jit(solution)/shard_map/ppermute | solution.py:323
  46.5 0.0 copy-start.2
  46.5 2.0 %collective-permute-start.2 = (bf16[128,2176]{1,0:T(8,128)(2,1)S(1)}, bf16[128,2176]{1,0:T(8,128)(2,1)S(1)}, u32[]{:S(2)}, u32[]{:S(2)}) collective-permute-start(bf16[128,2176]{1,0:T(8,128)(2,1)S(1)} %collective-permute-done.refs_1_), channel_id=1, source_target_pairs={{0,2},{1,17},{2,4},{3,19},{4,6},{5,21},{6,8},{7,23},{8,10},{9,25},... | collective-permute-start | bytes 1671176 | tf_op jit(solution)/shard_map/ppermute | solution.py:323
  48.6 0.0 collective-permute-done.1.refs_2_
  48.6 0.0 copy-done.2
  48.6 0.0 copy-start.3
  48.6 5.0 %collective-permute-start.3 = (bf16[128,2176]{1,0:T(8,128)(2,1)S(1)}, bf16[128,2176]{1,0:T(8,128)(2,1)S(1)}, u32[]{:S(2)}, u32[]{:S(2)}) collective-permute-start(bf16[128,2176]{1,0:T(8,128)(2,1)S(1)} %collective-permute-done.1.refs_2_), channel_id=1, source_target_pairs={{0,14},{1,113},{2,0},{3,115},{4,2},{5,117},{6,4},{7,119},{8,6},{9,... | collective-permute-start | bytes 1671176 | tf_op jit(solution)/shard_map/ppermute | solution.py:324
  53.6 5.5 %collective-permute-done.2.refs_3_ = bf16[128,2176]{1,0:T(8,128)(2,1)S(1)} collective-permute-done((bf16[128,2176]{1,0:T(8,128)(2,1)S(1)}, bf16[128,2176]{1,0:T(8,128)(2,1)S(1)}, u32[]{:S(2)}, u32[]{:S(2)}) %collective-permute-start.2) | collective-permute-done | bytes 557088 | tf_op jit(solution)/shard_map/ppermute | solution.py:323
  59.2 0.0 copy-done.3
  59.2 0.0 copy-start.4
  59.2 1.9 %collective-permute-start.4 = (bf16[128,2176]{1,0:T(8,128)(2,1)S(1)}, bf16[128,2176]{1,0:T(8,128)(2,1)S(1)}, u32[]{:S(2)}, u32[]{:S(2)}) collective-permute-start(bf16[128,2176]{1,0:T(8,128)(2,1)S(1)} %collective-permute-done.2.refs_3_), channel_id=1, source_target_pairs={{0,2},{1,17},{2,4},{3,19},{4,6},{5,21},{6,8},{7,23},{8,10},{9,25},... | collective-permute-start | bytes 1671176 | tf_op jit(solution)/shard_map/ppermute | solution.py:323
  61.1 0.0 collective-permute-done.3.refs_4_
  61.1 0.0 copy-done.4
  61.1 0.0 copy-start.5
  61.1 5.1 %collective-permute-start.5 = (bf16[128,2176]{1,0:T(8,128)(2,1)S(1)}, bf16[128,2176]{1,0:T(8,128)(2,1)}, u32[]{:S(2)}, u32[]{:S(2)}) collective-permute-start(bf16[128,2176]{1,0:T(8,128)(2,1)S(1)} %collective-permute-done.3.refs_4_), channel_id=1, source_target_pairs={{0,14},{1,113},{2,0},{3,115},{4,2},{5,117},{6,4},{7,119},{8,6},{9,... | collective-permute-start | bytes 1671176 | tf_op jit(solution)/shard_map/ppermute | solution.py:324
  66.2 5.5 %collective-permute-done.4.refs_5_ = bf16[128,2176]{1,0:T(8,128)(2,1)S(1)} collective-permute-done((bf16[128,2176]{1,0:T(8,128)(2,1)S(1)}, bf16[128,2176]{1,0:T(8,128)(2,1)S(1)}, u32[]{:S(2)}, u32[]{:S(2)}) %collective-permute-start.4) | collective-permute-done | bytes 557088 | tf_op jit(solution)/shard_map/ppermute | solution.py:323
  71.8 0.0 copy-done.5
  71.8 0.0 copy-start.6
  71.8 0.8 copy-done.6
  72.6 0.7 collective-permute-done.5.refs_6_
  73.3 0.0 all-gather.2.cloned.1.call-done
  73.3 1.9 %collective-permute-start.7 = (bf16[800,2048]{1,0:T(8,128)(2,1)}, bf16[800,2048]{1,0:T(8,128)(2,1)S(1)}, u32[]{:S(2)}, u32[]{:S(2)}) collective-permute-start(bf16[800,2048]{1,0:T(8,128)(2,1)} %bitcast.29), channel_id=1, source_target_pairs={{0,1},{1,0},{2,3},{3,2},{4,5},{5,4},{6,7},{7,6},{8,9},{9,8},{10,11... | collective-permute-start | bytes 9830408 | tf_op jit(solution)/shard_map/ppermute | solution.py:329
  75.2 3.3 %collective-permute-start.6 = (bf16[128,2176]{1,0:T(8,128)(2,1)}, bf16[128,2176]{1,0:T(8,128)(2,1)}, u32[]{:S(2)}, u32[]{:S(2)}) collective-permute-start(bf16[128,2176]{1,0:T(8,128)(2,1)} %copy-done.6), channel_id=1, source_target_pairs={{0,2},{1,17},{2,4},{3,19},{4,6},{5,21},{6,8},{7,23},{8,10},{9,25},... | collective-permute-start | bytes 1671176 | tf_op jit(solution)/shard_map/ppermute | solution.py:325
  78.5 8.3 %shard_map.69 = (f32[8,544]{1,0:T(8,128)}, bf16[34,16,2176]{2,1,0:T(8,128)(2,1)}) custom-call(s32[1,4]{1,0:T(1,128)} %len_ref.3, bf16[128,2176]{1,0:T(8,128)(2,1)} %bitcast.34, bf16[128,2176]{1,0:T(8,128)(2,1)} %copy-done.2, bf16[128,2176]{1,0:T(8,128)(2,1)} %copy-done.3, bf16[128,2176]{1,0:T(8,128)(2,1)} %copy-done.4, bf16[128,2176]{1,0:T(8,128)(2,1)} %copy-done.5, ...), custom_call_target="tpu_custom_call" | custom-call | flops 1782579200 | bytes 5505024 | tf_op jit(solution)/shard_map/pallas_call | solution.py:259
  86.8 1.9 %collective-permute-done.6.line_ref = bf16[128,2176]{1,0:T(8,128)(2,1)} collective-permute-done((bf16[128,2176]{1,0:T(8,128)(2,1)}, bf16[128,2176]{1,0:T(8,128)(2,1)}, u32[]{:S(2)}, u32[]{:S(2)}) %collective-permute-start.6) | collective-permute-done | bytes 557088 | tf_op jit(solution)/shard_map/ppermute | solution.py:325
  88.7 0.0 collective-permute-done.7.other_ref
  88.7 0.0 copy-start
  88.7 1.8 %copy-done = bf16[800,2048]{1,0:T(8,128)(2,1)} copy-done((bf16[800,2048]{1,0:T(8,128)(2,1)}, bf16[800,2048]{1,0:T(8,128)(2,1)S(1)}, u32[]{:S(2)}) %copy-start) | copy-done | bytes 3276824
  90.5 0.0 copy-start.7
  90.5 11.4 %shard_map.70 = f32[64,64]{1,0:T(8,128)} custom-call(s32[1,4]{1,0:T(1,128)} %len_ref.3, bf16[34,16,2176]{2,1,0:T(8,128)(2,1)} %get-tuple-element.6.packed_ref, bf16[128,2176]{1,0:T(8,128)(2,1)} %collective-permute-done.6.line_ref, bf16[800,2048]{1,0:T(8,128)(2,1)} %bitcast.31, bf16[800,2048]{1,0:T(8,128)(2,1)} %copy-done, f32[8,544]{1,0:T(8,128)} %get-tuple-element.7.early_ref), custom_call_target="tpu_custom_call" | custom-call | flops 1782579200 | bytes 5505024 | tf_op jit(solution)/shard_map/pallas_call | solution.py:273
  101.9 8.0 %all-to-all-start.1 = ((f32[64,1,64]{2,1,0:T(1,128)}), f32[64,1,64]{2,1,0:T(1,128)S(1)}, u32[]{:S(2)}, u32[]{:S(2)}) async-start(f32[64,1,64]{2,1,0:T(1,128)} %bitcast.37), calls=%async_computation.1 | async-start | bytes 65536 | tf_op jit(solution)/shard_map/all_to_all | solution.py:332
  109.8 0.0 copy-done.7
  109.8 0.1 select_reduce_fusion
  109.9 11.9 %all-to-all-done.1 = f32[64,1,64]{2,1,0:T(1,128)S(1)} async-done(((f32[64,1,64]{2,1,0:T(1,128)}), f32[64,1,64]{2,1,0:T(1,128)S(1)}, u32[]{:S(2)}, u32[]{:S(2)}) %all-to-all-start.1) | async-done | bytes 16416 | tf_op jit(solution)/shard_map/all_to_all | solution.py:332
  121.8 0.1 copy.13
  121.9 0.1 slice_reduce_fusion.1
  122.0 0.2 fusion.1
  122.2 0.5 subtract_select_fusion
  (1 shorter events, 0.0 us)
Async XLA Ops:
  7.2 66.1 %all-gather.2.cloned.1.call-start = ((), (), s32[]{:S(2)}) async-start(), calls=%async_computation.2 | async-start | bytes 4096000 | tf_op jit(solution)/shard_map/all_gather | solution.py:310
  33.7 3.5 %copy-start.1 = (bf16[8,16,2176]{2,1,0:T(8,128)(2,1)}, bf16[8,16,2176]{2,1,0:T(8,128)(2,1)S(1)}, u32[]{:S(2)}) copy-start(bf16[8,16,2176]{2,1,0:T(8,128)(2,1)S(1)} %all_to_all.14) | copy-start | bytes 1671172
  33.7 12.9 %collective-permute-start = (bf16[128,2176]{1,0:T(8,128)(2,1)S(1)}, bf16[128,2176]{1,0:T(8,128)(2,1)S(1)}, u32[]{:S(2)}, u32[]{:S(2)}) collective-permute-start(bf16[128,2176]{1,0:T(8,128)(2,1)S(1)} %bitcast.32), channel_id=1, source_target_pairs={{0,2},{1,17},{2,4},{3,19},{4,6},{5,21},{6,8},{7,23},{8,10},{9,25},... | collective-permute-start | bytes 1671176 | tf_op jit(solution)/shard_map/ppermute | solution.py:323
  37.1 11.4 %collective-permute-start.1 = (bf16[128,2176]{1,0:T(8,128)(2,1)S(1)}, bf16[128,2176]{1,0:T(8,128)(2,1)S(1)}, u32[]{:S(2)}, u32[]{:S(2)}) collective-permute-start(bf16[128,2176]{1,0:T(8,128)(2,1)S(1)} %bitcast.33), channel_id=1, source_target_pairs={{0,14},{1,113},{2,0},{3,115},{4,2},{5,117},{6,4},{7,119},{8,6},{9,... | collective-permute-start | bytes 1671176 | tf_op jit(solution)/shard_map/ppermute | solution.py:324
  46.5 2.0 %copy-start.2 = (bf16[128,2176]{1,0:T(8,128)(2,1)}, bf16[128,2176]{1,0:T(8,128)(2,1)S(1)}, u32[]{:S(2)}) copy-start(bf16[128,2176]{1,0:T(8,128)(2,1)S(1)} %collective-permute-done.refs_1_) | copy-start | bytes 1671172
  46.5 12.6 %collective-permute-start.2 = (bf16[128,2176]{1,0:T(8,128)(2,1)S(1)}, bf16[128,2176]{1,0:T(8,128)(2,1)S(1)}, u32[]{:S(2)}, u32[]{:S(2)}) collective-permute-start(bf16[128,2176]{1,0:T(8,128)(2,1)S(1)} %collective-permute-done.refs_1_), channel_id=1, source_target_pairs={{0,2},{1,17},{2,4},{3,19},{4,6},{5,21},{6,8},{7,23},{8,10},{9,25},... | collective-permute-start | bytes 1671176 | tf_op jit(solution)/shard_map/ppermute | solution.py:323
  48.6 10.6 %copy-start.3 = (bf16[128,2176]{1,0:T(8,128)(2,1)}, bf16[128,2176]{1,0:T(8,128)(2,1)S(1)}, u32[]{:S(2)}) copy-start(bf16[128,2176]{1,0:T(8,128)(2,1)S(1)} %collective-permute-done.1.refs_2_) | copy-start | bytes 1671172
  48.6 12.5 %collective-permute-start.3 = (bf16[128,2176]{1,0:T(8,128)(2,1)S(1)}, bf16[128,2176]{1,0:T(8,128)(2,1)S(1)}, u32[]{:S(2)}, u32[]{:S(2)}) collective-permute-start(bf16[128,2176]{1,0:T(8,128)(2,1)S(1)} %collective-permute-done.1.refs_2_), channel_id=1, source_target_pairs={{0,14},{1,113},{2,0},{3,115},{4,2},{5,117},{6,4},{7,119},{8,6},{9,... | collective-permute-start | bytes 1671176 | tf_op jit(solution)/shard_map/ppermute | solution.py:324
  59.2 1.9 %copy-start.4 = (bf16[128,2176]{1,0:T(8,128)(2,1)}, bf16[128,2176]{1,0:T(8,128)(2,1)S(1)}, u32[]{:S(2)}) copy-start(bf16[128,2176]{1,0:T(8,128)(2,1)S(1)} %collective-permute-done.2.refs_3_) | copy-start | bytes 1671172
  59.2 12.6 %collective-permute-start.4 = (bf16[128,2176]{1,0:T(8,128)(2,1)S(1)}, bf16[128,2176]{1,0:T(8,128)(2,1)S(1)}, u32[]{:S(2)}, u32[]{:S(2)}) collective-permute-start(bf16[128,2176]{1,0:T(8,128)(2,1)S(1)} %collective-permute-done.2.refs_3_), channel_id=1, source_target_pairs={{0,2},{1,17},{2,4},{3,19},{4,6},{5,21},{6,8},{7,23},{8,10},{9,25},... | collective-permute-start | bytes 1671176 | tf_op jit(solution)/shard_map/ppermute | solution.py:323
  61.1 10.7 %copy-start.5 = (bf16[128,2176]{1,0:T(8,128)(2,1)}, bf16[128,2176]{1,0:T(8,128)(2,1)S(1)}, u32[]{:S(2)}) copy-start(bf16[128,2176]{1,0:T(8,128)(2,1)S(1)} %collective-permute-done.3.refs_4_) | copy-start | bytes 1671172
  61.1 12.2 %collective-permute-start.5 = (bf16[128,2176]{1,0:T(8,128)(2,1)S(1)}, bf16[128,2176]{1,0:T(8,128)(2,1)}, u32[]{:S(2)}, u32[]{:S(2)}) collective-permute-start(bf16[128,2176]{1,0:T(8,128)(2,1)S(1)} %collective-permute-done.3.refs_4_), channel_id=1, source_target_pairs={{0,14},{1,113},{2,0},{3,115},{4,2},{5,117},{6,4},{7,119},{8,6},{9,... | collective-permute-start | bytes 1671176 | tf_op jit(solution)/shard_map/ppermute | solution.py:324
  71.8 0.8 copy-start.6
  73.3 15.4 %collective-permute-start.7 = (bf16[800,2048]{1,0:T(8,128)(2,1)}, bf16[800,2048]{1,0:T(8,128)(2,1)S(1)}, u32[]{:S(2)}, u32[]{:S(2)}) collective-permute-start(bf16[800,2048]{1,0:T(8,128)(2,1)} %bitcast.29), channel_id=1, source_target_pairs={{0,1},{1,0},{2,3},{3,2},{4,5},{5,4},{6,7},{7,6},{8,9},{9,8},{10,11... | collective-permute-start | bytes 9830408 | tf_op jit(solution)/shard_map/ppermute | solution.py:329
  75.2 13.5 %collective-permute-start.6 = (bf16[128,2176]{1,0:T(8,128)(2,1)}, bf16[128,2176]{1,0:T(8,128)(2,1)}, u32[]{:S(2)}, u32[]{:S(2)}) collective-permute-start(bf16[128,2176]{1,0:T(8,128)(2,1)} %copy-done.6), channel_id=1, source_target_pairs={{0,2},{1,17},{2,4},{3,19},{4,6},{5,21},{6,8},{7,23},{8,10},{9,25},... | collective-permute-start | bytes 1671176 | tf_op jit(solution)/shard_map/ppermute | solution.py:325
  88.7 1.8 %copy-start = (bf16[800,2048]{1,0:T(8,128)(2,1)}, bf16[800,2048]{1,0:T(8,128)(2,1)S(1)}, u32[]{:S(2)}) copy-start(bf16[800,2048]{1,0:T(8,128)(2,1)S(1)} %collective-permute-done.7.other_ref) | copy-start | bytes 9830404
  90.5 19.3 %copy-start.7 = (s32[1,4]{1,0:T(1,128)S(1)}, s32[1,4]{1,0:T(1,128)}, u32[]{:S(2)}) copy-start(s32[1,4]{1,0:T(1,128)} %len_ref.3) | copy-start | bytes 52
  101.9 20.0 %all-to-all-start.1 = ((f32[64,1,64]{2,1,0:T(1,128)}), f32[64,1,64]{2,1,0:T(1,128)S(1)}, u32[]{:S(2)}, u32[]{:S(2)}) async-start(f32[64,1,64]{2,1,0:T(1,128)} %bitcast.37), calls=%async_computation.1 | async-start | bytes 65536 | tf_op jit(solution)/shard_map/all_to_all | solution.py:332
Sparse Core Ops, SparseCore 0:
  10.1 48.6 all-gather.1

commit v10 on v9

--- a/solution.py
+++ b/solution.py
@@ -135,29 +135,30 @@
     n = owner.shape[1]
     chips = N_LINE * N_LINE
     here = owner == lax.broadcasted_iota(jnp.int32, (chips, n), 0)
+    here = jnp.where(here, 1.0, 0.0).astype(jnp.bfloat16)
+    spot = lax.broadcasted_iota(jnp.int32, (BLOCK, n), 1) & (BLOCK - 1)
+    spot = spot == lax.broadcasted_iota(jnp.int32, (BLOCK, n), 0)
     rows = []
-    for stat in stats:
-        for _ in range(3):
+    for _ in range(3):
+        for k, stat in enumerate(stats):
             part = stat.astype(jnp.bfloat16).astype(jnp.float32)
-            rows.append(jnp.where(here, part, 0.0).astype(jnp.bfloat16))
-            stat = stat - part
-    place = lax.broadcasted_iota(jnp.int32, (n, BLOCK), 0) % BLOCK
-    spot = jnp.where(place == lax.broadcasted_iota(jnp.int32, (n, BLOCK), 1), 1.0, 0.0)
-    moved = jnp.dot(
+            rows.append(jnp.where(spot, part, 0.0).astype(jnp.bfloat16))
+            stats = stats[:k] + (stat - part,) + stats[k + 1 :]
+    moved = lax.dot_general(
         jnp.concatenate(rows, axis=0),
-        spot.astype(jnp.bfloat16),
+        here,
+        (((1,), (1,)), ((), ())),
         preferred_element_type=jnp.float32,
-    ).reshape(STATS, 3, chips, BLOCK)
-    moved = moved[:, 0] + moved[:, 1] + moved[:, 2]
-    return [moved[k] for k in range(STATS)]
+    )
+    n = STATS * BLOCK
+    return jnp.transpose(moved[:n] + moved[n : 2 * n] + moved[2 * n :])
 
 
 def early_kernel(len_ref, *refs):
-    n_in = N_LINE - 1
-    line_refs, (own_ref, out_ref, x_ref, w_ref, sem) = refs[:n_in], refs[n_in:]
+    line_refs, (own_ref, out_ref, x_ref, w_ref, sem) = refs[:N_LINE], refs[N_LINE:]
     vocab_dev, width = own_ref.shape
     t, _, _ = my_core()
-    each = block_copies(len_ref, OFFSETS[:-1], line_refs, x_ref, sem)
+    each = block_copies(len_ref, OFFSETS, line_refs, x_ref, sem)
     tiles = weight_copies(own_ref, w_ref, 0, sem, N_LINE * N_LINE)
     each(lambda copy: copy.start())
     tiles[0].start()
@@ -176,71 +177,36 @@
         out_ref[k : k + 1, :] = stat
 
 
-def late_kernel(
-    len_ref, packed_ref, line_ref, own_ref, other_ref, early_ref, out_ref,
-    x_ref, last_ref, w_ref, sem,
-):
-    vocab_dev, width = own_ref.shape
-    t, core, mine = my_core()
+def late_kernel(len_ref, packed_ref, other_ref, early_ref, out_ref, x_ref, w_ref, sem):
+    vocab_dev, width = other_ref.shape
+    t, core, _ = my_core()
     starts, total_blocks = block_starts(len_ref, core)
-    line = lax.rem(mine + OFFSETS[-1] + N_LINE, N_LINE)
-    other = weight_copies(other_ref, w_ref, 0, sem, N_LINE)
-    own = weight_copies(own_ref, w_ref, len(other), sem, N_LINE)
-    spare = N_LINE + 2 * len(other)
-    last = pltpu.make_async_copy(line_ref, last_ref, sem.at[spare])
+    tiles = weight_copies(other_ref, w_ref, 0, sem, 0)
     half = LIVE // 2
     packed = [
         pltpu.make_async_copy(
             packed_ref.at[k * half : (k + 1) * half],
             x_ref.at[k * half : (k + 1) * half],
-            sem.at[spare + 1 + k],
+            sem.at[len(tiles) + k],
         )
         for k in range(2)
     ]
-    for copy in packed + [other[0], last]:
+    for copy in packed + tiles:
         copy.start()
+    n = LIVE * BLOCK
+    lane = lax.broadcasted_iota(jnp.int32, (1, n), 1) // BLOCK
+    owner = jnp.where(lane < total_blocks, owner_of(lane, starts), -1)
     for copy in packed:
         copy.wait()
-    each = block_copies(len_ref, OFFSETS[-1:], [line_ref], x_ref, sem)
-    each(lambda copy: copy.start())
-    each(lambda copy: copy.wait())
-    for copy in other[1:] + own:
-        copy.start()
-
-    n = LIVE * BLOCK
     x = x_ref[:, :, :width].reshape(n, width)
     ids = token_row(x_ref[:, :, width:].reshape(n, LANES)) - (t + 1 - 2 * core) * vocab_dev
-    lane = lax.broadcasted_iota(jnp.int32, (1, n), 1) // BLOCK
-    owner = jnp.where(lane < total_blocks, owner_of(lane, starts), -1)
-
-    def line_of(o):
-        return jnp.where(core == 0, o % N_LINE, o // N_LINE)
-
-    missing = line_of(owner) == line
-    parts = [
-        tuple(
-            jnp.where(missing, rest, early_ref[k : k + 1, :])
-            for k, rest in enumerate((-1e30, 0.0, 0.0, 0.0))
-        )
-    ]
-    for i, copy in enumerate(other):
+    parts = [tuple(early_ref[k : k + 1, :] for k in range(STATS))]
+    for i, copy in enumerate(tiles):
         copy.wait()
         parts.append(tile_stats(w_ref[i], x, ids - i * TILE))
-    most = to_owners(merge(parts), owner)
-
-    last.wait()
-    x = last_ref[:, :width]
-    ids = token_row(last_ref[:, width:]) - t * vocab_dev
-    parts = []
-    for i, copy in enumerate(own):
-        copy.wait()
-        parts.append(tile_stats(w_ref[len(other) + i], x, ids - i * TILE))
-    m = lax.broadcasted_iota(jnp.int32, (1, N_LINE * BLOCK), 1) // BLOCK
-    rest = to_owners(merge(parts), jnp.where(core == 0, m * N_LINE + line, line * N_LINE + m))
-    chips = N_LINE * N_LINE
-    added = line_of(lax.broadcasted_iota(jnp.int32, (chips, BLOCK), 0)) == line
-    rest[0] = jnp.where(added, rest[0], -1e30)
-    out_ref[...] = jnp.concatenate(merge([most, rest]), axis=1)
+    used = owner >= 0
+    stats = tuple(jnp.where(used, stat, 0.0) for stat in merge(parts))
+    out_ref[...] = to_owners(stats, owner)
 
 
 def run_heads(lengths, lines, weight, other):
@@ -258,7 +224,7 @@
     )
     early, packed = pl.pallas_call(
         early_kernel,
-        in_specs=[smem] + [anywhere] * N_LINE,
+        in_specs=[smem] + [anywhere] * (N_LINE + 1),
         out_specs=(vmem, vmem),
         out_shape=(
             jax.ShapeDtypeStruct((8, n), jnp.float32),
@@ -269,20 +235,19 @@
             pltpu.SemaphoreType.DMA((N_LINE * N_LINE + tiles,)),
         ],
         cost_estimate=cost,
-    )(lengths, *lines[:-1], weight)
+    )(lengths, *lines, weight)
     return pl.pallas_call(
         late_kernel,
-        in_specs=[smem] + [anywhere] * 4 + [vmem],
+        in_specs=[smem] + [anywhere] * 2 + [vmem],
         out_specs=vmem,
         out_shape=jax.ShapeDtypeStruct((N_LINE * N_LINE, STATS * BLOCK), jnp.float32),
         scratch_shapes=[
             pltpu.VMEM((LIVE, BLOCK, deep), jnp.bfloat16),
-            pltpu.VMEM((N_LINE * BLOCK, deep), jnp.bfloat16),
-            pltpu.VMEM((2 * tiles, TILE, width), jnp.bfloat16),
-            pltpu.SemaphoreType.DMA((N_LINE + 2 * tiles + 3,)),
+            pltpu.VMEM((tiles, TILE, width), jnp.bfloat16),
+            pltpu.SemaphoreType.DMA((tiles + 2,)),
         ],
         cost_estimate=cost,
-    )(lengths, packed, lines[-1], weight, other, early)
+    )(lengths, packed, other, early)
 
 
 def per_device(hidden, norm_gain, head_weight, token_ids, lengths):
@@ -319,11 +284,17 @@
     line = lax.all_to_all(block, "tensor", 0, 0, axis_index_groups=along_z + along_y)
     own = line.reshape(N_LINE * row_dev, width + LANES)
     up, down = [own], [own]
-    for _ in range(N_LINE // 2 - 1):
-        up.append(lax.ppermute(up[-1], "tensor", along(1)))
-        down.append(lax.ppermute(down[-1], "tensor", along(-1)))
-    up.append(lax.ppermute(up[-1], "tensor", along(1)))
-    lines = [own, up[1], down[1], up[2], down[2], up[3], down[3], up[4]]
+    far = lax.ppermute(own, "tensor", along(N_LINE // 2))
+    for k in range(N_LINE // 2 - 1):
+        pair = (
+            lax.ppermute(up[-1], "tensor", along(1)),
+            lax.ppermute(down[-1], "tensor", along(-1)),
+        )
+        if k == 1:
+            *pair, far = lax.optimization_barrier((*pair, far))
+        up.append(pair[0])
+        down.append(pair[1])
+    lines = [own, up[1], down[1], up[2], down[2], up[3], down[3], far]
 
     weight, _, _ = lax.optimization_barrier((weight, up[3], down[3]))
     other = lax.ppermute(weight, "tensor", other_core)

time: 130 us -> 135 us (1.038)
  waiting for transfers between devices: 31.8 us -> 37.6 us
  starting transfers between devices: 34.6 us -> 38.5 us
  Pallas kernels: 21.5 us -> 18.2 us
  local copies, waits for them, and re-layouts: 2.67 us -> 0.91 us
    ppermute x7, waiting for transfers between devices: 19.2 us -> 25.1 us  [the longest x3 10.1 us: per_device(): lax.ppermute(up[-1], 'tensor', along(1))]
    ppermute x7, starting transfers between devices: 24.7 us -> 28.9 us  [the longest x3 11.6 us: per_device(): lax.ppermute(down[-1], 'tensor', along(-1))]
    pallas_call x2, Pallas kernels: 19.7 us -> 16.4 us  [the longest x1 8.38 us: run_heads(): pl.pallas_call(early_kernel, in_specs=[smem] + [anywhere] * (N_LINE + 1),...]
    unnamed x16, local copies, waits for them, and re-layouts: 2.6 us -> 0.83 us
where the time goes in v10:
time: 135 us; the launch traced here: 134 us
  starting transfers between devices  38.5 us (29%)
  waiting for transfers between devices  37.6 us (28%)
  blocking collectives  24 us (18%)
  Pallas kernels  18.2 us (13%)
  between operations  14.2 us (11%)
    all_to_all x1, blocking collectives, per_device(): lax.all_to_all(block, 'tensor', 0, 0, axis_index_groups=along_z + along_y)  24 us
    all_to_all x1, waiting for transfers between devices, per_device(): lax.all_to_all(stats, 'tensor', 0, 0, axis_index_groups=same_core, tiled=...  11.9 us
    ppermute x3, starting transfers between devices, per_device(): lax.ppermute(down[-1], 'tensor', along(-1))  11.6 us
    ppermute x3, waiting for transfers between devices, per_device(): lax.ppermute(up[-1], 'tensor', along(1))  10.1 us
    ppermute x3, starting transfers between devices, per_device(): lax.ppermute(up[-1], 'tensor', along(1))  9.78 us
    pallas_call x1, Pallas kernels, run_heads(): pl.pallas_call(early_kernel, in_specs=[smem] + [anywhere] * (N_LINE + 1),...  8.38 us
    pallas_call x1, Pallas kernels, run_heads(): pl.pallas_call(late_kernel, in_specs=[smem] + [anywhere] * 2 + [vmem], ou...  8.02 us
    ppermute x3, waiting for transfers between devices, per_device(): lax.ppermute(down[-1], 'tensor', along(-1))  7.98 us
  transfers between devices with their start and end apart: 10, of which 6 were waited for; matrix products, arithmetic and copies ran while one was open for 0% of the time, Pallas kernels for 8%

profile of v10, /device:TPU:6, one launch (start us, length us, event | category | flops | bytes accessed | tf_op | source)
XLA Modules:
  0.0 134.3 jit_solution(10368854807881499521)
XLA Ops:
  7.2 0.0 all-gather.2.cloned.1.call-start
  7.2 0.7 all-gather.2.cloned.1.call-update
  7.9 1.8 %shard_map.68 = bf16[8,16,2176]{2,1,0:T(8,128)(2,1)} custom-call(bf16[16,2048]{1,0:T(8,128)(2,1)} %hidden_ref.1, f32[1,2048]{1,0:T(1,128)} %bitcast.38, s32[1,16]{1,0:T(1,128)} %bitcast.40), custom_call_target="tpu_custom_call" | custom-call | tf_op jit(solution)/shard_map/pallas_call | solution.py:278
  9.7 24.0 %all_to_all.14 = bf16[8,16,2176]{2,1,0:T(8,128)(2,1)S(1)} all-to-all(bf16[8,16,2176]{2,1,0:T(8,128)(2,1)} %shard_map.68), channel_id=1, replica_groups={{0,16,32,48,64,80,96,112},{2,18,34,50,66,82,98,114},{4,20,36,52,68,84,1..., dimensions={0} | all-to-all | bytes 1114112 | tf_op jit(solution)/shard_map/all_to_all | solution.py:284
  33.7 0.0 copy-start
  33.7 3.5 %collective-permute-start = (bf16[128,2176]{1,0:T(8,128)(2,1)S(1)}, bf16[128,2176]{1,0:T(8,128)(2,1)S(1)}, u32[]{:S(2)}, u32[]{:S(2)}) collective-permute-start(bf16[128,2176]{1,0:T(8,128)(2,1)S(1)} %bitcast.31), channel_id=1, source_target_pairs={{0,2},{1,17},{2,4},{3,19},{4,6},{5,21},{6,8},{7,23},{8,10},{9,25},... | collective-permute-start | bytes 1671176 | tf_op jit(solution)/shard_map/ppermute | solution.py:290
  37.1 3.8 %collective-permute-start.1 = (bf16[128,2176]{1,0:T(8,128)(2,1)S(1)}, bf16[128,2176]{1,0:T(8,128)(2,1)S(1)}, u32[]{:S(2)}, u32[]{:S(2)}) collective-permute-start(bf16[128,2176]{1,0:T(8,128)(2,1)S(1)} %bitcast.32), channel_id=1, source_target_pairs={{0,14},{1,113},{2,0},{3,115},{4,2},{5,117},{6,4},{7,119},{8,6},{9,... | collective-permute-start | bytes 1671176 | tf_op jit(solution)/shard_map/ppermute | solution.py:291
  41.0 7.5 %collective-permute-start.4 = (bf16[128,2176]{1,0:T(8,128)(2,1)S(1)}, bf16[128,2176]{1,0:T(8,128)(2,1)S(1)}, u32[]{:S(2)}, u32[]{:S(2)}) collective-permute-start(bf16[128,2176]{1,0:T(8,128)(2,1)S(1)} %bitcast.33), channel_id=1, source_target_pairs={{0,8},{1,65},{2,10},{3,67},{4,12},{5,69},{6,14},{7,71},{8,0},{9,73... | collective-permute-start | bytes 1671176 | tf_op jit(solution)/shard_map/ppermute | solution.py:287
  48.5 0.0 collective-permute-done.refs_1_
  48.5 0.0 copy-start.1
  48.5 1.9 %collective-permute-start.2 = (bf16[128,2176]{1,0:T(8,128)(2,1)S(1)}, bf16[128,2176]{1,0:T(8,128)(2,1)S(1)}, u32[]{:S(2)}, u32[]{:S(2)}) collective-permute-start(bf16[128,2176]{1,0:T(8,128)(2,1)S(1)} %collective-permute-done.refs_1_), channel_id=1, source_target_pairs={{0,2},{1,17},{2,4},{3,19},{4,6},{5,21},{6,8},{7,23},{8,10},{9,25},... | collective-permute-start | bytes 1671176 | tf_op jit(solution)/shard_map/ppermute | solution.py:290
  50.4 0.0 collective-permute-done.1.refs_2_
  50.4 0.0 copy-start.2
  50.4 5.1 %collective-permute-start.3 = (bf16[128,2176]{1,0:T(8,128)(2,1)S(1)}, bf16[128,2176]{1,0:T(8,128)(2,1)S(1)}, u32[]{:S(2)}, u32[]{:S(2)}) collective-permute-start(bf16[128,2176]{1,0:T(8,128)(2,1)S(1)} %collective-permute-done.1.refs_2_), channel_id=1, source_target_pairs={{0,14},{1,113},{2,0},{3,115},{4,2},{5,117},{6,4},{7,119},{8,6},{9,... | collective-permute-start | bytes 1671176 | tf_op jit(solution)/shard_map/ppermute | solution.py:291
  55.6 7.0 %collective-permute-done.4.refs_7_ = bf16[128,2176]{1,0:T(8,128)(2,1)S(1)} collective-permute-done((bf16[128,2176]{1,0:T(8,128)(2,1)S(1)}, bf16[128,2176]{1,0:T(8,128)(2,1)S(1)}, u32[]{:S(2)}, u32[]{:S(2)}) %collective-permute-start.4) | collective-permute-done | bytes 557088 | tf_op jit(solution)/shard_map/ppermute | solution.py:287
  62.5 0.0 copy-start.3
  62.5 4.5 %collective-permute-done.2.refs_3_ = bf16[128,2176]{1,0:T(8,128)(2,1)S(1)} collective-permute-done((bf16[128,2176]{1,0:T(8,128)(2,1)S(1)}, bf16[128,2176]{1,0:T(8,128)(2,1)S(1)}, u32[]{:S(2)}, u32[]{:S(2)}) %collective-permute-start.2) | collective-permute-done | bytes 557088 | tf_op jit(solution)/shard_map/ppermute | solution.py:290
  67.1 0.0 copy-start.4
  67.1 0.3 collective-permute-done.3.refs_4_
  67.4 0.0 copy-start.5
  67.4 4.4 %collective-permute-start.5 = (bf16[128,2176]{1,0:T(8,128)(2,1)S(1)}, bf16[128,2176]{1,0:T(8,128)(2,1)S(1)}, u32[]{:S(2)}, u32[]{:S(2)}) collective-permute-start(bf16[128,2176]{1,0:T(8,128)(2,1)S(1)} %collective-permute-done.2.refs_3_), channel_id=1, source_target_pairs={{0,2},{1,17},{2,4},{3,19},{4,6},{5,21},{6,8},{7,23},{8,10},{9,25},... | collective-permute-start | bytes 1671176 | tf_op jit(solution)/shard_map/ppermute | solution.py:290
  71.8 2.7 %collective-permute-start.6 = (bf16[128,2176]{1,0:T(8,128)(2,1)S(1)}, bf16[128,2176]{1,0:T(8,128)(2,1)}, u32[]{:S(2)}, u32[]{:S(2)}) collective-permute-start(bf16[128,2176]{1,0:T(8,128)(2,1)S(1)} %collective-permute-done.3.refs_4_), channel_id=1, source_target_pairs={{0,14},{1,113},{2,0},{3,115},{4,2},{5,117},{6,4},{7,119},{8,6},{9,... | collective-permute-start | bytes 1671176 | tf_op jit(solution)/shard_map/ppermute | solution.py:291
  74.4 5.6 %collective-permute-done.5.refs_5_ = bf16[128,2176]{1,0:T(8,128)(2,1)S(1)} collective-permute-done((bf16[128,2176]{1,0:T(8,128)(2,1)S(1)}, bf16[128,2176]{1,0:T(8,128)(2,1)S(1)}, u32[]{:S(2)}, u32[]{:S(2)}) %collective-permute-start.5) | collective-permute-done | bytes 557088 | tf_op jit(solution)/shard_map/ppermute | solution.py:290
  80.0 0.0 copy-start.6
  80.0 0.8 copy-done.6
  80.8 7.7 %collective-permute-done.6.refs_6_ = bf16[128,2176]{1,0:T(8,128)(2,1)} collective-permute-done((bf16[128,2176]{1,0:T(8,128)(2,1)S(1)}, bf16[128,2176]{1,0:T(8,128)(2,1)}, u32[]{:S(2)}, u32[]{:S(2)}) %collective-permute-start.6) | collective-permute-done | bytes 557088 | tf_op jit(solution)/shard_map/ppermute | solution.py:291
  88.5 0.0 all-gather.2.cloned.1.call-done
  88.5 1.9 %collective-permute-start.7 = (bf16[800,2048]{1,0:T(8,128)(2,1)}, bf16[800,2048]{1,0:T(8,128)(2,1)}, u32[]{:S(2)}, u32[]{:S(2)}) collective-permute-start(bf16[800,2048]{1,0:T(8,128)(2,1)} %bitcast.29), channel_id=1, source_target_pairs={{0,1},{1,0},{2,3},{3,2},{4,5},{5,4},{6,7},{7,6},{8,9},{9,8},{10,11... | collective-permute-start | bytes 9830408 | tf_op jit(solution)/shard_map/ppermute | solution.py:300
  90.4 0.0 copy-done
  90.4 0.0 copy-done.1
  90.4 0.0 copy-done.2
  90.5 0.0 copy-done.3
  90.5 0.0 copy-done.4
  90.5 0.0 copy-done.5
  90.5 8.4 %shard_map.69 = (f32[8,544]{1,0:T(8,128)}, bf16[34,16,2176]{2,1,0:T(8,128)(2,1)}) custom-call(s32[1,4]{1,0:T(1,128)} %len_ref.3, bf16[128,2176]{1,0:T(8,128)(2,1)} %bitcast.34, bf16[128,2176]{1,0:T(8,128)(2,1)} %copy-done.1, bf16[128,2176]{1,0:T(8,128)(2,1)} %copy-done.2, bf16[128,2176]{1,0:T(8,128)(2,1)} %copy-done.4, bf16[128,2176]{1,0:T(8,128)(2,1)} %copy-done.5, ...), custom_call_target="tpu_custom_call" | custom-call | flops 1782579200 | bytes 5505024 | tf_op jit(solution)/shard_map/pallas_call | solution.py:225
  98.9 0.0 collective-permute-done.7.other_ref
  98.9 0.0 copy-start.7
  98.9 8.0 %shard_map.70 = f32[64,64]{1,0:T(8,128)} custom-call(s32[1,4]{1,0:T(1,128)} %len_ref.3, bf16[34,16,2176]{2,1,0:T(8,128)(2,1)} %get-tuple-element.12.packed_ref, bf16[800,2048]{1,0:T(8,128)(2,1)} %collective-permute-done.7.other_ref, f32[8,544]{1,0:T(8,128)} %get-tuple-element.13.early_ref), custom_call_target="tpu_custom_call" | custom-call | flops 1782579200 | bytes 5505024 | tf_op jit(solution)/shard_map/pallas_call | solution.py:239
  106.9 7.6 %all-to-all-start.1 = ((f32[64,1,64]{2,1,0:T(1,128)}), f32[64,1,64]{2,1,0:T(1,128)S(1)}, u32[]{:S(2)}, u32[]{:S(2)}) async-start(f32[64,1,64]{2,1,0:T(1,128)} %bitcast.37), calls=%async_computation.1 | async-start | bytes 65536 | tf_op jit(solution)/shard_map/all_to_all | solution.py:303
  114.6 0.0 copy-done.7
  114.6 0.1 select_reduce_fusion
  114.7 11.9 %all-to-all-done.1 = f32[64,1,64]{2,1,0:T(1,128)S(1)} async-done(((f32[64,1,64]{2,1,0:T(1,128)}), f32[64,1,64]{2,1,0:T(1,128)S(1)}, u32[]{:S(2)}, u32[]{:S(2)}) %all-to-all-start.1) | async-done | bytes 16416 | tf_op jit(solution)/shard_map/all_to_all | solution.py:303
  126.5 0.1 copy.13
  126.6 0.1 slice_reduce_fusion.1
  126.7 0.2 fusion.1
  126.9 0.5 subtract_select_fusion
  (1 shorter events, 0.0 us)
Async XLA Ops:
  7.2 81.3 %all-gather.2.cloned.1.call-start = ((), (), s32[]{:S(2)}) async-start(), calls=%async_computation.2 | async-start | bytes 4096000 | tf_op jit(solution)/shard_map/all_gather | solution.py:275
  33.7 56.8 %copy-start = (bf16[8,16,2176]{2,1,0:T(8,128)(2,1)}, bf16[8,16,2176]{2,1,0:T(8,128)(2,1)S(1)}, u32[]{:S(2)}) copy-start(bf16[8,16,2176]{2,1,0:T(8,128)(2,1)S(1)} %all_to_all.14) | copy-start | bytes 1671172
  33.7 14.8 %collective-permute-start = (bf16[128,2176]{1,0:T(8,128)(2,1)S(1)}, bf16[128,2176]{1,0:T(8,128)(2,1)S(1)}, u32[]{:S(2)}, u32[]{:S(2)}) collective-permute-start(bf16[128,2176]{1,0:T(8,128)(2,1)S(1)} %bitcast.31), channel_id=1, source_target_pairs={{0,2},{1,17},{2,4},{3,19},{4,6},{5,21},{6,8},{7,23},{8,10},{9,25},... | collective-permute-start | bytes 1671176 | tf_op jit(solution)/shard_map/ppermute | solution.py:290
  37.1 13.3 %collective-permute-start.1 = (bf16[128,2176]{1,0:T(8,128)(2,1)S(1)}, bf16[128,2176]{1,0:T(8,128)(2,1)S(1)}, u32[]{:S(2)}, u32[]{:S(2)}) collective-permute-start(bf16[128,2176]{1,0:T(8,128)(2,1)S(1)} %bitcast.32), channel_id=1, source_target_pairs={{0,14},{1,113},{2,0},{3,115},{4,2},{5,117},{6,4},{7,119},{8,6},{9,... | collective-permute-start | bytes 1671176 | tf_op jit(solution)/shard_map/ppermute | solution.py:291
  41.0 21.6 %collective-permute-start.4 = (bf16[128,2176]{1,0:T(8,128)(2,1)S(1)}, bf16[128,2176]{1,0:T(8,128)(2,1)S(1)}, u32[]{:S(2)}, u32[]{:S(2)}) collective-permute-start(bf16[128,2176]{1,0:T(8,128)(2,1)S(1)} %bitcast.33), channel_id=1, source_target_pairs={{0,8},{1,65},{2,10},{3,67},{4,12},{5,69},{6,14},{7,71},{8,0},{9,73... | collective-permute-start | bytes 1671176 | tf_op jit(solution)/shard_map/ppermute | solution.py:287
  48.5 42.0 %copy-start.1 = (bf16[128,2176]{1,0:T(8,128)(2,1)}, bf16[128,2176]{1,0:T(8,128)(2,1)S(1)}, u32[]{:S(2)}) copy-start(bf16[128,2176]{1,0:T(8,128)(2,1)S(1)} %collective-permute-done.refs_1_) | copy-start | bytes 1671172
  48.5 18.6 %collective-permute-start.2 = (bf16[128,2176]{1,0:T(8,128)(2,1)S(1)}, bf16[128,2176]{1,0:T(8,128)(2,1)S(1)}, u32[]{:S(2)}, u32[]{:S(2)}) collective-permute-start(bf16[128,2176]{1,0:T(8,128)(2,1)S(1)} %collective-permute-done.refs_1_), channel_id=1, source_target_pairs={{0,2},{1,17},{2,4},{3,19},{4,6},{5,21},{6,8},{7,23},{8,10},{9,25},... | collective-permute-start | bytes 1671176 | tf_op jit(solution)/shard_map/ppermute | solution.py:290
  50.4 40.0 %copy-start.2 = (bf16[128,2176]{1,0:T(8,128)(2,1)}, bf16[128,2176]{1,0:T(8,128)(2,1)S(1)}, u32[]{:S(2)}) copy-start(bf16[128,2176]{1,0:T(8,128)(2,1)S(1)} %collective-permute-done.1.refs_2_) | copy-start | bytes 1671172
  50.4 17.0 %collective-permute-start.3 = (bf16[128,2176]{1,0:T(8,128)(2,1)S(1)}, bf16[128,2176]{1,0:T(8,128)(2,1)S(1)}, u32[]{:S(2)}, u32[]{:S(2)}) collective-permute-start(bf16[128,2176]{1,0:T(8,128)(2,1)S(1)} %collective-permute-done.1.refs_2_), channel_id=1, source_target_pairs={{0,14},{1,113},{2,0},{3,115},{4,2},{5,117},{6,4},{7,119},{8,6},{9,... | collective-permute-start | bytes 1671176 | tf_op jit(solution)/shard_map/ppermute | solution.py:291
  62.5 27.9 %copy-start.3 = (bf16[128,2176]{1,0:T(8,128)(2,1)}, bf16[128,2176]{1,0:T(8,128)(2,1)S(1)}, u32[]{:S(2)}) copy-start(bf16[128,2176]{1,0:T(8,128)(2,1)S(1)} %collective-permute-done.4.refs_7_) | copy-start | bytes 1671172
  67.1 23.4 %copy-start.4 = (bf16[128,2176]{1,0:T(8,128)(2,1)}, bf16[128,2176]{1,0:T(8,128)(2,1)S(1)}, u32[]{:S(2)}) copy-start(bf16[128,2176]{1,0:T(8,128)(2,1)S(1)} %collective-permute-done.2.refs_3_) | copy-start | bytes 1671172
  67.4 23.1 %copy-start.5 = (bf16[128,2176]{1,0:T(8,128)(2,1)}, bf16[128,2176]{1,0:T(8,128)(2,1)S(1)}, u32[]{:S(2)}) copy-start(bf16[128,2176]{1,0:T(8,128)(2,1)S(1)} %collective-permute-done.3.refs_4_) | copy-start | bytes 1671172
  67.4 12.6 %collective-permute-start.5 = (bf16[128,2176]{1,0:T(8,128)(2,1)S(1)}, bf16[128,2176]{1,0:T(8,128)(2,1)S(1)}, u32[]{:S(2)}, u32[]{:S(2)}) collective-permute-start(bf16[128,2176]{1,0:T(8,128)(2,1)S(1)} %collective-permute-done.2.refs_3_), channel_id=1, source_target_pairs={{0,2},{1,17},{2,4},{3,19},{4,6},{5,21},{6,8},{7,23},{8,10},{9,25},... | collective-permute-start | bytes 1671176 | tf_op jit(solution)/shard_map/ppermute | solution.py:290
  71.8 16.7 %collective-permute-start.6 = (bf16[128,2176]{1,0:T(8,128)(2,1)S(1)}, bf16[128,2176]{1,0:T(8,128)(2,1)}, u32[]{:S(2)}, u32[]{:S(2)}) collective-permute-start(bf16[128,2176]{1,0:T(8,128)(2,1)S(1)} %collective-permute-done.3.refs_4_), channel_id=1, source_target_pairs={{0,14},{1,113},{2,0},{3,115},{4,2},{5,117},{6,4},{7,119},{8,6},{9,... | collective-permute-start | bytes 1671176 | tf_op jit(solution)/shard_map/ppermute | solution.py:291
  80.0 0.8 copy-start.6
  88.5 10.4 %collective-permute-start.7 = (bf16[800,2048]{1,0:T(8,128)(2,1)}, bf16[800,2048]{1,0:T(8,128)(2,1)}, u32[]{:S(2)}, u32[]{:S(2)}) collective-permute-start(bf16[800,2048]{1,0:T(8,128)(2,1)} %bitcast.29), channel_id=1, source_target_pairs={{0,1},{1,0},{2,3},{3,2},{4,5},{5,4},{6,7},{7,6},{8,9},{9,8},{10,11... | collective-permute-start | bytes 9830408 | tf_op jit(solution)/shard_map/ppermute | solution.py:300
  98.9 15.7 %copy-start.7 = (s32[1,4]{1,0:T(1,128)S(1)}, s32[1,4]{1,0:T(1,128)}, u32[]{:S(2)}) copy-start(s32[1,4]{1,0:T(1,128)} %len_ref.3) | copy-start | bytes 52
  106.9 19.6 %all-to-all-start.1 = ((f32[64,1,64]{2,1,0:T(1,128)}), f32[64,1,64]{2,1,0:T(1,128)S(1)}, u32[]{:S(2)}, u32[]{:S(2)}) async-start(f32[64,1,64]{2,1,0:T(1,128)} %bitcast.37), calls=%async_computation.1 | async-start | bytes 65536 | tf_op jit(solution)/shard_map/all_to_all | solution.py:303
Sparse Core Ops, SparseCore 0:
  10.1 48.6 all-gather.1

commit v11 on v10

--- a/solution.py
+++ b/solution.py
@@ -290,7 +290,7 @@
             lax.ppermute(up[-1], "tensor", along(1)),
             lax.ppermute(down[-1], "tensor", along(-1)),
         )
-        if k == 1:
+        if k == 2:
             *pair, far = lax.optimization_barrier((*pair, far))
         up.append(pair[0])
         down.append(pair[1])

time: 135 us -> 133 us (0.985)
  waiting for transfers between devices: 37.6 us -> 24.3 us
  starting transfers between devices: 38.5 us -> 49.8 us
    ppermute x3, starting transfers between devices: 11.6 us -> 21.1 us  [per_device(): lax.ppermute(down[-1], 'tensor', along(-1))]
    ppermute x1, waiting for transfers between devices: 6.98 us -> 0.01 us  [per_device(): far = lax.ppermute(own, 'tensor', along(N_LINE // 2))]
    ppermute x3, waiting for transfers between devices: 7.98 us -> 2.76 us  [per_device(): lax.ppermute(down[-1], 'tensor', along(-1))]
    all_to_all x1, starting transfers between devices: 7.64 us -> 11.9 us  [per_device(): lax.all_to_all(stats, 'tensor', 0, 0, axis_index_groups=same_core, tiled=...]
    ppermute x3, starting transfers between devices: 9.78 us -> 7.41 us  [per_device(): lax.ppermute(up[-1], 'tensor', along(1))]
  transfers between devices with their start and end apart: 10 -> 10, of which waited for: 6 -> 4; matrix products, arithmetic and copies ran while one was open for 0% -> 0% of each run, Pallas kernels for 8% -> 8%
where the time goes in v11:
time: 133 us; the launch traced here: 132 us
  starting transfers between devices  49.8 us (37%)
  waiting for transfers between devices  24.3 us (18%)
  blocking collectives  24 us (18%)
  Pallas kernels  18.2 us (14%)
  between operations  14.3 us (11%)
    all_to_all x1, blocking collectives, per_device(): lax.all_to_all(block, 'tensor', 0, 0, axis_index_groups=along_z + along_y)  24 us
    ppermute x3, starting transfers between devices, per_device(): lax.ppermute(down[-1], 'tensor', along(-1))  21.1 us
    all_to_all x1, waiting for transfers between devices, per_device(): lax.all_to_all(stats, 'tensor', 0, 0, axis_index_groups=same_core, tiled=...  11.9 us
    all_to_all x1, starting transfers between devices, per_device(): lax.all_to_all(stats, 'tensor', 0, 0, axis_index_groups=same_core, tiled=...  11.9 us
    ppermute x3, waiting for transfers between devices, per_device(): lax.ppermute(up[-1], 'tensor', along(1))  9.02 us
    pallas_call x1, Pallas kernels, run_heads(): pl.pallas_call(early_kernel, in_specs=[smem] + [anywhere] * (N_LINE + 1),...  8.38 us
    pallas_call x1, Pallas kernels, run_heads(): pl.pallas_call(late_kernel, in_specs=[smem] + [anywhere] * 2 + [vmem], ou...  8.02 us
    ppermute x1, starting transfers between devices, per_device(): far = lax.ppermute(own, 'tensor', along(N_LINE // 2))  7.49 us
  transfers between devices with their start and end apart: 10, of which 4 were waited for; matrix products, arithmetic and copies ran while one was open for 0% of the time, Pallas kernels for 8%

profile of v11, /device:TPU:6, one launch (start us, length us, event | category | flops | bytes accessed | tf_op | source)
XLA Modules:
  0.0 132.4 jit_solution(16724052230737510974)
XLA Ops:
  7.2 0.0 all-gather.2.cloned.1.call-start
  7.2 0.7 all-gather.2.cloned.1.call-update
  7.9 1.8 %shard_map.68 = bf16[8,16,2176]{2,1,0:T(8,128)(2,1)} custom-call(bf16[16,2048]{1,0:T(8,128)(2,1)} %hidden_ref.1, f32[1,2048]{1,0:T(1,128)} %bitcast.38, s32[1,16]{1,0:T(1,128)} %bitcast.40), custom_call_target="tpu_custom_call" | custom-call | tf_op jit(solution)/shard_map/pallas_call | solution.py:278
  9.7 24.0 %all_to_all.14 = bf16[8,16,2176]{2,1,0:T(8,128)(2,1)S(1)} all-to-all(bf16[8,16,2176]{2,1,0:T(8,128)(2,1)} %shard_map.68), channel_id=1, replica_groups={{0,16,32,48,64,80,96,112},{2,18,34,50,66,82,98,114},{4,20,36,52,68,84,1..., dimensions={0} | all-to-all | bytes 1114112 | tf_op jit(solution)/shard_map/all_to_all | solution.py:284
  33.7 0.0 copy-start
  33.7 3.5 %collective-permute-start = (bf16[128,2176]{1,0:T(8,128)(2,1)S(1)}, bf16[128,2176]{1,0:T(8,128)(2,1)S(1)}, u32[]{:S(2)}, u32[]{:S(2)}) collective-permute-start(bf16[128,2176]{1,0:T(8,128)(2,1)S(1)} %bitcast.31), channel_id=1, source_target_pairs={{0,2},{1,17},{2,4},{3,19},{4,6},{5,21},{6,8},{7,23},{8,10},{9,25},... | collective-permute-start | bytes 1671176 | tf_op jit(solution)/shard_map/ppermute | solution.py:290
  37.1 3.8 %collective-permute-start.1 = (bf16[128,2176]{1,0:T(8,128)(2,1)S(1)}, bf16[128,2176]{1,0:T(8,128)(2,1)S(1)}, u32[]{:S(2)}, u32[]{:S(2)}) collective-permute-start(bf16[128,2176]{1,0:T(8,128)(2,1)S(1)} %bitcast.32), channel_id=1, source_target_pairs={{0,14},{1,113},{2,0},{3,115},{4,2},{5,117},{6,4},{7,119},{8,6},{9,... | collective-permute-start | bytes 1671176 | tf_op jit(solution)/shard_map/ppermute | solution.py:291
  41.0 5.6 %collective-permute-done.refs_1_ = bf16[128,2176]{1,0:T(8,128)(2,1)S(1)} collective-permute-done((bf16[128,2176]{1,0:T(8,128)(2,1)S(1)}, bf16[128,2176]{1,0:T(8,128)(2,1)S(1)}, u32[]{:S(2)}, u32[]{:S(2)}) %collective-permute-start) | collective-permute-done | bytes 557088 | tf_op jit(solution)/shard_map/ppermute | solution.py:290
  46.5 0.0 copy-start.1
  46.5 2.0 %collective-permute-start.2 = (bf16[128,2176]{1,0:T(8,128)(2,1)S(1)}, bf16[128,2176]{1,0:T(8,128)(2,1)S(1)}, u32[]{:S(2)}, u32[]{:S(2)}) collective-permute-start(bf16[128,2176]{1,0:T(8,128)(2,1)S(1)} %collective-permute-done.refs_1_), channel_id=1, source_target_pairs={{0,2},{1,17},{2,4},{3,19},{4,6},{5,21},{6,8},{7,23},{8,10},{9,25},... | collective-permute-start | bytes 1671176 | tf_op jit(solution)/shard_map/ppermute | solution.py:290
  48.6 0.0 collective-permute-done.1.refs_2_
  48.6 0.0 copy-start.2
  48.6 5.0 %collective-permute-start.3 = (bf16[128,2176]{1,0:T(8,128)(2,1)S(1)}, bf16[128,2176]{1,0:T(8,128)(2,1)S(1)}, u32[]{:S(2)}, u32[]{:S(2)}) collective-permute-start(bf16[128,2176]{1,0:T(8,128)(2,1)S(1)} %collective-permute-done.1.refs_2_), channel_id=1, source_target_pairs={{0,14},{1,113},{2,0},{3,115},{4,2},{5,117},{6,4},{7,119},{8,6},{9,... | collective-permute-start | bytes 1671176 | tf_op jit(solution)/shard_map/ppermute | solution.py:291
  53.6 7.5 %collective-permute-start.6 = (bf16[128,2176]{1,0:T(8,128)(2,1)S(1)}, bf16[128,2176]{1,0:T(8,128)(2,1)S(1)}, u32[]{:S(2)}, u32[]{:S(2)}) collective-permute-start(bf16[128,2176]{1,0:T(8,128)(2,1)S(1)} %bitcast.33), channel_id=1, source_target_pairs={{0,8},{1,65},{2,10},{3,67},{4,12},{5,69},{6,14},{7,71},{8,0},{9,73... | collective-permute-start | bytes 1671176 | tf_op jit(solution)/shard_map/ppermute | solution.py:287
  61.1 0.0 collective-permute-done.2.refs_3_
  61.1 0.0 copy-start.3
  61.1 1.9 %collective-permute-start.4 = (bf16[128,2176]{1,0:T(8,128)(2,1)S(1)}, bf16[128,2176]{1,0:T(8,128)(2,1)S(1)}, u32[]{:S(2)}, u32[]{:S(2)}) collective-permute-start(bf16[128,2176]{1,0:T(8,128)(2,1)S(1)} %collective-permute-done.2.refs_3_), channel_id=1, source_target_pairs={{0,2},{1,17},{2,4},{3,19},{4,6},{5,21},{6,8},{7,23},{8,10},{9,25},... | collective-permute-start | bytes 1671176 | tf_op jit(solution)/shard_map/ppermute | solution.py:290
  63.0 0.0 collective-permute-done.3.refs_4_
  63.1 0.0 copy-start.4
  63.1 12.2 %collective-permute-start.5 = (bf16[128,2176]{1,0:T(8,128)(2,1)S(1)}, bf16[128,2176]{1,0:T(8,128)(2,1)}, u32[]{:S(2)}, u32[]{:S(2)}) collective-permute-start(bf16[128,2176]{1,0:T(8,128)(2,1)S(1)} %collective-permute-done.3.refs_4_), channel_id=1, source_target_pairs={{0,14},{1,113},{2,0},{3,115},{4,2},{5,117},{6,4},{7,119},{8,6},{9,... | collective-permute-start | bytes 1671176 | tf_op jit(solution)/shard_map/ppermute | solution.py:291
  75.3 0.0 collective-permute-done.6.refs_7_
  75.3 0.0 copy-start.5
  75.3 3.5 %collective-permute-done.4.refs_5_ = bf16[128,2176]{1,0:T(8,128)(2,1)S(1)} collective-permute-done((bf16[128,2176]{1,0:T(8,128)(2,1)S(1)}, bf16[128,2176]{1,0:T(8,128)(2,1)S(1)}, u32[]{:S(2)}, u32[]{:S(2)}) %collective-permute-start.4) | collective-permute-done | bytes 557088 | tf_op jit(solution)/shard_map/ppermute | solution.py:290
  78.8 0.0 copy-start.6
  78.8 0.8 copy-done.6
  79.6 2.8 %collective-permute-done.5.refs_6_ = bf16[128,2176]{1,0:T(8,128)(2,1)} collective-permute-done((bf16[128,2176]{1,0:T(8,128)(2,1)S(1)}, bf16[128,2176]{1,0:T(8,128)(2,1)}, u32[]{:S(2)}, u32[]{:S(2)}) %collective-permute-start.5) | collective-permute-done | bytes 557088 | tf_op jit(solution)/shard_map/ppermute | solution.py:291
  82.4 0.0 all-gather.2.cloned.1.call-done
  82.4 1.9 %collective-permute-start.7 = (bf16[800,2048]{1,0:T(8,128)(2,1)}, bf16[800,2048]{1,0:T(8,128)(2,1)}, u32[]{:S(2)}, u32[]{:S(2)}) collective-permute-start(bf16[800,2048]{1,0:T(8,128)(2,1)} %bitcast.29), channel_id=1, source_target_pairs={{0,1},{1,0},{2,3},{3,2},{4,5},{5,4},{6,7},{7,6},{8,9},{9,8},{10,11... | collective-permute-start | bytes 9830408 | tf_op jit(solution)/shard_map/ppermute | solution.py:300
  84.3 0.0 copy-done
  84.3 0.0 copy-done.1
  84.3 0.0 copy-done.2
  84.3 0.0 copy-done.3
  84.3 0.0 copy-done.4
  84.3 0.0 copy-done.5
  84.4 8.4 %shard_map.69 = (f32[8,544]{1,0:T(8,128)}, bf16[34,16,2176]{2,1,0:T(8,128)(2,1)}) custom-call(s32[1,4]{1,0:T(1,128)} %len_ref.3, bf16[128,2176]{1,0:T(8,128)(2,1)} %bitcast.34, bf16[128,2176]{1,0:T(8,128)(2,1)} %copy-done.1, bf16[128,2176]{1,0:T(8,128)(2,1)} %copy-done.2, bf16[128,2176]{1,0:T(8,128)(2,1)} %copy-done.3, bf16[128,2176]{1,0:T(8,128)(2,1)} %copy-done.4, ...), custom_call_target="tpu_custom_call" | custom-call | flops 1782579200 | bytes 5505024 | tf_op jit(solution)/shard_map/pallas_call | solution.py:225
  92.7 0.0 collective-permute-done.7.other_ref
  92.8 0.0 copy-start.7
  92.8 8.0 %shard_map.70 = f32[64,64]{1,0:T(8,128)} custom-call(s32[1,4]{1,0:T(1,128)} %len_ref.3, bf16[34,16,2176]{2,1,0:T(8,128)(2,1)} %get-tuple-element.12.packed_ref, bf16[800,2048]{1,0:T(8,128)(2,1)} %collective-permute-done.7.other_ref, f32[8,544]{1,0:T(8,128)} %get-tuple-element.13.early_ref), custom_call_target="tpu_custom_call" | custom-call | flops 1782579200 | bytes 5505024 | tf_op jit(solution)/shard_map/pallas_call | solution.py:239
  100.8 11.9 %all-to-all-start.1 = ((f32[64,1,64]{2,1,0:T(1,128)}), f32[64,1,64]{2,1,0:T(1,128)S(1)}, u32[]{:S(2)}, u32[]{:S(2)}) async-start(f32[64,1,64]{2,1,0:T(1,128)} %bitcast.37), calls=%async_computation.1 | async-start | bytes 65536 | tf_op jit(solution)/shard_map/all_to_all | solution.py:303
  112.7 0.0 copy-done.7
  112.7 0.1 select_reduce_fusion
  112.7 11.9 %all-to-all-done.1 = f32[64,1,64]{2,1,0:T(1,128)S(1)} async-done(((f32[64,1,64]{2,1,0:T(1,128)}), f32[64,1,64]{2,1,0:T(1,128)S(1)}, u32[]{:S(2)}, u32[]{:S(2)}) %all-to-all-start.1) | async-done | bytes 16416 | tf_op jit(solution)/shard_map/all_to_all | solution.py:303
  124.6 0.1 copy.13
  124.7 0.1 slice_reduce_fusion.1
  124.8 0.2 fusion.1
  125.0 0.5 subtract_select_fusion
  (1 shorter events, 0.0 us)
Async XLA Ops:
  7.2 75.2 %all-gather.2.cloned.1.call-start = ((), (), s32[]{:S(2)}) async-start(), calls=%async_computation.2 | async-start | bytes 4096000 | tf_op jit(solution)/shard_map/all_gather | solution.py:275
  33.7 50.6 %copy-start = (bf16[8,16,2176]{2,1,0:T(8,128)(2,1)}, bf16[8,16,2176]{2,1,0:T(8,128)(2,1)S(1)}, u32[]{:S(2)}) copy-start(bf16[8,16,2176]{2,1,0:T(8,128)(2,1)S(1)} %all_to_all.14) | copy-start | bytes 1671172
  33.7 12.9 %collective-permute-start = (bf16[128,2176]{1,0:T(8,128)(2,1)S(1)}, bf16[128,2176]{1,0:T(8,128)(2,1)S(1)}, u32[]{:S(2)}, u32[]{:S(2)}) collective-permute-start(bf16[128,2176]{1,0:T(8,128)(2,1)S(1)} %bitcast.31), channel_id=1, source_target_pairs={{0,2},{1,17},{2,4},{3,19},{4,6},{5,21},{6,8},{7,23},{8,10},{9,25},... | collective-permute-start | bytes 1671176 | tf_op jit(solution)/shard_map/ppermute | solution.py:290
  37.1 11.4 %collective-permute-start.1 = (bf16[128,2176]{1,0:T(8,128)(2,1)S(1)}, bf16[128,2176]{1,0:T(8,128)(2,1)S(1)}, u32[]{:S(2)}, u32[]{:S(2)}) collective-permute-start(bf16[128,2176]{1,0:T(8,128)(2,1)S(1)} %bitcast.32), channel_id=1, source_target_pairs={{0,14},{1,113},{2,0},{3,115},{4,2},{5,117},{6,4},{7,119},{8,6},{9,... | collective-permute-start | bytes 1671176 | tf_op jit(solution)/shard_map/ppermute | solution.py:291
  46.5 37.8 %copy-start.1 = (bf16[128,2176]{1,0:T(8,128)(2,1)}, bf16[128,2176]{1,0:T(8,128)(2,1)S(1)}, u32[]{:S(2)}) copy-start(bf16[128,2176]{1,0:T(8,128)(2,1)S(1)} %collective-permute-done.refs_1_) | copy-start | bytes 1671172
  46.5 14.6 %collective-permute-start.2 = (bf16[128,2176]{1,0:T(8,128)(2,1)S(1)}, bf16[128,2176]{1,0:T(8,128)(2,1)S(1)}, u32[]{:S(2)}, u32[]{:S(2)}) collective-permute-start(bf16[128,2176]{1,0:T(8,128)(2,1)S(1)} %collective-permute-done.refs_1_), channel_id=1, source_target_pairs={{0,2},{1,17},{2,4},{3,19},{4,6},{5,21},{6,8},{7,23},{8,10},{9,25},... | collective-permute-start | bytes 1671176 | tf_op jit(solution)/shard_map/ppermute | solution.py:290
  48.6 35.8 %copy-start.2 = (bf16[128,2176]{1,0:T(8,128)(2,1)}, bf16[128,2176]{1,0:T(8,128)(2,1)S(1)}, u32[]{:S(2)}) copy-start(bf16[128,2176]{1,0:T(8,128)(2,1)S(1)} %collective-permute-done.1.refs_2_) | copy-start | bytes 1671172
  48.6 14.5 %collective-permute-start.3 = (bf16[128,2176]{1,0:T(8,128)(2,1)S(1)}, bf16[128,2176]{1,0:T(8,128)(2,1)S(1)}, u32[]{:S(2)}, u32[]{:S(2)}) collective-permute-start(bf16[128,2176]{1,0:T(8,128)(2,1)S(1)} %collective-permute-done.1.refs_2_), channel_id=1, source_target_pairs={{0,14},{1,113},{2,0},{3,115},{4,2},{5,117},{6,4},{7,119},{8,6},{9,... | collective-permute-start | bytes 1671176 | tf_op jit(solution)/shard_map/ppermute | solution.py:291
  53.6 21.7 %collective-permute-start.6 = (bf16[128,2176]{1,0:T(8,128)(2,1)S(1)}, bf16[128,2176]{1,0:T(8,128)(2,1)S(1)}, u32[]{:S(2)}, u32[]{:S(2)}) collective-permute-start(bf16[128,2176]{1,0:T(8,128)(2,1)S(1)} %bitcast.33), channel_id=1, source_target_pairs={{0,8},{1,65},{2,10},{3,67},{4,12},{5,69},{6,14},{7,71},{8,0},{9,73... | collective-permute-start | bytes 1671176 | tf_op jit(solution)/shard_map/ppermute | solution.py:287
  61.1 23.2 %copy-start.3 = (bf16[128,2176]{1,0:T(8,128)(2,1)}, bf16[128,2176]{1,0:T(8,128)(2,1)S(1)}, u32[]{:S(2)}) copy-start(bf16[128,2176]{1,0:T(8,128)(2,1)S(1)} %collective-permute-done.2.refs_3_) | copy-start | bytes 1671172
  61.1 17.7 %collective-permute-start.4 = (bf16[128,2176]{1,0:T(8,128)(2,1)S(1)}, bf16[128,2176]{1,0:T(8,128)(2,1)S(1)}, u32[]{:S(2)}, u32[]{:S(2)}) collective-permute-start(bf16[128,2176]{1,0:T(8,128)(2,1)S(1)} %collective-permute-done.2.refs_3_), channel_id=1, source_target_pairs={{0,2},{1,17},{2,4},{3,19},{4,6},{5,21},{6,8},{7,23},{8,10},{9,25},... | collective-permute-start | bytes 1671176 | tf_op jit(solution)/shard_map/ppermute | solution.py:290
  63.1 21.3 %copy-start.4 = (bf16[128,2176]{1,0:T(8,128)(2,1)}, bf16[128,2176]{1,0:T(8,128)(2,1)S(1)}, u32[]{:S(2)}) copy-start(bf16[128,2176]{1,0:T(8,128)(2,1)S(1)} %collective-permute-done.3.refs_4_) | copy-start | bytes 1671172
  63.1 19.3 %collective-permute-start.5 = (bf16[128,2176]{1,0:T(8,128)(2,1)S(1)}, bf16[128,2176]{1,0:T(8,128)(2,1)}, u32[]{:S(2)}, u32[]{:S(2)}) collective-permute-start(bf16[128,2176]{1,0:T(8,128)(2,1)S(1)} %collective-permute-done.3.refs_4_), channel_id=1, source_target_pairs={{0,14},{1,113},{2,0},{3,115},{4,2},{5,117},{6,4},{7,119},{8,6},{9,... | collective-permute-start | bytes 1671176 | tf_op jit(solution)/shard_map/ppermute | solution.py:291
  75.3 9.0 %copy-start.5 = (bf16[128,2176]{1,0:T(8,128)(2,1)}, bf16[128,2176]{1,0:T(8,128)(2,1)S(1)}, u32[]{:S(2)}) copy-start(bf16[128,2176]{1,0:T(8,128)(2,1)S(1)} %collective-permute-done.6.refs_7_) | copy-start | bytes 1671172
  78.8 0.8 copy-start.6
  82.4 10.4 %collective-permute-start.7 = (bf16[800,2048]{1,0:T(8,128)(2,1)}, bf16[800,2048]{1,0:T(8,128)(2,1)}, u32[]{:S(2)}, u32[]{:S(2)}) collective-permute-start(bf16[800,2048]{1,0:T(8,128)(2,1)} %bitcast.29), channel_id=1, source_target_pairs={{0,1},{1,0},{2,3},{3,2},{4,5},{5,4},{6,7},{7,6},{8,9},{9,8},{10,11... | collective-permute-start | bytes 9830408 | tf_op jit(solution)/shard_map/ppermute | solution.py:300
  92.8 19.9 %copy-start.7 = (s32[1,4]{1,0:T(1,128)S(1)}, s32[1,4]{1,0:T(1,128)}, u32[]{:S(2)}) copy-start(s32[1,4]{1,0:T(1,128)} %len_ref.3) | copy-start | bytes 52
  100.8 23.8 %all-to-all-start.1 = ((f32[64,1,64]{2,1,0:T(1,128)}), f32[64,1,64]{2,1,0:T(1,128)S(1)}, u32[]{:S(2)}, u32[]{:S(2)}) async-start(f32[64,1,64]{2,1,0:T(1,128)} %bitcast.37), calls=%async_computation.1 | async-start | bytes 65536 | tf_op jit(solution)/shard_map/all_to_all | solution.py:303
Sparse Core Ops, SparseCore 0:
  10.1 48.6 all-gather.1

commit v12 on v9

--- a/solution.py
+++ b/solution.py
@@ -135,21 +135,25 @@
     n = owner.shape[1]
     chips = N_LINE * N_LINE
     here = owner == lax.broadcasted_iota(jnp.int32, (chips, n), 0)
+    here = jnp.where(here, 1.0, 0.0).astype(jnp.bfloat16)
+    spot = lax.broadcasted_iota(jnp.int32, (BLOCK, n), 1) & (BLOCK - 1)
+    spot = spot == lax.broadcasted_iota(jnp.int32, (BLOCK, n), 0)
+    stats = tuple(jnp.where(owner >= 0, stat, 0.0) for stat in stats)
     rows = []
-    for stat in stats:
-        for _ in range(3):
+    for _ in range(3):
+        for k, stat in enumerate(stats):
             part = stat.astype(jnp.bfloat16).astype(jnp.float32)
-            rows.append(jnp.where(here, part, 0.0).astype(jnp.bfloat16))
-            stat = stat - part
-    place = lax.broadcasted_iota(jnp.int32, (n, BLOCK), 0) % BLOCK
-    spot = jnp.where(place == lax.broadcasted_iota(jnp.int32, (n, BLOCK), 1), 1.0, 0.0)
-    moved = jnp.dot(
+            rows.append(jnp.where(spot, part, 0.0).astype(jnp.bfloat16))
+            stats = stats[:k] + (stat - part,) + stats[k + 1 :]
+    moved = lax.dot_general(
         jnp.concatenate(rows, axis=0),
-        spot.astype(jnp.bfloat16),
+        here,
+        (((1,), (1,)), ((), ())),
         preferred_element_type=jnp.float32,
-    ).reshape(STATS, 3, chips, BLOCK)
-    moved = moved[:, 0] + moved[:, 1] + moved[:, 2]
-    return [moved[k] for k in range(STATS)]
+    )
+    n = STATS * BLOCK
+    moved = jnp.transpose(moved[:n] + moved[n : 2 * n] + moved[2 * n :])
+    return [moved[:, k * BLOCK : (k + 1) * BLOCK] for k in range(STATS)]
 
 
 def early_kernel(len_ref, *refs):
@@ -204,7 +208,7 @@
     each = block_copies(len_ref, OFFSETS[-1:], [line_ref], x_ref, sem)
     each(lambda copy: copy.start())
     each(lambda copy: copy.wait())
-    for copy in other[1:] + own:
+    for copy in other[1:]:
         copy.start()
 
     n = LIVE * BLOCK
@@ -225,6 +229,7 @@
     ]
     for i, copy in enumerate(other):
         copy.wait()
+        own[i].start()
         parts.append(tile_stats(w_ref[i], x, ids - i * TILE))
     most = to_owners(merge(parts), owner)
 

time: 130 us -> 131 us (level)
  no operation moved by 1% of the time
where the time goes in v12:
time: 131 us; the launch traced here: 130 us
  starting transfers between devices  34.5 us (26%)
  waiting for transfers between devices  31.8 us (24%)
  blocking collectives  24 us (18%)
  Pallas kernels  21.7 us (17%)
  between operations  14.2 us (11%)
  local copies, waits for them, and re-layouts  2.67 us (2%)
    all_to_all x1, blocking collectives, per_device(): lax.all_to_all(block, 'tensor', 0, 0, axis_index_groups=along_z + along_y)  24 us
    ppermute x4, waiting for transfers between devices, per_device(): up.append(lax.ppermute(up[-1], 'tensor', along(1)))  18.5 us
    ppermute x3, starting transfers between devices, per_device(): down.append(lax.ppermute(down[-1], 'tensor', along(-1)))  14 us
    all_to_all x1, waiting for transfers between devices, per_device(): lax.all_to_all(stats, 'tensor', 0, 0, axis_index_groups=same_core, tiled=...  11.9 us
    pallas_call x1, Pallas kernels, run_heads(): pl.pallas_call(late_kernel, in_specs=[smem] + [anywhere] * 4 + [vmem], ou...  11.6 us
    ppermute x4, starting transfers between devices, per_device(): up.append(lax.ppermute(up[-1], 'tensor', along(1)))  10.7 us
    pallas_call x1, Pallas kernels, run_heads(): pl.pallas_call(early_kernel, in_specs=[smem] + [anywhere] * N_LINE, out_s...  8.29 us
    all_to_all x1, starting transfers between devices, per_device(): lax.all_to_all(stats, 'tensor', 0, 0, axis_index_groups=same_core, tiled=...  7.92 us
  transfers between devices with their start and end apart: 10, of which 6 were waited for; matrix products, arithmetic and copies ran while one was open for 0% of the time, Pallas kernels for 8%

profile of v12, /device:TPU:6, one launch (start us, length us, event | category | flops | bytes accessed | tf_op | source)
XLA Modules:
  0.0 129.8 jit_solution(15488907098022112398)
XLA Ops:
  7.2 0.0 all-gather.2.cloned.1.call-start
  7.2 0.7 all-gather.2.cloned.1.call-update
  7.9 1.8 %shard_map.68 = bf16[8,16,2176]{2,1,0:T(8,128)(2,1)} custom-call(bf16[16,2048]{1,0:T(8,128)(2,1)} %hidden_ref.1, f32[1,2048]{1,0:T(1,128)} %bitcast.38, s32[1,16]{1,0:T(1,128)} %bitcast.40), custom_call_target="tpu_custom_call" | custom-call | tf_op jit(solution)/shard_map/pallas_call | solution.py:318
  9.7 24.0 %all_to_all.14 = bf16[8,16,2176]{2,1,0:T(8,128)(2,1)S(1)} all-to-all(bf16[8,16,2176]{2,1,0:T(8,128)(2,1)} %shard_map.68), channel_id=1, replica_groups={{0,16,32,48,64,80,96,112},{2,18,34,50,66,82,98,114},{4,20,36,52,68,84,1..., dimensions={0} | all-to-all | bytes 1114112 | tf_op jit(solution)/shard_map/all_to_all | solution.py:324
  33.7 0.0 copy-start.1
  33.7 3.5 %collective-permute-start = (bf16[128,2176]{1,0:T(8,128)(2,1)S(1)}, bf16[128,2176]{1,0:T(8,128)(2,1)S(1)}, u32[]{:S(2)}, u32[]{:S(2)}) collective-permute-start(bf16[128,2176]{1,0:T(8,128)(2,1)S(1)} %bitcast.32), channel_id=1, source_target_pairs={{0,2},{1,17},{2,4},{3,19},{4,6},{5,21},{6,8},{7,23},{8,10},{9,25},... | collective-permute-start | bytes 1671176 | tf_op jit(solution)/shard_map/ppermute | solution.py:328
  37.1 0.0 copy-done.1
  37.1 3.8 %collective-permute-start.1 = (bf16[128,2176]{1,0:T(8,128)(2,1)S(1)}, bf16[128,2176]{1,0:T(8,128)(2,1)S(1)}, u32[]{:S(2)}, u32[]{:S(2)}) collective-permute-start(bf16[128,2176]{1,0:T(8,128)(2,1)S(1)} %bitcast.33), channel_id=1, source_target_pairs={{0,14},{1,113},{2,0},{3,115},{4,2},{5,117},{6,4},{7,119},{8,6},{9,... | collective-permute-start | bytes 1671176 | tf_op jit(solution)/shard_map/ppermute | solution.py:329
  41.0 5.6 %collective-permute-done.refs_1_ = bf16[128,2176]{1,0:T(8,128)(2,1)S(1)} collective-permute-done((bf16[128,2176]{1,0:T(8,128)(2,1)S(1)}, bf16[128,2176]{1,0:T(8,128)(2,1)S(1)}, u32[]{:S(2)}, u32[]{:S(2)}) %collective-permute-start) | collective-permute-done | bytes 557088 | tf_op jit(solution)/shard_map/ppermute | solution.py:328
  46.5 0.0 copy-start.2
  46.5 2.0 %collective-permute-start.2 = (bf16[128,2176]{1,0:T(8,128)(2,1)S(1)}, bf16[128,2176]{1,0:T(8,128)(2,1)S(1)}, u32[]{:S(2)}, u32[]{:S(2)}) collective-permute-start(bf16[128,2176]{1,0:T(8,128)(2,1)S(1)} %collective-permute-done.refs_1_), channel_id=1, source_target_pairs={{0,2},{1,17},{2,4},{3,19},{4,6},{5,21},{6,8},{7,23},{8,10},{9,25},... | collective-permute-start | bytes 1671176 | tf_op jit(solution)/shard_map/ppermute | solution.py:328
  48.6 0.0 collective-permute-done.1.refs_2_
  48.6 0.0 copy-done.2
  48.6 0.0 copy-start.3
  48.6 5.0 %collective-permute-start.3 = (bf16[128,2176]{1,0:T(8,128)(2,1)S(1)}, bf16[128,2176]{1,0:T(8,128)(2,1)S(1)}, u32[]{:S(2)}, u32[]{:S(2)}) collective-permute-start(bf16[128,2176]{1,0:T(8,128)(2,1)S(1)} %collective-permute-done.1.refs_2_), channel_id=1, source_target_pairs={{0,14},{1,113},{2,0},{3,115},{4,2},{5,117},{6,4},{7,119},{8,6},{9,... | collective-permute-start | bytes 1671176 | tf_op jit(solution)/shard_map/ppermute | solution.py:329
  53.6 5.5 %collective-permute-done.2.refs_3_ = bf16[128,2176]{1,0:T(8,128)(2,1)S(1)} collective-permute-done((bf16[128,2176]{1,0:T(8,128)(2,1)S(1)}, bf16[128,2176]{1,0:T(8,128)(2,1)S(1)}, u32[]{:S(2)}, u32[]{:S(2)}) %collective-permute-start.2) | collective-permute-done | bytes 557088 | tf_op jit(solution)/shard_map/ppermute | solution.py:328
  59.2 0.0 copy-done.3
  59.2 0.0 copy-start.4
  59.2 1.9 %collective-permute-start.4 = (bf16[128,2176]{1,0:T(8,128)(2,1)S(1)}, bf16[128,2176]{1,0:T(8,128)(2,1)S(1)}, u32[]{:S(2)}, u32[]{:S(2)}) collective-permute-start(bf16[128,2176]{1,0:T(8,128)(2,1)S(1)} %collective-permute-done.2.refs_3_), channel_id=1, source_target_pairs={{0,2},{1,17},{2,4},{3,19},{4,6},{5,21},{6,8},{7,23},{8,10},{9,25},... | collective-permute-start | bytes 1671176 | tf_op jit(solution)/shard_map/ppermute | solution.py:328
  61.1 0.0 collective-permute-done.3.refs_4_
  61.1 0.0 copy-done.4
  61.1 0.0 copy-start.5
  61.1 5.1 %collective-permute-start.5 = (bf16[128,2176]{1,0:T(8,128)(2,1)S(1)}, bf16[128,2176]{1,0:T(8,128)(2,1)}, u32[]{:S(2)}, u32[]{:S(2)}) collective-permute-start(bf16[128,2176]{1,0:T(8,128)(2,1)S(1)} %collective-permute-done.3.refs_4_), channel_id=1, source_target_pairs={{0,14},{1,113},{2,0},{3,115},{4,2},{5,117},{6,4},{7,119},{8,6},{9,... | collective-permute-start | bytes 1671176 | tf_op jit(solution)/shard_map/ppermute | solution.py:329
  66.2 5.5 %collective-permute-done.4.refs_5_ = bf16[128,2176]{1,0:T(8,128)(2,1)S(1)} collective-permute-done((bf16[128,2176]{1,0:T(8,128)(2,1)S(1)}, bf16[128,2176]{1,0:T(8,128)(2,1)S(1)}, u32[]{:S(2)}, u32[]{:S(2)}) %collective-permute-start.4) | collective-permute-done | bytes 557088 | tf_op jit(solution)/shard_map/ppermute | solution.py:328
  71.8 0.0 copy-done.5
  71.8 0.0 copy-start.6
  71.8 0.8 copy-done.6
  72.6 0.7 collective-permute-done.5.refs_6_
  73.3 0.0 all-gather.2.cloned.1.call-done
  73.3 1.9 %collective-permute-start.7 = (bf16[800,2048]{1,0:T(8,128)(2,1)}, bf16[800,2048]{1,0:T(8,128)(2,1)S(1)}, u32[]{:S(2)}, u32[]{:S(2)}) collective-permute-start(bf16[800,2048]{1,0:T(8,128)(2,1)} %bitcast.29), channel_id=1, source_target_pairs={{0,1},{1,0},{2,3},{3,2},{4,5},{5,4},{6,7},{7,6},{8,9},{9,8},{10,11... | collective-permute-start | bytes 9830408 | tf_op jit(solution)/shard_map/ppermute | solution.py:334
  75.2 3.3 %collective-permute-start.6 = (bf16[128,2176]{1,0:T(8,128)(2,1)}, bf16[128,2176]{1,0:T(8,128)(2,1)}, u32[]{:S(2)}, u32[]{:S(2)}) collective-permute-start(bf16[128,2176]{1,0:T(8,128)(2,1)} %copy-done.6), channel_id=1, source_target_pairs={{0,2},{1,17},{2,4},{3,19},{4,6},{5,21},{6,8},{7,23},{8,10},{9,25},... | collective-permute-start | bytes 1671176 | tf_op jit(solution)/shard_map/ppermute | solution.py:330
  78.5 8.3 %shard_map.69 = (f32[8,544]{1,0:T(8,128)}, bf16[34,16,2176]{2,1,0:T(8,128)(2,1)}) custom-call(s32[1,4]{1,0:T(1,128)} %len_ref.3, bf16[128,2176]{1,0:T(8,128)(2,1)} %bitcast.34, bf16[128,2176]{1,0:T(8,128)(2,1)} %copy-done.2, bf16[128,2176]{1,0:T(8,128)(2,1)} %copy-done.3, bf16[128,2176]{1,0:T(8,128)(2,1)} %copy-done.4, bf16[128,2176]{1,0:T(8,128)(2,1)} %copy-done.5, ...), custom_call_target="tpu_custom_call" | custom-call | flops 1782579200 | bytes 5505024 | tf_op jit(solution)/shard_map/pallas_call | solution.py:264
  86.8 1.9 %collective-permute-done.6.line_ref = bf16[128,2176]{1,0:T(8,128)(2,1)} collective-permute-done((bf16[128,2176]{1,0:T(8,128)(2,1)}, bf16[128,2176]{1,0:T(8,128)(2,1)}, u32[]{:S(2)}, u32[]{:S(2)}) %collective-permute-start.6) | collective-permute-done | bytes 557088 | tf_op jit(solution)/shard_map/ppermute | solution.py:330
  88.7 0.0 collective-permute-done.7.other_ref
  88.7 0.0 copy-start
  88.7 1.8 %copy-done = bf16[800,2048]{1,0:T(8,128)(2,1)} copy-done((bf16[800,2048]{1,0:T(8,128)(2,1)}, bf16[800,2048]{1,0:T(8,128)(2,1)S(1)}, u32[]{:S(2)}) %copy-start) | copy-done | bytes 3276824
  90.5 0.0 copy-start.7
  90.5 11.6 %shard_map.70 = f32[64,64]{1,0:T(8,128)} custom-call(s32[1,4]{1,0:T(1,128)} %len_ref.3, bf16[34,16,2176]{2,1,0:T(8,128)(2,1)} %get-tuple-element.6.packed_ref, bf16[128,2176]{1,0:T(8,128)(2,1)} %collective-permute-done.6.line_ref, bf16[800,2048]{1,0:T(8,128)(2,1)} %bitcast.31, bf16[800,2048]{1,0:T(8,128)(2,1)} %copy-done, f32[8,544]{1,0:T(8,128)} %get-tuple-element.7.early_ref), custom_call_target="tpu_custom_call" | custom-call | flops 1782579200 | bytes 5505024 | tf_op jit(solution)/shard_map/pallas_call | solution.py:278
  102.1 7.9 %all-to-all-start.1 = ((f32[64,1,64]{2,1,0:T(1,128)}), f32[64,1,64]{2,1,0:T(1,128)S(1)}, u32[]{:S(2)}, u32[]{:S(2)}) async-start(f32[64,1,64]{2,1,0:T(1,128)} %bitcast.37), calls=%async_computation.1 | async-start | bytes 65536 | tf_op jit(solution)/shard_map/all_to_all | solution.py:337
  110.0 0.0 copy-done.7
  110.0 0.1 select_reduce_fusion
  110.1 11.9 %all-to-all-done.1 = f32[64,1,64]{2,1,0:T(1,128)S(1)} async-done(((f32[64,1,64]{2,1,0:T(1,128)}), f32[64,1,64]{2,1,0:T(1,128)S(1)}, u32[]{:S(2)}, u32[]{:S(2)}) %all-to-all-start.1) | async-done | bytes 16416 | tf_op jit(solution)/shard_map/all_to_all | solution.py:337
  122.0 0.1 copy.13
  122.1 0.1 slice_reduce_fusion.1
  122.2 0.2 fusion.1
  122.4 0.5 subtract_select_fusion
  (1 shorter events, 0.0 us)
Async XLA Ops:
  7.2 66.1 %all-gather.2.cloned.1.call-start = ((), (), s32[]{:S(2)}) async-start(), calls=%async_computation.2 | async-start | bytes 4096000 | tf_op jit(solution)/shard_map/all_gather | solution.py:315
  33.7 3.5 %copy-start.1 = (bf16[8,16,2176]{2,1,0:T(8,128)(2,1)}, bf16[8,16,2176]{2,1,0:T(8,128)(2,1)S(1)}, u32[]{:S(2)}) copy-start(bf16[8,16,2176]{2,1,0:T(8,128)(2,1)S(1)} %all_to_all.14) | copy-start | bytes 1671172
  33.7 12.9 %collective-permute-start = (bf16[128,2176]{1,0:T(8,128)(2,1)S(1)}, bf16[128,2176]{1,0:T(8,128)(2,1)S(1)}, u32[]{:S(2)}, u32[]{:S(2)}) collective-permute-start(bf16[128,2176]{1,0:T(8,128)(2,1)S(1)} %bitcast.32), channel_id=1, source_target_pairs={{0,2},{1,17},{2,4},{3,19},{4,6},{5,21},{6,8},{7,23},{8,10},{9,25},... | collective-permute-start | bytes 1671176 | tf_op jit(solution)/shard_map/ppermute | solution.py:328
  37.1 11.4 %collective-permute-start.1 = (bf16[128,2176]{1,0:T(8,128)(2,1)S(1)}, bf16[128,2176]{1,0:T(8,128)(2,1)S(1)}, u32[]{:S(2)}, u32[]{:S(2)}) collective-permute-start(bf16[128,2176]{1,0:T(8,128)(2,1)S(1)} %bitcast.33), channel_id=1, source_target_pairs={{0,14},{1,113},{2,0},{3,115},{4,2},{5,117},{6,4},{7,119},{8,6},{9,... | collective-permute-start | bytes 1671176 | tf_op jit(solution)/shard_map/ppermute | solution.py:329
  46.5 2.0 %copy-start.2 = (bf16[128,2176]{1,0:T(8,128)(2,1)}, bf16[128,2176]{1,0:T(8,128)(2,1)S(1)}, u32[]{:S(2)}) copy-start(bf16[128,2176]{1,0:T(8,128)(2,1)S(1)} %collective-permute-done.refs_1_) | copy-start | bytes 1671172
  46.5 12.6 %collective-permute-start.2 = (bf16[128,2176]{1,0:T(8,128)(2,1)S(1)}, bf16[128,2176]{1,0:T(8,128)(2,1)S(1)}, u32[]{:S(2)}, u32[]{:S(2)}) collective-permute-start(bf16[128,2176]{1,0:T(8,128)(2,1)S(1)} %collective-permute-done.refs_1_), channel_id=1, source_target_pairs={{0,2},{1,17},{2,4},{3,19},{4,6},{5,21},{6,8},{7,23},{8,10},{9,25},... | collective-permute-start | bytes 1671176 | tf_op jit(solution)/shard_map/ppermute | solution.py:328
  48.6 10.6 %copy-start.3 = (bf16[128,2176]{1,0:T(8,128)(2,1)}, bf16[128,2176]{1,0:T(8,128)(2,1)S(1)}, u32[]{:S(2)}) copy-start(bf16[128,2176]{1,0:T(8,128)(2,1)S(1)} %collective-permute-done.1.refs_2_) | copy-start | bytes 1671172
  48.6 12.5 %collective-permute-start.3 = (bf16[128,2176]{1,0:T(8,128)(2,1)S(1)}, bf16[128,2176]{1,0:T(8,128)(2,1)S(1)}, u32[]{:S(2)}, u32[]{:S(2)}) collective-permute-start(bf16[128,2176]{1,0:T(8,128)(2,1)S(1)} %collective-permute-done.1.refs_2_), channel_id=1, source_target_pairs={{0,14},{1,113},{2,0},{3,115},{4,2},{5,117},{6,4},{7,119},{8,6},{9,... | collective-permute-start | bytes 1671176 | tf_op jit(solution)/shard_map/ppermute | solution.py:329
  59.2 1.9 %copy-start.4 = (bf16[128,2176]{1,0:T(8,128)(2,1)}, bf16[128,2176]{1,0:T(8,128)(2,1)S(1)}, u32[]{:S(2)}) copy-start(bf16[128,2176]{1,0:T(8,128)(2,1)S(1)} %collective-permute-done.2.refs_3_) | copy-start | bytes 1671172
  59.2 12.6 %collective-permute-start.4 = (bf16[128,2176]{1,0:T(8,128)(2,1)S(1)}, bf16[128,2176]{1,0:T(8,128)(2,1)S(1)}, u32[]{:S(2)}, u32[]{:S(2)}) collective-permute-start(bf16[128,2176]{1,0:T(8,128)(2,1)S(1)} %collective-permute-done.2.refs_3_), channel_id=1, source_target_pairs={{0,2},{1,17},{2,4},{3,19},{4,6},{5,21},{6,8},{7,23},{8,10},{9,25},... | collective-permute-start | bytes 1671176 | tf_op jit(solution)/shard_map/ppermute | solution.py:328
  61.1 10.7 %copy-start.5 = (bf16[128,2176]{1,0:T(8,128)(2,1)}, bf16[128,2176]{1,0:T(8,128)(2,1)S(1)}, u32[]{:S(2)}) copy-start(bf16[128,2176]{1,0:T(8,128)(2,1)S(1)} %collective-permute-done.3.refs_4_) | copy-start | bytes 1671172
  61.1 12.2 %collective-permute-start.5 = (bf16[128,2176]{1,0:T(8,128)(2,1)S(1)}, bf16[128,2176]{1,0:T(8,128)(2,1)}, u32[]{:S(2)}, u32[]{:S(2)}) collective-permute-start(bf16[128,2176]{1,0:T(8,128)(2,1)S(1)} %collective-permute-done.3.refs_4_), channel_id=1, source_target_pairs={{0,14},{1,113},{2,0},{3,115},{4,2},{5,117},{6,4},{7,119},{8,6},{9,... | collective-permute-start | bytes 1671176 | tf_op jit(solution)/shard_map/ppermute | solution.py:329
  71.8 0.8 copy-start.6
  73.3 15.4 %collective-permute-start.7 = (bf16[800,2048]{1,0:T(8,128)(2,1)}, bf16[800,2048]{1,0:T(8,128)(2,1)S(1)}, u32[]{:S(2)}, u32[]{:S(2)}) collective-permute-start(bf16[800,2048]{1,0:T(8,128)(2,1)} %bitcast.29), channel_id=1, source_target_pairs={{0,1},{1,0},{2,3},{3,2},{4,5},{5,4},{6,7},{7,6},{8,9},{9,8},{10,11... | collective-permute-start | bytes 9830408 | tf_op jit(solution)/shard_map/ppermute | solution.py:334
  75.2 13.5 %collective-permute-start.6 = (bf16[128,2176]{1,0:T(8,128)(2,1)}, bf16[128,2176]{1,0:T(8,128)(2,1)}, u32[]{:S(2)}, u32[]{:S(2)}) collective-permute-start(bf16[128,2176]{1,0:T(8,128)(2,1)} %copy-done.6), channel_id=1, source_target_pairs={{0,2},{1,17},{2,4},{3,19},{4,6},{5,21},{6,8},{7,23},{8,10},{9,25},... | collective-permute-start | bytes 1671176 | tf_op jit(solution)/shard_map/ppermute | solution.py:330
  88.7 1.8 %copy-start = (bf16[800,2048]{1,0:T(8,128)(2,1)}, bf16[800,2048]{1,0:T(8,128)(2,1)S(1)}, u32[]{:S(2)}) copy-start(bf16[800,2048]{1,0:T(8,128)(2,1)S(1)} %collective-permute-done.7.other_ref) | copy-start | bytes 9830404
  90.5 19.6 %copy-start.7 = (s32[1,4]{1,0:T(1,128)S(1)}, s32[1,4]{1,0:T(1,128)}, u32[]{:S(2)}) copy-start(s32[1,4]{1,0:T(1,128)} %len_ref.3) | copy-start | bytes 52
  102.1 19.9 %all-to-all-start.1 = ((f32[64,1,64]{2,1,0:T(1,128)}), f32[64,1,64]{2,1,0:T(1,128)S(1)}, u32[]{:S(2)}, u32[]{:S(2)}) async-start(f32[64,1,64]{2,1,0:T(1,128)} %bitcast.37), calls=%async_computation.1 | async-start | bytes 65536 | tf_op jit(solution)/shard_map/all_to_all | solution.py:337
Sparse Core Ops, SparseCore 0:
  10.1 48.6 all-gather.1
